TPU v7x, 32 devices: a whole 2x2x4 slice. The times are simulated.
32 devices in a mesh: dp: 8 (over z, x), tensor: 4 (over y, core).
Axes of the slice: x: 2, y: 2, z: 4, core: 2. Of those that a mesh axis runs over, the one named last changes fastest.
Arguments:
- tokens: bfloat16 [24, 512, 768], P('dp', None, 'tensor'), may hold values from -6 to 6
- cotangent: bfloat16 [24, 512, 768], P('dp', None, 'tensor'), may hold values from -6 to 6
- prev_logits: bfloat16 [24, 12, 512, 512], P('dp', 'tensor'), may hold values from -6 to 6
- segment_ids: int32 [24, 512], P('dp'), may hold values from 0 to 5, never falling along the last dimension, each value on 1 to 256 neighbouring positions
- w_qkv: float32 [768, 3, 768], P('dp', None, 'tensor'), may hold values from -0.21875 to 0.21875
- b_qv: float32 [2, 768], P(None, 'tensor'), may hold values from -3 to 3
- w_out: float32 [768, 768], P('tensor', 'dp'), may hold values from -0.625 to 0.625
- w_up: float32 [768, 3072], P('dp', 'tensor'), may hold values from -0.21875 to 0.21875
- b_up: float32 [3072], P('tensor'), may hold values from -3 to 3
- w_down: float32 [3072, 768], P('tensor', 'dp'), may hold values from -0.109375 to 0.109375
- biases: float32 [2, 768], replicated, may hold values from -3 to 3
- gains: float32 [2, 768], replicated, may hold values from 0.25 to 1.75
- shifts: float32 [2, 768], replicated, may hold values from -3 to 3
Outputs:
- activations: bfloat16 [24, 512, 768], P('dp', None, 'tensor')
- raw_logits: bfloat16 [24, 12, 512, 512], P('dp', 'tensor')
- input_grad: bfloat16 [24, 512, 768], P('dp', None, 'tensor')
- logits_grad: bfloat16 [24, 12, 512, 512], P('dp', 'tensor')
- grad_qkv: float32 [768, 3, 768], P(None, None, 'tensor')
- grad_b_qv: float32 [2, 768], P(None, 'tensor')
- grad_out: float32 [768, 768], P('tensor')
- grad_up: float32 [768, 3072], P(None, 'tensor')
- grad_b_up: float32 [3072], P('tensor')
- grad_down: float32 [3072, 768], P('tensor')
- grad_biases: float32 [2, 768], replicated
- grad_gains: float32 [2, 768], replicated
- grad_shifts: float32 [2, 768], replicated
Inputs may be any that keep to these rules, and one draw needn't show every extreme that they name: `segment_ids`: in each row the segment number never falls; each segment has 1 to 256 slots and one has exactly that many; a query attends only to keys of its own segment.
All inputs are finite; a program needn't handle non-finite values.
Results may differ from a plain program's by a relative error of at most 0.02.
Values may be sent and summed in bfloat16 or wider, within the bound.
No kernel may reach another device: no remote copies, remote signals or barrier semaphores. Data moves between devices by JAX's collectives and lax.ppermute only.
A program may use at most 192 MiB of HBM per device.

v0:
```python
import math

import jax
import jax.numpy as jnp
from jax import lax
from jax.sharding import PartitionSpec as P

EPS = 1e-06
NEG = -1e30


def gelu_exact(values):
    return jax.nn.gelu(values, approximate=False)


def norm_forward(summed, gain_row, shift_row):
    row_mean = jnp.mean(summed, axis=-1, keepdims=True)
    centered = summed - row_mean
    inv_std = lax.rsqrt(jnp.mean(centered * centered, axis=-1, keepdims=True) + EPS)
    normed = centered * inv_std
    return (normed * gain_row + shift_row, normed, inv_std)


def norm_backward(grad_output, normed, inv_std, gain_row):
    scaled = grad_output * gain_row
    inner = (
        scaled
        - jnp.mean(scaled, axis=-1, keepdims=True)
        - normed * jnp.mean(scaled * normed, axis=-1, keepdims=True)
    )
    return inner * inv_std


def branch_total(partial_value):
    return lax.psum(partial_value.astype(jnp.bfloat16), "tensor").astype(jnp.float32)


def attend_rows(query, keys, values, previous, segment, inv_root):
    allowed = (segment[:, None] == segment[None, :])[None]
    scores = jnp.einsum(
        "qhe,khe->hqk", query, keys, preferred_element_type=jnp.float32
    ) * inv_root + previous.astype(jnp.float32)
    masked = jnp.where(allowed, scores, NEG)
    row_max = jnp.max(masked, axis=-1, keepdims=True)
    expanded = jnp.exp(masked - row_max)
    row_sum = jnp.sum(expanded, axis=-1, keepdims=True)
    probability = (expanded / row_sum).astype(jnp.bfloat16)
    output = jnp.einsum(
        "hqk,khe->qhe", probability, values, preferred_element_type=jnp.float32
    ).astype(jnp.bfloat16)
    log_total = row_max[..., 0] + jnp.log(row_sum[..., 0])
    return (output, scores.astype(jnp.bfloat16), log_total)


def attend_back(query, keys, values, previous, segment, log_total, grad_heads, inv_root):
    allowed = (segment[:, None] == segment[None, :])[None]
    scores = jnp.einsum(
        "qhe,khe->hqk", query, keys, preferred_element_type=jnp.float32
    ) * inv_root + previous.astype(jnp.float32)
    probability = jnp.where(allowed, jnp.exp(scores - log_total[..., None]), 0.0)
    grad_prob = jnp.einsum("qhe,khe->hqk", grad_heads, values, preferred_element_type=jnp.float32)
    grad_values = jnp.einsum(
        "hqk,qhe->khe",
        probability.astype(jnp.bfloat16),
        grad_heads,
        preferred_element_type=jnp.float32,
    )
    inner = jnp.sum(grad_prob * probability, axis=-1, keepdims=True)
    grad_scores = (probability * (grad_prob - inner)).astype(jnp.bfloat16)
    grad_query = (
        jnp.einsum("hqk,khe->qhe", grad_scores, keys, preferred_element_type=jnp.float32) * inv_root
    )
    grad_keys = (
        jnp.einsum("hqk,qhe->khe", grad_scores, query, preferred_element_type=jnp.float32)
        * inv_root
    )
    return (grad_query, grad_keys, grad_values, grad_scores)


def body(
    tokens,
    cotangent,
    prev_logits,
    segment_ids,
    w_qkv,
    b_qv,
    w_out,
    w_up,
    b_up,
    w_down,
    biases,
    gains,
    shifts,
):
    row_count, slot_count, part_width = tokens.shape
    full_width = part_width * lax.axis_size("tensor")
    local_width = b_qv.shape[1]
    heads_here = prev_logits.shape[1]
    head_size = local_width // heads_here
    token_count = row_count * slot_count
    inv_root = 1.0 / math.sqrt(head_size)
    my_cols = lax.axis_index("tensor") * part_width
    gathered_x, gathered_dy = (
        lax.all_gather(tokens, "tensor", axis=2, tiled=True),
        lax.all_gather(cotangent, "tensor", axis=2, tiled=True),
    )
    inputs_bf = gathered_x.reshape(token_count, full_width)
    grad_final = gathered_dy.reshape(token_count, full_width).astype(jnp.float32)
    qkv_weight, up_weight = (
        lax.all_gather(w_qkv.astype(jnp.bfloat16), "dp", axis=0, tiled=True),
        lax.all_gather(w_up.astype(jnp.bfloat16), "dp", axis=0, tiled=True),
    )
    out_weight, down_weight = (
        lax.all_gather(w_out.astype(jnp.bfloat16), "dp", axis=1, tiled=True),
        lax.all_gather(w_down.astype(jnp.bfloat16), "dp", axis=1, tiled=True),
    )
    qkv_matrix = qkv_weight.reshape(full_width, 3 * local_width)
    qkv_bias = jnp.stack([b_qv[0], jnp.zeros_like(b_qv[0]), b_qv[1]])

    def project(source, matrix):
        product = jnp.dot(source, matrix, preferred_element_type=jnp.float32).reshape(
            token_count, 3, local_width
        )
        return (
            (product + qkv_bias)
            .astype(jnp.bfloat16)
            .reshape(row_count, slot_count, 3, heads_here, head_size)
        )

    def attend_all(packed):

        def one_row(row_items):
            return attend_rows(
                row_items[0], row_items[1], row_items[2], row_items[3], row_items[4], inv_root
            )

        return lax.map(
            one_row, (packed[:, :, 0], packed[:, :, 1], packed[:, :, 2], prev_logits, segment_ids)
        )

    qkv_all = project(inputs_bf, qkv_matrix)
    attn_heads, raw_scores, log_total = attend_all(qkv_all)
    attn_flat = attn_heads.reshape(token_count, local_width)
    attn_partial = jnp.dot(attn_flat, out_weight, preferred_element_type=jnp.float32)
    first_out, normed_one, inv_one = norm_forward(
        inputs_bf.astype(jnp.float32) + branch_total(attn_partial) + biases[0], gains[0], shifts[0]
    )
    first_bf = first_out.astype(jnp.bfloat16)
    hidden = jnp.dot(first_bf, up_weight, preferred_element_type=jnp.float32) + b_up
    activated = gelu_exact(hidden).astype(jnp.bfloat16)
    ffn_partial = jnp.dot(activated, down_weight, preferred_element_type=jnp.float32)
    final_out, normed_two, inv_two = norm_forward(
        first_out + branch_total(ffn_partial) + biases[1], gains[1], shifts[1]
    )
    block_out = (
        lax.dynamic_slice_in_dim(final_out, my_cols, part_width, 1)
        .reshape(row_count, slot_count, part_width)
        .astype(jnp.bfloat16)
    )
    grad_gain_two = jnp.sum(grad_final * normed_two, axis=0)
    grad_shift_two = jnp.sum(grad_final, axis=0)
    grad_sum_two = norm_backward(grad_final, normed_two, inv_two, gains[1])
    grad_bias_down = jnp.sum(grad_sum_two, axis=0)
    grad_sum_two_bf = grad_sum_two.astype(jnp.bfloat16)
    again = lax.optimization_barrier((inputs_bf, qkv_matrix, first_bf, up_weight, grad_sum_two_bf))
    qkv_back = project(again[0], again[1])
    attn_back = attend_all(qkv_back)[0].reshape(token_count, local_width)
    first_back = again[2]
    hidden_back = jnp.dot(first_back, again[3], preferred_element_type=jnp.float32) + b_up
    act_back = gelu_exact(hidden_back).astype(jnp.bfloat16)
    grad_down = jnp.dot(act_back.T, grad_sum_two_bf, preferred_element_type=jnp.float32)
    grad_act = jnp.dot(grad_sum_two_bf, down_weight.T, preferred_element_type=jnp.float32)
    grad_hidden = jax.vjp(gelu_exact, hidden_back)[1](grad_act)[0]
    grad_bias_up = jnp.sum(grad_hidden, axis=0)
    grad_hidden_bf = grad_hidden.astype(jnp.bfloat16)
    grad_up = jnp.dot(first_back.T, grad_hidden_bf, preferred_element_type=jnp.float32)
    ffn_summed = (grad_up, grad_bias_up, grad_down, grad_bias_down, grad_gain_two, grad_shift_two)
    first_partial = jnp.dot(grad_hidden_bf, up_weight.T, preferred_element_type=jnp.float32)
    grad_first = grad_sum_two + branch_total(first_partial)
    grad_gain_one = jnp.sum(grad_first * normed_one, axis=0)
    grad_shift_one = jnp.sum(grad_first, axis=0)
    grad_sum_one = norm_backward(grad_first, normed_one, inv_one, gains[0])
    grad_bias_out = jnp.sum(grad_sum_one, axis=0)
    grad_sum_one_bf = grad_sum_one.astype(jnp.bfloat16)
    own_grad = lax.dynamic_slice_in_dim(grad_sum_one, my_cols, part_width, 1)
    grad_out = jnp.dot(attn_back.T, grad_sum_one_bf, preferred_element_type=jnp.float32)
    grad_heads = jnp.dot(grad_sum_one_bf, out_weight.T, preferred_element_type=jnp.float32).astype(
        jnp.bfloat16
    )
    grad_heads = grad_heads.reshape(row_count, slot_count, heads_here, head_size)

    def back_row(row_items):
        return attend_back(
            row_items[0],
            row_items[1],
            row_items[2],
            row_items[3],
            row_items[4],
            row_items[5],
            row_items[6],
            inv_root,
        )

    grad_query, grad_keys, grad_values, grad_scores = lax.map(
        back_row,
        (
            qkv_back[:, :, 0],
            qkv_back[:, :, 1],
            qkv_back[:, :, 2],
            prev_logits,
            segment_ids,
            log_total,
            grad_heads,
        ),
    )
    grad_qkv_full = jnp.stack([grad_query, grad_keys, grad_values], axis=2).reshape(
        token_count, 3, local_width
    )
    grad_b_qv = jnp.stack(
        [jnp.sum(grad_qkv_full[:, 0], axis=0), jnp.sum(grad_qkv_full[:, 2], axis=0)]
    )
    grad_qkv_bf = grad_qkv_full.reshape(token_count, 3 * local_width).astype(jnp.bfloat16)
    grad_qkv = jnp.dot(inputs_bf.T, grad_qkv_bf, preferred_element_type=jnp.float32).reshape(
        full_width, 3, local_width
    )
    grad_input_part = jnp.dot(grad_qkv_bf, qkv_matrix.T, preferred_element_type=jnp.float32)
    grad_input = (
        lax.psum_scatter(
            grad_input_part.astype(jnp.bfloat16), "tensor", scatter_dimension=1, tiled=True
        ).astype(jnp.float32)
        + own_grad
    )
    grad_input = grad_input.reshape(row_count, slot_count, part_width).astype(jnp.bfloat16)
    every_sum = lax.psum(
        (
            grad_qkv,
            grad_b_qv,
            grad_out,
            grad_bias_out,
            grad_gain_one,
            grad_shift_one,
            ffn_summed[0],
            ffn_summed[1],
            ffn_summed[2],
            ffn_summed[3],
            ffn_summed[4],
            ffn_summed[5],
        ),
        "dp",
    )
    attn_summed = every_sum[:6]
    ffn_final = every_sum[6:]
    grad_biases_all = jnp.stack([attn_summed[3], ffn_final[3]])
    grad_gains_all = jnp.stack([attn_summed[4], ffn_final[4]])
    grad_shifts_all = jnp.stack([attn_summed[5], ffn_final[5]])
    return (
        block_out,
        raw_scores,
        grad_input,
        grad_scores,
        attn_summed[0],
        attn_summed[1],
        attn_summed[2],
        ffn_final[0],
        ffn_final[1],
        ffn_final[2],
        grad_biases_all,
        grad_gains_all,
        grad_shifts_all,
    )


def solution(mesh):
    placed = (
        P("dp", None, "tensor"),
        P("dp", None, "tensor"),
        P("dp", "tensor", None, None),
        P("dp", None),
        P("dp", None, "tensor"),
        P(None, "tensor"),
        P("tensor", "dp"),
        P("dp", "tensor"),
        P("tensor"),
        P("tensor", "dp"),
        P(),
        P(),
        P(),
    )
    return jax.shard_map(
        body,
        mesh=mesh,
        in_specs=placed,
        out_specs=(
            P("dp", None, "tensor"),
            P("dp", "tensor", None, None),
            P("dp", None, "tensor"),
            P("dp", "tensor", None, None),
            P(None, None, "tensor"),
            P(None, "tensor"),
            P("tensor", None),
            P(None, "tensor"),
            P("tensor"),
            P("tensor", None),
            P(),
            P(),
            P(),
        ),
        check_vma=False,
    )
```

profile of v0, /device:TPU:0, one launch (start us, length us, event | category | flops | bytes accessed | tf_op | source)
XLA Modules:
  0.0 772.9 jit_solution(10725266084257419247)
XLA Ops:
  10.9 38.8 %all_gather.19 = bf16[768,3,192]{2,1,0:T(4,128)(2,1)S(1)} all-gather(bf16[96,3,192]{2,1,0:T(4,128)(2,1)S(1)} %copy.112), channel_id=1, replica_groups=mesh['dp'=8,'tensor'=4] {'dp'}, dimensions={0}, use_global_device_ids=true | all-gather | bytes 995328 | tf_op jit(solution)/shard_map/all_gather | solution.py:110
  50.7 7.0 copy.117
  57.7 33.0 %all_gather.20 = bf16[192,768]{0,1:T(8,128)(2,1)} all-gather(bf16[192,96]{0,1:T(8,128)(2,1)S(1)} %copy.119), channel_id=1, replica_groups=mesh['dp'=8,'tensor'=4] {'dp'}, dimensions={1}, use_global_device_ids=true | all-gather | bytes 331776 | tf_op jit(solution)/shard_map/all_gather | solution.py:114
  90.7 2.8 copy.111
  93.6 2.8 add_convert_fusion.1
  96.4 5.2 reshape.263
  101.5 2.7 slice_bitcast_fusion.3
  108.9 40.5 %while.40 = (s32[]{:T(128)}, bf16[3,512,3,64]{1,3,2,0:T(8,128)(2,1)}, bf16[3,3,512,512]{3,2,1,0:T(8,128)(2,1)}, f32[3,3,512]{2,1,0:T(4,128)}, bf16[3,512,3,64]{1...) while((s32[]{:T(128)}, ...), condition=%wide.region_3.4_spmd, body=%wide.region_0.3_spmd.sunk | while | flops 211909120 | bytes 20769400 | solution.py:137
  119.8 2.7 constant_dynamic-update-slice_fusion.4
  151.3 3.2 convolution_convert_fusion.3
  157.6 52.0 %all-reduce.7.cloned.1.call-done = bf16[1536,768]{1,0:T(8,128)(2,1)} async-done(((bf16[1536,768]{1,0:T(8,128)(2,1)}), bf16[1536,768]{1,0:T(8,128)(2,1)}) %all-reduce.7.cloned.1.call-update) | async-done | bytes 2359312 | tf_op jit(solution)/shard_map/psum | solution.py:35
  213.6 2.7 fusion.110
  216.3 24.9 %all-gather.9.cloned.1.call-done = bf16[768,768]{0,1:T(8,128)(2,1)} async-done(((bf16[768,96]{0,1:T(8,128)(2,1)}), bf16[768,768]{0,1:T(8,128)(2,1)}) %all-gather.9.cloned.1.call-update) | async-done | bytes 1179664 | tf_op jit(solution)/shard_map/all_gather | solution.py:115
  241.2 16.5 %convolution_convert_fusion.2 = bf16[1536,768]{1,0:T(8,128)(2,1)} fusion(bf16[768,768]{0,1:T(8,128)(2,1)} %all-gather.9.cloned.1.call-done, bf16[1536,768]{1,0:T(8,128)(2,1)} %fusion.110, bf16[768,768]{1,0:T(8,128)(2,1)} %all-gather.7.cloned.1.call-done, f32[768]{0:T(1024)S(1)} %copy-done.36), kind=kOutput, calls=%fused_computation.153 | convolution fusion | flops 3702915072 | bytes 7080960 | tf_op jit(solution)/shard_map/dot_general | solution.py:151
  258.3 6.8 all-gather.11.cloned.1.call-done
  265.1 3.2 convert_reduce_fusion
  268.3 4.5 copy.120
  272.8 39.2 %all-reduce.9.cloned.1.call-done = bf16[1536,768]{1,0:T(8,128)(2,1)} async-done(((bf16[1536,768]{1,0:T(8,128)(2,1)}), bf16[1536,768]{1,0:T(8,128)(2,1)}) %all-reduce.9.cloned.1.call-update) | async-done | bytes 2359312 | tf_op jit(solution)/shard_map/psum | solution.py:35
  312.1 4.6 fusion.125
  316.7 2.7 multiply_reduce_fusion.5
  319.4 4.4 fusion.97
  323.8 2.9 fusion.161
  330.4 14.0 %fusion.159 = (f32[768]{0:T(1024)S(1)}, bf16[1536,768]{1,0:T(8,128)(2,1)S(1)}, f32[1536,768]{1,0:T(8,128)}) fusion(f32[1536,768]{1,0:T(8,128)S(1)} %fusion.171, f32[768]{0:T(1024)S(1)} %copy-done.36, bf16[1536,768]{1,0:T(8,128)(2,1)S(1)} %get-tuple-element.432, bf16[768,768]{0,1:T(8,128)(2,1)S(1)} %copy-done.35), kind=kOutput, calls=%fused_computation.235 | convolution fusion | flops 1899232512 | bytes 15341568 | tf_op jit(solution)/shard_map/dot_general | solution.py:172
  345.8 3.5 convolution_convert_fusion.1
  349.6 3.4 fusion.170
  352.9 6.7 reshape.265
  359.7 3.0 add_convert_fusion
  366.3 38.8 %all-reduce.11.cloned.1.call-done = bf16[1536,768]{1,0:T(8,128)(2,1)} async-done(((bf16[1536,768]{1,0:T(8,128)(2,1)}), bf16[1536,768]{1,0:T(8,128)(2,1)}) %all-reduce.11.cloned.1.call-update) | async-done | bytes 2359312 | tf_op jit(solution)/shard_map/psum | solution.py:35
  405.1 5.8 multiply_reduce_fusion.1
  411.1 4.6 fusion.158
  422.8 46.1 %while.41 = (s32[]{:T(128)}, f32[3,512,3,64]{1,3,2,0:T(8,128)}, bf16[3,512,3,64]{1,3,2,0:T(8,128)(2,1)}, f32[3,512,3,64]{1,3,2,0:T(8,128)}, bf16[3,3,512,512]{3,...) while((s32[]{:T(128)}, f32[3,512,3,64]{1,3,2,0:T(8,128)}, ...), condition=%wide.region_17.18_spmd, body=%wide.region_15.17_spmd.sunk | while | flops 512424448 | bytes 34580112 | solution.py:204
  424.4 2.7 fusion.229
  439.8 2.7 fusion.229
  455.1 2.7 fusion.229
  476.2 3.5 fusion.112
  479.8 23.6 %while.42 = (s32[]{:T(128)}, bf16[3,512,3,64]{1,3,2,0:T(8,128)(2,1)S(1)}, bf16[3,512,3,64]{1,3,2,0:T(8,128)(2,1)}, s32[3,512]{1,0:T(4,128)}, bf16[3,512,3,64]{1,...) while((s32[]{:T(128)}, ...), condition=%wide.region_26.27_spmd, body=%wide.region_23.26_spmd.sunk | while | flops 312576512 | bytes 5136481 | solution.py:137
  481.0 3.1 fusion.238
  484.1 3.9 fusion.239
  489.0 3.2 fusion.238
  492.1 3.5 fusion.239
  496.6 3.3 fusion.238
  499.9 3.5 fusion.239
  504.1 5.3 fusion.121
  509.4 7.4 fusion.113
  519.2 2.7 fusion.172
  527.0 39.7 %all-reduce = (f32[2,192]{1,0:T(2,128)}, f32[768]{0:T(1024)}, f32[1,768]{1,0:T(1,128)S(1)}, f32[1,768]{1,0:T(1,128)S(1)}, f32[1,768]{1,0:T(1,128)S(1)}, /*index=...) all-reduce(f32[2,192]{1,0:T(2,128)S(1)} %pad_maximum_fusion.5, ...), channel_id=1, replica_groups=mesh['dp'=8,'tensor'=4] {'dp'}, use_global_device_ids=true, to_apply=%region_22.23 | all-reduce | flops 5760 | bytes 46080 | tf_op jit(solution)/shard_map/psum | solution.py:234
  573.2 184.3 %all-reduce.13.cloned.1.call-done = (f32[768,3,192]{0,2,1:T(8,128)}, f32[192,768]{1,0:T(8,128)}, f32[768,768]{1,0:T(8,128)}, f32[768,768]{1,0:T(8,128)}) async-done(((f32[768,3,192]{0,2,1:T(8,128)}, f32[192,768]{1,0:T(8,128)}, f32[768,768]{1,0:T(8,128)}, f32[768,768]{1,0:T(8,128)}), (f32[768,3,192]{0,2,1:T(8,128)}, f32[192,768]{1,0:T(8,128)}, f32[768,768]{1,0:T(8,128)}, ...) | async-done | bytes 7077904 | tf_op jit(solution)/shard_map/psum | solution.py:234
  757.5 2.9 copy.203
  (235 shorter events, 139.0 us)
Async XLA Ops:
  8.0 82.7 %all-gather.5.cloned.1.call-start = ((), (), s32[]{:S(2)}) async-start(), calls=%async_computation.1 | async-start | bytes 2949120 | tf_op jit(solution)/shard_map/all_gather | solution.py:104
  8.7 200.9 %all-reduce.7.cloned.1.call-start = ((), (), s32[]{:S(2)}) async-start(), calls=%async_computation.2 | async-start | bytes 4718592 | tf_op jit(solution)/shard_map/psum | solution.py:35
  50.6 43.0 %copy-start.20 = (bf16[768,3,192]{0,2,1:T(8,128)(2,1)}, bf16[768,3,192]{0,2,1:T(8,128)(2,1)S(1)}, u32[]{:S(2)}) copy-start(bf16[768,3,192]{0,2,1:T(8,128)(2,1)S(1)} %copy.113) | copy-start | bytes 2654212
  50.6 40.0 %copy-start.33 = (f32[2,192]{1,0:T(2,128)S(1)}, f32[2,192]{1,0:T(2,128)}, u32[]{:S(2)}) copy-start(f32[2,192]{1,0:T(2,128)} %param.24) | copy-start | bytes 4612
  90.7 5.7 copy-start.27
  93.6 317.4 %copy-start = (bf16[3,512,768]{2,1,0:T(8,128)(2,1)}, bf16[3,512,768]{2,1,0:T(8,128)(2,1)S(1)}, u32[]{:S(2)}) copy-start(bf16[3,512,768]{2,1,0:T(8,128)(2,1)S(1)} %copy.111) | copy-start | bytes 7077892
  149.4 5.2 copy-start.23
  149.4 5.9 copy-start.24
  151.1 5.8 copy-start.30
  151.1 5.9 copy-start.31
  151.1 5.9 copy-start.32
  154.6 61.8 %all-gather.7.cloned.1.call-start = ((), (), s32[]{:S(2)}) async-start(), calls=%async_computation.3 | async-start | bytes 1327104 | tf_op jit(solution)/shard_map/all_gather | solution.py:111
  155.3 85.9 %all-gather.9.cloned.1.call-start = ((), (), s32[]{:S(2)}) async-start(), calls=%async_computation.4 | async-start | bytes 1327104 | tf_op jit(solution)/shard_map/all_gather | solution.py:115
  156.1 109.0 %all-gather.11.cloned.1.call-start = ((), (), s32[]{:S(2)}) async-start(), calls=%async_computation.6 | async-start | bytes 2949120 | tf_op jit(solution)/shard_map/all_gather | solution.py:105
  156.7 155.4 %all-reduce.9.cloned.1.call-start = ((), (), s32[]{:S(2)}) async-start(), calls=%async_computation.5 | async-start | bytes 4718592 | tf_op jit(solution)/shard_map/psum | solution.py:35
  157.0 166.8 %copy-start.25 = (f32[768]{0:T(1024)}, f32[768]{0:T(1024)S(1)}, u32[]{:S(2)}) copy-start(f32[768]{0:T(1024)S(1)} %get-tuple-element.353) | copy-start | bytes 9220
  209.7 2.7 copy-start.2
  213.6 27.6 %copy-start.36 = (f32[768]{0:T(1024)S(1)}, f32[768]{0:T(1024)}, u32[]{:S(2)}) copy-start(f32[768]{0:T(1024)} %param.27) | copy-start | bytes 9220
  257.8 147.4 %all-reduce.11.cloned.1.call-start = ((), (), s32[]{:S(2)}) async-start(), calls=%async_computation.7 | async-start | bytes 4718592 | tf_op jit(solution)/shard_map/psum | solution.py:35
  312.1 4.6 copy-start.3
  312.1 4.6 copy-start.8
  316.6 2.8 copy-start.6
  323.8 4.3 copy-start.7
  323.8 4.3 copy-start.9
  323.8 4.5 copy-start.34
  328.1 2.2 copy-start.13
  328.3 2.0 copy-start.35
  330.4 14.0 %copy-start.37 = (f32[1536,768]{1,0:T(8,128)}, f32[1536,768]{1,0:T(8,128)S(1)}, u32[]{:S(2)}) copy-start(f32[1536,768]{1,0:T(8,128)S(1)} %fusion.171) | copy-start | bytes 14155780
  344.3 1.4 copy-start.15
  345.8 3.7 copy-start.28
  345.8 3.8 copy-start.21
  349.2 219.3 %reduce-scatter.4.cloned.1.call-start = ((), (), s32[]{:S(2)}) async-start(), calls=%async_computation.8 | async-start | bytes 2949120
  405.1 5.9 copy-start.4
  405.1 5.9 copy-start.11
  411.1 6.8 copy-start.12
  415.7 2.2 copy-start.5
  472.8 3.4 copy-start.22
  479.6 277.8 %all-reduce.13.cloned.1.call-start = ((), (), s32[]{:S(2)}) async-start(), calls=%async_computation.9 | async-start | bytes 14155776 | tf_op jit(solution)/shard_map/psum | solution.py:234
  479.8 24.3 %copy-start.10 = (bf16[1536,768]{1,0:T(8,128)(2,1)S(1)}, bf16[1536,768]{1,0:T(8,128)(2,1)}, u32[]{:S(2)}) copy-start(bf16[1536,768]{1,0:T(8,128)(2,1)} %fusion.110) | copy-start | bytes 7077892
  503.4 6.0 copy-start.14
  504.1 12.7 %slice-start = ((s8[4718592]{0:T(1024)(128)(4,1)}), s8[4194304]{0:T(1024)(128)(4,1)S(1)}, s32[]{:S(2)}) async-start(s8[4718592]{0:T(1024)(128)(4,1)} %bitcast.304), calls=%async_computation.10 | async-start | bytes 8388608
  509.4 7.4 slice-start.1
  516.8 1.8 copy-start.1
  516.8 2.4 copy-start.19
  522.0 1.6 copy-start.26
  522.0 1.6 copy-start.29
  757.5 4.9 copy-start.17
  757.5 6.3 copy-start.16
  (1 other events, 1.2 us)
Sparse Core Ops, SparseCore 0:
  10.4 26.7 all-gather.4
  154.7 54.9 all-reduce.6
  257.9 54.1 all-reduce.8
  349.4 55.7 all-reduce.10
  479.8 33.1 reduce-scatter.3
Sparse Core Ops, SparseCore 1:
  157.8 40.7 all-gather.6
  201.2 40.0 all-gather.8
  242.6 22.4 all-gather.10
  522.1 235.4 all-reduce.12
where the time goes:
time: 782 us; the launch traced here: 773 us
  waiting for transfers between devices  347 us (44%)
  matrix products  135 us (17%)
  blocking collectives  112 us (14%)
  local copies, waits for them, and re-layouts  99 us (13%)
  other arithmetic  61.8 us (8%)
  between operations  16.5 us (2%)
    psum x1, waiting for transfers between devices, body(): lax.psum((grad_qkv, grad_b_qv, grad_out, grad_bias_out, grad_gain_one, gr...  184 us
    psum x3, waiting for transfers between devices, branch_total(): lax.psum(partial_value.astype(jnp.bfloat16), 'tensor').astype(jnp.float32)  130 us
    psum x1, blocking collectives, body(): lax.psum((grad_qkv, grad_b_qv, grad_out, grad_bias_out, grad_gain_one, gr...  39.7 us
    all_gather x1, blocking collectives, body(): lax.all_gather(w_qkv.astype(jnp.bfloat16), 'dp', axis=0, tiled=True)  38.8 us
    all_gather x1, blocking collectives, body(): lax.all_gather(w_out.astype(jnp.bfloat16), 'dp', axis=1, tiled=True)  33 us
    all_gather x1, waiting for transfers between devices, body(): lax.all_gather(w_down.astype(jnp.bfloat16), 'dp', axis=1, tiled=True)  24.9 us
    dynamic_update_slice x12, local copies, waits for them, and re-layouts, attend_all(): lax.map(one_row, (packed[:, :, 0], packed[:, :, 1], packed[:, :, 2], prev...  21.5 us
    unnamed x91, local copies, waits for them, and re-layouts  20.5 us
  transfers between devices with their start and end apart: 9, of which 6 were waited for; matrix products, arithmetic and copies ran while one was open for 15% of the time, Pallas kernels for 0%

commit v1 on v0

v1 whole, which is shorter than its diff:
```python
import functools

import jax
import jax.numpy as jnp
from jax import lax
from jax.experimental import pallas as pl
from jax.experimental.pallas import tpu as pltpu
from jax.sharding import PartitionSpec as P

EPS = 1e-06
NEG = -1e30
BF = jnp.bfloat16
F32 = jnp.float32
CHUNKS = ((0, 3),)
VMEM_LIMIT = 48 * 1024 * 1024


def dot(a, b):
    return lax.dot_general(a, b, (((1,), (0,)), ((), ())), preferred_element_type=F32)


def dot_nt(a, b):
    return lax.dot_general(a, b, (((1,), (1,)), ((), ())), preferred_element_type=F32)


def dot_tn(a, b):
    return lax.dot_general(a, b, (((0,), (0,)), ((), ())), preferred_element_type=F32)


def place_of(me, step):
    core, chip = lax.rem(me, 2), me // 2
    core = 1 - core if step % 2 else core
    chip = 1 - chip if step // 2 else chip
    return 2 * chip + core


def ln_stats(summed):
    row_mean = jnp.mean(summed, axis=-1, keepdims=True)
    centered = summed - row_mean
    inv_std = lax.rsqrt(jnp.mean(centered * centered, axis=-1, keepdims=True) + EPS)
    return centered * inv_std, inv_std


def ln_back(grad, normed, inv_std, gain):
    scaled = grad * gain
    inner = (
        scaled
        - jnp.mean(scaled, axis=-1, keepdims=True)
        - normed * jnp.mean(scaled * normed, axis=-1, keepdims=True)
    )
    return inner * inv_std


def attend_kernel(
    first, heads, aliased, me_ref, x0, x1, x2, x3, w_ref, b_ref, prev_ref, seg_ref, *rest
):
    if aliased:
        rest = rest[1:]
    raw_ref, p_ref, qkv_ref, own_ref, oth_ref, xt_ref, xh_ref, o_scr = rest
    me = me_ref[0]
    core = lax.rem(me, 2)
    width, slots = x0.shape[1], x0.shape[2]
    half = slots // 2
    size = width // heads
    for step, piece in enumerate((x0, x1, x2, x3)):
        start = pl.multiple_of(place_of(me, step) * width, width)
        xt_ref[0, pl.ds(start, width), :] = piece[0]
    bias = jnp.transpose(jnp.broadcast_to(b_ref[0:1, :], (128, width)))[:, 0:1]
    bias_v = jnp.transpose(jnp.broadcast_to(b_ref[1:2, :], (128, width)))[:, 0:1]
    packed = dot_tn(w_ref[:, : 3 * width], xt_ref[0])
    qkv_ref[0, 0] = (packed[:width] + bias).astype(BF)
    qkv_ref[0, 1] = packed[width : 2 * width].astype(BF)
    qkv_ref[0, 2] = (packed[2 * width :] + bias_v).astype(BF)
    mine = pl.ds(pl.multiple_of(core * half, half), half)
    other = pl.ds(pl.multiple_of((1 - core) * half, half), half)
    xh_ref[0] = jnp.transpose(xt_ref[0, :, mine])
    row = seg_ref[pl.ds(first + pl.program_id(0), 1), :].astype(F32)
    column = jnp.transpose(jnp.broadcast_to(row, (128, slots)))[:, 0:1]
    scale = 1.0 / (size**0.5)
    for block in range(2):
        rows = slice(block * half, (block + 1) * half)
        allowed = column[rows] == row
        for h in range(heads):
            feats = slice(h * size, (h + 1) * size)
            scores = dot_tn(qkv_ref[0, 0, feats, rows], qkv_ref[0, 1, feats, :]) * scale
            scores = scores + prev_ref[0, h, rows, :].astype(F32)
            raw_ref[0, h, rows, :] = scores.astype(BF)
            masked = jnp.where(allowed, scores, NEG)
            expanded = jnp.exp(masked - jnp.max(masked, axis=-1, keepdims=True))
            prob = expanded * (1.0 / jnp.sum(expanded, axis=-1, keepdims=True))
            prob = prob.astype(BF)
            p_ref[0, h, rows, :] = prob
            o_scr[feats, rows] = dot_nt(qkv_ref[0, 2, feats, :], prob).astype(BF)
    own_ref[0] = o_scr[:, mine]
    oth_ref[0] = o_scr[:, other]


def up_kernel(
    me_ref, o0, o1, o2, o3, wo0, wo1, wo2, wo3, big_a, big_b, xh_ref, bias_ref, gain_ref, shift_ref,
    b_up_a, b_up_b,
    n1_ref, r1_ref, x1_ref, ga_ref, gb_ref, gp_ref, part_ref,
):
    units = b_up_a.shape[1]
    w1a, w1b = big_a.at[:, :units], big_b.at[:, :units]
    w2a, w2b = big_a.at[:, units : 2 * units], big_b.at[:, units : 2 * units]
    total = xh_ref[0].astype(F32) + bias_ref[0:1, :]
    for left, right in ((o0, wo0), (o1, wo1), (o2, wo2), (o3, wo3)):
        total = total + dot_nt(jnp.transpose(left[0]), right[...])
    normed, inv_std = ln_stats(total)
    n1_ref[0] = normed
    r1_ref[0] = jnp.broadcast_to(inv_std, r1_ref.shape[1:])
    x1_ref[0] = (normed * gain_ref[0:1, :] + shift_ref[0:1, :]).astype(BF)
    block = 256
    for index, (w1, b_up, g_ref) in enumerate(((w1a, b_up_a, ga_ref), (w1b, b_up_b, gb_ref))):
        for start in range(0, units, block):
            hidden = dot(x1_ref[0], w1[:, start : start + block]) + b_up[:, start : start + block]
            cdf = 0.5 * (1.0 + lax.erf(hidden * (0.5**0.5)))
            pdf = jnp.exp(-0.5 * hidden * hidden) * 0.3989422804014327
            g_ref[0, :, start : start + block] = (hidden * cdf).astype(BF)
            lanes = slice(index * units + start, index * units + start + block)
            gp_ref[0, :, lanes] = (cdf + hidden * pdf).astype(BF)
    part_ref[0] = (dot_nt(ga_ref[0], w2a[...]) + dot_nt(gb_ref[0], w2b[...])).astype(BF)


def down_kernel(
    me_ref, n1_ref, pa_ref, pb_ref, dy0, dy1, dy2, dy3, bias_ref, gain_ref, shift_ref,
    big_a, big_b, gp_ref,
    act_own_ref, act_oth_ref, ds_ref, dsb_ref, da_ref, db_ref, part_ref, vec_ref, bup_ref,
    scr,
):
    me = me_ref[0]
    width = dy0.shape[1]
    units = gp_ref.shape[2] // 2
    w1a, w1b = big_a.at[:, :units], big_b.at[:, :units]
    w2a, w2b = big_a.at[:, units : 2 * units], big_b.at[:, units : 2 * units]
    branch = pa_ref[0].astype(F32) + pb_ref[0].astype(F32)
    first_out = n1_ref[0] * gain_ref[0:1, :] + shift_ref[0:1, :]
    normed, inv_std = ln_stats(first_out + branch + bias_ref[1:2, :])
    gain = gain_ref[1:2, :]
    scr[...] = jnp.transpose(normed * gain + shift_ref[1:2, :])
    for step, out in ((0, act_own_ref), (1, act_oth_ref)):
        start = pl.multiple_of(place_of(me, step) * width, width)
        out[0] = scr[pl.ds(start, width), :].astype(BF)
    for step, piece in enumerate((dy0, dy1, dy2, dy3)):
        start = pl.multiple_of(place_of(me, step) * width, width)
        scr[pl.ds(start, width), :] = piece[0].astype(F32)
    grad = jnp.transpose(scr[...])
    inner = ln_back(grad, normed, inv_std, gain)
    ds_ref[0] = inner
    vec_ref[0, 0:1, :] = jnp.sum(grad * normed, axis=0, keepdims=True)
    vec_ref[0, 1:2, :] = jnp.sum(grad, axis=0, keepdims=True)
    vec_ref[0, 2:3, :] = jnp.sum(inner, axis=0, keepdims=True)
    dsb_ref[0] = inner.astype(BF)
    block = 256
    for index, (w2, dh_ref) in enumerate(((w2a, da_ref), (w2b, db_ref))):
        for start in range(0, units, block):
            lanes = slice(index * units + start, index * units + start + block)
            grad_hidden = dot(dsb_ref[0], w2[:, start : start + block]) * gp_ref[
                0, :, lanes
            ].astype(F32)
            bup_ref[0, 0:1, lanes] = jnp.sum(grad_hidden, axis=0, keepdims=True)
            dh_ref[0, :, start : start + block] = grad_hidden.astype(BF)
    part_ref[0] = (dot_nt(da_ref[0], w1a[...]) + dot_nt(db_ref[0], w1b[...])).astype(BF)


def mid_kernel(
    me_ref, ds_ref, pa_ref, pb_ref, n1_ref, r1_ref, gain_ref, wo0, wo1,
    dsb_ref, near_ref, do_own_ref, do_oth_ref, vec_ref, scr,
):
    chip = me_ref[0] // 2
    width = do_own_ref.shape[1]
    grad = ds_ref[0] + (pa_ref[0].astype(F32) + pb_ref[0].astype(F32))
    normed = n1_ref[0]
    inner = ln_back(grad, normed, r1_ref[0, :, 0:1], gain_ref[0:1, :])
    vec_ref[0, 0:1, :] = jnp.sum(grad * normed, axis=0, keepdims=True)
    vec_ref[0, 1:2, :] = jnp.sum(grad, axis=0, keepdims=True)
    vec_ref[0, 2:3, :] = jnp.sum(inner, axis=0, keepdims=True)
    dsb = inner.astype(BF)
    dsb_ref[0] = dsb
    scr[...] = inner
    chip_lanes = pl.ds(pl.multiple_of(chip * 2 * width, 128), 2 * width)
    near_ref[0] = jnp.transpose(scr[:, chip_lanes])
    do_own_ref[0] = jnp.transpose(dot(dsb, wo0[...])).astype(BF)
    do_oth_ref[0] = jnp.transpose(dot(dsb, wo1[...])).astype(BF)


def back_kernel(
    heads, aliased, me_ref, p_ref, qkv_ref, do_own_ref, do_oth_ref, w_ref, near_ref, *rest
):
    if aliased:
        rest = rest[1:]
    lg_ref, dqkv_ref, e0, e1, e2, e3, vec_ref, do_scr, dx_scr = rest
    me = me_ref[0]
    core, chip = lax.rem(me, 2), me // 2
    width, slots = qkv_ref.shape[2], qkv_ref.shape[3]
    half = slots // 2
    size = width // heads
    mine = pl.ds(pl.multiple_of(core * half, half), half)
    other = pl.ds(pl.multiple_of((1 - core) * half, half), half)
    do_scr[:, mine] = do_own_ref[0]
    do_scr[:, other] = do_oth_ref[0]
    scale = 1.0 / (size**0.5)
    for h in range(heads):
        feats = slice(h * size, (h + 1) * size)
        query, key, value = (qkv_ref[0, part, feats, :] for part in range(3))
        out_grad = do_scr[feats, :]
        for block in range(2):
            rows = slice(block * half, (block + 1) * half)
            prob = p_ref[0, h, rows, :].astype(F32)
            grad_prob = dot_tn(do_scr[feats, rows], value)
            weighted = grad_prob * prob
            inner = jnp.sum(weighted, axis=-1, keepdims=True)
            lg_ref[0, h, rows, :] = (weighted - prob * inner).astype(BF)
        grad_query = dot_nt(key, lg_ref[0, h]) * scale
        grad_key = dot(query, lg_ref[0, h]) * scale
        grad_value = dot(out_grad, p_ref[0, h])
        vec_ref[0, feats, 0:1] = jnp.sum(grad_query, axis=1, keepdims=True)
        vec_ref[0, feats, 1:2] = jnp.sum(grad_value, axis=1, keepdims=True)
        dqkv_ref[0, pl.ds(h * size, size), :] = grad_query.astype(BF)
        dqkv_ref[0, pl.ds(width + h * size, size), :] = grad_key.astype(BF)
        dqkv_ref[0, pl.ds(2 * width + h * size, size), :] = grad_value.astype(BF)
    dx_scr[...] = dot(w_ref[:, : 3 * width], dqkv_ref[0])
    near = pl.ds(pl.multiple_of(chip * 2 * width, width), 2 * width)
    dx_scr[near, mine] = dx_scr[near, mine] + near_ref[0]
    for step, out in enumerate((e0, e1, e2, e3)):
        start = pl.multiple_of(place_of(me, step) * width, width)
        out[0] = dx_scr[pl.ds(start, width), :].astype(BF)


def ffn_grad_kernel(count, split, me_ref, *rest):
    lefts, rights = rest[:count], rest[count : 2 * count]
    keep_ref, send_ref, scr = rest[2 * count :]
    side = me_ref[1]
    total = None
    for left, right in zip(lefts, rights):
        a = left[...].reshape(-1, left.shape[-1])
        b = right[...].reshape(-1, right.shape[-1])
        product = dot_tn(a, b)
        total = product if total is None else total + product
    part = keep_ref.shape[0]
    scr[...] = total
    keep_ref[...] = scr[pl.ds(pl.multiple_of(side * part, part), part), :].astype(BF)
    send_ref[...] = scr[pl.ds(pl.multiple_of((1 - side) * part, part), part), :].astype(BF)


def qkv_grad_kernel(count, me_ref, *rest):
    groups = [rest[i * count : (i + 1) * count] for i in range(6)]
    keep_ref, send_ref, scr = rest[6 * count :]
    side = me_ref[1]
    total = None
    for x, grad in zip(groups[0], groups[1]):
        for index in range(grad.shape[0]):
            product = dot_nt(grad[index], x[index])
            total = product if total is None else total + product
    used = total.shape[0]
    scr[:used, :] = total
    total = None
    for lefts, rights in ((groups[2], groups[3]), (groups[4], groups[5])):
        for left, right in zip(lefts, rights):
            for index in range(left.shape[0]):
                product = dot(left[index], right[index])
                total = product if total is None else total + product
    scr[used:, :] = total
    part = scr.shape[0] // 2
    keep_ref[...] = scr[pl.ds(pl.multiple_of(side * part, part), part), :].astype(BF)
    send_ref[...] = scr[pl.ds(pl.multiple_of((1 - side) * part, part), part), :].astype(BF)


def fold_kernel(me_ref, keep_ref, got_ref, *outs):
    depth = me_ref[2]
    rows = outs[0].shape[0]
    count = len(outs)
    for step, out in enumerate(outs):
        start = pl.multiple_of(lax.rem(depth + step, count) * rows, rows)
        total = keep_ref[pl.ds(start, rows), :].astype(F32) + got_ref[pl.ds(start, rows), :].astype(F32)
        out[...] = total.astype(BF)


def finish_kernel(steps, pair, me_ref, *rest):
    count = len(steps)
    blocks, outs = rest[:count], rest[count:]
    here = ring_place(me_ref[3], count)
    rows = blocks[0].shape[0]
    for number, back in enumerate(steps):
        there = lax.rem(here + count - back, count)
        index = jnp.where(there < count // 2, there, (count - 1 - there) + count // 2)
        if pair:
            part = rows // 2
            place = pl.ds(pl.multiple_of(index * part, part), part)
            outs[0][place, :] = blocks[number][:part, :].astype(F32)
            outs[1][place, :] = blocks[number][part:, :].astype(F32)
            continue
        block = blocks[number][...].astype(F32)
        before = 0
        for out in outs:
            held = out.shape[0] // rows

            @pl.when((index >= before) & (index < before + held))
            def _():
                out[pl.ds(pl.multiple_of((index - before) * rows, rows), rows), :] = block

            before += held


def ring_place(group, groups):
    return jnp.where(lax.rem(group, 2) == 0, group // 2, groups - 1 - group // 2)


def gather_kernel(cuts, steps, me_ref, *rest):
    count = len(steps)
    blocks, outs, sems = rest[:count], rest[count:-1], rest[-1]
    here = ring_place(me_ref[3], count)
    rows = blocks[0].shape[0]
    copies = []
    for number, back in enumerate(steps):
        there = lax.rem(here + count - back, count)
        group = jnp.where(there < count // 2, 2 * there, 2 * (count - 1 - there) + 1)
        place = pl.ds(pl.multiple_of(group * rows, rows), rows)
        for index, (low, high) in enumerate(cuts):
            copies.append(
                pltpu.make_async_copy(
                    blocks[number].at[:, pl.ds(low, high - low)],
                    outs[index].at[place, :],
                    sems.at[number, index],
                )
            )
    for copy in copies:
        copy.start()
    for copy in copies:
        copy.wait()


def whole(array):
    shape = array.shape
    return pl.BlockSpec(shape, lambda i, s: (0,) * len(shape))


def fixed(array):
    shape = array.shape
    return pl.BlockSpec(shape, lambda i, s: (0,) * len(shape), pipeline_mode=pl.Buffered(1))


def by_row(array, first=0):
    shape = array.shape
    rest = (0,) * (len(shape) - 1)
    return pl.BlockSpec((1,) + shape[1:], lambda i, s: (first + i,) + rest)


def call(kernel, grid, ins, outs, out_specs, scratch, name, micros, alias=None):
    flops = int(micros * 1e8)
    return pl.pallas_call(
        kernel,
        out_shape=outs,
        grid_spec=pltpu.PrefetchScalarGridSpec(
            num_scalar_prefetch=1,
            grid=grid,
            in_specs=[spec for _, spec in ins[1:]],
            out_specs=out_specs,
            scratch_shapes=scratch,
        ),
        input_output_aliases=alias or {},
        compiler_params=pltpu.CompilerParams(vmem_limit_bytes=VMEM_LIMIT),
        cost_estimate=pl.CostEstimate(flops=flops, bytes_accessed=1 << 10, transcendentals=0),
        name=name,
    )(*[a for a, _ in ins])


def body(
    tokens, cotangent, prev_logits, segment_ids, w_qkv, b_qv, w_out, w_up, b_up, w_down,
    biases, gains, shifts,
):
    rows, slots, width = tokens.shape
    full = width * lax.axis_size("tensor")
    groups = lax.axis_size("dp")
    near_dp = groups == 8
    heads = prev_logits.shape[1]
    half = slots // 2
    units = w_up.shape[1]
    me = lax.axis_index("tensor").astype(jnp.int32)
    dp = lax.axis_index("dp").astype(jnp.int32)
    me_ref = jnp.stack([me, lax.rem(dp, 2), dp // 2, dp])
    core = lax.rem(me, 2)
    sds = jax.ShapeDtypeStruct

    def after(value, *others):
        return lax.optimization_barrier((value, others))[0]

    def pp(array, step):
        return lax.ppermute(array, "tensor", [(i, i ^ step) for i in range(4)])

    def pp_x(array):
        return lax.ppermute(array, "dp", [(i, i ^ 1) for i in range(groups)])

    def pp_z(array, step):
        deep = groups // 2
        pairs = [(i, (i // 2 + step) % deep * 2 + i % 2) for i in range(groups)]
        return lax.ppermute(array, "dp", pairs)

    order = list(range(0, groups, 2)) + list(range(groups - 1, 0, -2))
    onward = [(order[i], order[(i + 1) % groups]) for i in range(groups)]
    backward = [(b, a) for a, b in onward]

    ring_steps = [0]
    for step in range(1, groups // 2):
        ring_steps += [step, groups - step]
    ring_steps += [groups // 2]

    def ring_step(ahead, behind):
        return lax.ppermute(ahead, "dp", onward), lax.ppermute(behind, "dp", backward)

    def place_rows(blocks, cuts):
        outs = [sds((full, high - low), BF) for low, high in cuts]
        anywhere = pl.BlockSpec(memory_space=pl.ANY)
        return call(
            functools.partial(gather_kernel, cuts, ring_steps), (1,),
            [(me_ref, None)] + [(b, anywhere) for b in blocks], outs, [anywhere] * len(outs),
            [pltpu.SemaphoreType.DMA((groups, len(cuts)))], "gather", 2,
        )

    tokens = jnp.swapaxes(tokens, 1, 2)
    cotangent = jnp.swapaxes(cotangent, 1, 2)
    shard_in = w_qkv.astype(BF).reshape(w_qkv.shape[0], 3 * width)
    x_y = pp(tokens, 2)
    x_c = pp(tokens, 1)
    shard_in = jnp.concatenate([shard_in, w_out.T.astype(BF)], 1)
    shard_big = jnp.concatenate([w_up.astype(BF), w_down.T.astype(BF)], 1)
    big = []
    if near_dp:
        ring = [ring_step(shard_in, shard_in)]
        ring.append(ring_step(*ring[-1]))
        ring.append(ring_step(*ring[-1]))
        last = lax.ppermute(ring[-1][0], "dp", onward)
        shard_big = after(shard_big, last)
        big.append(ring_step(shard_big, shard_big))
        w_in = place_rows([shard_in, *ring[0], *ring[1], *ring[2], last], ((0, full),))[0]
        if len(CHUNKS) == 1:
            w_in = after(w_in, *big[0])
            big.append(ring_step(*big[0]))
    else:
        w_in = lax.all_gather(shard_in, "dp", axis=0, tiled=True)
        big_a = lax.all_gather(shard_big, "dp", axis=0, tiled=True)
    wo0 = w_in[:, 3 * width :]
    wo2 = pp(wo0, 2)
    wo1, wo3 = pp(wo0, 1), pp(wo2, 1)
    x_d = pp(x_y, 1)
    x_pieces = (tokens, x_c, x_y, x_d)
    cot = after(cotangent, x_y)
    dy_mine = lax.dynamic_slice_in_dim(cot, core * half, half, 2)
    dy_other = lax.dynamic_slice_in_dim(cot, (1 - core) * half, half, 2)
    dy1, dy2, dy3 = pp(dy_other, 1), pp(dy_mine, 2), pp(dy_other, 3)
    b_up_a = b_up.reshape(1, units)
    b_up_b = pp(b_up_a, 1)

    raw = None
    state = []
    for first, count in CHUNKS:
        ins = [(me_ref, None)] + [(p, by_row(p, first)) for p in x_pieces]
        ins += [(w_in, fixed(w_in)), (b_qv, whole(b_qv)), (prev_logits, by_row(prev_logits, first))]
        ins += [(segment_ids, whole(segment_ids))]
        alias = None
        if raw is not None:
            alias = {len(ins): 0}
            ins += [(raw, pl.BlockSpec(memory_space=pl.ANY))]
        outs = [
            sds(prev_logits.shape, BF),
            sds((count,) + prev_logits.shape[1:], BF),
            sds((count, 3, width, slots), BF),
            sds((count, width, half), BF),
            sds((count, width, half), BF),
            sds((count, full, slots), BF),
            sds((count, half, full), BF),
        ]
        specs = [by_row(outs[0], first)] + [by_row(o) for o in outs[1:]]
        raw, prob, qkv, o_own, o_oth, xt, xh = call(
            functools.partial(attend_kernel, first, heads, alias is not None),
            (count,), ins, outs, specs, [pltpu.VMEM((width, slots), BF)], "attend",
            4.3 * count, alias,
        )
        state.append(dict(prob=prob, qkv=qkv, o_own=o_own, o_oth=o_oth, xh=xh, xt=xt))
        if near_dp and len(big) < 3 and len(CHUNKS) > 1:
            w_in = after(w_in, *big[-1])
            big.append(ring_step(*after(big[-1], o_own)))

    for s in state:
        s["o1"], s["o2"], s["o3"] = pp(s["o_oth"], 1), pp(s["o_own"], 2), pp(s["o_oth"], 3)
    here = [wo1, wo3, dy1, dy2, dy3] + [s[k] for s in state for k in ("o1", "o2", "o3")]
    if near_dp:
        while len(big) < 3:
            big.append(ring_step(*after(big[-1], state[-1]["o_own"])))
        last = lax.ppermute(after(big[2][0], *here), "dp", onward)
        big_a = place_rows([shard_big, *big[0], *big[1], *big[2], last], ((0, 2 * units),))[0]
    else:
        big_a = after(big_a, state[-1]["o_own"])
    big_b = pp(big_a, 1)
    for (first, count), s in zip(CHUNKS, state):
        ins = [(me_ref, None)]
        ins += [(s[k], by_row(s[k])) for k in ("o_own", "o1", "o2", "o3")]
        ins += [(w, fixed(w)) for w in (wo0, wo1, wo2, wo3, big_a, big_b)]
        ins += [(s["xh"], by_row(s["xh"]))]
        ins += [(w, whole(w)) for w in (biases, gains, shifts)]
        ins += [(w, fixed(w)) for w in (b_up_a, b_up_b)]
        outs = [
            sds((count, half, full), F32),
            sds((count, half, 128), F32),
            sds((count, half, full), BF),
            sds((count, half, units), BF),
            sds((count, half, units), BF),
            sds((count, half, 2 * units), BF),
            sds((count, half, full), BF),
        ]
        s["n1"], s["r1"], s["x1"], s["ga"], s["gb"], s["gp"], s["part"] = call(
            up_kernel, (count,), ins, outs, [by_row(o) for o in outs], [], "up", 4 * count,
        )
        s["part_y"] = pp(s["part"], 2)
        s["gc"], s["x1_c"] = pp(s["gb"], 1), pp(s["x1"], 1)

    for (first, count), s in zip(CHUNKS, state):
        ins = [(me_ref, None)]
        ins += [(s[k], by_row(s[k])) for k in ("n1", "part", "part_y")]
        ins += [(d, by_row(d, first)) for d in (dy_mine, dy1, dy2, dy3)]
        ins += [(w, whole(w)) for w in (biases, gains, shifts)]
        ins += [(w, fixed(w)) for w in (big_a, big_b)]
        ins += [(s["gp"], by_row(s["gp"]))]
        outs = [
            sds((count, width, half), BF),
            sds((count, width, half), BF),
            sds((count, half, full), F32),
            sds((count, half, full), BF),
            sds((count, half, units), BF),
            sds((count, half, units), BF),
            sds((count, half, full), BF),
            sds((count, 3, full), F32),
            sds((count, 1, 2 * units), F32),
        ]
        (
            s["act_own"], s["act_oth"], s["ds2"], s["ds2b"], s["da"], s["db"], s["part2"], s["vec2"],
            s["bup"],
        ) = call(
            down_kernel, (count,), ins, outs, [by_row(o) for o in outs],
            [pltpu.VMEM((full, half), F32)], "down", 4 * count,
        )
        s["part2_y"] = pp(s["part2"], 2)
        s["ds2b_c"], s["dc"] = pp(s["ds2b"], 1), pp(s["db"], 1)

    def ffn_grad(lefts, rights):
        block = 256
        def part(a):
            return pl.BlockSpec(a.shape[:2] + (block,), lambda i, s: (0, 0, i))
        ins = [(me_ref, None)] + [(a, fixed(a)) for a in lefts] + [(a, part(a)) for a in rights]
        across, down = rights[0].shape[-1], lefts[0].shape[-1]
        outs = [sds((down // 2, across), BF)] * 2
        specs = [pl.BlockSpec((down // 2, block), lambda i, s: (0, i))] * 2
        return call(
            functools.partial(ffn_grad_kernel, len(lefts), True),
            (across // block,), ins, outs, specs, [pltpu.VMEM((down, block), F32)], "ffn_grad", 3,
        )

    def fold(keep, got):
        outs = [sds((keep.shape[0] // 4, keep.shape[1]), BF)] * 4
        return call(
            fold_kernel, (1,), [(me_ref, None), (keep, whole(keep)), (got, whole(got))],
            outs, [whole(o) for o in outs], [], "fold", 1,
        )

    def total_of(parts):
        return functools.reduce(jnp.add, [p.astype(F32) for p in parts]).astype(BF)

    def scatter_z(cut):
        return [cut[0]] + [pp_z(cut[step], step) for step in (1, 2, 3)]

    def finish(blocks, outs, pair=False):
        return call(
            functools.partial(finish_kernel, ring_steps, pair), (1,),
            [(me_ref, None)] + [(b, whole(b)) for b in blocks],
            outs, [whole(o) for o in outs], [], "finish", 2,
        )

    def both(own, other):
        return [s[own] for s in state] + [s[other] for s in state]

    keep_d, send_d = ffn_grad(both("ga", "gc"), both("ds2b", "ds2b_c"))
    keep_u, send_u = ffn_grad(both("x1", "x1_c"), both("da", "dc"))

    def whole_of(keep, send):
        low = jnp.where(lax.rem(dp, 2) == 0, keep, send)
        high = jnp.where(lax.rem(dp, 2) == 0, send, keep)
        return jnp.concatenate([low, high], 0)

    if near_dp:
        got_d = pp_x(send_d)
        cut_d = fold(keep_d, got_d)
        state[0]["part2_y"] = after(state[0]["part2_y"], keep_u, *cut_d)
        z_d = scatter_z(cut_d)
        got_u = pp_x(after(send_u, got_d))
    else:
        grad_down, grad_up = lax.psum((whole_of(keep_d, send_d), whole_of(keep_u, send_u)), "dp")
        grad_down, grad_up = grad_down.astype(F32), grad_up.astype(F32)

    lg = None
    for (first, count), s in zip(CHUNKS, state):
        ins = [(me_ref, None)]
        ins += [(s[k], by_row(s[k])) for k in ("ds2", "part2", "part2_y", "n1", "r1")]
        ins += [(gains, whole(gains)), (wo0, fixed(wo0)), (wo1, fixed(wo1))]
        outs = [
            sds((count, half, full), BF),
            sds((count, 2 * width, half), F32),
            sds((count, width, half), BF),
            sds((count, width, half), BF),
            sds((count, 3, full), F32),
        ]
        s["ds1b"], s["near"], s["do_own"], s["do_oth"], s["vec1"] = call(
            mid_kernel, (count,), ins, outs,
            [by_row(o) for o in outs], [pltpu.VMEM((half, full), F32)], "mid", 2 * count,
        )
        s["do_c"], s["ds1b_c"] = pp(s["do_oth"], 1), pp(s["ds1b"], 1)

    def over_rows(key):
        return functools.reduce(jnp.add, [jnp.sum(s[key], axis=0) for s in state])

    if near_dp:
        cut_u = fold(keep_u, got_u)
        state[0]["do_c"] = after(state[0]["do_c"], *cut_u)
        z_u = scatter_z(cut_u)
        total_d = total_of(z_d)

    for (first, count), s in zip(CHUNKS, state):
        ins = [(me_ref, None)]
        ins += [(s[k], by_row(s[k])) for k in ("prob", "qkv", "do_own", "do_c")]
        ins += [(w_in, fixed(w_in)), (s["near"], by_row(s["near"]))]
        alias = None
        if lg is not None:
            alias = {len(ins): 0}
            ins += [(lg, pl.BlockSpec(memory_space=pl.ANY))]
        outs = [sds(prev_logits.shape, BF), sds((count, 3 * width, slots), BF)]
        outs += [sds((count, width, slots), BF)] * 4
        outs += [sds((count, width, 2), F32)]
        specs = [by_row(outs[0], first)] + [by_row(o) for o in outs[1:]]
        scratch = [pltpu.VMEM((width, slots), BF), pltpu.VMEM((full, slots), F32)]
        lg, s["dqkv"], s["e0"], s["e1"], s["e2"], s["e3"], s["bqv"] = call(
            functools.partial(back_kernel, heads, alias is not None),
            (count,), ins, outs, specs, scratch, "back", 4.3 * count, alias,
        )

    ins = [(me_ref, None)]
    for key in ("xt", "dqkv", "o_own", "ds1b", "o_oth", "ds1b_c"):
        ins += [(s[key], whole(s[key])) for s in state]
    outs = [sds((full // 2, full), BF)] * 2
    keep, send = call(
        functools.partial(qkv_grad_kernel, len(state)), (1,), ins, outs, [whole(o) for o in outs],
        [pltpu.VMEM((full, full), F32)], "qkv_grad", 4,
    )

    outs = [sds((3 * width, full), F32), sds((width, full), F32)]
    if near_dp:
        total_u = total_of(z_u)
        pair = jnp.concatenate([total_d, total_u], 0)
        ring_u = [ring_step(pair, pair)]
        got = pp_x(send)
        ring_u.append(ring_step(*ring_u[-1]))
        z_t = scatter_z(fold(keep, got))
        ring_u.append(ring_step(*ring_u[-1]))
        last_u = lax.ppermute(ring_u[-1][0], "dp", onward)
        total = total_of(z_t)
        ring = [ring_step(total, total)]
        ring.append(ring_step(*ring[-1]))
        ring.append(ring_step(*ring[-1]))
        last = lax.ppermute(ring[-1][0], "dp", onward)
        grad_down, grad_up = finish(
            [pair, *ring_u[0], *ring_u[1], *ring_u[2], last_u],
            [sds((units, full), F32), sds((full, units), F32)], True,
        )
        grad_in, grad_out = finish([total, *ring[0], *ring[1], *ring[2], last], outs)
    else:
        tail = lax.psum(whole_of(keep, send), "dp").astype(F32)
        grad_in, grad_out = tail[: 3 * width], tail[3 * width :]
    vec = jnp.concatenate([over_rows("vec1"), over_rows("vec2")], 0)
    bup = over_rows("bup").reshape(2, units)
    bqv = over_rows("bqv").T
    vec = vec + pp(vec, 1)
    vec = (vec + pp(vec, 2)) * 0.5
    bup = bup[0:1] + pp(bup[1:2], 1)
    small = jnp.concatenate(
        [vec, bup, jnp.pad(bqv.reshape(1, -1), ((0, 0), (0, full - 2 * width)))], 0
    )
    if near_dp:
        small = after(small, total)
    step = 1
    while step < groups:
        small = small + lax.ppermute(small, "dp", [(i, i ^ step) for i in range(groups)])
        step *= 2
    grad_b_up = small[6]
    grad_b_qv = small[7, : 2 * width].reshape(2, width)

    grad_in = jnp.transpose(grad_in.reshape(3, width, full), (2, 0, 1))

    def joined(key):
        return state[0][key] if len(state) == 1 else jnp.concatenate([s[key] for s in state], 0)

    act_own, act_c = joined("act_own"), pp(joined("act_oth"), 1)
    block_out = jnp.concatenate(
        [jnp.where(core == 0, act_own, act_c), jnp.where(core == 0, act_c, act_own)], 2
    )

    def dx_of(s):
        near = s["e2"].astype(F32) + pp(s["e3"], 1).astype(F32)
        far = pp(near.astype(BF), 2).astype(F32)
        return s["e0"].astype(F32) + pp(s["e1"], 1).astype(F32) + far

    parts = [dx_of(s) for s in state]
    grad_x = (parts[0] if len(parts) == 1 else jnp.concatenate(parts, 0)).astype(BF)
    return (
        jnp.swapaxes(block_out, 1, 2),
        raw,
        jnp.swapaxes(grad_x, 1, 2),
        lg,
        grad_in,
        grad_b_qv,
        grad_out,
        grad_up,
        grad_b_up,
        grad_down,
        jnp.stack([small[2], small[5]]),
        jnp.stack([small[0], small[3]]),
        jnp.stack([small[1], small[4]]),
    )


def solution(mesh):
    placed = (
        P("dp", None, "tensor"),
        P("dp", None, "tensor"),
        P("dp", "tensor", None, None),
        P("dp", None),
        P("dp", None, "tensor"),
        P(None, "tensor"),
        P("tensor", "dp"),
        P("dp", "tensor"),
        P("tensor"),
        P("tensor", "dp"),
        P(),
        P(),
        P(),
    )
    return jax.shard_map(
        body,
        mesh=mesh,
        in_specs=placed,
        out_specs=(
            P("dp", None, "tensor"),
            P("dp", "tensor", None, None),
            P("dp", None, "tensor"),
            P("dp", "tensor", None, None),
            P(None, None, "tensor"),
            P(None, "tensor"),
            P("tensor", None),
            P(None, "tensor"),
            P("tensor"),
            P("tensor", None),
            P(),
            P(),
            P(),
        ),
        check_vma=False,
    )
```

time: 782 us -> 335 us (0.43); the launches traced: 773 us -> 334 us
  waiting for transfers between devices: 347 us -> 137 us
  matrix products: 135 us -> 0 us
  blocking collectives: 112 us -> 0 us
  Pallas kernels: 0 us -> 81.9 us
  local copies, waits for them, and re-layouts: 99 us -> 24.4 us
  starting transfers between devices: 1.23 us -> 73.6 us
  other arithmetic: 61.8 us -> 16.3 us
  between operations: 16.5 us -> 1.17 us
    psum x4 -> x0, waiting for transfers between devices: 314 us -> none  [the longest x1 184 us: body(): lax.psum((grad_qkv, grad_b_qv, grad_out, grad_bias_out, grad_gain_one, gr...]
    ppermute x0 -> x72, waiting for transfers between devices: none -> 137 us  [the longest x29 46.3 us: pp(): return lax.ppermute(array, 'tensor', [(i, i ^ step) for i in range(4)])]
    dot_general x37 -> x0, matrix products: 125 us -> none  [the longest x6 18.7 us: attend_rows(): jnp.einsum('hqk,khe->qhe', probability, values, preferred_element_type=jn...]
    pallas_call x0 -> x15, Pallas kernels: none -> 81.9 us  [call(): pl.pallas_call(kernel, out_shape=outs, grid_spec=pltpu.PrefetchScalarGrid...]
    ppermute x0 -> x72, starting transfers between devices: none -> 73.6 us  [the longest x12 18 us: ring_step(): lax.ppermute(behind, 'dp', backward)]
    all_gather x2 -> x0, blocking collectives: 71.8 us -> none  [the longest x1 38.8 us: body(): lax.all_gather(w_qkv.astype(jnp.bfloat16), 'dp', axis=0, tiled=True)]
    psum x1 -> x0, blocking collectives: 39.7 us -> none  [body(): lax.psum((grad_qkv, grad_b_qv, grad_out, grad_bias_out, grad_gain_one, gr...]
    all_gather x4 -> x0, waiting for transfers between devices: 31.7 us -> none  [the longest x1 24.9 us: body(): lax.all_gather(w_down.astype(jnp.bfloat16), 'dp', axis=1, tiled=True)]
  transfers between devices with their start and end apart: 9 -> 72, of which waited for: 6 -> 26; matrix products, arithmetic and copies ran while one was open for 15% -> 5% of each run, Pallas kernels for 0% -> 18%
where the time goes in v1:
time: 335 us; the launch traced here: 334 us
  waiting for transfers between devices  137 us (41%)
  Pallas kernels  81.9 us (24%)
  starting transfers between devices  73.6 us (22%)
  local copies, waits for them, and re-layouts  24.4 us (7%)
  other arithmetic  16.3 us (5%)
    pallas_call x15, Pallas kernels, call(): pl.pallas_call(kernel, out_shape=outs, grid_spec=pltpu.PrefetchScalarGrid...  81.9 us
    ppermute x29, waiting for transfers between devices, pp(): return lax.ppermute(array, 'tensor', [(i, i ^ step) for i in range(4)])  46.3 us
    ppermute x12, waiting for transfers between devices, ring_step(): lax.ppermute(ahead, 'dp', onward)  32.2 us
    unnamed x109, local copies, waits for them, and re-layouts  21.3 us
    ppermute x12, starting transfers between devices, ring_step(): lax.ppermute(behind, 'dp', backward)  18 us
    ppermute x12, waiting for transfers between devices, ring_step(): lax.ppermute(behind, 'dp', backward)  16.8 us
    ppermute x9, starting transfers between devices, pp_z(): return lax.ppermute(array, 'dp', pairs)  14.8 us
    ppermute x12, starting transfers between devices, ring_step(): lax.ppermute(ahead, 'dp', onward)  14.6 us
  transfers between devices with their start and end apart: 72, of which 26 were waited for; matrix products, arithmetic and copies ran while one was open for 5% of the time, Pallas kernels for 18%

profile of v1, /device:TPU:0, one launch (start us, length us, event | category | flops | bytes accessed | tf_op | source)
XLA Modules:
  0.0 334.1 jit_solution(17362124282931235966)
XLA Ops:
  3.2 3.1 collective-permute-start.3
  6.2 3.8 %collective-permute-done.3.rest_1_ = bf16[96,768]{1,0:T(8,128)(2,1)S(1)} collective-permute-done((bf16[96,768]{1,0:T(8,128)(2,1)S(1)}, bf16[96,768]{1,0:T(8,128)(2,1)S(1)}, u32[]{:S(2)}, u32[]{:S(2)}) %collective-permute-start.3) | collective-permute-done | bytes 147488 | tf_op jit(solution)/shard_map/ppermute | solution.py:409
  17.0 3.3 collective-permute-done.7.rest_5_
  22.1 3.4 %collective-permute-done.9.rest_7_ = bf16[96,768]{1,0:T(8,128)(2,1)S(1)} collective-permute-done((bf16[96,768]{1,0:T(8,128)(2,1)S(1)}, bf16[96,768]{1,0:T(8,128)(2,1)S(1)}, u32[]{:S(2)}, u32[]{:S(2)}) %collective-permute-start.9) | collective-permute-done | bytes 147488 | tf_op jit(solution)/shard_map/ppermute | solution.py:432
  26.2 2.0 collective-permute-start.11
  28.3 2.0 collective-permute-start.4
  30.3 5.8 %collective-permute-done.4.rest_2_ = bf16[96,768]{1,0:T(8,128)(2,1)S(1)} collective-permute-done((bf16[96,768]{1,0:T(8,128)(2,1)S(1)}, bf16[96,768]{1,0:T(8,128)(2,1)S(1)}, u32[]{:S(2)}, u32[]{:S(2)}) %collective-permute-start.4) | collective-permute-done | bytes 147488 | tf_op jit(solution)/shard_map/ppermute | solution.py:409
  36.1 2.0 collective-permute-start.6
  40.2 2.6 collective-permute-done.6.rest_4_
  42.8 2.2 collective-permute-start.8
  46.2 4.2 %collective-permute-done.8.rest_6_ = bf16[96,768]{1,0:T(8,128)(2,1)S(1)} collective-permute-done((bf16[96,768]{1,0:T(8,128)(2,1)S(1)}, bf16[96,768]{1,0:T(8,128)(2,1)S(1)}, u32[]{:S(2)}, u32[]{:S(2)}) %collective-permute-start.8) | collective-permute-done | bytes 147488 | tf_op jit(solution)/shard_map/ppermute | solution.py:409
  55.7 2.3 gather.2.w_ref
  58.4 2.0 collective-permute-start.22
  60.4 12.7 %attend.1 = (bf16[3,3,512,512]{3,2,1,0:T(8,128)(2,1)}, bf16[3,3,512,512]{3,2,1,0:T(8,128)(2,1)}, bf16[3,3,192,512]{3,2,1,0:T(8,128)(2,1)}, bf16[3,192,256]{2,1,0...) custom-call(s32[4]{0:T(128)S(1)} %pad_add_fusion.me_ref, ...), custom_call_target="tpu_custom_call" | custom-call | flops 1290000000 | bytes 1024 | tf_op jit(solution)/shard_map/attend/pallas_call | solution.py:351
  80.7 3.7 %collective-permute-done.20.rest_5_ = bf16[96,1536]{1,0:T(8,128)(2,1)S(1)} collective-permute-done((bf16[96,1536]{1,0:T(8,128)(2,1)}, bf16[96,1536]{1,0:T(8,128)(2,1)S(1)}, u32[]{:S(2)}, u32[]{:S(2)}) %collective-permute-start.20) | collective-permute-done | bytes 294944 | tf_op jit(solution)/shard_map/ppermute | solution.py:409
  86.4 6.8 %collective-permute-done.13.o2 = bf16[3,192,256]{2,1,0:T(8,128)(2,1)S(1)} collective-permute-done((bf16[3,192,256]{2,1,0:T(8,128)(2,1)S(1)}, bf16[3,192,256]{2,1,0:T(8,128)(2,1)S(1)}, u32[]{:S(2)}, u32[]{:S(2)}) %collective-permute-start.13) | collective-permute-done | bytes 294944 | tf_op jit(solution)/shard_map/ppermute | solution.py:389
  94.8 7.0 %collective-permute-done.25.rest_7_ = bf16[96,1536]{1,0:T(8,128)(2,1)S(1)} collective-permute-done((bf16[96,1536]{1,0:T(8,128)(2,1)S(1)}, bf16[96,1536]{1,0:T(8,128)(2,1)S(1)}, u32[]{:S(2)}, u32[]{:S(2)}) %collective-permute-start.25) | collective-permute-done | bytes 294944 | tf_op jit(solution)/shard_map/ppermute | solution.py:490
  104.4 4.0 %collective-permute-done.27.b_up_b = f32[1,768]{1,0:T(1,128)S(1)} collective-permute-done((f32[1,768]{1,0:T(1,128)S(1)}, f32[1,768]{1,0:T(1,128)S(1)}, u32[]{:S(2)}, u32[]{:S(2)}) %collective-permute-start.27) | collective-permute-done | bytes 3104 | tf_op jit(solution)/shard_map/ppermute | solution.py:389
  109.8 12.8 %up.1 = (f32[3,256,768]{2,1,0:T(8,128)}, f32[3,256,128]{2,1,0:T(8,128)S(1)}, bf16[3,256,768]{2,1,0:T(8,128)(2,1)S(1)}, bf16[3,256,768]{2,1,0:T(8,128)(2,1)S(1)},...) custom-call(s32[4]{0:T(128)S(1)} %pad_add_fusion.me_ref, ...), custom_call_target="tpu_custom_call" | custom-call | flops 1200000000 | bytes 1024 | tf_op jit(solution)/shard_map/up/pallas_call | solution.py:351
  122.8 28.0 %collective-permute-done.28.pb_ref = bf16[3,256,768]{2,1,0:T(8,128)(2,1)S(1)} collective-permute-done((bf16[3,256,768]{2,1,0:T(8,128)(2,1)}, bf16[3,256,768]{2,1,0:T(8,128)(2,1)S(1)}, u32[]{:S(2)}, u32[]{:S(2)}) %collective-permute-start.28) | collective-permute-done | bytes 1179680 | tf_op jit(solution)/shard_map/ppermute | solution.py:389
  151.8 13.4 %down.1 = (bf16[3,192,256]{2,1,0:T(8,128)(2,1)S(1)}, bf16[3,192,256]{2,1,0:T(8,128)(2,1)}, f32[3,256,768]{2,1,0:T(8,128)}, bf16[3,256,768]{2,1,0:T(8,128)(2,1)S(...) custom-call(s32[4]{0:T(128)S(1)} %pad_add_fusion.me_ref, ...), custom_call_target="tpu_custom_call" | custom-call | flops 1200000000 | bytes 1024 | tf_op jit(solution)/shard_map/down/pallas_call | solution.py:351
  168.0 2.0 collective-permute-done.34.rest_3_
  170.0 4.1 %ffn_grad.3 = (bf16[384,768]{1,0:T(8,128)(2,1)S(1)}, bf16[384,768]{1,0:T(8,128)(2,1)}) custom-call(s32[4]{0:T(128)S(1)} %pad_add_fusion.me_ref, bf16[3,256,768]{2,1,0:T(8,128)(2,1)S(1)} %get-tuple-element.103.rest_0_, bf16[3,256,768]{2,1,0:T(8,128)(2,1)S(1)} %collective-permute-done.33.rest_1_, bf16[3,256,768]{2,1,0:T(8,128)(2,1)S(1)} %get-tuple-element.105.rest_2_, ...), custom_call_target="tpu_custom_call" | custom-call | flops 300000000 | bytes 1024 | tf_op jit(solution)/shard_map/ffn_grad/pallas_call | solution.py:351
  174.4 3.5 %ffn_grad.2 = (bf16[384,768]{1,0:T(8,128)(2,1)S(1)}, bf16[384,768]{1,0:T(8,128)(2,1)S(1)}) custom-call(s32[4]{0:T(128)S(1)} %pad_add_fusion.me_ref, bf16[3,256,768]{2,1,0:T(8,128)(2,1)S(1)} %get-tuple-element.99.rest_0_, bf16[3,256,768]{2,1,0:T(8,128)(2,1)S(1)} %collective-permute-done.31.rest_1_, bf16[3,256,768]{2,1,0:T(8,128)(2,1)S(1)} %get-tuple-element.100.rest_2_, ...), custom_call_target="tpu_custom_call" | custom-call | flops 300000000 | bytes 1024 | tf_op jit(solution)/shard_map/ffn_grad/pallas_call | solution.py:351
  178.7 11.0 %collective-permute-done.35.got_ref = bf16[384,768]{1,0:T(8,128)(2,1)S(1)} collective-permute-done((bf16[384,768]{1,0:T(8,128)(2,1)}, bf16[384,768]{1,0:T(8,128)(2,1)S(1)}, u32[]{:S(2)}, u32[]{:S(2)}) %collective-permute-start.35) | collective-permute-done | bytes 589856 | tf_op jit(solution)/shard_map/ppermute | solution.py:392
  193.0 3.4 %collective-permute-done.30.pb_ref = bf16[3,256,768]{2,1,0:T(8,128)(2,1)} collective-permute-done((bf16[3,256,768]{2,1,0:T(8,128)(2,1)}, bf16[3,256,768]{2,1,0:T(8,128)(2,1)}, u32[]{:S(2)}, u32[]{:S(2)}) %collective-permute-start.30) | collective-permute-done | bytes 1179680 | tf_op jit(solution)/shard_map/ppermute | solution.py:389
  196.4 6.0 %mid.1 = (bf16[3,256,768]{2,1,0:T(8,128)(2,1)}, f32[3,384,256]{2,1,0:T(8,128)S(1)}, bf16[3,192,256]{2,1,0:T(8,128)(2,1)S(1)}, bf16[3,192,256]{2,1,0:T(8,128)(2,1)S(1)}, f32[3,3,768]{2,1,0:T(4,128)S(1)}) custom-call(s32[4]{0:T(128)S(1)} %pad_add_fusion.me_ref, f32[3,256,768]{2,1,0:T(8,128)} %get-tuple-element.97.ds_ref, bf16[3,256,768]{2,1,0:T(8,128)(2,1)S(1)} %copy-done.3, ...), custom_call_target="tpu_custom_call" | custom-call | flops 600000000 | bytes 1024 | tf_op jit(solution)/shard_map/mid/pallas_call | solution.py:351
  211.5 2.8 collective-permute-start.60
  216.3 6.2 %collective-permute-done.60 = bf16[96,768]{1,0:T(8,128)(2,1)S(1)} collective-permute-done((bf16[96,768]{1,0:T(8,128)(2,1)}, bf16[96,768]{1,0:T(8,128)(2,1)S(1)}, u32[]{:S(2)}, u32[]{:S(2)}) %collective-permute-start.60) | collective-permute-done | bytes 147488 | tf_op jit(solution)/shard_map/ppermute | solution.py:397
  224.0 2.7 collective-permute-done.37.got_ref
  230.3 2.5 collective-permute-start.64
  232.8 12.1 %back.1 = (bf16[3,3,512,512]{3,2,1,0:T(8,128)(2,1)}, bf16[3,576,512]{2,1,0:T(8,128)(2,1)}, bf16[3,192,512]{2,1,0:T(8,128)(2,1)S(1)}, bf16[3,192,512]{2,1,0:T(8,1...) custom-call(s32[4]{0:T(128)S(1)} %pad_add_fusion.me_ref, ...), custom_call_target="tpu_custom_call" | custom-call | flops 1290000000 | bytes 1024 | tf_op jit(solution)/shard_map/back/pallas_call | solution.py:351
  248.2 5.8 %qkv_grad.1 = (bf16[384,768]{1,0:T(8,128)(2,1)S(1)}, bf16[384,768]{1,0:T(8,128)(2,1)}) custom-call(s32[4]{0:T(128)S(1)} %pad_add_fusion.me_ref, bf16[3,768,512]{2,1,0:T(8,128)(2,1)} %get-tuple-element.129.rest_0_, bf16[3,576,512]{2,1,0:T(8,128)(2,1)S(1)} %copy-done.1, bf16[3,192,256]{2,1,0:T(8,128)(2,1)S(1)} %get-tuple-element.82.o0.rest_2_, ...), custom_call_target="tpu_custom_call" | custom-call | flops 400000000 | bytes 1024 | tf_op jit(solution)/shard_map/qkv_grad/pallas_call | solution.py:351
  256.9 19.3 %collective-permute-done.65.rest_1_ = bf16[192,768]{1,0:T(8,128)(2,1)S(1)} collective-permute-done((bf16[192,768]{1,0:T(8,128)(2,1)S(1)}, bf16[192,768]{1,0:T(8,128)(2,1)S(1)}, u32[]{:S(2)}, u32[]{:S(2)}) %collective-permute-start.65) | collective-permute-done | bytes 294944 | tf_op jit(solution)/shard_map/ppermute | solution.py:409
  278.5 2.3 collective-permute-start.45
  280.8 2.1 add_convert_fusion.1
  282.9 3.9 %collective-permute-done.43 = bf16[96,768]{1,0:T(8,128)(2,1)S(1)} collective-permute-done((bf16[96,768]{1,0:T(8,128)(2,1)S(1)}, bf16[96,768]{1,0:T(8,128)(2,1)S(1)}, u32[]{:S(2)}, u32[]{:S(2)}) %collective-permute-start.43) | collective-permute-done | bytes 147488 | tf_op jit(solution)/shard_map/ppermute | solution.py:397
  286.8 3.8 %collective-permute-done.44 = bf16[96,768]{1,0:T(8,128)(2,1)S(1)} collective-permute-done((bf16[96,768]{1,0:T(8,128)(2,1)S(1)}, bf16[96,768]{1,0:T(8,128)(2,1)S(1)}, u32[]{:S(2)}, u32[]{:S(2)}) %collective-permute-start.44) | collective-permute-done | bytes 147488 | tf_op jit(solution)/shard_map/ppermute | solution.py:397
  290.6 2.1 collective-permute-start.68
  294.2 3.0 collective-permute-done.56
  299.1 4.1 %collective-permute-start.57 = (f32[8,768]{1,0:T(8,128)S(1)}, f32[8,768]{1,0:T(8,128)S(1)}, u32[]{:S(2)}, u32[]{:S(2)}) collective-permute-start(f32[8,768]{1,0:T(8,128)S(1)} %add.74), channel_id=1, source_target_pairs={{0,8},{4,12},{8,0},{12,4},{16,24},{20,28},{24,16},{28,20},{1,9},{5... | collective-permute-start | bytes 73736 | tf_op jit(solution)/shard_map/ppermute | solution.py:689
  304.6 2.3 collective-permute-start.70
  306.9 2.1 collective-permute-start.71
  311.5 2.1 collective-permute-start.58
  315.5 2.2 fusion
  317.7 3.0 finish.3
  323.5 2.9 collective-permute-done.49.rest_4_
  331.9 2.2 finish.2
  (260 shorter events, 86.4 us)
Async XLA Ops:
  11.8 16.4 %collective-permute-start.1 = (bf16[3,192,512]{2,1,0:T(8,128)(2,1)S(1)}, bf16[3,192,512]{2,1,0:T(8,128)(2,1)S(1)}, u32[]{:S(2)}, u32[]{:S(2)}) collective-permute-start(bf16[3,192,512]{2,1,0:T(8,128)(2,1)S(1)} %bitcast.20), channel_id=1, source_target_pairs={{0,2},{1,3},{2,0},{3,1},{4,6},{5,7},{6,4},{7,5},{8,10},{9,11},{10,... | collective-permute-start | bytes 1769480 | tf_op jit(solution)/shard_map/ppermute | solution.py:389
  13.3 44.8 %collective-permute-start = (bf16[3,192,512]{2,1,0:T(8,128)(2,1)S(1)}, bf16[3,192,512]{2,1,0:T(8,128)(2,1)S(1)}, u32[]{:S(2)}, u32[]{:S(2)}) collective-permute-start(bf16[3,192,512]{2,1,0:T(8,128)(2,1)S(1)} %bitcast.21), channel_id=1, source_target_pairs={{0,1},{1,0},{2,3},{3,2},{4,5},{5,4},{6,7},{7,6},{8,9},{9,8},{10,11... | collective-permute-start | bytes 1769480 | tf_op jit(solution)/shard_map/ppermute | solution.py:389
  26.2 11.9 %collective-permute-start.11 = (bf16[96,1536]{1,0:T(8,128)(2,1)S(1)}, bf16[96,1536]{1,0:T(8,128)(2,1)}, u32[]{:S(2)}, u32[]{:S(2)}) collective-permute-start(bf16[96,1536]{1,0:T(8,128)(2,1)S(1)} %pad_maximum_fusion.rest_0_), channel_id=1, source_target_pairs={{8,0},{16,8},{24,16},{28,24},{20,28},{12,20},{4,12},{0,4},{9,1},{1... | collective-permute-start | bytes 884744 | tf_op jit(solution)/shard_map/ppermute | solution.py:409
  28.3 11.5 %collective-permute-start.10 = (bf16[96,1536]{1,0:T(8,128)(2,1)S(1)}, bf16[96,1536]{1,0:T(8,128)(2,1)}, u32[]{:S(2)}, u32[]{:S(2)}) collective-permute-start(bf16[96,1536]{1,0:T(8,128)(2,1)S(1)} %pad_maximum_fusion.rest_0_), channel_id=1, source_target_pairs={{0,8},{8,16},{16,24},{24,28},{28,20},{20,12},{12,4},{4,0},{1,9},{9... | collective-permute-start | bytes 884744 | tf_op jit(solution)/shard_map/ppermute | solution.py:409
  28.3 32.1 %collective-permute-start.2 = (bf16[3,192,512]{2,1,0:T(8,128)(2,1)S(1)}, bf16[3,192,512]{2,1,0:T(8,128)(2,1)}, u32[]{:S(2)}, u32[]{:S(2)}) collective-permute-start(bf16[3,192,512]{2,1,0:T(8,128)(2,1)S(1)} %collective-permute-done.1.x2), channel_id=1, source_target_pairs={{0,1},{1,0},{2,3},{3,2},{4,5},{5,4},{6,7},{7,6},{8,9},{9,8},{10,11... | collective-permute-start | bytes 1769480 | tf_op jit(solution)/shard_map/ppermute | solution.py:389
  38.1 20.2 %collective-permute-start.19 = (bf16[96,1536]{1,0:T(8,128)(2,1)}, bf16[96,1536]{1,0:T(8,128)(2,1)}, u32[]{:S(2)}, u32[]{:S(2)}) collective-permute-start(bf16[96,1536]{1,0:T(8,128)(2,1)} %collective-permute-done.11.rest_2_), channel_id=1, source_target_pairs={{8,0},{16,8},{24,16},{28,24},{20,28},{12,20},{4,12},{0,4},{9,1},{1... | collective-permute-start | bytes 884744 | tf_op jit(solution)/shard_map/ppermute | solution.py:409
  39.7 18.6 %collective-permute-start.18 = (bf16[96,1536]{1,0:T(8,128)(2,1)}, bf16[96,1536]{1,0:T(8,128)(2,1)}, u32[]{:S(2)}, u32[]{:S(2)}) collective-permute-start(bf16[96,1536]{1,0:T(8,128)(2,1)} %collective-permute-done.10.rest_1_), channel_id=1, source_target_pairs={{0,8},{8,16},{16,24},{24,28},{28,20},{20,12},{12,4},{4,0},{1,9},{9... | collective-permute-start | bytes 884744 | tf_op jit(solution)/shard_map/ppermute | solution.py:409
  51.0 23.1 %collective-permute-start.23 = (bf16[3,192,256]{2,1,0:T(8,128)(2,1)S(1)}, bf16[3,192,256]{2,1,0:T(8,128)(2,1)S(1)}, u32[]{:S(2)}, u32[]{:S(2)}) collective-permute-start(bf16[3,192,256]{2,1,0:T(8,128)(2,1)S(1)} %get-tuple-element.149.dy0), channel_id=1, source_target_pairs={{0,2},{1,3},{2,0},{3,1},{4,6},{5,7},{6,4},{7,5},{8,10},{9,11},{10,... | collective-permute-start | bytes 884744 | tf_op jit(solution)/shard_map/ppermute | solution.py:389
  58.1 18.5 %collective-permute-start.16 = (bf16[768,192]{1,0:T(8,128)(2,1)S(1)}, bf16[768,192]{1,0:T(8,128)(2,1)S(1)}, u32[]{:S(2)}, u32[]{:S(2)}) collective-permute-start(bf16[768,192]{1,0:T(8,128)(2,1)S(1)} %slice.35.wo0), channel_id=1, source_target_pairs={{0,2},{1,3},{2,0},{3,1},{4,6},{5,7},{6,4},{7,5},{8,10},{9,11},{10,... | collective-permute-start | bytes 884744 | tf_op jit(solution)/shard_map/ppermute | solution.py:389
  58.3 18.5 %collective-permute-start.24 = (bf16[3,192,256]{2,1,0:T(8,128)(2,1)S(1)}, bf16[3,192,256]{2,1,0:T(8,128)(2,1)S(1)}, u32[]{:S(2)}, u32[]{:S(2)}) collective-permute-start(bf16[3,192,256]{2,1,0:T(8,128)(2,1)S(1)} %get-tuple-element.150), channel_id=1, source_target_pairs={{0,3},{1,2},{2,1},{3,0},{4,7},{5,6},{6,5},{7,4},{8,11},{9,10},{10,... | collective-permute-start | bytes 884744 | tf_op jit(solution)/shard_map/ppermute | solution.py:389
  58.4 19.6 %collective-permute-start.22 = (bf16[3,192,256]{2,1,0:T(8,128)(2,1)S(1)}, bf16[3,192,256]{2,1,0:T(8,128)(2,1)S(1)}, u32[]{:S(2)}, u32[]{:S(2)}) collective-permute-start(bf16[3,192,256]{2,1,0:T(8,128)(2,1)S(1)} %get-tuple-element.150), channel_id=1, source_target_pairs={{0,1},{1,0},{2,3},{3,2},{4,5},{5,4},{6,7},{7,6},{8,9},{9,8},{10,11... | collective-permute-start | bytes 884744 | tf_op jit(solution)/shard_map/ppermute | solution.py:389
  60.4 18.3 %collective-permute-start.15 = (bf16[768,192]{1,0:T(8,128)(2,1)S(1)}, bf16[768,192]{1,0:T(8,128)(2,1)S(1)}, u32[]{:S(2)}, u32[]{:S(2)}) collective-permute-start(bf16[768,192]{1,0:T(8,128)(2,1)S(1)} %slice.35.wo0), channel_id=1, source_target_pairs={{0,1},{1,0},{2,3},{3,2},{4,5},{5,4},{6,7},{7,6},{8,9},{9,8},{10,11... | collective-permute-start | bytes 884744 | tf_op jit(solution)/shard_map/ppermute | solution.py:389
  74.9 9.6 %collective-permute-start.20 = (bf16[96,1536]{1,0:T(8,128)(2,1)}, bf16[96,1536]{1,0:T(8,128)(2,1)S(1)}, u32[]{:S(2)}, u32[]{:S(2)}) collective-permute-start(bf16[96,1536]{1,0:T(8,128)(2,1)} %collective-permute-done.18.rest_3_), channel_id=1, source_target_pairs={{0,8},{8,16},{16,24},{24,28},{28,20},{20,12},{12,4},{4,0},{1,9},{9... | collective-permute-start | bytes 884744 | tf_op jit(solution)/shard_map/ppermute | solution.py:409
  77.5 8.9 %collective-permute-start.14 = (bf16[3,192,256]{2,1,0:T(8,128)(2,1)S(1)}, bf16[3,192,256]{2,1,0:T(8,128)(2,1)S(1)}, u32[]{:S(2)}, u32[]{:S(2)}) collective-permute-start(bf16[3,192,256]{2,1,0:T(8,128)(2,1)S(1)} %get-tuple-element.83.rest_4_), channel_id=1, source_target_pairs={{0,3},{1,2},{2,1},{3,0},{4,7},{5,6},{6,5},{7,4},{8,11},{9,10},{10,... | collective-permute-start | bytes 884744 | tf_op jit(solution)/shard_map/ppermute | solution.py:389
  78.7 14.5 %collective-permute-start.13 = (bf16[3,192,256]{2,1,0:T(8,128)(2,1)S(1)}, bf16[3,192,256]{2,1,0:T(8,128)(2,1)S(1)}, u32[]{:S(2)}, u32[]{:S(2)}) collective-permute-start(bf16[3,192,256]{2,1,0:T(8,128)(2,1)S(1)} %get-tuple-element.82.o0.rest_2_), channel_id=1, source_target_pairs={{0,2},{1,3},{2,0},{3,1},{4,6},{5,7},{6,4},{7,5},{8,10},{9,11},{10,... | collective-permute-start | bytes 884744 | tf_op jit(solution)/shard_map/ppermute | solution.py:389
  80.5 14.3 %collective-permute-start.21 = (bf16[96,1536]{1,0:T(8,128)(2,1)}, bf16[96,1536]{1,0:T(8,128)(2,1)S(1)}, u32[]{:S(2)}, u32[]{:S(2)}) collective-permute-start(bf16[96,1536]{1,0:T(8,128)(2,1)} %collective-permute-done.19.rest_4_), channel_id=1, source_target_pairs={{8,0},{16,8},{24,16},{28,24},{20,28},{12,20},{4,12},{0,4},{9,1},{1... | collective-permute-start | bytes 884744 | tf_op jit(solution)/shard_map/ppermute | solution.py:409
  93.2 8.6 %collective-permute-start.25 = (bf16[96,1536]{1,0:T(8,128)(2,1)S(1)}, bf16[96,1536]{1,0:T(8,128)(2,1)S(1)}, u32[]{:S(2)}, u32[]{:S(2)}) collective-permute-start(bf16[96,1536]{1,0:T(8,128)(2,1)S(1)} %collective-permute-done.20.rest_5_), channel_id=1, source_target_pairs={{0,8},{8,16},{16,24},{24,28},{28,20},{20,12},{12,4},{4,0},{1,9},{9... | collective-permute-start | bytes 884744 | tf_op jit(solution)/shard_map/ppermute | solution.py:490
  122.6 28.2 %collective-permute-start.28 = (bf16[3,256,768]{2,1,0:T(8,128)(2,1)}, bf16[3,256,768]{2,1,0:T(8,128)(2,1)S(1)}, u32[]{:S(2)}, u32[]{:S(2)}) collective-permute-start(bf16[3,256,768]{2,1,0:T(8,128)(2,1)} %get-tuple-element.90.pa_ref), channel_id=1, source_target_pairs={{0,2},{1,3},{2,0},{3,1},{4,6},{5,7},{6,4},{7,5},{8,10},{9,11},{10,... | collective-permute-start | bytes 3538952 | tf_op jit(solution)/shard_map/ppermute | solution.py:389
  122.6 45.3 %collective-permute-start.33 = (bf16[3,256,768]{2,1,0:T(8,128)(2,1)}, bf16[3,256,768]{2,1,0:T(8,128)(2,1)S(1)}, u32[]{:S(2)}, u32[]{:S(2)}) collective-permute-start(bf16[3,256,768]{2,1,0:T(8,128)(2,1)} %get-tuple-element.104), channel_id=1, source_target_pairs={{0,1},{1,0},{2,3},{3,2},{4,5},{5,4},{6,7},{7,6},{8,9},{9,8},{10,11... | collective-permute-start | bytes 3538952 | tf_op jit(solution)/shard_map/ppermute | solution.py:389
  167.7 28.7 %collective-permute-start.30 = (bf16[3,256,768]{2,1,0:T(8,128)(2,1)}, bf16[3,256,768]{2,1,0:T(8,128)(2,1)}, u32[]{:S(2)}, u32[]{:S(2)}) collective-permute-start(bf16[3,256,768]{2,1,0:T(8,128)(2,1)} %get-tuple-element.98.pa_ref), channel_id=1, source_target_pairs={{0,2},{1,3},{2,0},{3,1},{4,6},{5,7},{6,4},{7,5},{8,10},{9,11},{10,... | collective-permute-start | bytes 3538952 | tf_op jit(solution)/shard_map/ppermute | solution.py:389
  174.1 15.6 %collective-permute-start.35 = (bf16[384,768]{1,0:T(8,128)(2,1)}, bf16[384,768]{1,0:T(8,128)(2,1)S(1)}, u32[]{:S(2)}, u32[]{:S(2)}) collective-permute-start(bf16[384,768]{1,0:T(8,128)(2,1)} %get-tuple-element.107), channel_id=1, source_target_pairs={{0,4},{4,0},{8,12},{12,8},{16,20},{20,16},{24,28},{28,24},{1,5},{5... | collective-permute-start | bytes 1769480 | tf_op jit(solution)/shard_map/ppermute | solution.py:392
  203.7 42.8 %collective-permute-start.41 = (bf16[3,256,768]{2,1,0:T(8,128)(2,1)}, bf16[3,256,768]{2,1,0:T(8,128)(2,1)}, u32[]{:S(2)}, u32[]{:S(2)}) collective-permute-start(bf16[3,256,768]{2,1,0:T(8,128)(2,1)} %get-tuple-element.131.rest_3_), channel_id=1, source_target_pairs={{0,1},{1,0},{2,3},{3,2},{4,5},{5,4},{6,7},{7,6},{8,9},{9,8},{10,11... | collective-permute-start | bytes 3538952 | tf_op jit(solution)/shard_map/ppermute | solution.py:389
  207.0 8.6 %collective-permute-start.59 = (bf16[96,768]{1,0:T(8,128)(2,1)}, bf16[96,768]{1,0:T(8,128)(2,1)}, u32[]{:S(2)}, u32[]{:S(2)}) collective-permute-start(bf16[96,768]{1,0:T(8,128)(2,1)} %copy-done.46), channel_id=1, source_target_pairs={{0,8},{4,12},{8,16},{12,20},{16,24},{20,28},{24,0},{28,4},{1,9},{5... | collective-permute-start | bytes 442376 | tf_op jit(solution)/shard_map/ppermute | solution.py:397
  210.8 16.0 %collective-permute-start.37 = (bf16[384,768]{1,0:T(8,128)(2,1)}, bf16[384,768]{1,0:T(8,128)(2,1)S(1)}, u32[]{:S(2)}, u32[]{:S(2)}) collective-permute-start(bf16[384,768]{1,0:T(8,128)(2,1)} %copy-done.42), channel_id=1, source_target_pairs={{0,4},{4,0},{8,12},{12,8},{16,20},{20,16},{24,28},{28,24},{1,5},{5... | collective-permute-start | bytes 1769480 | tf_op jit(solution)/shard_map/ppermute | solution.py:392
  211.5 11.0 %collective-permute-start.60 = (bf16[96,768]{1,0:T(8,128)(2,1)}, bf16[96,768]{1,0:T(8,128)(2,1)S(1)}, u32[]{:S(2)}, u32[]{:S(2)}) collective-permute-start(bf16[96,768]{1,0:T(8,128)(2,1)} %copy-done.45), channel_id=1, source_target_pairs={{0,16},{4,20},{8,24},{12,28},{16,0},{20,4},{24,8},{28,12},{1,17},{... | collective-permute-start | bytes 442376 | tf_op jit(solution)/shard_map/ppermute | solution.py:397
  214.3 8.7 %collective-permute-start.61 = (bf16[96,768]{1,0:T(8,128)(2,1)}, bf16[96,768]{1,0:T(8,128)(2,1)S(1)}, u32[]{:S(2)}, u32[]{:S(2)}) collective-permute-start(bf16[96,768]{1,0:T(8,128)(2,1)} %copy-done.44), channel_id=1, source_target_pairs={{0,24},{4,28},{8,0},{12,4},{16,8},{20,12},{24,16},{28,20},{1,25},{... | collective-permute-start | bytes 442376 | tf_op jit(solution)/shard_map/ppermute | solution.py:397
  215.6 14.7 %collective-permute-start.36 = (bf16[3,192,256]{2,1,0:T(8,128)(2,1)}, bf16[3,192,256]{2,1,0:T(8,128)(2,1)S(1)}, u32[]{:S(2)}, u32[]{:S(2)}) collective-permute-start(bf16[3,192,256]{2,1,0:T(8,128)(2,1)} %copy-done.43), channel_id=1, source_target_pairs={{0,1},{1,0},{2,3},{3,2},{4,5},{5,4},{6,7},{7,6},{8,9},{9,8},{10,11... | collective-permute-start | bytes 884744 | tf_op jit(solution)/shard_map/ppermute | solution.py:389
  222.5 32.8 %collective-permute-start.54 = (f32[6,768]{1,0:T(8,128)S(1)}, f32[6,768]{1,0:T(8,128)S(1)}, u32[]{:S(2)}, u32[]{:S(2)}) collective-permute-start(f32[6,768]{1,0:T(8,128)S(1)} %fusion.1), channel_id=1, source_target_pairs={{0,2},{1,3},{2,0},{3,1},{4,6},{5,7},{6,4},{7,5},{8,10},{9,11},{10,... | collective-permute-start | bytes 55304 | tf_op jit(solution)/shard_map/ppermute | solution.py:389
  227.4 26.6 %collective-permute-start.62 = (bf16[96,768]{1,0:T(8,128)(2,1)S(1)}, bf16[96,768]{1,0:T(8,128)(2,1)S(1)}, u32[]{:S(2)}, u32[]{:S(2)}) collective-permute-start(bf16[96,768]{1,0:T(8,128)(2,1)S(1)} %get-tuple-element.119), channel_id=1, source_target_pairs={{0,8},{4,12},{8,16},{12,20},{16,24},{20,28},{24,0},{28,4},{1,9},{5... | collective-permute-start | bytes 442376 | tf_op jit(solution)/shard_map/ppermute | solution.py:397
  229.0 25.5 %collective-permute-start.63 = (bf16[96,768]{1,0:T(8,128)(2,1)S(1)}, bf16[96,768]{1,0:T(8,128)(2,1)S(1)}, u32[]{:S(2)}, u32[]{:S(2)}) collective-permute-start(bf16[96,768]{1,0:T(8,128)(2,1)S(1)} %get-tuple-element.120), channel_id=1, source_target_pairs={{0,16},{4,20},{8,24},{12,28},{16,0},{20,4},{24,8},{28,12},{1,17},{... | collective-permute-start | bytes 442376 | tf_op jit(solution)/shard_map/ppermute | solution.py:397
  230.3 24.2 %collective-permute-start.64 = (bf16[96,768]{1,0:T(8,128)(2,1)S(1)}, bf16[96,768]{1,0:T(8,128)(2,1)S(1)}, u32[]{:S(2)}, u32[]{:S(2)}) collective-permute-start(bf16[96,768]{1,0:T(8,128)(2,1)S(1)} %get-tuple-element.121), channel_id=1, source_target_pairs={{0,24},{4,28},{8,0},{12,4},{16,8},{20,12},{24,16},{28,20},{1,25},{... | collective-permute-start | bytes 442376 | tf_op jit(solution)/shard_map/ppermute | solution.py:397
  246.6 31.9 %collective-permute-start.39 = (bf16[3,192,512]{2,1,0:T(8,128)(2,1)}, bf16[3,192,512]{2,1,0:T(8,128)(2,1)}, u32[]{:S(2)}, u32[]{:S(2)}) collective-permute-start(bf16[3,192,512]{2,1,0:T(8,128)(2,1)} %get-tuple-element.127), channel_id=1, source_target_pairs={{0,1},{1,0},{2,3},{3,2},{4,5},{5,4},{6,7},{7,6},{8,9},{9,8},{10,11... | collective-permute-start | bytes 1769480 | tf_op jit(solution)/shard_map/ppermute | solution.py:389
  254.0 22.2 %collective-permute-start.42 = (bf16[384,768]{1,0:T(8,128)(2,1)}, bf16[384,768]{1,0:T(8,128)(2,1)S(1)}, u32[]{:S(2)}, u32[]{:S(2)}) collective-permute-start(bf16[384,768]{1,0:T(8,128)(2,1)} %get-tuple-element.133), channel_id=1, source_target_pairs={{0,4},{4,0},{8,12},{12,8},{16,20},{20,16},{24,28},{28,24},{1,5},{5... | collective-permute-start | bytes 1769480 | tf_op jit(solution)/shard_map/ppermute | solution.py:392
  254.6 21.6 %collective-permute-start.65 = (bf16[192,768]{1,0:T(8,128)(2,1)S(1)}, bf16[192,768]{1,0:T(8,128)(2,1)S(1)}, u32[]{:S(2)}, u32[]{:S(2)}) collective-permute-start(bf16[192,768]{1,0:T(8,128)(2,1)S(1)} %pad_maximum_fusion.1.rest_0_), channel_id=1, source_target_pairs={{0,8},{8,16},{16,24},{24,28},{28,20},{20,12},{12,4},{4,0},{1,9},{9... | collective-permute-start | bytes 884744 | tf_op jit(solution)/shard_map/ppermute | solution.py:409
  255.6 27.4 %collective-permute-start.66 = (bf16[192,768]{1,0:T(8,128)(2,1)S(1)}, bf16[192,768]{1,0:T(8,128)(2,1)S(1)}, u32[]{:S(2)}, u32[]{:S(2)}) collective-permute-start(bf16[192,768]{1,0:T(8,128)(2,1)S(1)} %pad_maximum_fusion.1.rest_0_), channel_id=1, source_target_pairs={{8,0},{16,8},{24,16},{28,24},{20,28},{12,20},{4,12},{0,4},{9,1},{1... | collective-permute-start | bytes 884744 | tf_op jit(solution)/shard_map/ppermute | solution.py:409
  276.2 16.8 %collective-permute-start.67 = (bf16[192,768]{1,0:T(8,128)(2,1)S(1)}, bf16[192,768]{1,0:T(8,128)(2,1)S(1)}, u32[]{:S(2)}, u32[]{:S(2)}) collective-permute-start(bf16[192,768]{1,0:T(8,128)(2,1)S(1)} %collective-permute-done.65.rest_1_), channel_id=1, source_target_pairs={{0,8},{8,16},{16,24},{24,28},{28,20},{20,12},{12,4},{4,0},{1,9},{9... | collective-permute-start | bytes 884744 | tf_op jit(solution)/shard_map/ppermute | solution.py:409
  276.9 9.9 %collective-permute-start.43 = (bf16[96,768]{1,0:T(8,128)(2,1)S(1)}, bf16[96,768]{1,0:T(8,128)(2,1)S(1)}, u32[]{:S(2)}, u32[]{:S(2)}) collective-permute-start(bf16[96,768]{1,0:T(8,128)(2,1)S(1)} %get-tuple-element.135), channel_id=1, source_target_pairs={{0,8},{4,12},{8,16},{12,20},{16,24},{20,28},{24,0},{28,4},{1,9},{5... | collective-permute-start | bytes 442376 | tf_op jit(solution)/shard_map/ppermute | solution.py:397
  277.0 13.6 %collective-permute-start.44 = (bf16[96,768]{1,0:T(8,128)(2,1)S(1)}, bf16[96,768]{1,0:T(8,128)(2,1)S(1)}, u32[]{:S(2)}, u32[]{:S(2)}) collective-permute-start(bf16[96,768]{1,0:T(8,128)(2,1)S(1)} %get-tuple-element.136), channel_id=1, source_target_pairs={{0,16},{4,20},{8,24},{12,28},{16,0},{20,4},{24,8},{28,12},{1,17},{... | collective-permute-start | bytes 442376 | tf_op jit(solution)/shard_map/ppermute | solution.py:397
  278.5 14.2 %collective-permute-start.45 = (bf16[96,768]{1,0:T(8,128)(2,1)S(1)}, bf16[96,768]{1,0:T(8,128)(2,1)S(1)}, u32[]{:S(2)}, u32[]{:S(2)}) collective-permute-start(bf16[96,768]{1,0:T(8,128)(2,1)S(1)} %get-tuple-element.137), channel_id=1, source_target_pairs={{0,24},{4,28},{8,0},{12,4},{16,8},{20,12},{24,16},{28,20},{1,25},{... | collective-permute-start | bytes 442376 | tf_op jit(solution)/shard_map/ppermute | solution.py:397
  282.9 16.1 %collective-permute-start.29 = (bf16[3,192,256]{2,1,0:T(8,128)(2,1)}, bf16[3,192,256]{2,1,0:T(8,128)(2,1)}, u32[]{:S(2)}, u32[]{:S(2)}) collective-permute-start(bf16[3,192,256]{2,1,0:T(8,128)(2,1)} %get-tuple-element.93), channel_id=1, source_target_pairs={{0,1},{1,0},{2,3},{3,2},{4,5},{5,4},{6,7},{7,6},{8,9},{9,8},{10,11... | collective-permute-start | bytes 884744 | tf_op jit(solution)/shard_map/ppermute | solution.py:389
  286.8 23.1 %collective-permute-start.38 = (bf16[3,192,512]{2,1,0:T(8,128)(2,1)S(1)}, bf16[3,192,512]{2,1,0:T(8,128)(2,1)S(1)}, u32[]{:S(2)}, u32[]{:S(2)}) collective-permute-start(bf16[3,192,512]{2,1,0:T(8,128)(2,1)S(1)} %copy-done.41), channel_id=1, source_target_pairs={{0,1},{1,0},{2,3},{3,2},{4,5},{5,4},{6,7},{7,6},{8,9},{9,8},{10,11... | collective-permute-start | bytes 1769480 | tf_op jit(solution)/shard_map/ppermute | solution.py:389
  290.6 8.5 %collective-permute-start.68 = (bf16[192,768]{1,0:T(8,128)(2,1)S(1)}, bf16[192,768]{1,0:T(8,128)(2,1)S(1)}, u32[]{:S(2)}, u32[]{:S(2)}) collective-permute-start(bf16[192,768]{1,0:T(8,128)(2,1)S(1)} %collective-permute-done.66.rest_2_), channel_id=1, source_target_pairs={{8,0},{16,8},{24,16},{28,24},{20,28},{12,20},{4,12},{0,4},{9,1},{1... | collective-permute-start | bytes 884744 | tf_op jit(solution)/shard_map/ppermute | solution.py:409
  292.7 18.8 %collective-permute-start.40 = (bf16[3,192,512]{2,1,0:T(8,128)(2,1)}, bf16[3,192,512]{2,1,0:T(8,128)(2,1)}, u32[]{:S(2)}, u32[]{:S(2)}) collective-permute-start(bf16[3,192,512]{2,1,0:T(8,128)(2,1)} %add_convert_fusion.1), channel_id=1, source_target_pairs={{0,2},{1,3},{2,0},{3,1},{4,6},{5,7},{6,4},{7,5},{8,10},{9,11},{10,... | collective-permute-start | bytes 1769480 | tf_op jit(solution)/shard_map/ppermute | solution.py:389
  299.0 14.6 %collective-permute-start.46 = (bf16[96,768]{1,0:T(8,128)(2,1)S(1)}, bf16[96,768]{1,0:T(8,128)(2,1)S(1)}, u32[]{:S(2)}, u32[]{:S(2)}) collective-permute-start(bf16[96,768]{1,0:T(8,128)(2,1)S(1)} %add_convert_fusion.4.rest_0_), channel_id=1, source_target_pairs={{0,8},{8,16},{16,24},{24,28},{28,20},{20,12},{12,4},{4,0},{1,9},{9... | collective-permute-start | bytes 442376 | tf_op jit(solution)/shard_map/ppermute | solution.py:409
  304.6 13.1 %collective-permute-start.70 = (bf16[192,768]{1,0:T(8,128)(2,1)S(1)}, bf16[192,768]{1,0:T(8,128)(2,1)S(1)}, u32[]{:S(2)}, u32[]{:S(2)}) collective-permute-start(bf16[192,768]{1,0:T(8,128)(2,1)S(1)} %collective-permute-done.68.rest_4_), channel_id=1, source_target_pairs={{8,0},{16,8},{24,16},{28,24},{20,28},{12,20},{4,12},{0,4},{9,1},{1... | collective-permute-start | bytes 884744 | tf_op jit(solution)/shard_map/ppermute | solution.py:409
  306.9 10.8 %collective-permute-start.71 = (bf16[192,768]{1,0:T(8,128)(2,1)S(1)}, bf16[192,768]{1,0:T(8,128)(2,1)S(1)}, u32[]{:S(2)}, u32[]{:S(2)}) collective-permute-start(bf16[192,768]{1,0:T(8,128)(2,1)S(1)} %collective-permute-done.69.rest_5_), channel_id=1, source_target_pairs={{0,8},{8,16},{16,24},{24,28},{28,20},{20,12},{12,4},{4,0},{1,9},{9... | collective-permute-start | bytes 884744 | tf_op jit(solution)/shard_map/ppermute | solution.py:662
  309.9 10.8 %collective-permute-start.47 = (bf16[96,768]{1,0:T(8,128)(2,1)S(1)}, bf16[96,768]{1,0:T(8,128)(2,1)S(1)}, u32[]{:S(2)}, u32[]{:S(2)}) collective-permute-start(bf16[96,768]{1,0:T(8,128)(2,1)S(1)} %add_convert_fusion.4.rest_0_), channel_id=1, source_target_pairs={{8,0},{16,8},{24,16},{28,24},{20,28},{12,20},{4,12},{0,4},{9,1},{1... | collective-permute-start | bytes 442376 | tf_op jit(solution)/shard_map/ppermute | solution.py:409
  311.5 9.2 %collective-permute-start.58 = (f32[8,768]{1,0:T(8,128)S(1)}, f32[8,768]{1,0:T(8,128)S(1)}, u32[]{:S(2)}, u32[]{:S(2)}) collective-permute-start(f32[8,768]{1,0:T(8,128)S(1)} %add.75), channel_id=1, source_target_pairs={{0,16},{4,20},{8,24},{12,28},{16,0},{20,4},{24,8},{28,12},{1,17},{... | collective-permute-start | bytes 73736 | tf_op jit(solution)/shard_map/ppermute | solution.py:689
  (78 other events, 685.8 us)

commit v2 on v1

--- a/solution.py
+++ b/solution.py
@@ -11,7 +11,6 @@
 NEG = -1e30
 BF = jnp.bfloat16
 F32 = jnp.float32
-CHUNKS = ((0, 3),)
 VMEM_LIMIT = 48 * 1024 * 1024
 
 
@@ -52,11 +51,9 @@
 
 
 def attend_kernel(
-    first, heads, aliased, me_ref, x0, x1, x2, x3, w_ref, b_ref, prev_ref, seg_ref, *rest
+    heads, me_ref, x0, x1, x2, x3, w_ref, b_ref, prev_ref, seg_ref,
+    raw_ref, p_ref, qkv_ref, own_ref, oth_ref, xt_ref, xh_ref, o_scr,
 ):
-    if aliased:
-        rest = rest[1:]
-    raw_ref, p_ref, qkv_ref, own_ref, oth_ref, xt_ref, xh_ref, o_scr = rest
     me = me_ref[0]
     core = lax.rem(me, 2)
     width, slots = x0.shape[1], x0.shape[2]
@@ -74,7 +71,7 @@
     mine = pl.ds(pl.multiple_of(core * half, half), half)
     other = pl.ds(pl.multiple_of((1 - core) * half, half), half)
     xh_ref[0] = jnp.transpose(xt_ref[0, :, mine])
-    row = seg_ref[pl.ds(first + pl.program_id(0), 1), :].astype(F32)
+    row = seg_ref[pl.ds(pl.program_id(0), 1), :].astype(F32)
     column = jnp.transpose(jnp.broadcast_to(row, (128, slots)))[:, 0:1]
     scale = 1.0 / (size**0.5)
     for block in range(2):
@@ -125,7 +122,7 @@
 def down_kernel(
     me_ref, n1_ref, pa_ref, pb_ref, dy0, dy1, dy2, dy3, bias_ref, gain_ref, shift_ref,
     big_a, big_b, gp_ref,
-    act_own_ref, act_oth_ref, ds_ref, dsb_ref, da_ref, db_ref, part_ref, vec_ref, bup_ref,
+    act_own_ref, act_oth_ref, ds_ref, dsb_ref, da_ref, db_ref, vec_ref, bup_ref, part_ref,
     scr,
 ):
     me = me_ref[0]
@@ -165,7 +162,7 @@
 
 def mid_kernel(
     me_ref, ds_ref, pa_ref, pb_ref, n1_ref, r1_ref, gain_ref, wo0, wo1,
-    dsb_ref, near_ref, do_own_ref, do_oth_ref, vec_ref, scr,
+    dsb_ref, near_ref, vec_ref, do_own_ref, do_oth_ref, scr,
 ):
     chip = me_ref[0] // 2
     width = do_own_ref.shape[1]
@@ -185,11 +182,9 @@
 
 
 def back_kernel(
-    heads, aliased, me_ref, p_ref, qkv_ref, do_own_ref, do_oth_ref, w_ref, near_ref, *rest
+    heads, me_ref, p_ref, qkv_ref, do_own_ref, do_oth_ref, w_ref, near_ref,
+    lg_ref, dqkv_ref, e0, e1, e2, e3, vec_ref, do_scr, dx_scr,
 ):
-    if aliased:
-        rest = rest[1:]
-    lg_ref, dqkv_ref, e0, e1, e2, e3, vec_ref, do_scr, dx_scr = rest
     me = me_ref[0]
     core, chip = lax.rem(me, 2), me // 2
     width, slots = qkv_ref.shape[2], qkv_ref.shape[3]
@@ -227,7 +222,7 @@
         out[0] = dx_scr[pl.ds(start, width), :].astype(BF)
 
 
-def ffn_grad_kernel(count, split, me_ref, *rest):
+def ffn_grad_kernel(count, me_ref, *rest):
     lefts, rights = rest[:count], rest[count : 2 * count]
     keep_ref, send_ref, scr = rest[2 * count :]
     side = me_ref[1]
@@ -335,15 +330,21 @@
     return pl.BlockSpec(shape, lambda i, s: (0,) * len(shape))
 
 
-def fixed(array):
-    shape = array.shape
-    return pl.BlockSpec(shape, lambda i, s: (0,) * len(shape), pipeline_mode=pl.Buffered(1))
+def held(array):
+    return pl.BlockSpec(memory_space=pltpu.VMEM)
 
 
 def by_row(array, first=0):
     shape = array.shape
     rest = (0,) * (len(shape) - 1)
     return pl.BlockSpec((1,) + shape[1:], lambda i, s: (first + i,) + rest)
+
+
+def without(low, high, kernel):
+    def inner(*refs):
+        kernel(*refs[:low], *refs[high:])
+
+    return inner
 
 
 def call(kernel, grid, ins, outs, out_specs, scratch, name, micros, alias=None):
@@ -385,6 +386,8 @@
     def after(value, *others):
         return lax.optimization_barrier((value, others))[0]
 
+    together = lax.optimization_barrier
+
     def pp(array, step):
         return lax.ppermute(array, "tensor", [(i, i ^ step) for i in range(4)])
 
@@ -427,15 +430,14 @@
     big = []
     if near_dp:
         ring = [ring_step(shard_in, shard_in)]
-        ring.append(ring_step(*ring[-1]))
-        ring.append(ring_step(*ring[-1]))
-        last = lax.ppermute(ring[-1][0], "dp", onward)
+        ring.append(ring_step(*together(ring[-1])))
+        ring.append(ring_step(*together(ring[-1])))
+        last = lax.ppermute(together(ring[-1])[0], "dp", onward)
         shard_big = after(shard_big, last)
         big.append(ring_step(shard_big, shard_big))
         w_in = place_rows([shard_in, *ring[0], *ring[1], *ring[2], last], ((0, full),))[0]
-        if len(CHUNKS) == 1:
-            w_in = after(w_in, *big[0])
-            big.append(ring_step(*big[0]))
+        w_in = after(w_in, *big[0])
+        big.append(ring_step(*big[0]))
     else:
         w_in = lax.all_gather(shard_in, "dp", axis=0, tiled=True)
         big_a = lax.all_gather(shard_big, "dp", axis=0, tiled=True)
@@ -451,107 +453,94 @@
     b_up_a = b_up.reshape(1, units)
     b_up_b = pp(b_up_a, 1)
 
-    raw = None
-    state = []
-    for first, count in CHUNKS:
-        ins = [(me_ref, None)] + [(p, by_row(p, first)) for p in x_pieces]
-        ins += [(w_in, fixed(w_in)), (b_qv, whole(b_qv)), (prev_logits, by_row(prev_logits, first))]
-        ins += [(segment_ids, whole(segment_ids))]
-        alias = None
-        if raw is not None:
-            alias = {len(ins): 0}
-            ins += [(raw, pl.BlockSpec(memory_space=pl.ANY))]
-        outs = [
-            sds(prev_logits.shape, BF),
-            sds((count,) + prev_logits.shape[1:], BF),
-            sds((count, 3, width, slots), BF),
-            sds((count, width, half), BF),
-            sds((count, width, half), BF),
-            sds((count, full, slots), BF),
-            sds((count, half, full), BF),
-        ]
-        specs = [by_row(outs[0], first)] + [by_row(o) for o in outs[1:]]
-        raw, prob, qkv, o_own, o_oth, xt, xh = call(
-            functools.partial(attend_kernel, first, heads, alias is not None),
-            (count,), ins, outs, specs, [pltpu.VMEM((width, slots), BF)], "attend",
-            4.3 * count, alias,
-        )
-        state.append(dict(prob=prob, qkv=qkv, o_own=o_own, o_oth=o_oth, xh=xh, xt=xt))
-        if near_dp and len(big) < 3 and len(CHUNKS) > 1:
-            w_in = after(w_in, *big[-1])
-            big.append(ring_step(*after(big[-1], o_own)))
-
-    for s in state:
-        s["o1"], s["o2"], s["o3"] = pp(s["o_oth"], 1), pp(s["o_own"], 2), pp(s["o_oth"], 3)
-    here = [wo1, wo3, dy1, dy2, dy3] + [s[k] for s in state for k in ("o1", "o2", "o3")]
+    sds3 = lambda *shape_type: sds((rows,) + shape_type[:-1], shape_type[-1])
+
+    def per_row(kernel, inputs, fulls, parts, scratch, name, micros):
+        kept, out_parts = None, []
+        for row in range(rows):
+            ins = [(me_ref, None)] + inputs(row)
+            low = len(ins)
+            alias = {}
+            body_kernel = kernel
+            if kept is not None:
+                alias = {low + i: i for i in range(len(fulls))}
+                ins += [(k, pl.BlockSpec(memory_space=pl.ANY)) for k in kept]
+                body_kernel = without(low, low + len(kept), kernel)
+            outs = list(fulls) + list(parts)
+            specs = [by_row(o, row) for o in fulls] + [by_row(o) for o in parts]
+            result = call(body_kernel, (1,), ins, outs, specs, scratch, name, micros, alias)
+            kept = result[: len(fulls)]
+            out_parts.append(result[len(fulls) :])
+        return kept, list(zip(*out_parts))
+
+    ins = [(me_ref, None)] + [(p, by_row(p)) for p in x_pieces]
+    ins += [(w_in, held(w_in)), (b_qv, whole(b_qv)), (prev_logits, by_row(prev_logits))]
+    ins += [(segment_ids, whole(segment_ids))]
+    outs = [
+        sds(prev_logits.shape, BF),
+        sds(prev_logits.shape, BF),
+        sds3(3, width, slots, BF),
+        sds3(width, half, BF),
+        sds3(width, half, BF),
+        sds3(full, slots, BF),
+        sds3(half, full, BF),
+    ]
+    raw, prob, qkv, o_own, o_oth, xt, xh = call(
+        functools.partial(attend_kernel, heads), (rows,), ins, outs, [by_row(o) for o in outs],
+        [pltpu.VMEM((width, slots), BF)], "attend", 4.3 * rows,
+    )
+    o1, o2, o3 = pp(o_oth, 1), pp(o_own, 2), pp(o_oth, 3)
     if near_dp:
-        while len(big) < 3:
-            big.append(ring_step(*after(big[-1], state[-1]["o_own"])))
-        last = lax.ppermute(after(big[2][0], *here), "dp", onward)
+        big.append(ring_step(*after(big[-1], o_own)))
+        last = lax.ppermute(after(big[2][0], wo1, wo3, dy1, dy2, dy3, o1, o2, o3), "dp", onward)
         big_a = place_rows([shard_big, *big[0], *big[1], *big[2], last], ((0, 2 * units),))[0]
     else:
-        big_a = after(big_a, state[-1]["o_own"])
+        big_a = after(big_a, o_own)
     big_b = pp(big_a, 1)
-    for (first, count), s in zip(CHUNKS, state):
-        ins = [(me_ref, None)]
-        ins += [(s[k], by_row(s[k])) for k in ("o_own", "o1", "o2", "o3")]
-        ins += [(w, fixed(w)) for w in (wo0, wo1, wo2, wo3, big_a, big_b)]
-        ins += [(s["xh"], by_row(s["xh"]))]
-        ins += [(w, whole(w)) for w in (biases, gains, shifts)]
-        ins += [(w, fixed(w)) for w in (b_up_a, b_up_b)]
-        outs = [
-            sds((count, half, full), F32),
-            sds((count, half, 128), F32),
-            sds((count, half, full), BF),
-            sds((count, half, units), BF),
-            sds((count, half, units), BF),
-            sds((count, half, 2 * units), BF),
-            sds((count, half, full), BF),
-        ]
-        s["n1"], s["r1"], s["x1"], s["ga"], s["gb"], s["gp"], s["part"] = call(
-            up_kernel, (count,), ins, outs, [by_row(o) for o in outs], [], "up", 4 * count,
-        )
-        s["part_y"] = pp(s["part"], 2)
-        s["gc"], s["x1_c"] = pp(s["gb"], 1), pp(s["x1"], 1)
-
-    for (first, count), s in zip(CHUNKS, state):
-        ins = [(me_ref, None)]
-        ins += [(s[k], by_row(s[k])) for k in ("n1", "part", "part_y")]
-        ins += [(d, by_row(d, first)) for d in (dy_mine, dy1, dy2, dy3)]
-        ins += [(w, whole(w)) for w in (biases, gains, shifts)]
-        ins += [(w, fixed(w)) for w in (big_a, big_b)]
-        ins += [(s["gp"], by_row(s["gp"]))]
-        outs = [
-            sds((count, width, half), BF),
-            sds((count, width, half), BF),
-            sds((count, half, full), F32),
-            sds((count, half, full), BF),
-            sds((count, half, units), BF),
-            sds((count, half, units), BF),
-            sds((count, half, full), BF),
-            sds((count, 3, full), F32),
-            sds((count, 1, 2 * units), F32),
-        ]
-        (
-            s["act_own"], s["act_oth"], s["ds2"], s["ds2b"], s["da"], s["db"], s["part2"], s["vec2"],
-            s["bup"],
-        ) = call(
-            down_kernel, (count,), ins, outs, [by_row(o) for o in outs],
-            [pltpu.VMEM((full, half), F32)], "down", 4 * count,
-        )
-        s["part2_y"] = pp(s["part2"], 2)
-        s["ds2b_c"], s["dc"] = pp(s["ds2b"], 1), pp(s["db"], 1)
+
+    one = (1, half, full)
+    (n1, r1, x1, ga, gb, gp), (part,) = per_row(
+        up_kernel,
+        lambda row: [(o, by_row(o, row)) for o in (o_own, o1, o2, o3)]
+        + [(w, held(w)) for w in (wo0, wo1, wo2, wo3, big_a, big_b)]
+        + [(xh, by_row(xh, row))]
+        + [(w, whole(w)) for w in (biases, gains, shifts, b_up_a, b_up_b)],
+        [
+            sds3(half, full, F32), sds3(half, 128, F32), sds3(half, full, BF),
+            sds3(half, units, BF), sds3(half, units, BF), sds3(half, 2 * units, BF),
+        ],
+        [sds(one, BF)], [], "up", 4,
+    )
+    part_y = [pp(p, 2) for p in part]
+    gc, x1_c = pp(gb, 1), pp(x1, 1)
+
+    (act_own, act_oth, ds2, ds2b, da, db, vec2, bup), (part2,) = per_row(
+        down_kernel,
+        lambda row: [(n1, by_row(n1, row)), (part[row], by_row(part[row])), (part_y[row], by_row(part_y[row]))]
+        + [(d, by_row(d, row)) for d in (dy_mine, dy1, dy2, dy3)]
+        + [(w, whole(w)) for w in (biases, gains, shifts)]
+        + [(w, held(w)) for w in (big_a, big_b)]
+        + [(gp, by_row(gp, row))],
+        [
+            sds3(width, half, BF), sds3(width, half, BF), sds3(half, full, F32),
+            sds3(half, full, BF), sds3(half, units, BF), sds3(half, units, BF),
+            sds3(3, full, F32), sds3(1, 2 * units, F32),
+        ],
+        [sds(one, BF)], [pltpu.VMEM((full, half), F32)], "down", 4,
+    )
+    part2_y = [pp(p, 2) for p in part2]
+    ds2b_c, dc = pp(ds2b, 1), pp(db, 1)
 
     def ffn_grad(lefts, rights):
         block = 256
         def part(a):
             return pl.BlockSpec(a.shape[:2] + (block,), lambda i, s: (0, 0, i))
-        ins = [(me_ref, None)] + [(a, fixed(a)) for a in lefts] + [(a, part(a)) for a in rights]
+        ins = [(me_ref, None)] + [(a, whole(a)) for a in lefts] + [(a, part(a)) for a in rights]
         across, down = rights[0].shape[-1], lefts[0].shape[-1]
         outs = [sds((down // 2, across), BF)] * 2
         specs = [pl.BlockSpec((down // 2, block), lambda i, s: (0, i))] * 2
         return call(
-            functools.partial(ffn_grad_kernel, len(lefts), True),
+            functools.partial(ffn_grad_kernel, len(lefts)),
             (across // block,), ins, outs, specs, [pltpu.VMEM((down, block), F32)], "ffn_grad", 3,
         )
 
@@ -575,78 +564,54 @@
             outs, [whole(o) for o in outs], [], "finish", 2,
         )
 
-    def both(own, other):
-        return [s[own] for s in state] + [s[other] for s in state]
-
-    keep_d, send_d = ffn_grad(both("ga", "gc"), both("ds2b", "ds2b_c"))
-    keep_u, send_u = ffn_grad(both("x1", "x1_c"), both("da", "dc"))
-
     def whole_of(keep, send):
         low = jnp.where(lax.rem(dp, 2) == 0, keep, send)
         high = jnp.where(lax.rem(dp, 2) == 0, send, keep)
         return jnp.concatenate([low, high], 0)
 
+    keep_d, send_d = ffn_grad((ga, gc), (ds2b, ds2b_c))
+    keep_u, send_u = ffn_grad((x1, x1_c), (da, dc))
     if near_dp:
         got_d = pp_x(send_d)
+        part2_y[0] = after(part2_y[0], keep_d, keep_u)
+        got_u = pp_x(after(send_u, got_d))
         cut_d = fold(keep_d, got_d)
-        state[0]["part2_y"] = after(state[0]["part2_y"], keep_u, *cut_d)
+        part2_y[2] = after(part2_y[2], *cut_d)
         z_d = scatter_z(cut_d)
-        got_u = pp_x(after(send_u, got_d))
+        cut_u = fold(keep_u, got_u)
+        z_u = scatter_z(cut_u)
+        total_d = total_of(z_d)
     else:
         grad_down, grad_up = lax.psum((whole_of(keep_d, send_d), whole_of(keep_u, send_u)), "dp")
         grad_down, grad_up = grad_down.astype(F32), grad_up.astype(F32)
 
-    lg = None
-    for (first, count), s in zip(CHUNKS, state):
-        ins = [(me_ref, None)]
-        ins += [(s[k], by_row(s[k])) for k in ("ds2", "part2", "part2_y", "n1", "r1")]
-        ins += [(gains, whole(gains)), (wo0, fixed(wo0)), (wo1, fixed(wo1))]
-        outs = [
-            sds((count, half, full), BF),
-            sds((count, 2 * width, half), F32),
-            sds((count, width, half), BF),
-            sds((count, width, half), BF),
-            sds((count, 3, full), F32),
-        ]
-        s["ds1b"], s["near"], s["do_own"], s["do_oth"], s["vec1"] = call(
-            mid_kernel, (count,), ins, outs,
-            [by_row(o) for o in outs], [pltpu.VMEM((half, full), F32)], "mid", 2 * count,
-        )
-        s["do_c"], s["ds1b_c"] = pp(s["do_oth"], 1), pp(s["ds1b"], 1)
-
-    def over_rows(key):
-        return functools.reduce(jnp.add, [jnp.sum(s[key], axis=0) for s in state])
+    (ds1b, near, vec1), (do_own, do_oth) = per_row(
+        mid_kernel,
+        lambda row: [(ds2, by_row(ds2, row)), (part2[row], by_row(part2[row])), (part2_y[row], by_row(part2_y[row]))]
+        + [(n1, by_row(n1, row)), (r1, by_row(r1, row)), (gains, whole(gains))]
+        + [(wo0, held(wo0)), (wo1, held(wo1))],
+        [sds3(half, full, BF), sds3(2 * width, half, F32), sds3(3, full, F32)],
+        [sds((1, width, half), BF)] * 2, [pltpu.VMEM((half, full), F32)], "mid", 2,
+    )
+    do_c = [pp(d, 1) for d in do_oth]
+    ds1b_c = pp(ds1b, 1)
 
     if near_dp:
-        cut_u = fold(keep_u, got_u)
-        state[0]["do_c"] = after(state[0]["do_c"], *cut_u)
-        z_u = scatter_z(cut_u)
-        total_d = total_of(z_d)
-
-    for (first, count), s in zip(CHUNKS, state):
-        ins = [(me_ref, None)]
-        ins += [(s[k], by_row(s[k])) for k in ("prob", "qkv", "do_own", "do_c")]
-        ins += [(w_in, fixed(w_in)), (s["near"], by_row(s["near"]))]
-        alias = None
-        if lg is not None:
-            alias = {len(ins): 0}
-            ins += [(lg, pl.BlockSpec(memory_space=pl.ANY))]
-        outs = [sds(prev_logits.shape, BF), sds((count, 3 * width, slots), BF)]
-        outs += [sds((count, width, slots), BF)] * 4
-        outs += [sds((count, width, 2), F32)]
-        specs = [by_row(outs[0], first)] + [by_row(o) for o in outs[1:]]
-        scratch = [pltpu.VMEM((width, slots), BF), pltpu.VMEM((full, slots), F32)]
-        lg, s["dqkv"], s["e0"], s["e1"], s["e2"], s["e3"], s["bqv"] = call(
-            functools.partial(back_kernel, heads, alias is not None),
-            (count,), ins, outs, specs, scratch, "back", 4.3 * count, alias,
-        )
-
-    ins = [(me_ref, None)]
-    for key in ("xt", "dqkv", "o_own", "ds1b", "o_oth", "ds1b_c"):
-        ins += [(s[key], whole(s[key])) for s in state]
+        do_c[2] = after(do_c[2], *cut_u)
+    (lg, dqkv, e0, e1, e2, e3, bqv), _ = per_row(
+        functools.partial(back_kernel, heads),
+        lambda row: [(prob, by_row(prob, row)), (qkv, by_row(qkv, row))]
+        + [(do_own[row], by_row(do_own[row])), (do_c[row], by_row(do_c[row]))]
+        + [(w_in, held(w_in)), (near, by_row(near, row))],
+        [sds(prev_logits.shape, BF), sds3(3 * width, slots, BF)]
+        + [sds3(width, slots, BF)] * 4 + [sds3(width, 2, F32)],
+        [], [pltpu.VMEM((width, slots), BF), pltpu.VMEM((full, slots), F32)], "back", 4.3,
+    )
+
+    ins = [(me_ref, None)] + [(a, whole(a)) for a in (xt, dqkv, o_own, ds1b, o_oth, ds1b_c)]
     outs = [sds((full // 2, full), BF)] * 2
     keep, send = call(
-        functools.partial(qkv_grad_kernel, len(state)), (1,), ins, outs, [whole(o) for o in outs],
+        functools.partial(qkv_grad_kernel, 1), (1,), ins, outs, [whole(o) for o in outs],
         [pltpu.VMEM((full, full), F32)], "qkv_grad", 4,
     )
 
@@ -673,9 +638,9 @@
     else:
         tail = lax.psum(whole_of(keep, send), "dp").astype(F32)
         grad_in, grad_out = tail[: 3 * width], tail[3 * width :]
-    vec = jnp.concatenate([over_rows("vec1"), over_rows("vec2")], 0)
-    bup = over_rows("bup").reshape(2, units)
-    bqv = over_rows("bqv").T
+    vec = jnp.concatenate([jnp.sum(vec1, 0), jnp.sum(vec2, 0)], 0)
+    bup = jnp.sum(bup, 0).reshape(2, units)
+    bqv = jnp.sum(bqv, 0).T
     vec = vec + pp(vec, 1)
     vec = (vec + pp(vec, 2)) * 0.5
     bup = bup[0:1] + pp(bup[1:2], 1)
@@ -693,21 +658,13 @@
 
     grad_in = jnp.transpose(grad_in.reshape(3, width, full), (2, 0, 1))
 
-    def joined(key):
-        return state[0][key] if len(state) == 1 else jnp.concatenate([s[key] for s in state], 0)
-
-    act_own, act_c = joined("act_own"), pp(joined("act_oth"), 1)
+    act_c = pp(act_oth, 1)
     block_out = jnp.concatenate(
         [jnp.where(core == 0, act_own, act_c), jnp.where(core == 0, act_c, act_own)], 2
     )
-
-    def dx_of(s):
-        near = s["e2"].astype(F32) + pp(s["e3"], 1).astype(F32)
-        far = pp(near.astype(BF), 2).astype(F32)
-        return s["e0"].astype(F32) + pp(s["e1"], 1).astype(F32) + far
-
-    parts = [dx_of(s) for s in state]
-    grad_x = (parts[0] if len(parts) == 1 else jnp.concatenate(parts, 0)).astype(BF)
+    near_sum = e2.astype(F32) + pp(e3, 1).astype(F32)
+    far = pp(near_sum.astype(BF), 2).astype(F32)
+    grad_x = (e0.astype(F32) + pp(e1, 1).astype(F32) + far).astype(BF)
     return (
         jnp.swapaxes(block_out, 1, 2),
         raw,

time: 335 us -> 321 us (0.958); the launches traced: 334 us -> 315 us
  waiting for transfers between devices: 137 us -> 97.8 us
  Pallas kernels: 81.9 us -> 104 us
    ppermute x29 -> x35, waiting for transfers between devices: 46.3 us -> 23.8 us  [pp(): return lax.ppermute(array, 'tensor', [(i, i ^ step) for i in range(4)])]
    pallas_call x15 -> x23, Pallas kernels: 81.9 us -> 104 us  [call(): pl.pallas_call(kernel, out_shape=outs, grid_spec=pltpu.PrefetchScalarGrid...]
    ppermute x3, waiting for transfers between devices: 13.6 us -> 0.01 us  [pp_x(): return lax.ppermute(array, 'dp', [(i, i ^ 1) for i in range(groups)])]
    ppermute x12, waiting for transfers between devices: 32.2 us -> 41.5 us  [ring_step(): lax.ppermute(ahead, 'dp', onward)]
    ppermute x12, starting transfers between devices: 18 us -> 9.92 us  [ring_step(): lax.ppermute(behind, 'dp', backward)]
    ppermute x29 -> x35, starting transfers between devices: 10.9 us -> 18.5 us  [pp(): return lax.ppermute(array, 'tensor', [(i, i ^ step) for i in range(4)])]
    ppermute x12, waiting for transfers between devices: 16.8 us -> 11.1 us  [ring_step(): lax.ppermute(behind, 'dp', backward)]
    ppermute x9, waiting for transfers between devices: 13.9 us -> 8.51 us  [pp_z(): return lax.ppermute(array, 'dp', pairs)]
  transfers between devices with their start and end apart: 72 -> 78, of which waited for: 26 -> 27; matrix products, arithmetic and copies ran while one was open for 5% -> 5% of each run, Pallas kernels for 18% -> 29%
where the time goes in v2:
time: 321 us; the launch traced here: 315 us
  Pallas kernels  104 us (32%)
  waiting for transfers between devices  97.8 us (30%)
  starting transfers between devices  74.4 us (23%)
  local copies, waits for them, and re-layouts  23.2 us (7%)
  other arithmetic  13.9 us (4%)
    pallas_call x23, Pallas kernels, call(): pl.pallas_call(kernel, out_shape=outs, grid_spec=pltpu.PrefetchScalarGrid...  104 us
    ppermute x12, waiting for transfers between devices, ring_step(): lax.ppermute(ahead, 'dp', onward)  41.5 us
    ppermute x35, waiting for transfers between devices, pp(): return lax.ppermute(array, 'tensor', [(i, i ^ step) for i in range(4)])  23.8 us
    unnamed x139, local copies, waits for them, and re-layouts  19.5 us
    ppermute x35, starting transfers between devices, pp(): return lax.ppermute(array, 'tensor', [(i, i ^ step) for i in range(4)])  18.5 us
    ppermute x12, starting transfers between devices, ring_step(): lax.ppermute(ahead, 'dp', onward)  15.5 us
    ppermute x9, starting transfers between devices, pp_z(): return lax.ppermute(array, 'dp', pairs)  13.8 us
    ppermute x12, waiting for transfers between devices, ring_step(): lax.ppermute(behind, 'dp', backward)  11.1 us
  transfers between devices with their start and end apart: 78, of which 27 were waited for; matrix products, arithmetic and copies ran while one was open for 5% of the time, Pallas kernels for 29%

profile of v2, /device:TPU:0, one launch (start us, length us, event | category | flops | bytes accessed | tf_op | source)
XLA Modules:
  0.0 315.4 jit_solution(2033366206938917677)
XLA Ops:
  3.1 3.1 collective-permute-start.3
  6.2 3.8 %collective-permute-done.3.rest_1_ = bf16[96,768]{1,0:T(8,128)(2,1)S(1)} collective-permute-done((bf16[96,768]{1,0:T(8,128)(2,1)S(1)}, bf16[96,768]{1,0:T(8,128)(2,1)S(1)}, u32[]{:S(2)}, u32[]{:S(2)}) %collective-permute-start.3) | collective-permute-done | bytes 147488 | tf_op jit(solution)/shard_map/ppermute | solution.py:412
  20.3 3.1 collective-permute-done.7.rest_5_
  26.9 3.4 %collective-permute-done.9.rest_7_ = bf16[96,768]{1,0:T(8,128)(2,1)S(1)} collective-permute-done((bf16[96,768]{1,0:T(8,128)(2,1)S(1)}, bf16[96,768]{1,0:T(8,128)(2,1)S(1)}, u32[]{:S(2)}, u32[]{:S(2)}) %collective-permute-start.9) | collective-permute-done | bytes 147488 | tf_op jit(solution)/shard_map/ppermute | solution.py:435
  32.3 5.7 %collective-permute-done.10.rest_1_ = bf16[96,1536]{1,0:T(8,128)(2,1)} collective-permute-done((bf16[96,1536]{1,0:T(8,128)(2,1)S(1)}, bf16[96,1536]{1,0:T(8,128)(2,1)}, u32[]{:S(2)}, u32[]{:S(2)}) %collective-permute-start.10) | collective-permute-done | bytes 294944 | tf_op jit(solution)/shard_map/ppermute | solution.py:412
  46.7 2.3 gather.2.w_ref.refs_5_
  51.5 12.7 %attend.1 = (bf16[3,3,512,512]{3,2,1,0:T(8,128)(2,1)}, bf16[3,3,512,512]{3,2,1,0:T(8,128)(2,1)}, bf16[3,3,192,512]{3,2,1,0:T(8,128)(2,1)}, bf16[3,192,256]{2,1,0...) custom-call(s32[4]{0:T(128)S(1)} %pad_add_fusion.me_ref.refs_0_, ...), custom_call_target="tpu_custom_call" | custom-call | flops 1290000000 | bytes 1024 | tf_op jit(solution)/shard_map/attend/pallas_call | solution.py:352
  68.7 6.4 %collective-permute-done.20.rest_5_ = bf16[96,1536]{1,0:T(8,128)(2,1)S(1)} collective-permute-done((bf16[96,1536]{1,0:T(8,128)(2,1)}, bf16[96,1536]{1,0:T(8,128)(2,1)S(1)}, u32[]{:S(2)}, u32[]{:S(2)}) %collective-permute-start.20) | collective-permute-done | bytes 294944 | tf_op jit(solution)/shard_map/ppermute | solution.py:412
  75.1 5.5 %collective-permute-done.14.o3.refs_4_ = bf16[3,192,256]{2,1,0:T(8,128)(2,1)S(1)} collective-permute-done((bf16[3,192,256]{2,1,0:T(8,128)(2,1)S(1)}, bf16[3,192,256]{2,1,0:T(8,128)(2,1)S(1)}, u32[]{:S(2)}, u32[]{:S(2)}) %collective-permute-start.14) | collective-permute-done | bytes 294944 | tf_op jit(solution)/shard_map/ppermute | solution.py:392
  81.7 1.9 collective-permute-done.21.rest_6_
  83.6 6.4 %collective-permute-done.25.rest_7_ = bf16[96,1536]{1,0:T(8,128)(2,1)S(1)} collective-permute-done((bf16[96,1536]{1,0:T(8,128)(2,1)S(1)}, bf16[96,1536]{1,0:T(8,128)(2,1)S(1)}, u32[]{:S(2)}, u32[]{:S(2)}) %collective-permute-start.25) | collective-permute-done | bytes 294944 | tf_op jit(solution)/shard_map/ppermute | solution.py:495
  90.0 1.9 gather.3.big_a.refs_9_.refs_11_
  92.6 4.0 %collective-permute-done.27.b_up_b.refs_16_ = f32[1,768]{1,0:T(1,128)S(1)} collective-permute-done((f32[1,768]{1,0:T(1,128)S(1)}, f32[1,768]{1,0:T(1,128)S(1)}, u32[]{:S(2)}, u32[]{:S(2)}) %collective-permute-start.27) | collective-permute-done | bytes 3104 | tf_op jit(solution)/shard_map/ppermute | solution.py:392
  98.0 6.0 %up.3 = (f32[3,256,768]{2,1,0:T(8,128)}, f32[3,256,128]{2,1,0:T(8,128)S(1)}, bf16[3,256,768]{2,1,0:T(8,128)(2,1)S(1)}, bf16[3,256,768]{2,1,0:T(8,128)(2,1)S(1)},...) custom-call(s32[4]{0:T(128)S(1)} %pad_add_fusion.me_ref.refs_0_, ...), custom_call_target="tpu_custom_call" | custom-call | flops 400000000 | bytes 1024 | tf_op jit(solution)/shard_map/up/pallas_call | solution.py:352
  104.6 6.5 %up.4 = (f32[3,256,768]{2,1,0:T(8,128)}, f32[3,256,128]{2,1,0:T(8,128)S(1)}, bf16[3,256,768]{2,1,0:T(8,128)(2,1)S(1)}, bf16[3,256,768]{2,1,0:T(8,128)(2,1)S(1)},...) custom-call(s32[4]{0:T(128)S(1)} %pad_add_fusion.me_ref.refs_0_, ...), custom_call_target="tpu_custom_call", output_to_operand_aliasing={{0}: (17, {}), {1}: (18, {}), {2}: (19, {}), {3}: (20, {}),... | custom-call | flops 400000000 | bytes 1024 | tf_op jit(solution)/shard_map/up/pallas_call | solution.py:352
  112.5 6.4 %up.5 = (f32[3,256,768]{2,1,0:T(8,128)}, f32[3,256,128]{2,1,0:T(8,128)S(1)}, bf16[3,256,768]{2,1,0:T(8,128)(2,1)S(1)}, bf16[3,256,768]{2,1,0:T(8,128)(2,1)S(1)},...) custom-call(s32[4]{0:T(128)S(1)} %pad_add_fusion.me_ref.refs_0_, ...), custom_call_target="tpu_custom_call", output_to_operand_aliasing={{0}: (17, {}), {1}: (18, {}), {2}: (19, {}), {3}: (20, {}),... | custom-call | flops 400000000 | bytes 1024 | tf_op jit(solution)/shard_map/up/pallas_call | solution.py:352
  119.5 6.8 %down.3 = (bf16[3,192,256]{2,1,0:T(8,128)(2,1)S(1)}, bf16[3,192,256]{2,1,0:T(8,128)(2,1)S(1)}, f32[3,256,768]{2,1,0:T(8,128)}, bf16[3,256,768]{2,1,0:T(8,128)(2,...) custom-call(s32[4]{0:T(128)S(1)} %pad_add_fusion.me_ref.refs_0_, ...), custom_call_target="tpu_custom_call" | custom-call | flops 400000000 | bytes 1024 | tf_op jit(solution)/shard_map/down/pallas_call | solution.py:352
  126.3 7.2 %down.4 = (bf16[3,192,256]{2,1,0:T(8,128)(2,1)S(1)}, bf16[3,192,256]{2,1,0:T(8,128)(2,1)S(1)}, f32[3,256,768]{2,1,0:T(8,128)}, bf16[3,256,768]{2,1,0:T(8,128)(2,...) custom-call(s32[4]{0:T(128)S(1)} %pad_add_fusion.me_ref.refs_0_, ...), custom_call_target="tpu_custom_call", output_to_operand_aliasing={{0}: (14, {}), {1}: (15, {}), {2}: (16, {}), {3}: (17, {}),... | custom-call | flops 400000000 | bytes 1024 | tf_op jit(solution)/shard_map/down/pallas_call | solution.py:352
  133.5 6.5 %down.5 = (bf16[3,192,256]{2,1,0:T(8,128)(2,1)S(1)}, bf16[3,192,256]{2,1,0:T(8,128)(2,1)S(1)}, f32[3,256,768]{2,1,0:T(8,128)}, bf16[3,256,768]{2,1,0:T(8,128)(2,...) custom-call(s32[4]{0:T(128)S(1)} %pad_add_fusion.me_ref.refs_0_, ...), custom_call_target="tpu_custom_call", output_to_operand_aliasing={{0}: (14, {}), {1}: (15, {}), {2}: (16, {}), {3}: (17, {}),... | custom-call | flops 400000000 | bytes 1024 | tf_op jit(solution)/shard_map/down/pallas_call | solution.py:352
  143.0 2.0 collective-permute-done.34.rest_3_
  144.9 4.1 %ffn_grad.2 = (bf16[384,768]{1,0:T(8,128)(2,1)S(1)}, bf16[384,768]{1,0:T(8,128)(2,1)}) custom-call(s32[4]{0:T(128)S(1)} %pad_add_fusion.me_ref.refs_0_, bf16[3,256,768]{2,1,0:T(8,128)(2,1)S(1)} %get-tuple-element.196.rest_0_, bf16[3,256,768]{2,1,0:T(8,128)(2,1)S(1)} %collective-permute-done.33.rest_1_, bf16[3,256,768]{2,1,0:T(8,128)(2,1)S(1)} %get-tuple-element.198.rest_2_, ...), custom_call_target="tpu_custom_call" | custom-call | flops 300000000 | bytes 1024 | tf_op jit(solution)/shard_map/ffn_grad/pallas_call | solution.py:352
  152.7 3.4 %ffn_grad.3 = (bf16[384,768]{1,0:T(8,128)(2,1)S(1)}, bf16[384,768]{1,0:T(8,128)(2,1)S(1)}) custom-call(s32[4]{0:T(128)S(1)} %pad_add_fusion.me_ref.refs_0_, bf16[3,256,768]{2,1,0:T(8,128)(2,1)S(1)} %get-tuple-element.209.rest_0_, bf16[3,256,768]{2,1,0:T(8,128)(2,1)S(1)} %collective-permute-done.38.rest_1_, ...), custom_call_target="tpu_custom_call" | custom-call | flops 300000000 | bytes 1024 | tf_op jit(solution)/shard_map/ffn_grad/pallas_call | solution.py:352
  156.1 4.9 %collective-permute-done.37.pb_ref = bf16[1,256,768]{2,1,0:T(8,128)(2,1)S(1)} collective-permute-done((bf16[1,256,768]{2,1,0:T(8,128)(2,1)S(1)}, bf16[1,256,768]{2,1,0:T(8,128)(2,1)S(1)}, u32[]{:S(2)}, u32[]{:S(2)}) %collective-permute-start.37) | collective-permute-done | bytes 393248 | tf_op jit(solution)/shard_map/ppermute | solution.py:392
  161.0 2.9 mid.3
  165.2 4.2 %collective-permute-done.36.refs_3_ = bf16[1,256,768]{2,1,0:T(8,128)(2,1)S(1)} collective-permute-done((bf16[1,256,768]{2,1,0:T(8,128)(2,1)}, bf16[1,256,768]{2,1,0:T(8,128)(2,1)S(1)}, u32[]{:S(2)}, u32[]{:S(2)}) %collective-permute-start.36) | collective-permute-done | bytes 393248 | tf_op jit(solution)/shard_map/ppermute | solution.py:392
  169.5 3.0 mid.4
  174.5 2.8 collective-permute-done.32.refs_3_
  177.3 2.9 mid.5
  192.9 5.9 %back.3 = (bf16[3,3,512,512]{3,2,1,0:T(8,128)(2,1)}, bf16[3,576,512]{2,1,0:T(8,128)(2,1)}, bf16[3,192,512]{2,1,0:T(8,128)(2,1)S(1)}, bf16[3,192,512]{2,1,0:T(8,1...) custom-call(s32[4]{0:T(128)S(1)} %pad_add_fusion.me_ref.refs_0_, ...), custom_call_target="tpu_custom_call" | custom-call | flops 430000000 | bytes 1024 | tf_op jit(solution)/shard_map/back/pallas_call | solution.py:352
  198.9 5.9 %back.4 = (bf16[3,3,512,512]{3,2,1,0:T(8,128)(2,1)}, bf16[3,576,512]{2,1,0:T(8,128)(2,1)}, bf16[3,192,512]{2,1,0:T(8,128)(2,1)S(1)}, bf16[3,192,512]{2,1,0:T(8,1...) custom-call(s32[4]{0:T(128)S(1)} %pad_add_fusion.me_ref.refs_0_, ...), custom_call_target="tpu_custom_call", output_to_operand_aliasing={{0}: (7, {}), {1}: (8, {}), {2}: (9, {}), {3}: (10, {}), {4... | custom-call | flops 430000000 | bytes 1024 | tf_op jit(solution)/shard_map/back/pallas_call | solution.py:352
  211.5 3.4 %collective-permute-start.70 = (bf16[96,768]{1,0:T(8,128)(2,1)S(1)}, bf16[96,768]{1,0:T(8,128)(2,1)S(1)}, u32[]{:S(2)}, u32[]{:S(2)}) collective-permute-start(bf16[96,768]{1,0:T(8,128)(2,1)S(1)} %get-tuple-element.227), channel_id=1, source_target_pairs={{0,24},{4,28},{8,0},{12,4},{16,8},{20,12},{24,16},{28,20},{1,25},{... | collective-permute-start | bytes 442376 | tf_op jit(solution)/shard_map/ppermute | solution.py:400
  217.5 5.8 %back.5 = (bf16[3,3,512,512]{3,2,1,0:T(8,128)(2,1)}, bf16[3,576,512]{2,1,0:T(8,128)(2,1)}, bf16[3,192,512]{2,1,0:T(8,128)(2,1)S(1)}, bf16[3,192,512]{2,1,0:T(8,1...) custom-call(s32[4]{0:T(128)S(1)} %pad_add_fusion.me_ref.refs_0_, ...), custom_call_target="tpu_custom_call", output_to_operand_aliasing={{0}: (7, {}), {1}: (8, {}), {2}: (9, {}), {3}: (10, {}), {4... | custom-call | flops 430000000 | bytes 1024 | tf_op jit(solution)/shard_map/back/pallas_call | solution.py:352
  228.1 5.5 %qkv_grad.1 = (bf16[384,768]{1,0:T(8,128)(2,1)S(1)}, bf16[384,768]{1,0:T(8,128)(2,1)}) custom-call(s32[4]{0:T(128)S(1)} %pad_add_fusion.me_ref.refs_0_, bf16[3,768,512]{2,1,0:T(8,128)(2,1)} %get-tuple-element.253.rest_0_, bf16[3,576,512]{2,1,0:T(8,128)(2,1)S(1)} %copy-done.1, bf16[3,192,256]{2,1,0:T(8,128)(2,1)S(1)} %copy-done.8, ...), custom_call_target="tpu_custom_call" | custom-call | flops 400000000 | bytes 1024 | tf_op jit(solution)/shard_map/qkv_grad/pallas_call | solution.py:352
  236.5 19.4 %collective-permute-done.71.rest_1_ = bf16[192,768]{1,0:T(8,128)(2,1)S(1)} collective-permute-done((bf16[192,768]{1,0:T(8,128)(2,1)S(1)}, bf16[192,768]{1,0:T(8,128)(2,1)S(1)}, u32[]{:S(2)}, u32[]{:S(2)}) %collective-permute-start.71) | collective-permute-done | bytes 294944 | tf_op jit(solution)/shard_map/ppermute | solution.py:412
  257.6 2.9 collective-permute-start.51
  260.5 2.1 add_convert_fusion.1
  262.6 3.9 %collective-permute-done.49 = bf16[96,768]{1,0:T(8,128)(2,1)S(1)} collective-permute-done((bf16[96,768]{1,0:T(8,128)(2,1)S(1)}, bf16[96,768]{1,0:T(8,128)(2,1)S(1)}, u32[]{:S(2)}, u32[]{:S(2)}) %collective-permute-start.49) | collective-permute-done | bytes 147488 | tf_op jit(solution)/shard_map/ppermute | solution.py:400
  266.4 4.0 %collective-permute-done.50 = bf16[96,768]{1,0:T(8,128)(2,1)S(1)} collective-permute-done((bf16[96,768]{1,0:T(8,128)(2,1)S(1)}, bf16[96,768]{1,0:T(8,128)(2,1)S(1)}, u32[]{:S(2)}, u32[]{:S(2)}) %collective-permute-start.50) | collective-permute-done | bytes 147488 | tf_op jit(solution)/shard_map/ppermute | solution.py:400
  270.4 2.0 collective-permute-start.74
  274.2 2.8 collective-permute-done.62
  279.4 4.0 %collective-permute-start.63 = (f32[8,768]{1,0:T(8,128)S(1)}, f32[8,768]{1,0:T(8,128)S(1)}, u32[]{:S(2)}, u32[]{:S(2)}) collective-permute-start(f32[8,768]{1,0:T(8,128)S(1)} %add.74), channel_id=1, source_target_pairs={{0,8},{4,12},{8,0},{12,4},{16,24},{20,28},{24,16},{28,20},{1,9},{5... | collective-permute-start | bytes 73736 | tf_op jit(solution)/shard_map/ppermute | solution.py:654
  286.8 2.4 collective-permute-start.77
  291.4 2.5 collective-permute-start.64
  293.9 1.9 collective-permute-start.54
  295.8 2.3 fusion
  298.1 3.0 finish.3
  303.9 3.2 %collective-permute-done.55.rest_4_ = bf16[96,768]{1,0:T(8,128)(2,1)S(1)} collective-permute-done((bf16[96,768]{1,0:T(8,128)(2,1)S(1)}, bf16[96,768]{1,0:T(8,128)(2,1)S(1)}, u32[]{:S(2)}, u32[]{:S(2)}) %collective-permute-start.55) | collective-permute-done | bytes 147488 | tf_op jit(solution)/shard_map/ppermute | solution.py:412
  312.6 2.2 finish.2
  (310 shorter events, 98.5 us)
Async XLA Ops:
  13.6 13.3 %collective-permute-start.1 = (bf16[3,192,512]{2,1,0:T(8,128)(2,1)S(1)}, bf16[3,192,512]{2,1,0:T(8,128)(2,1)S(1)}, u32[]{:S(2)}, u32[]{:S(2)}) collective-permute-start(bf16[3,192,512]{2,1,0:T(8,128)(2,1)S(1)} %bitcast.20), channel_id=1, source_target_pairs={{0,2},{1,3},{2,0},{3,1},{4,6},{5,7},{6,4},{7,5},{8,10},{9,11},{10,... | collective-permute-start | bytes 1769480 | tf_op jit(solution)/shard_map/ppermute | solution.py:392
  15.1 33.9 %collective-permute-start = (bf16[3,192,512]{2,1,0:T(8,128)(2,1)S(1)}, bf16[3,192,512]{2,1,0:T(8,128)(2,1)S(1)}, u32[]{:S(2)}, u32[]{:S(2)}) collective-permute-start(bf16[3,192,512]{2,1,0:T(8,128)(2,1)S(1)} %bitcast.21), channel_id=1, source_target_pairs={{0,1},{1,0},{2,3},{3,2},{4,5},{5,4},{6,7},{7,6},{8,9},{9,8},{10,11... | collective-permute-start | bytes 1769480 | tf_op jit(solution)/shard_map/ppermute | solution.py:392
  26.9 22.2 %collective-permute-start.2 = (bf16[3,192,512]{2,1,0:T(8,128)(2,1)S(1)}, bf16[3,192,512]{2,1,0:T(8,128)(2,1)}, u32[]{:S(2)}, u32[]{:S(2)}) collective-permute-start(bf16[3,192,512]{2,1,0:T(8,128)(2,1)S(1)} %collective-permute-done.1.x2), channel_id=1, source_target_pairs={{0,1},{1,0},{2,3},{3,2},{4,5},{5,4},{6,7},{7,6},{8,9},{9,8},{10,11... | collective-permute-start | bytes 1769480 | tf_op jit(solution)/shard_map/ppermute | solution.py:392
  38.0 11.9 %collective-permute-start.18 = (bf16[96,1536]{1,0:T(8,128)(2,1)}, bf16[96,1536]{1,0:T(8,128)(2,1)}, u32[]{:S(2)}, u32[]{:S(2)}) collective-permute-start(bf16[96,1536]{1,0:T(8,128)(2,1)} %collective-permute-done.10.rest_1_), channel_id=1, source_target_pairs={{0,8},{8,16},{16,24},{24,28},{28,20},{20,12},{12,4},{4,0},{1,9},{9... | collective-permute-start | bytes 884744 | tf_op jit(solution)/shard_map/ppermute | solution.py:412
  39.3 12.2 %collective-permute-start.19 = (bf16[96,1536]{1,0:T(8,128)(2,1)}, bf16[96,1536]{1,0:T(8,128)(2,1)}, u32[]{:S(2)}, u32[]{:S(2)}) collective-permute-start(bf16[96,1536]{1,0:T(8,128)(2,1)} %collective-permute-done.11.rest_2_), channel_id=1, source_target_pairs={{8,0},{16,8},{24,16},{28,24},{20,28},{12,20},{4,12},{0,4},{9,1},{1... | collective-permute-start | bytes 884744 | tf_op jit(solution)/shard_map/ppermute | solution.py:412
  41.5 23.8 %collective-permute-start.23 = (bf16[3,192,256]{2,1,0:T(8,128)(2,1)S(1)}, bf16[3,192,256]{2,1,0:T(8,128)(2,1)S(1)}, u32[]{:S(2)}, u32[]{:S(2)}) collective-permute-start(bf16[3,192,256]{2,1,0:T(8,128)(2,1)S(1)} %get-tuple-element.273.dy0.refs_4_), channel_id=1, source_target_pairs={{0,2},{1,3},{2,0},{3,1},{4,6},{5,7},{6,4},{7,5},{8,10},{9,11},{10,... | collective-permute-start | bytes 884744 | tf_op jit(solution)/shard_map/ppermute | solution.py:392
  49.0 16.8 %collective-permute-start.22 = (bf16[3,192,256]{2,1,0:T(8,128)(2,1)S(1)}, bf16[3,192,256]{2,1,0:T(8,128)(2,1)S(1)}, u32[]{:S(2)}, u32[]{:S(2)}) collective-permute-start(bf16[3,192,256]{2,1,0:T(8,128)(2,1)S(1)} %get-tuple-element.274), channel_id=1, source_target_pairs={{0,1},{1,0},{2,3},{3,2},{4,5},{5,4},{6,7},{7,6},{8,9},{9,8},{10,11... | collective-permute-start | bytes 884744 | tf_op jit(solution)/shard_map/ppermute | solution.py:392
  49.1 17.8 %collective-permute-start.24 = (bf16[3,192,256]{2,1,0:T(8,128)(2,1)S(1)}, bf16[3,192,256]{2,1,0:T(8,128)(2,1)S(1)}, u32[]{:S(2)}, u32[]{:S(2)}) collective-permute-start(bf16[3,192,256]{2,1,0:T(8,128)(2,1)S(1)} %get-tuple-element.274), channel_id=1, source_target_pairs={{0,3},{1,2},{2,1},{3,0},{4,7},{5,6},{6,5},{7,4},{8,11},{9,10},{10,... | collective-permute-start | bytes 884744 | tf_op jit(solution)/shard_map/ppermute | solution.py:392
  49.9 17.1 %collective-permute-start.16 = (bf16[768,192]{1,0:T(8,128)(2,1)S(1)}, bf16[768,192]{1,0:T(8,128)(2,1)S(1)}, u32[]{:S(2)}, u32[]{:S(2)}) collective-permute-start(bf16[768,192]{1,0:T(8,128)(2,1)S(1)} %slice.35.wo0.refs_5_.refs_7_), channel_id=1, source_target_pairs={{0,2},{1,3},{2,0},{3,1},{4,6},{5,7},{6,4},{7,5},{8,10},{9,11},{10,... | collective-permute-start | bytes 884744 | tf_op jit(solution)/shard_map/ppermute | solution.py:392
  51.5 17.1 %collective-permute-start.15 = (bf16[768,192]{1,0:T(8,128)(2,1)S(1)}, bf16[768,192]{1,0:T(8,128)(2,1)S(1)}, u32[]{:S(2)}, u32[]{:S(2)}) collective-permute-start(bf16[768,192]{1,0:T(8,128)(2,1)S(1)} %slice.35.wo0.refs_5_.refs_7_), channel_id=1, source_target_pairs={{0,1},{1,0},{2,3},{3,2},{4,5},{5,4},{6,7},{7,6},{8,9},{9,8},{10,11... | collective-permute-start | bytes 884744 | tf_op jit(solution)/shard_map/ppermute | solution.py:392
  65.3 9.9 %collective-permute-start.13 = (bf16[3,192,256]{2,1,0:T(8,128)(2,1)S(1)}, bf16[3,192,256]{2,1,0:T(8,128)(2,1)S(1)}, u32[]{:S(2)}, u32[]{:S(2)}) collective-permute-start(bf16[3,192,256]{2,1,0:T(8,128)(2,1)S(1)} %get-tuple-element.149.o0.refs_1_.rest_2_), channel_id=1, source_target_pairs={{0,2},{1,3},{2,0},{3,1},{4,6},{5,7},{6,4},{7,5},{8,10},{9,11},{10,... | collective-permute-start | bytes 884744 | tf_op jit(solution)/shard_map/ppermute | solution.py:392
  67.0 13.6 %collective-permute-start.14 = (bf16[3,192,256]{2,1,0:T(8,128)(2,1)S(1)}, bf16[3,192,256]{2,1,0:T(8,128)(2,1)S(1)}, u32[]{:S(2)}, u32[]{:S(2)}) collective-permute-start(bf16[3,192,256]{2,1,0:T(8,128)(2,1)S(1)} %get-tuple-element.150.rest_4_), channel_id=1, source_target_pairs={{0,3},{1,2},{2,1},{3,0},{4,7},{5,6},{6,5},{7,4},{8,11},{9,10},{10,... | collective-permute-start | bytes 884744 | tf_op jit(solution)/shard_map/ppermute | solution.py:392
  68.7 11.9 %collective-permute-start.17 = (bf16[768,192]{1,0:T(8,128)(2,1)S(1)}, bf16[768,192]{1,0:T(8,128)(2,1)S(1)}, u32[]{:S(2)}, u32[]{:S(2)}) collective-permute-start(bf16[768,192]{1,0:T(8,128)(2,1)S(1)} %collective-permute-done.16.wo2.refs_7_), channel_id=1, source_target_pairs={{0,1},{1,0},{2,3},{3,2},{4,5},{5,4},{6,7},{7,6},{8,9},{9,8},{10,11... | collective-permute-start | bytes 884744 | tf_op jit(solution)/shard_map/ppermute | solution.py:392
  80.6 9.4 %collective-permute-start.25 = (bf16[96,1536]{1,0:T(8,128)(2,1)S(1)}, bf16[96,1536]{1,0:T(8,128)(2,1)S(1)}, u32[]{:S(2)}, u32[]{:S(2)}) collective-permute-start(bf16[96,1536]{1,0:T(8,128)(2,1)S(1)} %collective-permute-done.20.rest_5_), channel_id=1, source_target_pairs={{0,8},{8,16},{16,24},{24,28},{28,20},{20,12},{12,4},{4,0},{1,9},{9... | collective-permute-start | bytes 884744 | tf_op jit(solution)/shard_map/ppermute | solution.py:495
  104.1 15.4 %collective-permute-start.30 = (bf16[1,256,768]{2,1,0:T(8,128)(2,1)S(1)}, bf16[1,256,768]{2,1,0:T(8,128)(2,1)S(1)}, u32[]{:S(2)}, u32[]{:S(2)}) collective-permute-start(bf16[1,256,768]{2,1,0:T(8,128)(2,1)S(1)} %get-tuple-element.172.pa_ref), channel_id=1, source_target_pairs={{0,2},{1,3},{2,0},{3,1},{4,6},{5,7},{6,4},{7,5},{8,10},{9,11},{10,... | collective-permute-start | bytes 1179656 | tf_op jit(solution)/shard_map/ppermute | solution.py:392
  111.0 15.3 %collective-permute-start.29 = (bf16[1,256,768]{2,1,0:T(8,128)(2,1)S(1)}, bf16[1,256,768]{2,1,0:T(8,128)(2,1)S(1)}, u32[]{:S(2)}, u32[]{:S(2)}) collective-permute-start(bf16[1,256,768]{2,1,0:T(8,128)(2,1)S(1)} %get-tuple-element.171.refs_2_), channel_id=1, source_target_pairs={{0,2},{1,3},{2,0},{3,1},{4,6},{5,7},{6,4},{7,5},{8,10},{9,11},{10,... | collective-permute-start | bytes 1179656 | tf_op jit(solution)/shard_map/ppermute | solution.py:392
  119.0 14.5 %collective-permute-start.28 = (bf16[1,256,768]{2,1,0:T(8,128)(2,1)S(1)}, bf16[1,256,768]{2,1,0:T(8,128)(2,1)S(1)}, u32[]{:S(2)}, u32[]{:S(2)}) collective-permute-start(bf16[1,256,768]{2,1,0:T(8,128)(2,1)S(1)} %get-tuple-element.169.refs_2_), channel_id=1, source_target_pairs={{0,2},{1,3},{2,0},{3,1},{4,6},{5,7},{6,4},{7,5},{8,10},{9,11},{10,... | collective-permute-start | bytes 1179656 | tf_op jit(solution)/shard_map/ppermute | solution.py:392
  119.5 23.5 %collective-permute-start.33 = (bf16[3,256,768]{2,1,0:T(8,128)(2,1)}, bf16[3,256,768]{2,1,0:T(8,128)(2,1)S(1)}, u32[]{:S(2)}, u32[]{:S(2)}) collective-permute-start(bf16[3,256,768]{2,1,0:T(8,128)(2,1)} %get-tuple-element.197), channel_id=1, source_target_pairs={{0,1},{1,0},{2,3},{3,2},{4,5},{5,4},{6,7},{7,6},{8,9},{9,8},{10,11... | collective-permute-start | bytes 3538952 | tf_op jit(solution)/shard_map/ppermute | solution.py:392
  142.5 10.2 %collective-permute-start.39 = (bf16[3,256,768]{2,1,0:T(8,128)(2,1)}, bf16[3,256,768]{2,1,0:T(8,128)(2,1)S(1)}, u32[]{:S(2)}, u32[]{:S(2)}) collective-permute-start(bf16[3,256,768]{2,1,0:T(8,128)(2,1)} %get-tuple-element.211), channel_id=1, source_target_pairs={{0,1},{1,0},{2,3},{3,2},{4,5},{5,4},{6,7},{7,6},{8,9},{9,8},{10,11... | collective-permute-start | bytes 3538952 | tf_op jit(solution)/shard_map/ppermute | solution.py:392
  149.0 24.8 %collective-permute-start.35 = (bf16[384,768]{1,0:T(8,128)(2,1)}, bf16[384,768]{1,0:T(8,128)(2,1)S(1)}, u32[]{:S(2)}, u32[]{:S(2)}) collective-permute-start(bf16[384,768]{1,0:T(8,128)(2,1)} %get-tuple-element.200), channel_id=1, source_target_pairs={{0,4},{4,0},{8,12},{12,8},{16,20},{20,16},{24,28},{28,24},{1,5},{5... | collective-permute-start | bytes 1769480 | tf_op jit(solution)/shard_map/ppermute | solution.py:395
  149.0 12.0 %collective-permute-start.37 = (bf16[1,256,768]{2,1,0:T(8,128)(2,1)S(1)}, bf16[1,256,768]{2,1,0:T(8,128)(2,1)S(1)}, u32[]{:S(2)}, u32[]{:S(2)}) collective-permute-start(bf16[1,256,768]{2,1,0:T(8,128)(2,1)S(1)} %get-tuple-element.208.pa_ref), channel_id=1, source_target_pairs={{0,2},{1,3},{2,0},{3,1},{4,6},{5,7},{6,4},{7,5},{8,10},{9,11},{10,... | collective-permute-start | bytes 1179656 | tf_op jit(solution)/shard_map/ppermute | solution.py:392
  150.6 18.8 %collective-permute-start.36 = (bf16[1,256,768]{2,1,0:T(8,128)(2,1)}, bf16[1,256,768]{2,1,0:T(8,128)(2,1)S(1)}, u32[]{:S(2)}, u32[]{:S(2)}) collective-permute-start(bf16[1,256,768]{2,1,0:T(8,128)(2,1)} %get-tuple-element.207.refs_2_), channel_id=1, source_target_pairs={{0,2},{1,3},{2,0},{3,1},{4,6},{5,7},{6,4},{7,5},{8,10},{9,11},{10,... | collective-permute-start | bytes 1179656 | tf_op jit(solution)/shard_map/ppermute | solution.py:392
  151.1 26.2 %collective-permute-start.32 = (bf16[1,256,768]{2,1,0:T(8,128)(2,1)S(1)}, bf16[1,256,768]{2,1,0:T(8,128)(2,1)S(1)}, u32[]{:S(2)}, u32[]{:S(2)}) collective-permute-start(bf16[1,256,768]{2,1,0:T(8,128)(2,1)S(1)} %get-tuple-element.195.refs_2_), channel_id=1, source_target_pairs={{0,2},{1,3},{2,0},{3,1},{4,6},{5,7},{6,4},{7,5},{8,10},{9,11},{10,... | collective-permute-start | bytes 1179656 | tf_op jit(solution)/shard_map/ppermute | solution.py:392
  182.2 44.4 %collective-permute-start.47 = (bf16[3,256,768]{2,1,0:T(8,128)(2,1)S(1)}, bf16[3,256,768]{2,1,0:T(8,128)(2,1)}, u32[]{:S(2)}, u32[]{:S(2)}) collective-permute-start(bf16[3,256,768]{2,1,0:T(8,128)(2,1)S(1)} %get-tuple-element.255.rest_3_), channel_id=1, source_target_pairs={{0,1},{1,0},{2,3},{3,2},{4,5},{5,4},{6,7},{7,6},{8,9},{9,8},{10,11... | collective-permute-start | bytes 3538952 | tf_op jit(solution)/shard_map/ppermute | solution.py:392
  184.9 21.6 %collective-permute-start.41 = (bf16[384,768]{1,0:T(8,128)(2,1)}, bf16[384,768]{1,0:T(8,128)(2,1)}, u32[]{:S(2)}, u32[]{:S(2)}) collective-permute-start(bf16[384,768]{1,0:T(8,128)(2,1)} %copy-done.52), channel_id=1, source_target_pairs={{0,4},{4,0},{8,12},{12,8},{16,20},{20,16},{24,28},{28,24},{1,5},{5... | collective-permute-start | bytes 1769480 | tf_op jit(solution)/shard_map/ppermute | solution.py:395
  187.9 10.9 %collective-permute-start.42 = (bf16[1,192,256]{2,1,0:T(8,128)(2,1)}, bf16[1,192,256]{2,1,0:T(8,128)(2,1)}, u32[]{:S(2)}, u32[]{:S(2)}) collective-permute-start(bf16[1,192,256]{2,1,0:T(8,128)(2,1)} %copy-done.59), channel_id=1, source_target_pairs={{0,1},{1,0},{2,3},{3,2},{4,5},{5,4},{6,7},{7,6},{8,9},{9,8},{10,11... | collective-permute-start | bytes 294920 | tf_op jit(solution)/shard_map/ppermute | solution.py:392
  188.1 20.4 %collective-permute-start.65 = (bf16[96,768]{1,0:T(8,128)(2,1)}, bf16[96,768]{1,0:T(8,128)(2,1)}, u32[]{:S(2)}, u32[]{:S(2)}) collective-permute-start(bf16[96,768]{1,0:T(8,128)(2,1)} %copy-done.56), channel_id=1, source_target_pairs={{0,8},{4,12},{8,16},{12,20},{16,24},{20,28},{24,0},{28,4},{1,9},{5... | collective-permute-start | bytes 442376 | tf_op jit(solution)/shard_map/ppermute | solution.py:400
  190.8 18.6 %collective-permute-start.66 = (bf16[96,768]{1,0:T(8,128)(2,1)}, bf16[96,768]{1,0:T(8,128)(2,1)S(1)}, u32[]{:S(2)}, u32[]{:S(2)}) collective-permute-start(bf16[96,768]{1,0:T(8,128)(2,1)} %copy-done.55), channel_id=1, source_target_pairs={{0,16},{4,20},{8,24},{12,28},{16,0},{20,4},{24,8},{28,12},{1,17},{... | collective-permute-start | bytes 442376 | tf_op jit(solution)/shard_map/ppermute | solution.py:400
  208.5 25.1 %collective-permute-start.68 = (bf16[96,768]{1,0:T(8,128)(2,1)S(1)}, bf16[96,768]{1,0:T(8,128)(2,1)S(1)}, u32[]{:S(2)}, u32[]{:S(2)}) collective-permute-start(bf16[96,768]{1,0:T(8,128)(2,1)S(1)} %get-tuple-element.225), channel_id=1, source_target_pairs={{0,8},{4,12},{8,16},{12,20},{16,24},{20,28},{24,0},{28,4},{1,9},{5... | collective-permute-start | bytes 442376 | tf_op jit(solution)/shard_map/ppermute | solution.py:400
  209.4 24.6 %collective-permute-start.69 = (bf16[96,768]{1,0:T(8,128)(2,1)S(1)}, bf16[96,768]{1,0:T(8,128)(2,1)S(1)}, u32[]{:S(2)}, u32[]{:S(2)}) collective-permute-start(bf16[96,768]{1,0:T(8,128)(2,1)S(1)} %get-tuple-element.226), channel_id=1, source_target_pairs={{0,16},{4,20},{8,24},{12,28},{16,0},{20,4},{24,8},{28,12},{1,17},{... | collective-permute-start | bytes 442376 | tf_op jit(solution)/shard_map/ppermute | solution.py:400
  211.5 22.5 %collective-permute-start.70 = (bf16[96,768]{1,0:T(8,128)(2,1)S(1)}, bf16[96,768]{1,0:T(8,128)(2,1)S(1)}, u32[]{:S(2)}, u32[]{:S(2)}) collective-permute-start(bf16[96,768]{1,0:T(8,128)(2,1)S(1)} %get-tuple-element.227), channel_id=1, source_target_pairs={{0,24},{4,28},{8,0},{12,4},{16,8},{20,12},{24,16},{28,20},{1,25},{... | collective-permute-start | bytes 442376 | tf_op jit(solution)/shard_map/ppermute | solution.py:400
  215.9 18.3 %collective-permute-start.60 = (f32[6,768]{1,0:T(8,128)S(1)}, f32[6,768]{1,0:T(8,128)S(1)}, u32[]{:S(2)}, u32[]{:S(2)}) collective-permute-start(f32[6,768]{1,0:T(8,128)S(1)} %fusion.1), channel_id=1, source_target_pairs={{0,2},{1,3},{2,0},{3,1},{4,6},{5,7},{6,4},{7,5},{8,10},{9,11},{10,... | collective-permute-start | bytes 55304 | tf_op jit(solution)/shard_map/ppermute | solution.py:392
  226.6 31.0 %collective-permute-start.45 = (bf16[3,192,512]{2,1,0:T(8,128)(2,1)}, bf16[3,192,512]{2,1,0:T(8,128)(2,1)}, u32[]{:S(2)}, u32[]{:S(2)}) collective-permute-start(bf16[3,192,512]{2,1,0:T(8,128)(2,1)} %get-tuple-element.251), channel_id=1, source_target_pairs={{0,1},{1,0},{2,3},{3,2},{4,5},{5,4},{6,7},{7,6},{8,9},{9,8},{10,11... | collective-permute-start | bytes 1769480 | tf_op jit(solution)/shard_map/ppermute | solution.py:392
  233.6 22.3 %collective-permute-start.48 = (bf16[384,768]{1,0:T(8,128)(2,1)}, bf16[384,768]{1,0:T(8,128)(2,1)S(1)}, u32[]{:S(2)}, u32[]{:S(2)}) collective-permute-start(bf16[384,768]{1,0:T(8,128)(2,1)} %get-tuple-element.257), channel_id=1, source_target_pairs={{0,4},{4,0},{8,12},{12,8},{16,20},{20,16},{24,28},{28,24},{1,5},{5... | collective-permute-start | bytes 1769480 | tf_op jit(solution)/shard_map/ppermute | solution.py:395
  234.1 21.7 %collective-permute-start.71 = (bf16[192,768]{1,0:T(8,128)(2,1)S(1)}, bf16[192,768]{1,0:T(8,128)(2,1)S(1)}, u32[]{:S(2)}, u32[]{:S(2)}) collective-permute-start(bf16[192,768]{1,0:T(8,128)(2,1)S(1)} %pad_maximum_fusion.1.rest_0_), channel_id=1, source_target_pairs={{0,8},{8,16},{16,24},{24,28},{28,20},{20,12},{12,4},{4,0},{1,9},{9... | collective-permute-start | bytes 884744 | tf_op jit(solution)/shard_map/ppermute | solution.py:412
  234.7 27.9 %collective-permute-start.72 = (bf16[192,768]{1,0:T(8,128)(2,1)S(1)}, bf16[192,768]{1,0:T(8,128)(2,1)S(1)}, u32[]{:S(2)}, u32[]{:S(2)}) collective-permute-start(bf16[192,768]{1,0:T(8,128)(2,1)S(1)} %pad_maximum_fusion.1.rest_0_), channel_id=1, source_target_pairs={{8,0},{16,8},{24,16},{28,24},{20,28},{12,20},{4,12},{0,4},{9,1},{1... | collective-permute-start | bytes 884744 | tf_op jit(solution)/shard_map/ppermute | solution.py:412
  255.9 17.1 %collective-permute-start.73 = (bf16[192,768]{1,0:T(8,128)(2,1)S(1)}, bf16[192,768]{1,0:T(8,128)(2,1)S(1)}, u32[]{:S(2)}, u32[]{:S(2)}) collective-permute-start(bf16[192,768]{1,0:T(8,128)(2,1)S(1)} %collective-permute-done.71.rest_1_), channel_id=1, source_target_pairs={{0,8},{8,16},{16,24},{24,28},{28,20},{20,12},{12,4},{4,0},{1,9},{9... | collective-permute-start | bytes 884744 | tf_op jit(solution)/shard_map/ppermute | solution.py:412
  256.6 9.8 %collective-permute-start.49 = (bf16[96,768]{1,0:T(8,128)(2,1)S(1)}, bf16[96,768]{1,0:T(8,128)(2,1)S(1)}, u32[]{:S(2)}, u32[]{:S(2)}) collective-permute-start(bf16[96,768]{1,0:T(8,128)(2,1)S(1)} %get-tuple-element.259), channel_id=1, source_target_pairs={{0,8},{4,12},{8,16},{12,20},{16,24},{20,28},{24,0},{28,4},{1,9},{5... | collective-permute-start | bytes 442376 | tf_op jit(solution)/shard_map/ppermute | solution.py:400
  256.7 13.7 %collective-permute-start.50 = (bf16[96,768]{1,0:T(8,128)(2,1)S(1)}, bf16[96,768]{1,0:T(8,128)(2,1)S(1)}, u32[]{:S(2)}, u32[]{:S(2)}) collective-permute-start(bf16[96,768]{1,0:T(8,128)(2,1)S(1)} %get-tuple-element.260), channel_id=1, source_target_pairs={{0,16},{4,20},{8,24},{12,28},{16,0},{20,4},{24,8},{28,12},{1,17},{... | collective-permute-start | bytes 442376 | tf_op jit(solution)/shard_map/ppermute | solution.py:400
  257.6 14.8 %collective-permute-start.51 = (bf16[96,768]{1,0:T(8,128)(2,1)S(1)}, bf16[96,768]{1,0:T(8,128)(2,1)S(1)}, u32[]{:S(2)}, u32[]{:S(2)}) collective-permute-start(bf16[96,768]{1,0:T(8,128)(2,1)S(1)} %get-tuple-element.261), channel_id=1, source_target_pairs={{0,24},{4,28},{8,0},{12,4},{16,8},{20,12},{24,16},{28,20},{1,25},{... | collective-permute-start | bytes 442376 | tf_op jit(solution)/shard_map/ppermute | solution.py:400
  262.6 16.6 %collective-permute-start.31 = (bf16[3,192,256]{2,1,0:T(8,128)(2,1)S(1)}, bf16[3,192,256]{2,1,0:T(8,128)(2,1)S(1)}, u32[]{:S(2)}, u32[]{:S(2)}) collective-permute-start(bf16[3,192,256]{2,1,0:T(8,128)(2,1)S(1)} %copy-done.16), channel_id=1, source_target_pairs={{0,1},{1,0},{2,3},{3,2},{4,5},{5,4},{6,7},{7,6},{8,9},{9,8},{10,11... | collective-permute-start | bytes 884744 | tf_op jit(solution)/shard_map/ppermute | solution.py:392
  266.4 23.6 %collective-permute-start.44 = (bf16[3,192,512]{2,1,0:T(8,128)(2,1)S(1)}, bf16[3,192,512]{2,1,0:T(8,128)(2,1)}, u32[]{:S(2)}, u32[]{:S(2)}) collective-permute-start(bf16[3,192,512]{2,1,0:T(8,128)(2,1)S(1)} %copy-done.14), channel_id=1, source_target_pairs={{0,1},{1,0},{2,3},{3,2},{4,5},{5,4},{6,7},{7,6},{8,9},{9,8},{10,11... | collective-permute-start | bytes 1769480 | tf_op jit(solution)/shard_map/ppermute | solution.py:392
  272.4 18.9 %collective-permute-start.46 = (bf16[3,192,512]{2,1,0:T(8,128)(2,1)}, bf16[3,192,512]{2,1,0:T(8,128)(2,1)}, u32[]{:S(2)}, u32[]{:S(2)}) collective-permute-start(bf16[3,192,512]{2,1,0:T(8,128)(2,1)} %add_convert_fusion.1), channel_id=1, source_target_pairs={{0,2},{1,3},{2,0},{3,1},{4,6},{5,7},{6,4},{7,5},{8,10},{9,11},{10,... | collective-permute-start | bytes 1769480 | tf_op jit(solution)/shard_map/ppermute | solution.py:392
  279.2 14.7 %collective-permute-start.52 = (bf16[96,768]{1,0:T(8,128)(2,1)S(1)}, bf16[96,768]{1,0:T(8,128)(2,1)S(1)}, u32[]{:S(2)}, u32[]{:S(2)}) collective-permute-start(bf16[96,768]{1,0:T(8,128)(2,1)S(1)} %add_convert_fusion.4.rest_0_), channel_id=1, source_target_pairs={{0,8},{8,16},{16,24},{24,28},{28,20},{20,12},{12,4},{4,0},{1,9},{9... | collective-permute-start | bytes 442376 | tf_op jit(solution)/shard_map/ppermute | solution.py:412
  285.0 13.1 %collective-permute-start.76 = (bf16[192,768]{1,0:T(8,128)(2,1)S(1)}, bf16[192,768]{1,0:T(8,128)(2,1)S(1)}, u32[]{:S(2)}, u32[]{:S(2)}) collective-permute-start(bf16[192,768]{1,0:T(8,128)(2,1)S(1)} %collective-permute-done.74.rest_4_), channel_id=1, source_target_pairs={{8,0},{16,8},{24,16},{28,24},{20,28},{12,20},{4,12},{0,4},{9,1},{1... | collective-permute-start | bytes 884744 | tf_op jit(solution)/shard_map/ppermute | solution.py:412
  286.8 11.3 %collective-permute-start.77 = (bf16[192,768]{1,0:T(8,128)(2,1)S(1)}, bf16[192,768]{1,0:T(8,128)(2,1)S(1)}, u32[]{:S(2)}, u32[]{:S(2)}) collective-permute-start(bf16[192,768]{1,0:T(8,128)(2,1)S(1)} %collective-permute-done.75.rest_5_), channel_id=1, source_target_pairs={{0,8},{8,16},{16,24},{24,28},{28,20},{20,12},{12,4},{4,0},{1,9},{9... | collective-permute-start | bytes 884744 | tf_op jit(solution)/shard_map/ppermute | solution.py:627
  290.1 11.1 %collective-permute-start.53 = (bf16[96,768]{1,0:T(8,128)(2,1)S(1)}, bf16[96,768]{1,0:T(8,128)(2,1)S(1)}, u32[]{:S(2)}, u32[]{:S(2)}) collective-permute-start(bf16[96,768]{1,0:T(8,128)(2,1)S(1)} %add_convert_fusion.4.rest_0_), channel_id=1, source_target_pairs={{8,0},{16,8},{24,16},{28,24},{20,28},{12,20},{4,12},{0,4},{9,1},{1... | collective-permute-start | bytes 442376 | tf_op jit(solution)/shard_map/ppermute | solution.py:412
  291.4 9.8 %collective-permute-start.64 = (f32[8,768]{1,0:T(8,128)S(1)}, f32[8,768]{1,0:T(8,128)S(1)}, u32[]{:S(2)}, u32[]{:S(2)}) collective-permute-start(f32[8,768]{1,0:T(8,128)S(1)} %add.75), channel_id=1, source_target_pairs={{0,16},{4,20},{8,24},{12,28},{16,0},{20,4},{24,8},{28,12},{1,17},{... | collective-permute-start | bytes 73736 | tf_op jit(solution)/shard_map/ppermute | solution.py:654
  (99 other events, 824.9 us)

commit v3 on v2

v3 whole, which is shorter than its diff:
```python
import functools

import jax
import jax.numpy as jnp
from jax import lax
from jax.experimental import pallas as pl
from jax.experimental.pallas import tpu as pltpu
from jax.sharding import PartitionSpec as P

EPS = 1e-06
NEG = -1e30
BF = jnp.bfloat16
F32 = jnp.float32


def dot(a, b):
    return lax.dot_general(a, b, (((1,), (0,)), ((), ())), preferred_element_type=F32)


def dot_nt(a, b):
    return lax.dot_general(a, b, (((1,), (1,)), ((), ())), preferred_element_type=F32)


def dot_tn(a, b):
    return lax.dot_general(a, b, (((0,), (0,)), ((), ())), preferred_element_type=F32)


def place_of(me, step):
    core, chip = lax.rem(me, 2), me // 2
    core = 1 - core if step % 2 else core
    chip = 1 - chip if step // 2 else chip
    return 2 * chip + core


def ln_stats(summed):
    row_mean = jnp.mean(summed, axis=-1, keepdims=True)
    centered = summed - row_mean
    inv_std = lax.rsqrt(jnp.mean(centered * centered, axis=-1, keepdims=True) + EPS)
    return centered * inv_std, inv_std


def ln_back(grad, normed, inv_std, gain):
    scaled = grad * gain
    inner = (
        scaled
        - jnp.mean(scaled, axis=-1, keepdims=True)
        - normed * jnp.mean(scaled * normed, axis=-1, keepdims=True)
    )
    return inner * inv_std


def attend_kernel(
    heads, steps, me_ref, x0, x1, x2, x3, b_ref, prev_ref, seg_ref, *rest
):
    count = len(steps)
    blocks = rest[:count]
    raw_ref, p_ref, qkv_ref, own_ref, oth_ref, xt_ref, xh_ref, w_ref, o_scr = rest[count:]

    @pl.when(pl.program_id(0) == 0)
    def _():
        rows = blocks[0].shape[0]
        for block, back in zip(blocks, steps):
            group = group_at(me_ref, back, count) if count > 1 else 0
            w_ref[pl.ds(pl.multiple_of(group * rows, rows), rows), :] = block[...]

    me = me_ref[0]
    core = lax.rem(me, 2)
    width, slots = x0.shape[1], x0.shape[2]
    half = slots // 2
    size = width // heads
    for step, piece in enumerate((x0, x1, x2, x3)):
        start = pl.multiple_of(place_of(me, step) * width, width)
        xt_ref[0, pl.ds(start, width), :] = piece[0]
    bias = jnp.transpose(jnp.broadcast_to(b_ref[0:1, :], (128, width)))[:, 0:1]
    bias_v = jnp.transpose(jnp.broadcast_to(b_ref[1:2, :], (128, width)))[:, 0:1]
    packed = dot_tn(w_ref[:, : 3 * width], xt_ref[0])
    qkv_ref[0, 0] = (packed[:width] + bias).astype(BF)
    qkv_ref[0, 1] = packed[width : 2 * width].astype(BF)
    qkv_ref[0, 2] = (packed[2 * width :] + bias_v).astype(BF)
    mine = pl.ds(pl.multiple_of(core * half, half), half)
    other = pl.ds(pl.multiple_of((1 - core) * half, half), half)
    xh_ref[0] = jnp.transpose(xt_ref[0, :, mine])
    row = seg_ref[pl.ds(pl.program_id(0), 1), :].astype(F32)
    column = jnp.transpose(jnp.broadcast_to(row, (128, slots)))[:, 0:1]
    scale = 1.0 / (size**0.5)
    for block in range(2):
        rows = slice(block * half, (block + 1) * half)
        allowed = column[rows] == row
        for h in range(heads):
            feats = slice(h * size, (h + 1) * size)
            scores = dot_tn(qkv_ref[0, 0, feats, rows], qkv_ref[0, 1, feats, :]) * scale
            scores = scores + prev_ref[0, h, rows, :].astype(F32)
            raw_ref[0, h, rows, :] = scores.astype(BF)
            masked = jnp.where(allowed, scores, NEG)
            expanded = jnp.exp(masked - jnp.max(masked, axis=-1, keepdims=True))
            prob = expanded * (1.0 / jnp.sum(expanded, axis=-1, keepdims=True))
            prob = prob.astype(BF)
            p_ref[0, h, rows, :] = prob
            o_scr[feats, rows] = dot_nt(qkv_ref[0, 2, feats, :], prob).astype(BF)
    own_ref[0] = o_scr[:, mine]
    oth_ref[0] = o_scr[:, other]


def up_kernel(
    me_ref, o0, o1, o2, o3, wo0, wo1, wo2, wo3, big_a, big_b, xh_ref, bias_ref, gain_ref, shift_ref,
    b_up_a, b_up_b,
    n1_ref, r1_ref, x1_ref, ga_ref, gb_ref, gpa_ref, gpb_ref, part_ref,
):
    units = b_up_a.shape[1]
    w1a, w1b = big_a.at[:, :units], big_b.at[:, :units]
    w2a, w2b = big_a.at[:, units : 2 * units], big_b.at[:, units : 2 * units]
    total = xh_ref[0].astype(F32) + bias_ref[0:1, :]
    for left, right in ((o0, wo0), (o1, wo1), (o2, wo2), (o3, wo3)):
        total = total + dot_nt(jnp.transpose(left[0]), right[...])
    normed, inv_std = ln_stats(total)
    n1_ref[0] = normed
    r1_ref[0] = jnp.broadcast_to(inv_std, r1_ref.shape[1:])
    x1_ref[0] = (normed * gain_ref[0:1, :] + shift_ref[0:1, :]).astype(BF)
    block = 256

    def one_block(step, carry):
        lanes = pl.ds(pl.multiple_of(step * block, block), block)
        sides = ((w1a, b_up_a, ga_ref, gpa_ref), (w1b, b_up_b, gb_ref, gpb_ref))
        for w1, b_up, g_ref, gp_ref in sides:
            hidden = dot(x1_ref[0], w1[:, lanes]) + b_up[:, lanes]
            cdf = 0.5 * (1.0 + lax.erf(hidden * (0.5**0.5)))
            pdf = jnp.exp(-0.5 * hidden * hidden) * 0.3989422804014327
            g_ref[0, :, lanes] = (hidden * cdf).astype(BF)
            gp_ref[0, :, lanes] = (cdf + hidden * pdf).astype(BF)
        return carry

    lax.fori_loop(0, units // block, one_block, 0)
    part_ref[0] = (dot_nt(ga_ref[0], w2a[...]) + dot_nt(gb_ref[0], w2b[...])).astype(BF)


def down_kernel(
    me_ref, n1_ref, pa_ref, pb_ref, dy0, dy1, dy2, dy3, bias_ref, gain_ref, shift_ref,
    big_a, big_b, gpa_ref, gpb_ref,
    act_own_ref, act_oth_ref, ds_ref, dsb_ref, da_ref, db_ref, vec_ref, bup_a_ref, bup_b_ref, part_ref,
    scr,
):
    me = me_ref[0]
    width = dy0.shape[1]
    units = gpa_ref.shape[2]
    w1a, w1b = big_a.at[:, :units], big_b.at[:, :units]
    w2a, w2b = big_a.at[:, units : 2 * units], big_b.at[:, units : 2 * units]
    branch = pa_ref[0].astype(F32) + pb_ref[0].astype(F32)
    first_out = n1_ref[0] * gain_ref[0:1, :] + shift_ref[0:1, :]
    normed, inv_std = ln_stats(first_out + branch + bias_ref[1:2, :])
    gain = gain_ref[1:2, :]
    scr[...] = jnp.transpose(normed * gain + shift_ref[1:2, :])
    for step, out in ((0, act_own_ref), (1, act_oth_ref)):
        start = pl.multiple_of(place_of(me, step) * width, width)
        out[0] = scr[pl.ds(start, width), :].astype(BF)
    for step, piece in enumerate((dy0, dy1, dy2, dy3)):
        start = pl.multiple_of(place_of(me, step) * width, width)
        scr[pl.ds(start, width), :] = piece[0].astype(F32)
    grad = jnp.transpose(scr[...])
    inner = ln_back(grad, normed, inv_std, gain)
    ds_ref[0] = inner
    vec_ref[0, 0:1, :] = jnp.sum(grad * normed, axis=0, keepdims=True)
    vec_ref[0, 1:2, :] = jnp.sum(grad, axis=0, keepdims=True)
    vec_ref[0, 2:3, :] = jnp.sum(inner, axis=0, keepdims=True)
    dsb_ref[0] = inner.astype(BF)
    block = 256

    def one_block(step, carry):
        lanes = pl.ds(pl.multiple_of(step * block, block), block)
        sides = ((w2a, da_ref, gpa_ref, bup_a_ref), (w2b, db_ref, gpb_ref, bup_b_ref))
        for w2, dh_ref, gp_ref, bup_ref in sides:
            grad_hidden = dot(dsb_ref[0], w2[:, lanes]) * gp_ref[0, :, lanes].astype(F32)
            bup_ref[0, 0:1, lanes] = jnp.sum(grad_hidden, axis=0, keepdims=True)
            dh_ref[0, :, lanes] = grad_hidden.astype(BF)
        return carry

    lax.fori_loop(0, units // block, one_block, 0)
    part_ref[0] = (dot_nt(da_ref[0], w1a[...]) + dot_nt(db_ref[0], w1b[...])).astype(BF)


def mid_kernel(
    me_ref, ds_ref, pa_ref, pb_ref, n1_ref, r1_ref, gain_ref, wo0, wo1,
    dsb_ref, vec_ref, do_own_ref, do_oth_ref, near_ref, scr,
):
    chip = me_ref[0] // 2
    width = do_own_ref.shape[1]
    grad = ds_ref[0] + (pa_ref[0].astype(F32) + pb_ref[0].astype(F32))
    normed = n1_ref[0]
    inner = ln_back(grad, normed, r1_ref[0, :, 0:1], gain_ref[0:1, :])
    vec_ref[0, 0:1, :] = jnp.sum(grad * normed, axis=0, keepdims=True)
    vec_ref[0, 1:2, :] = jnp.sum(grad, axis=0, keepdims=True)
    vec_ref[0, 2:3, :] = jnp.sum(inner, axis=0, keepdims=True)
    dsb = inner.astype(BF)
    dsb_ref[0] = dsb
    scr[...] = inner
    chip_lanes = pl.ds(pl.multiple_of(chip * 2 * width, 128), 2 * width)
    near_ref[0] = jnp.transpose(scr[:, chip_lanes])
    do_own_ref[0] = jnp.transpose(dot(dsb, wo0[...])).astype(BF)
    do_oth_ref[0] = jnp.transpose(dot(dsb, wo1[...])).astype(BF)


def back_kernel(
    heads, me_ref, p_ref, qkv_ref, do_own_ref, do_oth_ref, w_ref, near_ref,
    lg_ref, dqkv_ref, e0, e1, e2, e3, vec_ref, do_scr, dx_scr, sum_scr,
):
    me = me_ref[0]
    core, chip = lax.rem(me, 2), me // 2
    width, slots = qkv_ref.shape[2], qkv_ref.shape[3]
    half = slots // 2
    size = width // heads
    mine = pl.ds(pl.multiple_of(core * half, half), half)
    other = pl.ds(pl.multiple_of((1 - core) * half, half), half)
    do_scr[:, mine] = do_own_ref[0]
    do_scr[:, other] = do_oth_ref[0]
    scale = 1.0 / (size**0.5)
    def one_head(h, carry):
        feats = pl.ds(pl.multiple_of(h * size, size), size)
        query, key, value = (qkv_ref[0, part, feats, :] for part in range(3))
        out_grad = do_scr[feats, :]
        for block in range(2):
            rows = slice(block * half, (block + 1) * half)
            prob = p_ref[0, h, rows, :].astype(F32)
            grad_prob = dot_tn(do_scr[feats, rows], value)
            weighted = grad_prob * prob
            inner = jnp.sum(weighted, axis=-1, keepdims=True)
            lg_ref[0, h, rows, :] = (weighted - prob * inner).astype(BF)
        grad_query = dot_nt(key, lg_ref[0, h]) * scale
        grad_key = dot(query, lg_ref[0, h]) * scale
        grad_value = dot(out_grad, p_ref[0, h])
        for number, grad in ((0, grad_query), (1, grad_value)):
            line = jnp.sum(grad, axis=1, keepdims=True)
            sum_scr[number, feats, :] = jnp.broadcast_to(line, (size, 128))
        dqkv_ref[0, feats, :] = grad_query.astype(BF)
        dqkv_ref[0, pl.ds(pl.multiple_of(width + h * size, size), size), :] = grad_key.astype(BF)
        dqkv_ref[0, pl.ds(pl.multiple_of(2 * width + h * size, size), size), :] = grad_value.astype(BF)
        return carry

    lax.fori_loop(0, heads, one_head, 0)
    for number in range(2):
        vec_ref[0, number : number + 1, :] = jnp.transpose(sum_scr[number])[0:1, :]
    dx_scr[...] = dot(w_ref[:, : 3 * width], dqkv_ref[0])
    near = pl.ds(pl.multiple_of(chip * 2 * width, width), 2 * width)
    dx_scr[near, mine] = dx_scr[near, mine] + near_ref[0]
    for step, out in enumerate((e0, e1, e2, e3)):
        start = pl.multiple_of(place_of(me, step) * width, width)
        out[0] = dx_scr[pl.ds(start, width), :].astype(BF)


def ffn_grad_kernel(count, bit, me_ref, *rest):
    lefts, rights = rest[:count], rest[count : 2 * count]
    keep_ref, send_ref, scr = rest[2 * count :]
    side = me_ref[2 + bit]
    total = None
    for left, right in zip(lefts, rights):
        a = left[...].reshape(-1, left.shape[-1])
        b = right[...].reshape(-1, right.shape[-1])
        product = dot_tn(a, b)
        total = product if total is None else total + product
    part = keep_ref.shape[0]
    scr[...] = total
    keep_ref[...] = scr[pl.ds(pl.multiple_of(side * part, part), part), :].astype(BF)
    send_ref[...] = scr[pl.ds(pl.multiple_of((1 - side) * part, part), part), :].astype(BF)


def qkv_grad_kernel(count, me_ref, *rest):
    groups = [rest[i * count : (i + 1) * count] for i in range(6)]
    small_ref, came_ref, *bqv, keep_ref, send_ref, scr = rest[6 * count :]
    side = me_ref[2]
    width = bqv[0].shape[2]
    line = lax.broadcasted_iota(jnp.int32, small_ref.shape, 0)
    small = small_ref[...]
    scr[:8, :] = jnp.where(line < 6, (small + came_ref[...]) * 0.5, small)
    total = functools.reduce(jnp.add, [b[0] for b in bqv])
    scr[7:8, :width] = total[0:1, :]
    scr[7:8, width : 2 * width] = total[1:2, :]
    halves = as_halves(scr[:8, :])
    total = None
    for x, grad in zip(groups[0], groups[1]):
        for index in range(grad.shape[0]):
            product = dot_nt(grad[index], x[index])
            total = product if total is None else total + product
    used = total.shape[0]
    scr[:used, :] = total
    total = None
    for lefts, rights in ((groups[2], groups[3]), (groups[4], groups[5])):
        for left, right in zip(lefts, rights):
            for index in range(left.shape[0]):
                product = dot(left[index], right[index])
                total = product if total is None else total + product
    scr[used:, :] = total
    part = scr.shape[0] // 2
    for out, half in ((keep_ref, side), (send_ref, 1 - side)):
        place = pl.ds(pl.multiple_of(half * part, part), part)
        out[:part, :] = scr[place, :].astype(BF)
        out[part:, :] = halves


def halve_kernel(bit, tail, me_ref, *rest):
    count = (len(rest) - 2) // 2
    keep_ref, send_ref = rest[-2:]
    side = me_ref[2 + bit]
    rows = (rest[0].shape[0] - tail) // 2
    for number in range(count):
        kept, came = rest[2 * number], rest[2 * number + 1]
        for out, half in ((keep_ref, side), (send_ref, 1 - side)):
            place = pl.ds(pl.multiple_of(half * rows, rows), rows)
            total = kept[place, :].astype(F32) + came[place, :].astype(F32)
            out[number * rows : (number + 1) * rows, :] = total.astype(BF)
    if tail:
        both = as_halves(from_halves(kept[2 * rows :, :]) + from_halves(came[2 * rows :, :]))
        keep_ref[rows:, :] = both
        send_ref[rows:, :] = both


def last_kernel(me_ref, kept, came, out_ref, small_ref):
    rows = out_ref.shape[0]
    out_ref[...] = (kept[:rows, :].astype(F32) + came[:rows, :].astype(F32)).astype(BF)
    small_ref[...] = from_halves(kept[rows:, :]) + from_halves(came[rows:, :])


def finish_kernel(steps, pair, me_ref, *rest):
    count = len(steps)
    blocks, outs = rest[:count], rest[count:]
    rows = blocks[0].shape[0]
    for number, back in enumerate(steps):
        group = group_at(me_ref, back, count)
        bits = lax.rem(group, 2), lax.rem(group // 2, 2), group // 4
        index = bits[0] * 4 + bits[1] * 2 + bits[2]
        if pair:
            part = rows // 2
            other = bits[1] * 4 + bits[0] * 2 + bits[2]
            for out, place, low in ((outs[0], index, 0), (outs[1], other, part)):
                place = pl.ds(pl.multiple_of(place * part, part), part)
                out[place, :] = blocks[number][low : low + part, :].astype(F32)
            continue
        block = blocks[number][...].astype(F32)
        before = 0
        for out in outs:
            held = out.shape[0] // rows

            @pl.when((index >= before) & (index < before + held))
            def _():
                out[pl.ds(pl.multiple_of((index - before) * rows, rows), rows), :] = block

            before += held


def ring_place(group, groups):
    return jnp.where(lax.rem(group, 2) == 0, group // 2, groups - 1 - group // 2)


def group_at(me_ref, back, count):
    there = lax.rem(ring_place(me_ref[1], count) + count - back, count)
    return jnp.where(there < count // 2, 2 * there, 2 * (count - 1 - there) + 1)


def pairs_kernel(me_ref, *rest):
    count = len(rest) - 3
    blocks, out_a, out_b, sems = rest[:count], rest[-3], rest[-2], rest[-1]
    core = lax.rem(me_ref[0], 2)
    rows = blocks[0].shape[0] // 2
    copies = []
    for number in range(count):
        steps = number if number <= count // 2 else number - count // 2
        ahead = core if number <= count // 2 else 1 - core
        back = jnp.where(ahead == 1, lax.rem(count - steps, count), steps)
        place = pl.ds(pl.multiple_of(group_at(me_ref, back, count) * rows, rows), rows)
        first, second = (out_a, out_b) if number <= count // 2 else (out_b, out_a)
        for part, out in enumerate((first, second)):
            copies.append(
                pltpu.make_async_copy(
                    blocks[number].at[pl.ds(part * rows, rows), :],
                    out.at[place, :],
                    sems.at[number, part],
                )
            )
    for copy in copies:
        copy.start()
    for copy in copies:
        copy.wait()


def small_kernel(me_ref, vec1, vec2, bup_a, bup_b, own_ref, oth_ref):
    own_ref[...] = jnp.zeros_like(own_ref)
    oth_ref[...] = jnp.zeros_like(oth_ref)
    for low, vec in ((0, vec1), (3, vec2)):
        total = jnp.sum(vec[...], axis=0)
        own_ref[low : low + 3, :] = total
        oth_ref[low : low + 3, :] = total
    own_ref[6:7, :] = jnp.sum(bup_a[...], axis=0)
    oth_ref[6:7, :] = jnp.sum(bup_b[...], axis=0)


def as_halves(value):
    high = value.astype(BF).astype(F32)
    return jnp.concatenate([high, value - high], 0).astype(BF)


def from_halves(both):
    both = both.astype(F32)
    return both[:8] + both[8:]


def whole(array):
    shape = array.shape
    return pl.BlockSpec(shape, lambda i, s: (0,) * len(shape))


def held(array):
    return pl.BlockSpec(memory_space=pltpu.VMEM)


def by_row(array, first=0):
    shape = array.shape
    rest = (0,) * (len(shape) - 1)
    return pl.BlockSpec((1,) + shape[1:], lambda i, s: (first + i,) + rest)


def on_row(row, rowed, skip, kernel):
    def inner(*refs):
        kernel(*[
            ref.at[pl.ds(row, 1)] if number in rowed else ref
            for number, ref in enumerate(refs)
            if number not in skip
        ])

    return inner


def call(kernel, grid, ins, outs, out_specs, scratch, name, micros, alias=None, room=32):
    flops = int(micros * 10)
    return pl.pallas_call(
        kernel,
        out_shape=outs,
        grid_spec=pltpu.PrefetchScalarGridSpec(
            num_scalar_prefetch=1,
            grid=grid,
            in_specs=[spec for _, spec in ins[1:]],
            out_specs=out_specs,
            scratch_shapes=scratch,
        ),
        input_output_aliases=alias or {},
        compiler_params=pltpu.CompilerParams(vmem_limit_bytes=room << 20),
        cost_estimate=pl.CostEstimate(flops=flops, bytes_accessed=1, transcendentals=0),
        name=name,
    )(*[a for a, _ in ins])


def body(
    tokens, cotangent, prev_logits, segment_ids, w_qkv, b_qv, w_out, w_up, b_up, w_down,
    biases, gains, shifts,
):
    rows, slots, width = tokens.shape
    full = width * lax.axis_size("tensor")
    groups = lax.axis_size("dp")
    near_dp = groups == 8
    heads = prev_logits.shape[1]
    half = slots // 2
    units = w_up.shape[1]
    me = lax.axis_index("tensor").astype(jnp.int32)
    dp = lax.axis_index("dp").astype(jnp.int32)
    me_ref = jnp.stack([me, dp, lax.rem(dp, 2), lax.rem(dp // 2, 2), dp // 4])
    core = lax.rem(me, 2)
    sds = jax.ShapeDtypeStruct

    def after(value, *others):
        return lax.optimization_barrier((value, others))[0]

    together = lax.optimization_barrier

    def pp(array, step):
        return lax.ppermute(array, "tensor", [(i, i ^ step) for i in range(4)])

    def swap(array, bit):
        return lax.ppermute(array, "dp", [(i, i ^ (1 << bit)) for i in range(groups)])

    order = list(range(0, groups, 2)) + list(range(groups - 1, 0, -2))
    onward = [(order[i], order[(i + 1) % groups]) for i in range(groups)]
    backward = [(b, a) for a, b in onward]

    ring_steps = [0]
    for step in range(1, groups // 2):
        ring_steps += [step, groups - step]
    ring_steps += [groups // 2]

    def ring_step(ahead, behind):
        return lax.ppermute(ahead, "dp", onward), lax.ppermute(behind, "dp", backward)

    def place_pairs(blocks):
        outs = [sds((full, blocks[0].shape[1]), BF)] * 2
        return call(
            pairs_kernel, (1,),
            [(me_ref, None)] + [(b, held(b)) for b in blocks], outs, [held(o) for o in outs],
            [pltpu.SemaphoreType.DMA((groups, 2))], "pairs", 2, None, 8,
        )

    both_ways = []
    for i, j in onward:
        both_ways += [(i * 4 + t, j * 4 + t) if t % 2 == 0 else (j * 4 + t, i * 4 + t) for t in range(4)]

    def pair_step(pair):
        return lax.ppermute(pair, ("dp", "tensor"), both_ways)

    tokens = jnp.swapaxes(tokens, 1, 2)
    cotangent = jnp.swapaxes(cotangent, 1, 2)
    shard_in = w_qkv.astype(BF).reshape(w_qkv.shape[0], 3 * width)
    x_y = pp(tokens, 2)
    x_c = pp(tokens, 1)
    shard_in = jnp.concatenate([shard_in, w_out.T.astype(BF)], 1)
    shard_big = jnp.concatenate([w_up.astype(BF), w_down.T.astype(BF)], 1)
    if near_dp:
        pair_big = jnp.concatenate([shard_big, pp(shard_big, 1)], 0)
        ring = [ring_step(shard_in, shard_in)]
        ring.append(ring_step(*together(ring[-1])))
        ring.append(ring_step(*together(ring[-1])))
        last = lax.ppermute(together(ring[-1])[0], "dp", onward)
        pair_big = after(pair_big, last)
        came = [pair_step(pair_big)]
        pieces_in = [shard_in, *ring[0], *ring[1], *ring[2], last]
    else:
        pieces_in = [lax.all_gather(shard_in, "dp", axis=0, tiled=True)]
        big_a = lax.all_gather(shard_big, "dp", axis=0, tiled=True)
    x_d = pp(x_y, 1)
    x_pieces = (tokens, x_c, x_y, x_d)
    cot = after(cotangent, x_y)
    dy_mine = lax.dynamic_slice_in_dim(cot, core * half, half, 2)
    dy_other = lax.dynamic_slice_in_dim(cot, (1 - core) * half, half, 2)
    dy1, dy2, dy3 = pp(dy_other, 1), pp(dy_mine, 2), pp(dy_other, 3)
    b_up_a = b_up.reshape(1, units)
    b_up_b = pp(b_up_a, 1)

    sds3 = lambda *shape_type: sds((rows,) + shape_type[:-1], shape_type[-1])

    class Stage:
        def __init__(self, kernel, fulls, parts, scratch, name, room, far=()):
            self.kernel, self.fulls, self.parts, self.scratch = kernel, fulls, parts, scratch
            self.name, self.room, self.far, self.kept = name, room, far, None

        def step(self, row, given):
            fulls, far = self.fulls, self.far
            ins = [(me_ref, None)]
            ins += [(a, held(a) if isinstance(k, str) else k) for a, k in given]
            rowed = {1 + i for i, (_, k) in enumerate(given) if isinstance(k, str) and k == "row"}
            low, alias = len(ins), {}
            if self.kept is not None:
                alias = {low + i: i for i in range(len(fulls))}
                ins += [
                    (k, pl.BlockSpec(memory_space=pl.ANY) if i in far else held(k))
                    for i, k in enumerate(self.kept)
                ]
            base = len(ins)
            outs = list(fulls) + list(self.parts)
            specs = [by_row(o, row) if i in far else held(o) for i, o in enumerate(fulls)]
            specs += [held(o) for o in self.parts]
            rowed |= {base + i for i in range(len(fulls)) if i not in far}
            result = call(
                on_row(row, rowed, set(alias), self.kernel), (1,), ins, outs, specs,
                self.scratch, self.name, 1, alias, self.room,
            )
            self.kept = result[: len(fulls)]
            return result[len(fulls) :]

    ins = [(me_ref, None)] + [(p, by_row(p)) for p in x_pieces]
    ins += [(b_qv, whole(b_qv)), (prev_logits, by_row(prev_logits))]
    ins += [(segment_ids, whole(segment_ids))] + [(b, whole(b)) for b in pieces_in]
    outs = [
        sds(prev_logits.shape, BF),
        sds(prev_logits.shape, BF),
        sds3(3, width, slots, BF),
        sds3(width, half, BF),
        sds3(width, half, BF),
        sds3(full, slots, BF),
        sds3(half, full, BF),
        sds((full, full), BF),
    ]
    raw, prob, qkv, o_own, o_oth, xt, xh, w_in = call(
        functools.partial(attend_kernel, heads, ring_steps if near_dp else [0]), (rows,), ins,
        outs, [by_row(o) for o in outs[:-1]] + [held(outs[-1])],
        [pltpu.VMEM((width, slots), BF)], "attend", 1, None, 48,
    )
    o1, o2, o3 = pp(o_oth, 1), pp(o_own, 2), pp(o_oth, 3)
    wo0 = w_in[:, 3 * width :]
    wo2 = pp(wo0, 2)
    wo1, wo3 = pp(wo0, 1), pp(wo2, 1)
    if near_dp:
        came.append(pair_step(after(came[0], o_own, dy1, dy2, dy3)))
        came.append(pair_step(after(came[1], o2)))
        came.append(pair_step(after(came[2], o1, o3)))
        big_a, big_b = place_pairs(
            [pair_big, *came[:3], after(came[3], wo2), *[pp(b, 1) for b in came[:3]]]
        )
    else:
        big_a = after(big_a, o_own)
        big_b = pp(big_a, 1)

    one = (1, half, full)
    up = Stage(
        up_kernel,
        [
            sds3(half, full, F32), sds3(half, 128, F32), sds3(half, full, BF),
            sds3(half, units, BF), sds3(half, units, BF), sds3(half, units, BF), sds3(half, units, BF),
        ],
        [sds(one, BF)], [], "up", 16,
    )
    part, part_y = [], []
    for row in range(rows):
        given = [(o, "row") for o in (o_own, o1, o2, o3)]
        given += [(w, "all") for w in (wo0, wo1, wo2, wo3, big_a, big_b)] + [(xh, "row")]
        given += [(w, "all") for w in (biases, gains, shifts, b_up_a, b_up_b)]
        part += up.step(row, given)
        part_y.append(pp(part[row], 2))
    n1, r1, x1, ga, gb, gpa, gpb = up.kept
    gc, x1_c = pp(gb, 1), pp(x1, 1)

    down = Stage(
        down_kernel,
        [
            sds3(width, half, BF), sds3(width, half, BF), sds3(half, full, F32),
            sds3(half, full, BF), sds3(half, units, BF), sds3(half, units, BF),
            sds3(3, full, F32), sds3(1, units, F32), sds3(1, units, F32),
        ],
        [sds(one, BF)], [pltpu.VMEM((full, half), F32)], "down", 16,
    )
    part2, part2_y = [], []
    for row in range(rows):
        got = after(part_y[row], part2_y[0]) if row == 2 else part_y[row]
        given = [(n1, "row"), (part[row], "all"), (got, "all")]
        given += [(d, "row") for d in (dy_mine, dy1, dy2, dy3)]
        given += [(w, "all") for w in (biases, gains, shifts, big_a, big_b)]
        given += [(gpa, "row"), (gpb, "row")]
        part2 += down.step(row, given)
        part2_y.append(pp(part2[row], 2))
    act_own, act_oth, ds2, ds2b, da, db, vec2, bup_a, bup_b = down.kept
    ds2b_c, dc = pp(ds2b, 1), pp(db, 1)

    def ffn_grad(lefts, rights, bit):
        block = 256
        def part(a):
            return pl.BlockSpec(a.shape[:2] + (block,), lambda i, s: (0, 0, i))
        ins = [(me_ref, None)] + [(a, whole(a)) for a in lefts] + [(a, part(a)) for a in rights]
        across, down = rights[0].shape[-1], lefts[0].shape[-1]
        outs = [sds((down // 2, across), BF)] * 2
        specs = [pl.BlockSpec((down // 2, block), lambda i, s: (0, i))] * 2
        return call(
            functools.partial(ffn_grad_kernel, len(lefts), bit),
            (across // block,), ins, outs, specs, [pltpu.VMEM((down, block), F32)], "ffn_grad", 3,
        )

    def halve(bit, *pairs, tail=0):
        down, across = pairs[0][0].shape
        outs = [sds((len(pairs) * (down - tail) // 2 + tail, across), BF)] * 2
        ins = [(me_ref, None)] + [(a, whole(a)) for pair in pairs for a in pair]
        return call(
            functools.partial(halve_kernel, bit, tail), (1,), ins, outs, [whole(o) for o in outs], [],
            "halve", 1,
        )

    def added(keep, got):
        return (keep.astype(F32) + got.astype(F32)).astype(BF)

    def finish(blocks, outs, pair=False):
        return call(
            functools.partial(finish_kernel, ring_steps, pair), (1,),
            [(me_ref, None)] + [(b, whole(b)) for b in blocks],
            outs, [whole(o) for o in outs], [], "finish", 2,
        )

    def whole_of(keep, send, bit):
        low = jnp.where(lax.rem(dp >> bit, 2) == 0, keep, send)
        high = jnp.where(lax.rem(dp >> bit, 2) == 0, send, keep)
        return jnp.concatenate([low, high], 0)

    mid = Stage(
        mid_kernel, [sds3(half, full, BF), sds3(3, full, F32)],
        [sds((1, width, half), BF)] * 2 + [sds((1, 2 * width, half), F32)],
        [pltpu.VMEM((half, full), F32)], "mid", 16,
    )
    back = Stage(
        functools.partial(back_kernel, heads),
        [sds(prev_logits.shape, BF), sds3(3 * width, slots, BF)] + [sds3(width, slots, BF)] * 4,
        [sds((1, 2, width), F32)],
        [pltpu.VMEM((width, slots), BF), pltpu.VMEM((full, slots), F32), pltpu.VMEM((2, width, 128), F32)],
        "back", 32, (0,),
    )

    def mid_step(row, *earlier):
        given = [(ds2, "row"), (part2[row], "all"), (after(part2_y[row], *earlier), "all")]
        given += [(n1, "row"), (r1, "row"), (gains, "all"), (wo0, "all"), (wo1, "all")]
        own, oth, near = mid.step(row, given)
        return own, pp(oth, 1), near

    def back_step(row, held_by, *earlier):
        own, got, near = held_by
        given = [(prob, by_row(prob, row)), (qkv, by_row(qkv, row)), (own, "all")]
        given += [(after(got, *earlier), "all"), (w_in, "all"), (near, "all")]
        return back.step(row, given)[0]

    keep_d, send_d = ffn_grad((ga, gc), (ds2b, ds2b_c), 0)
    mids = [mid_step(0)]
    keep_u, send_u = ffn_grad((x1, x1_c), (da, dc), 1)
    mids.append(mid_step(1, keep_d, keep_u, mids[0][0]))
    sums = [back_step(0, mids[0], mids[1][0]), back_step(1, mids[1])]
    if near_dp:
        got_d, got_u = (swap(after(g, mids[1][0]), b) for g, b in ((send_d, 0), (send_u, 1)))
        mids.append(mid_step(2, sums[1], got_d, got_u))
        keep_d, send_d = halve(1, (keep_d, after(got_d, mids[2][0])))
        keep_u, send_u = halve(0, (keep_u, got_u))
        got_d, got_u = swap(send_d, 1), swap(send_u, 0)
        sums.append(back_step(2, mids[2], keep_d, keep_u))
    else:
        mids.append(mid_step(2, sums[1]))
        grad_down, grad_up = lax.psum((whole_of(keep_d, send_d, 0), whole_of(keep_u, send_u, 1)), "dp")
        grad_down, grad_up = grad_down.astype(F32), grad_up.astype(F32)
        sums.append(back_step(2, mids[2]))
    ds1b, vec1 = mid.kept
    ds1b_c = pp(ds1b, 1)
    ins = [(me_ref, None)] + [(a, whole(a)) for a in (vec1, vec2, bup_a, bup_b)]
    outs = [sds((8, full), F32)] * 2
    small, other = call(small_kernel, (1,), ins, outs, [whole(o) for o in outs], [], "small", 1)
    small = small + pp(other, 1)
    small_y = pp(small, 2)
    lg, dqkv, e0, e1, e2, e3 = back.kept

    ins = [(me_ref, None)] + [(a, whole(a)) for a in (xt, dqkv, o_own, ds1b, o_oth, ds1b_c)]
    ins += [(a, whole(a)) for a in (small, small_y, *sums)]
    outs = [sds((full // 2 + 16, full), BF)] * 2
    keep, send = call(
        functools.partial(qkv_grad_kernel, 1), (1,), ins, outs, [whole(o) for o in outs],
        [pltpu.VMEM((full, full), F32)], "qkv_grad", 4,
    )

    if near_dp:
        got = swap(send, 0)
        keep_du, send_du = halve(2, (keep_d, after(got_d, send)), (keep_u, got_u))
        got_du = swap(send_du, 2)
        keep, send = halve(1, (keep, got), tail=16)
        got = swap(send, 1)
        pair = added(keep_du, got_du)
        ring_u = [ring_step(pair, pair)]
        keep, send = halve(2, (keep, got), tail=16)
        got = swap(send, 2)
        ring_u.append(ring_step(*together(ring_u[-1])))
        outs = [sds((full // 8, full), BF), sds((8, full), F32)]
        total, small = call(
            last_kernel, (1,), [(me_ref, None), (keep, whole(keep)), (got, whole(got))], outs,
            [whole(o) for o in outs], [], "last", 1,
        )
        ring = [ring_step(total, total)]
        ring_u.append(ring_step(*together(ring_u[-1])))
        ring.append(ring_step(*together(ring[-1])))
        last_u = lax.ppermute(ring_u[-1][0], "dp", onward)
        ring.append(ring_step(*together(ring[-1])))
        last = lax.ppermute(ring[-1][0], "dp", onward)
        grad_down, grad_up = finish(
            [after(pair, *ring[2]), *ring_u[0], *ring_u[1], *ring_u[2], last_u],
            [sds((units, full), F32), sds((full, units), F32)], True,
        )
        grad_in, grad_out = finish(
            [total, *ring[0], *ring[1], *ring[2], last],
            [sds((3 * width, full), F32), sds((width, full), F32)],
        )
    else:
        part = full // 2
        tail = lax.psum(whole_of(keep[:part], send[:part], 0), "dp").astype(F32)
        small = lax.psum(keep[part : part + 8].astype(F32) + keep[part + 8 :].astype(F32), "dp")
        grad_in, grad_out = tail[: 3 * width], tail[3 * width :]
    grad_b_up = small[6]
    grad_b_qv = small[7, : 2 * width].reshape(2, width)

    grad_in = jnp.transpose(grad_in.reshape(3, width, full), (2, 0, 1))

    act_c = pp(act_oth, 1)
    block_out = jnp.concatenate(
        [jnp.where(core == 0, act_own, act_c), jnp.where(core == 0, act_c, act_own)], 2
    )
    near_sum = e2.astype(F32) + pp(e3, 1).astype(F32)
    far = pp(near_sum.astype(BF), 2).astype(F32)
    grad_x = (e0.astype(F32) + pp(e1, 1).astype(F32) + far).astype(BF)
    return (
        jnp.swapaxes(block_out, 1, 2),
        raw,
        jnp.swapaxes(grad_x, 1, 2),
        lg,
        grad_in,
        grad_b_qv,
        grad_out,
        grad_up,
        grad_b_up,
        grad_down,
        jnp.stack([small[2], small[5]]),
        jnp.stack([small[0], small[3]]),
        jnp.stack([small[1], small[4]]),
    )


def solution(mesh):
    placed = (
        P("dp", None, "tensor"),
        P("dp", None, "tensor"),
        P("dp", "tensor", None, None),
        P("dp", None),
        P("dp", None, "tensor"),
        P(None, "tensor"),
        P("tensor", "dp"),
        P("dp", "tensor"),
        P("tensor"),
        P("tensor", "dp"),
        P(),
        P(),
        P(),
    )
    return jax.shard_map(
        body,
        mesh=mesh,
        in_specs=placed,
        out_specs=(
            P("dp", None, "tensor"),
            P("dp", "tensor", None, None),
            P("dp", None, "tensor"),
            P("dp", "tensor", None, None),
            P(None, None, "tensor"),
            P(None, "tensor"),
            P("tensor", None),
            P(None, "tensor"),
            P("tensor"),
            P("tensor", None),
            P(),
            P(),
            P(),
        ),
        check_vma=False,
    )
```

time: 321 us -> 267 us (0.83); the launches traced: 315 us -> 266 us
  Pallas kernels: 104 us -> 81 us
  starting transfers between devices: 74.4 us -> 51.7 us
  waiting for transfers between devices: 97.8 us -> 108 us
  local copies, waits for them, and re-layouts: 23.2 us -> 16.2 us
  other arithmetic: 13.9 us -> 7.69 us
    pallas_call x23 -> x26, Pallas kernels: 104 us -> 81 us  [call(): pl.pallas_call(kernel, out_shape=outs, grid_spec=pltpu.PrefetchScalarGrid...]
    ppermute x12 -> x9, waiting for transfers between devices: 41.5 us -> 19.9 us  [ring_step(): lax.ppermute(ahead, 'dp', onward)]
    ppermute x35 -> x37, waiting for transfers between devices: 23.8 us -> 43.4 us  [pp(): return lax.ppermute(array, 'tensor', [(i, i ^ step) for i in range(4)])]
    ppermute x16 -> x12, starting transfers between devices: 24.7 us -> 10.9 us  [the longest x8 7.31 us: swap(): return lax.ppermute(array, 'dp', [(i, i ^ 1 << bit) for i in range(groups)])]
    ppermute x16 -> x12, waiting for transfers between devices: 17.7 us -> 28.2 us  [the longest x8 27.1 us: swap(): return lax.ppermute(array, 'dp', [(i, i ^ 1 << bit) for i in range(groups)])]
    ppermute x12 -> x9, starting transfers between devices: 15.5 us -> 7.13 us  [ring_step(): lax.ppermute(ahead, 'dp', onward)]
    unnamed x139 -> x83, local copies, waits for them, and re-layouts: 19.5 us -> 12.6 us
    ppermute x35 -> x37, starting transfers between devices: 18.5 us -> 22.4 us  [pp(): return lax.ppermute(array, 'tensor', [(i, i ^ step) for i in range(4)])]
  transfers between devices with their start and end apart: 78 -> 70, of which waited for: 27 -> 29; matrix products, arithmetic and copies ran while one was open for 5% -> 4% of each run, Pallas kernels for 29% -> 26%
where the time goes in v3:
time: 267 us; the launch traced here: 266 us
  waiting for transfers between devices  108 us (40%)
  Pallas kernels  81 us (30%)
  starting transfers between devices  51.7 us (19%)
  local copies, waits for them, and re-layouts  16.2 us (6%)
  other arithmetic  7.69 us (3%)
    pallas_call x26, Pallas kernels, call(): pl.pallas_call(kernel, out_shape=outs, grid_spec=pltpu.PrefetchScalarGrid...  81 us
    ppermute x37, waiting for transfers between devices, pp(): return lax.ppermute(array, 'tensor', [(i, i ^ step) for i in range(4)])  43.4 us
    ppermute x8, waiting for transfers between devices, swap(): return lax.ppermute(array, 'dp', [(i, i ^ 1 << bit) for i in range(groups)])  27.1 us
    ppermute x37, starting transfers between devices, pp(): return lax.ppermute(array, 'tensor', [(i, i ^ step) for i in range(4)])  22.4 us
    ppermute x9, waiting for transfers between devices, ring_step(): lax.ppermute(ahead, 'dp', onward)  19.9 us
    unnamed x83, local copies, waits for them, and re-layouts  12.6 us
    ppermute x9, waiting for transfers between devices, ring_step(): lax.ppermute(behind, 'dp', backward)  11.2 us
    ppermute x9, starting transfers between devices, ring_step(): lax.ppermute(behind, 'dp', backward)  9.79 us
  transfers between devices with their start and end apart: 70, of which 29 were waited for; matrix products, arithmetic and copies ran while one was open for 4% of the time, Pallas kernels for 26%

profile of v3, /device:TPU:0, one launch (start us, length us, event | category | flops | bytes accessed | tf_op | source)
XLA Modules:
  0.0 266.3 jit_solution(7124208477038717524)
XLA Ops:
  3.2 3.1 %collective-permute-start.3 = (bf16[96,768]{1,0:T(8,128)(2,1)S(1)}, bf16[96,768]{1,0:T(8,128)(2,1)S(1)}, u32[]{:S(2)}, u32[]{:S(2)}) collective-permute-start(bf16[96,768]{1,0:T(8,128)(2,1)S(1)} %pad_maximum_fusion.2.rest_0_), channel_id=1, source_target_pairs={{0,8},{8,16},{16,24},{24,28},{28,20},{20,12},{12,4},{4,0},{1,9},{9... | collective-permute-start | bytes 442376 | tf_op jit(solution)/shard_map/ppermute | solution.py:486
  6.2 2.0 collective-permute-start.1
  8.3 1.7 collective-permute-done.3.rest_1_
  13.7 3.0 %collective-permute-done.5.rest_3_ = bf16[96,768]{1,0:T(8,128)(2,1)S(1)} collective-permute-done((bf16[96,768]{1,0:T(8,128)(2,1)S(1)}, bf16[96,768]{1,0:T(8,128)(2,1)S(1)}, u32[]{:S(2)}, u32[]{:S(2)}) %collective-permute-start.5) | collective-permute-done | bytes 147488 | tf_op jit(solution)/shard_map/ppermute | solution.py:486
  21.0 2.5 collective-permute-done.7.rest_5_
  27.2 3.6 %collective-permute-done.9.rest_7_ = bf16[96,768]{1,0:T(8,128)(2,1)S(1)} collective-permute-done((bf16[96,768]{1,0:T(8,128)(2,1)S(1)}, bf16[96,768]{1,0:T(8,128)(2,1)S(1)}, u32[]{:S(2)}, u32[]{:S(2)}) %collective-permute-start.9) | collective-permute-done | bytes 147488 | tf_op jit(solution)/shard_map/ppermute | solution.py:515
  43.2 13.6 %attend.1 = (bf16[3,3,512,512]{3,2,1,0:T(8,128)(2,1)}, bf16[3,3,512,512]{3,2,1,0:T(8,128)(2,1)}, bf16[3,3,192,512]{3,2,1,0:T(8,128)(2,1)}, bf16[3,192,256]{2,1,0...) custom-call(s32[5]{0:T(128)S(1)} %stack.32.me_ref.refs_0_, ...), custom_call_target="tpu_custom_call" | custom-call | flops 10 | bytes 1 | tf_op jit(solution)/shard_map/attend/pallas_call | solution.py:431
  58.9 7.2 %collective-permute-done.11.refs_3_ = bf16[3,192,256]{2,1,0:T(8,128)(2,1)S(1)} collective-permute-done((bf16[3,192,256]{2,1,0:T(8,128)(2,1)S(1)}, bf16[3,192,256]{2,1,0:T(8,128)(2,1)S(1)}, u32[]{:S(2)}, u32[]{:S(2)}) %collective-permute-start.11) | collective-permute-done | bytes 294944 | tf_op jit(solution)/shard_map/ppermute | solution.py:471
  67.6 1.6 collective-permute-start.12
  69.2 7.0 %collective-permute-done.12.refs_4_ = bf16[3,192,256]{2,1,0:T(8,128)(2,1)S(1)} collective-permute-done((bf16[3,192,256]{2,1,0:T(8,128)(2,1)S(1)}, bf16[3,192,256]{2,1,0:T(8,128)(2,1)S(1)}, u32[]{:S(2)}, u32[]{:S(2)}) %collective-permute-start.12) | collective-permute-done | bytes 294944 | tf_op jit(solution)/shard_map/ppermute | solution.py:471
  79.1 1.6 collective-permute-start.14
  80.7 9.7 %collective-permute-done.14.refs_7_ = bf16[768,192]{1,0:T(8,128)(2,1)S(1)} collective-permute-done((bf16[768,192]{1,0:T(8,128)(2,1)S(1)}, bf16[768,192]{1,0:T(8,128)(2,1)S(1)}, u32[]{:S(2)}, u32[]{:S(2)}) %collective-permute-start.14) | collective-permute-done | bytes 294944 | tf_op jit(solution)/shard_map/ppermute | solution.py:471
  91.1 2.0 pairs.1
  93.1 3.9 %up.3 = (f32[3,256,768]{2,1,0:T(8,128)S(1)}, f32[3,256,128]{2,1,0:T(8,128)S(1)}, bf16[3,256,768]{2,1,0:T(8,128)(2,1)S(1)}, bf16[3,256,768]{2,1,0:T(8,128)(2,1)S(...) custom-call(s32[5]{0:T(128)S(1)} %stack.32.me_ref.refs_0_, ...), custom_call_target="tpu_custom_call" | custom-call | flops 10 | bytes 1 | tf_op jit(solution)/shard_map/up/pallas_call | solution.py:431
  97.0 1.6 collective-permute-start.29
  98.6 3.8 %up.4 = (f32[3,256,768]{2,1,0:T(8,128)S(1)}, f32[3,256,128]{2,1,0:T(8,128)S(1)}, bf16[3,256,768]{2,1,0:T(8,128)(2,1)S(1)}, bf16[3,256,768]{2,1,0:T(8,128)(2,1)S(...) custom-call(s32[5]{0:T(128)S(1)} %stack.32.me_ref.refs_0_, ...), custom_call_target="tpu_custom_call", output_to_operand_aliasing={{0}: (17, {}), {1}: (18, {}), {2}: (19, {}), {3}: (20, {}),... | custom-call | flops 10 | bytes 1 | tf_op jit(solution)/shard_map/up/pallas_call | solution.py:431
  103.0 3.8 %up.5 = (f32[3,256,768]{2,1,0:T(8,128)S(1)}, f32[3,256,128]{2,1,0:T(8,128)S(1)}, bf16[3,256,768]{2,1,0:T(8,128)(2,1)S(1)}, bf16[3,256,768]{2,1,0:T(8,128)(2,1)S(...) custom-call(s32[5]{0:T(128)S(1)} %stack.32.me_ref.refs_0_, ...), custom_call_target="tpu_custom_call", output_to_operand_aliasing={{0}: (17, {}), {1}: (18, {}), {2}: (19, {}), {3}: (20, {}),... | custom-call | flops 10 | bytes 1 | tf_op jit(solution)/shard_map/up/pallas_call | solution.py:431
  106.9 1.6 collective-permute-start.28
  109.0 3.7 %down.3 = (bf16[3,192,256]{2,1,0:T(8,128)(2,1)S(1)}, bf16[3,192,256]{2,1,0:T(8,128)(2,1)S(1)}, f32[3,256,768]{2,1,0:T(8,128)S(1)}, bf16[3,256,768]{2,1,0:T(8,128...) custom-call(s32[5]{0:T(128)S(1)} %stack.32.me_ref.refs_0_, ...), custom_call_target="tpu_custom_call" | custom-call | flops 10 | bytes 1 | tf_op jit(solution)/shard_map/down/pallas_call | solution.py:431
  114.3 3.1 %collective-permute-done.31.refs_3_ = bf16[1,256,768]{2,1,0:T(8,128)(2,1)S(1)} collective-permute-done((bf16[1,256,768]{2,1,0:T(8,128)(2,1)S(1)}, bf16[1,256,768]{2,1,0:T(8,128)(2,1)S(1)}, u32[]{:S(2)}, u32[]{:S(2)}) %collective-permute-start.31) | collective-permute-done | bytes 393248 | tf_op jit(solution)/shard_map/ppermute | solution.py:471
  117.4 3.7 %down.4 = (bf16[3,192,256]{2,1,0:T(8,128)(2,1)S(1)}, bf16[3,192,256]{2,1,0:T(8,128)(2,1)S(1)}, f32[3,256,768]{2,1,0:T(8,128)S(1)}, bf16[3,256,768]{2,1,0:T(8,128...) custom-call(s32[5]{0:T(128)S(1)} %stack.32.me_ref.refs_0_, ...), custom_call_target="tpu_custom_call", output_to_operand_aliasing={{0}: (15, {}), {1}: (16, {}), {2}: (17, {}), {3}: (18, {}),... | custom-call | flops 10 | bytes 1 | tf_op jit(solution)/shard_map/down/pallas_call | solution.py:431
  121.1 4.7 %collective-permute-done.28.refs_3_ = bf16[1,256,768]{2,1,0:T(8,128)(2,1)S(1)} collective-permute-done((bf16[1,256,768]{2,1,0:T(8,128)(2,1)S(1)}, bf16[1,256,768]{2,1,0:T(8,128)(2,1)S(1)}, u32[]{:S(2)}, u32[]{:S(2)}) %collective-permute-start.28) | collective-permute-done | bytes 393248 | tf_op jit(solution)/shard_map/ppermute | solution.py:471
  125.9 8.0 %collective-permute-done.30.refs_3_ = bf16[1,256,768]{2,1,0:T(8,128)(2,1)S(1)} collective-permute-done((bf16[1,256,768]{2,1,0:T(8,128)(2,1)S(1)}, bf16[1,256,768]{2,1,0:T(8,128)(2,1)S(1)}, u32[]{:S(2)}, u32[]{:S(2)}) %collective-permute-start.30) | collective-permute-done | bytes 393248 | tf_op jit(solution)/shard_map/ppermute | solution.py:471
  133.9 3.9 %down.5 = (bf16[3,192,256]{2,1,0:T(8,128)(2,1)S(1)}, bf16[3,192,256]{2,1,0:T(8,128)(2,1)S(1)}, f32[3,256,768]{2,1,0:T(8,128)S(1)}, bf16[3,256,768]{2,1,0:T(8,128...) custom-call(s32[5]{0:T(128)S(1)} %stack.32.me_ref.refs_0_, ...), custom_call_target="tpu_custom_call", output_to_operand_aliasing={{0}: (15, {}), {1}: (16, {}), {2}: (17, {}), {3}: (18, {}),... | custom-call | flops 10 | bytes 1 | tf_op jit(solution)/shard_map/down/pallas_call | solution.py:431
  139.9 1.6 mid.3
  141.6 3.5 %ffn_grad.3 = (bf16[384,768]{1,0:T(8,128)(2,1)S(1)}, bf16[384,768]{1,0:T(8,128)(2,1)S(1)}) custom-call(s32[5]{0:T(128)S(1)} %stack.32.me_ref.refs_0_, bf16[3,256,768]{2,1,0:T(8,128)(2,1)S(1)} %get-tuple-element.235.rest_0_, bf16[3,256,768]{2,1,0:T(8,128)(2,1)S(1)} %collective-permute-done.37.rest_1_, bf16[3,256,768]{2,1,0:T(8,128)(2,1)S(1)} %get-tuple-element.236.rest_2_, ...), custom_call_target="tpu_custom_call" | custom-call | flops 30 | bytes 1 | tf_op jit(solution)/shard_map/ffn_grad/pallas_call | solution.py:431
  145.1 3.4 %ffn_grad.2 = (bf16[384,768]{1,0:T(8,128)(2,1)S(1)}, bf16[384,768]{1,0:T(8,128)(2,1)S(1)}) custom-call(s32[5]{0:T(128)S(1)} %stack.32.me_ref.refs_0_, bf16[3,256,768]{2,1,0:T(8,128)(2,1)S(1)} %get-tuple-element.231.rest_0_, bf16[3,256,768]{2,1,0:T(8,128)(2,1)S(1)} %collective-permute-done.35.rest_1_, bf16[3,256,768]{2,1,0:T(8,128)(2,1)S(1)} %get-tuple-element.233.rest_2_, ...), custom_call_target="tpu_custom_call" | custom-call | flops 30 | bytes 1 | tf_op jit(solution)/shard_map/ffn_grad/pallas_call | solution.py:431
  149.9 1.6 mid.4
  156.3 5.5 %back.3 = (bf16[3,3,512,512]{3,2,1,0:T(8,128)(2,1)}, bf16[3,576,512]{2,1,0:T(8,128)(2,1)S(1)}, bf16[3,192,512]{2,1,0:T(8,128)(2,1)S(1)}, bf16[3,192,512]{2,1,0:T...) custom-call(s32[5]{0:T(128)S(1)} %stack.32.me_ref.refs_0_, ...), custom_call_target="tpu_custom_call" | custom-call | flops 10 | bytes 1 | tf_op jit(solution)/shard_map/back/pallas_call | solution.py:431
  161.8 5.5 %back.4 = (bf16[3,3,512,512]{3,2,1,0:T(8,128)(2,1)}, bf16[3,576,512]{2,1,0:T(8,128)(2,1)S(1)}, bf16[3,192,512]{2,1,0:T(8,128)(2,1)S(1)}, bf16[3,192,512]{2,1,0:T...) custom-call(s32[5]{0:T(128)S(1)} %stack.32.me_ref.refs_0_, ...), custom_call_target="tpu_custom_call", output_to_operand_aliasing={{0}: (7, {}), {1}: (8, {}), {2}: (9, {}), {3}: (10, {}), {4... | custom-call | flops 10 | bytes 1 | tf_op jit(solution)/shard_map/back/pallas_call | solution.py:431
  167.2 1.6 mid.5
  176.0 5.7 %back.5 = (bf16[3,3,512,512]{3,2,1,0:T(8,128)(2,1)}, bf16[3,576,512]{2,1,0:T(8,128)(2,1)S(1)}, bf16[3,192,512]{2,1,0:T(8,128)(2,1)S(1)}, bf16[3,192,512]{2,1,0:T...) custom-call(s32[5]{0:T(128)S(1)} %stack.32.me_ref.refs_0_, ...), custom_call_target="tpu_custom_call", output_to_operand_aliasing={{0}: (7, {}), {1}: (8, {}), {2}: (9, {}), {3}: (10, {}), {4... | custom-call | flops 10 | bytes 1 | tf_op jit(solution)/shard_map/back/pallas_call | solution.py:431
  181.7 2.7 %qkv_grad.1 = (bf16[400,768]{1,0:T(8,128)(2,1)S(1)}, bf16[400,768]{1,0:T(8,128)(2,1)S(1)}) custom-call(s32[5]{0:T(128)S(1)} %stack.32.me_ref.refs_0_, bf16[3,768,512]{2,1,0:T(8,128)(2,1)S(1)} %copy-done.2, bf16[3,576,512]{2,1,0:T(8,128)(2,1)S(1)} %get-tuple-element.283.rest_1_, bf16[3,192,256]{2,1,0:T(8,128)(2,1)S(1)} %get-tuple-element.171.refs_1_.rest_2_, ...), custom_call_target="tpu_custom_call" | custom-call | flops 40 | bytes 1 | tf_op jit(solution)/shard_map/qkv_grad/pallas_call | solution.py:431
  187.1 14.2 %collective-permute-done.62 = bf16[192,768]{1,0:T(8,128)(2,1)S(1)} collective-permute-done((bf16[192,768]{1,0:T(8,128)(2,1)S(1)}, bf16[192,768]{1,0:T(8,128)(2,1)S(1)}, u32[]{:S(2)}, u32[]{:S(2)}) %collective-permute-start.62) | collective-permute-done | bytes 294944 | tf_op jit(solution)/shard_map/ppermute | solution.py:474
  201.5 2.0 collective-permute-start.64
  204.4 5.8 %collective-permute-done.63.rest_1_ = bf16[192,768]{1,0:T(8,128)(2,1)S(1)} collective-permute-done((bf16[192,768]{1,0:T(8,128)(2,1)S(1)}, bf16[192,768]{1,0:T(8,128)(2,1)S(1)}, u32[]{:S(2)}, u32[]{:S(2)}) %collective-permute-start.63) | collective-permute-done | bytes 294944 | tf_op jit(solution)/shard_map/ppermute | solution.py:486
  213.3 3.8 %collective-permute-done.51.rest_1_ = bf16[208,768]{1,0:T(8,128)(2,1)S(1)} collective-permute-done((bf16[208,768]{1,0:T(8,128)(2,1)S(1)}, bf16[208,768]{1,0:T(8,128)(2,1)S(1)}, u32[]{:S(2)}, u32[]{:S(2)}) %collective-permute-start.51) | collective-permute-done | bytes 319520 | tf_op jit(solution)/shard_map/ppermute | solution.py:474
  219.2 9.1 %collective-permute-done.52.came = bf16[112,768]{1,0:T(8,128)(2,1)S(1)} collective-permute-done((bf16[112,768]{1,0:T(8,128)(2,1)}, bf16[112,768]{1,0:T(8,128)(2,1)S(1)}, u32[]{:S(2)}, u32[]{:S(2)}) %collective-permute-start.52) | collective-permute-done | bytes 172064 | tf_op jit(solution)/shard_map/ppermute | solution.py:474
  235.7 3.2 %collective-permute-done.66.rest_4_ = bf16[192,768]{1,0:T(8,128)(2,1)S(1)} collective-permute-done((bf16[192,768]{1,0:T(8,128)(2,1)S(1)}, bf16[192,768]{1,0:T(8,128)(2,1)S(1)}, u32[]{:S(2)}, u32[]{:S(2)}) %collective-permute-start.66) | collective-permute-done | bytes 294944 | tf_op jit(solution)/shard_map/ppermute | solution.py:486
  238.9 2.0 collective-permute-done.54.rest_2_
  240.9 2.0 collective-permute-start.56
  242.9 2.3 fusion
  245.5 3.6 %collective-permute-done.55.rest_3_ = bf16[96,768]{1,0:T(8,128)(2,1)S(1)} collective-permute-done((bf16[96,768]{1,0:T(8,128)(2,1)S(1)}, bf16[96,768]{1,0:T(8,128)(2,1)S(1)}, u32[]{:S(2)}, u32[]{:S(2)}) %collective-permute-start.55) | collective-permute-done | bytes 147488 | tf_op jit(solution)/shard_map/ppermute | solution.py:486
  250.4 2.1 collective-permute-start.58
  252.5 3.4 %collective-permute-done.57.rest_5_ = bf16[96,768]{1,0:T(8,128)(2,1)S(1)} collective-permute-done((bf16[96,768]{1,0:T(8,128)(2,1)S(1)}, bf16[96,768]{1,0:T(8,128)(2,1)S(1)}, u32[]{:S(2)}, u32[]{:S(2)}) %collective-permute-start.57) | collective-permute-done | bytes 147488 | tf_op jit(solution)/shard_map/ppermute | solution.py:486
  257.8 2.1 collective-permute-done.69.rest_7_
  259.9 3.1 %finish.3 = (f32[768,768]{1,0:T(8,128)}, f32[768,768]{1,0:T(8,128)}) custom-call(s32[5]{0:T(128)S(1)} %stack.32.me_ref.refs_0_, bf16[192,768]{1,0:T(8,128)(2,1)S(1)} %add_convert_fusion.2.rest_0_, bf16[192,768]{1,0:T(8,128)(2,1)S(1)} %collective-permute-done.63.rest_1_, bf16[192,768]{1,0:T(8,128)(2,1)S(1)} %collective-permute-done.64.rest_2_, ...), custom_call_target="tpu_custom_call" | custom-call | flops 20 | bytes 1 | tf_op jit(solution)/shard_map/finish/pallas_call | solution.py:431
  263.0 3.3 %finish.2 = (f32[576,768]{1,0:T(8,128)}, f32[192,768]{1,0:T(8,128)}) custom-call(s32[5]{0:T(128)S(1)} %stack.32.me_ref.refs_0_, bf16[96,768]{1,0:T(8,128)(2,1)S(1)} %copy-done.12, bf16[96,768]{1,0:T(8,128)(2,1)S(1)} %copy-done.14, bf16[96,768]{1,0:T(8,128)(2,1)S(1)} %copy-done.16, bf16[96,768]{1,0:T(8,128)(2,1)S(1)} %copy-done.18, ...), custom_call_target="tpu_custom_call" | custom-call | flops 20 | bytes 1 | tf_op jit(solution)/shard_map/finish/pallas_call | solution.py:431
  (225 shorter events, 71.7 us)
Async XLA Ops:
  6.2 20.9 %collective-permute-start.1 = (bf16[3,192,512]{2,1,0:T(8,128)(2,1)S(1)}, bf16[3,192,512]{2,1,0:T(8,128)(2,1)S(1)}, u32[]{:S(2)}, u32[]{:S(2)}) collective-permute-start(bf16[3,192,512]{2,1,0:T(8,128)(2,1)S(1)} %bitcast.22), channel_id=1, source_target_pairs={{0,2},{1,3},{2,0},{3,1},{4,6},{5,7},{6,4},{7,5},{8,10},{9,11},{10,... | collective-permute-start | bytes 1769480 | tf_op jit(solution)/shard_map/ppermute | solution.py:471
  13.6 13.5 %collective-permute-start.16 = (bf16[96,1536]{1,0:T(8,128)(2,1)S(1)}, bf16[96,1536]{1,0:T(8,128)(2,1)S(1)}, u32[]{:S(2)}, u32[]{:S(2)}) collective-permute-start(bf16[96,1536]{1,0:T(8,128)(2,1)S(1)} %pad_maximum_fusion.1), channel_id=1, source_target_pairs={{0,1},{1,0},{2,3},{3,2},{4,5},{5,4},{6,7},{7,6},{8,9},{9,8},{10,11... | collective-permute-start | bytes 884744 | tf_op jit(solution)/shard_map/ppermute | solution.py:471
  21.0 14.3 %collective-permute-start = (bf16[3,192,512]{2,1,0:T(8,128)(2,1)S(1)}, bf16[3,192,512]{2,1,0:T(8,128)(2,1)}, u32[]{:S(2)}, u32[]{:S(2)}) collective-permute-start(bf16[3,192,512]{2,1,0:T(8,128)(2,1)S(1)} %bitcast.23), channel_id=1, source_target_pairs={{0,1},{1,0},{2,3},{3,2},{4,5},{5,4},{6,7},{7,6},{8,9},{9,8},{10,11... | collective-permute-start | bytes 1769480 | tf_op jit(solution)/shard_map/ppermute | solution.py:471
  27.1 8.8 %collective-permute-start.2 = (bf16[3,192,512]{2,1,0:T(8,128)(2,1)S(1)}, bf16[3,192,512]{2,1,0:T(8,128)(2,1)}, u32[]{:S(2)}, u32[]{:S(2)}) collective-permute-start(bf16[3,192,512]{2,1,0:T(8,128)(2,1)S(1)} %collective-permute-done.1.x2), channel_id=1, source_target_pairs={{0,1},{1,0},{2,3},{3,2},{4,5},{5,4},{6,7},{7,6},{8,9},{9,8},{10,11... | collective-permute-start | bytes 1769480 | tf_op jit(solution)/shard_map/ppermute | solution.py:471
  31.5 25.4 %collective-permute-start.17 = (bf16[192,1536]{1,0:T(8,128)(2,1)S(1)}, bf16[192,1536]{1,0:T(8,128)(2,1)S(1)}, u32[]{:S(2)}, u32[]{:S(2)}) collective-permute-start(bf16[192,1536]{1,0:T(8,128)(2,1)S(1)} %pad_maximum_fusion.rest_0_), channel_id=1, source_target_pairs={{0,8},{9,1},{2,10},{11,3},{8,16},{17,9},{10,18},{19,11},{16,24},{2... | collective-permute-start | bytes 1769480 | tf_op jit(solution)/shard_map/ppermute | solution.py:501
  33.7 23.1 %collective-permute-start.19 = (bf16[3,192,256]{2,1,0:T(8,128)(2,1)S(1)}, bf16[3,192,256]{2,1,0:T(8,128)(2,1)S(1)}, u32[]{:S(2)}, u32[]{:S(2)}) collective-permute-start(bf16[3,192,256]{2,1,0:T(8,128)(2,1)S(1)} %get-tuple-element.321.refs_4_), channel_id=1, source_target_pairs={{0,2},{1,3},{2,0},{3,1},{4,6},{5,7},{6,4},{7,5},{8,10},{9,11},{10,... | collective-permute-start | bytes 884744 | tf_op jit(solution)/shard_map/ppermute | solution.py:471
  35.2 21.6 %collective-permute-start.18 = (bf16[3,192,256]{2,1,0:T(8,128)(2,1)}, bf16[3,192,256]{2,1,0:T(8,128)(2,1)S(1)}, u32[]{:S(2)}, u32[]{:S(2)}) collective-permute-start(bf16[3,192,256]{2,1,0:T(8,128)(2,1)} %get-tuple-element.322), channel_id=1, source_target_pairs={{0,1},{1,0},{2,3},{3,2},{4,5},{5,4},{6,7},{7,6},{8,9},{9,8},{10,11... | collective-permute-start | bytes 884744 | tf_op jit(solution)/shard_map/ppermute | solution.py:471
  35.2 21.6 %collective-permute-start.20 = (bf16[3,192,256]{2,1,0:T(8,128)(2,1)}, bf16[3,192,256]{2,1,0:T(8,128)(2,1)S(1)}, u32[]{:S(2)}, u32[]{:S(2)}) collective-permute-start(bf16[3,192,256]{2,1,0:T(8,128)(2,1)} %get-tuple-element.322), channel_id=1, source_target_pairs={{0,3},{1,2},{2,1},{3,0},{4,7},{5,6},{6,5},{7,4},{8,11},{9,10},{10,... | collective-permute-start | bytes 884744 | tf_op jit(solution)/shard_map/ppermute | solution.py:471
  56.8 9.9 %collective-permute-start.21 = (bf16[192,1536]{1,0:T(8,128)(2,1)S(1)}, bf16[192,1536]{1,0:T(8,128)(2,1)S(1)}, u32[]{:S(2)}, u32[]{:S(2)}) collective-permute-start(bf16[192,1536]{1,0:T(8,128)(2,1)S(1)} %collective-permute-done.17.rest_1_), channel_id=1, source_target_pairs={{0,8},{9,1},{2,10},{11,3},{8,16},{17,9},{10,18},{19,11},{16,24},{2... | collective-permute-start | bytes 1769480 | tf_op jit(solution)/shard_map/ppermute | solution.py:501
  57.3 8.7 %collective-permute-start.11 = (bf16[3,192,256]{2,1,0:T(8,128)(2,1)S(1)}, bf16[3,192,256]{2,1,0:T(8,128)(2,1)S(1)}, u32[]{:S(2)}, u32[]{:S(2)}) collective-permute-start(bf16[3,192,256]{2,1,0:T(8,128)(2,1)S(1)} %get-tuple-element.171.refs_1_.rest_2_), channel_id=1, source_target_pairs={{0,2},{1,3},{2,0},{3,1},{4,6},{5,7},{6,4},{7,5},{8,10},{9,11},{10,... | collective-permute-start | bytes 884744 | tf_op jit(solution)/shard_map/ppermute | solution.py:471
  66.8 9.9 %collective-permute-start.22 = (bf16[192,1536]{1,0:T(8,128)(2,1)S(1)}, bf16[192,1536]{1,0:T(8,128)(2,1)S(1)}, u32[]{:S(2)}, u32[]{:S(2)}) collective-permute-start(bf16[192,1536]{1,0:T(8,128)(2,1)S(1)} %collective-permute-done.21.rest_2_), channel_id=1, source_target_pairs={{0,8},{9,1},{2,10},{11,3},{8,16},{17,9},{10,18},{19,11},{16,24},{2... | collective-permute-start | bytes 1769480 | tf_op jit(solution)/shard_map/ppermute | solution.py:501
  67.6 8.7 %collective-permute-start.12 = (bf16[3,192,256]{2,1,0:T(8,128)(2,1)S(1)}, bf16[3,192,256]{2,1,0:T(8,128)(2,1)S(1)}, u32[]{:S(2)}, u32[]{:S(2)}) collective-permute-start(bf16[3,192,256]{2,1,0:T(8,128)(2,1)S(1)} %get-tuple-element.172.rest_4_), channel_id=1, source_target_pairs={{0,3},{1,2},{2,1},{3,0},{4,7},{5,6},{6,5},{7,4},{8,11},{9,10},{10,... | collective-permute-start | bytes 884744 | tf_op jit(solution)/shard_map/ppermute | solution.py:471
  69.2 21.2 %collective-permute-start.24 = (bf16[192,1536]{1,0:T(8,128)(2,1)S(1)}, bf16[192,1536]{1,0:T(8,128)(2,1)S(1)}, u32[]{:S(2)}, u32[]{:S(2)}) collective-permute-start(bf16[192,1536]{1,0:T(8,128)(2,1)S(1)} %collective-permute-done.17.rest_1_), channel_id=1, source_target_pairs={{0,1},{1,0},{2,3},{3,2},{4,5},{5,4},{6,7},{7,6},{8,9},{9,8},{10,11... | collective-permute-start | bytes 1769480 | tf_op jit(solution)/shard_map/ppermute | solution.py:471
  76.7 14.3 %collective-permute-start.23 = (bf16[192,1536]{1,0:T(8,128)(2,1)S(1)}, bf16[192,1536]{1,0:T(8,128)(2,1)S(1)}, u32[]{:S(2)}, u32[]{:S(2)}) collective-permute-start(bf16[192,1536]{1,0:T(8,128)(2,1)S(1)} %collective-permute-done.22.rest_3_), channel_id=1, source_target_pairs={{0,8},{9,1},{2,10},{11,3},{8,16},{17,9},{10,18},{19,11},{16,24},{2... | collective-permute-start | bytes 1769480 | tf_op jit(solution)/shard_map/ppermute | solution.py:501
  77.5 13.6 %collective-permute-start.25 = (bf16[192,1536]{1,0:T(8,128)(2,1)S(1)}, bf16[192,1536]{1,0:T(8,128)(2,1)S(1)}, u32[]{:S(2)}, u32[]{:S(2)}) collective-permute-start(bf16[192,1536]{1,0:T(8,128)(2,1)S(1)} %collective-permute-done.21.rest_2_), channel_id=1, source_target_pairs={{0,1},{1,0},{2,3},{3,2},{4,5},{5,4},{6,7},{7,6},{8,9},{9,8},{10,11... | collective-permute-start | bytes 1769480 | tf_op jit(solution)/shard_map/ppermute | solution.py:471
  77.7 13.4 %collective-permute-start.26 = (bf16[192,1536]{1,0:T(8,128)(2,1)S(1)}, bf16[192,1536]{1,0:T(8,128)(2,1)S(1)}, u32[]{:S(2)}, u32[]{:S(2)}) collective-permute-start(bf16[192,1536]{1,0:T(8,128)(2,1)S(1)} %collective-permute-done.22.rest_3_), channel_id=1, source_target_pairs={{0,1},{1,0},{2,3},{3,2},{4,5},{5,4},{6,7},{7,6},{8,9},{9,8},{10,11... | collective-permute-start | bytes 1769480 | tf_op jit(solution)/shard_map/ppermute | solution.py:471
  79.1 11.3 %collective-permute-start.14 = (bf16[768,192]{1,0:T(8,128)(2,1)S(1)}, bf16[768,192]{1,0:T(8,128)(2,1)S(1)}, u32[]{:S(2)}, u32[]{:S(2)}) collective-permute-start(bf16[768,192]{1,0:T(8,128)(2,1)S(1)} %slice.27.refs_5_.refs_7_), channel_id=1, source_target_pairs={{0,2},{1,3},{2,0},{3,1},{4,6},{5,7},{6,4},{7,5},{8,10},{9,11},{10,... | collective-permute-start | bytes 884744 | tf_op jit(solution)/shard_map/ppermute | solution.py:471
  97.0 12.0 %collective-permute-start.29 = (bf16[1,256,768]{2,1,0:T(8,128)(2,1)S(1)}, bf16[1,256,768]{2,1,0:T(8,128)(2,1)S(1)}, u32[]{:S(2)}, u32[]{:S(2)}) collective-permute-start(bf16[1,256,768]{2,1,0:T(8,128)(2,1)S(1)} %get-tuple-element.199.refs_2_), channel_id=1, source_target_pairs={{0,2},{1,3},{2,0},{3,1},{4,6},{5,7},{6,4},{7,5},{8,10},{9,11},{10,... | collective-permute-start | bytes 1179656 | tf_op jit(solution)/shard_map/ppermute | solution.py:471
  102.5 15.0 %collective-permute-start.31 = (bf16[1,256,768]{2,1,0:T(8,128)(2,1)S(1)}, bf16[1,256,768]{2,1,0:T(8,128)(2,1)S(1)}, u32[]{:S(2)}, u32[]{:S(2)}) collective-permute-start(bf16[1,256,768]{2,1,0:T(8,128)(2,1)S(1)} %get-tuple-element.204.refs_2_), channel_id=1, source_target_pairs={{0,2},{1,3},{2,0},{3,1},{4,6},{5,7},{6,4},{7,5},{8,10},{9,11},{10,... | collective-permute-start | bytes 1179656 | tf_op jit(solution)/shard_map/ppermute | solution.py:471
  106.9 19.0 %collective-permute-start.28 = (bf16[1,256,768]{2,1,0:T(8,128)(2,1)S(1)}, bf16[1,256,768]{2,1,0:T(8,128)(2,1)S(1)}, u32[]{:S(2)}, u32[]{:S(2)}) collective-permute-start(bf16[1,256,768]{2,1,0:T(8,128)(2,1)S(1)} %get-tuple-element.198.refs_2_), channel_id=1, source_target_pairs={{0,2},{1,3},{2,0},{3,1},{4,6},{5,7},{6,4},{7,5},{8,10},{9,11},{10,... | collective-permute-start | bytes 1179656 | tf_op jit(solution)/shard_map/ppermute | solution.py:471
  112.7 21.2 %collective-permute-start.30 = (bf16[1,256,768]{2,1,0:T(8,128)(2,1)S(1)}, bf16[1,256,768]{2,1,0:T(8,128)(2,1)S(1)}, u32[]{:S(2)}, u32[]{:S(2)}) collective-permute-start(bf16[1,256,768]{2,1,0:T(8,128)(2,1)S(1)} %get-tuple-element.202.refs_2_), channel_id=1, source_target_pairs={{0,2},{1,3},{2,0},{3,1},{4,6},{5,7},{6,4},{7,5},{8,10},{9,11},{10,... | collective-permute-start | bytes 1179656 | tf_op jit(solution)/shard_map/ppermute | solution.py:471
  114.3 27.3 %collective-permute-start.37 = (bf16[3,256,768]{2,1,0:T(8,128)(2,1)S(1)}, bf16[3,256,768]{2,1,0:T(8,128)(2,1)S(1)}, u32[]{:S(2)}, u32[]{:S(2)}) collective-permute-start(bf16[3,256,768]{2,1,0:T(8,128)(2,1)S(1)} %get-tuple-element.235.rest_0_), channel_id=1, source_target_pairs={{0,1},{1,0},{2,3},{3,2},{4,5},{5,4},{6,7},{7,6},{8,9},{9,8},{10,11... | collective-permute-start | bytes 3538952 | tf_op jit(solution)/shard_map/ppermute | solution.py:471
  138.4 11.5 %collective-permute-start.34 = (bf16[1,256,768]{2,1,0:T(8,128)(2,1)S(1)}, bf16[1,256,768]{2,1,0:T(8,128)(2,1)S(1)}, u32[]{:S(2)}, u32[]{:S(2)}) collective-permute-start(bf16[1,256,768]{2,1,0:T(8,128)(2,1)S(1)} %get-tuple-element.230.refs_2_), channel_id=1, source_target_pairs={{0,2},{1,3},{2,0},{3,1},{4,6},{5,7},{6,4},{7,5},{8,10},{9,11},{10,... | collective-permute-start | bytes 1179656 | tf_op jit(solution)/shard_map/ppermute | solution.py:471
  151.5 15.7 %collective-permute-start.42 = (bf16[384,768]{1,0:T(8,128)(2,1)S(1)}, bf16[384,768]{1,0:T(8,128)(2,1)S(1)}, u32[]{:S(2)}, u32[]{:S(2)}) collective-permute-start(bf16[384,768]{1,0:T(8,128)(2,1)S(1)} %get-tuple-element.260), channel_id=1, source_target_pairs={{0,8},{4,12},{8,0},{12,4},{16,24},{20,28},{24,16},{28,20},{1,9},{5... | collective-permute-start | bytes 1769480 | tf_op jit(solution)/shard_map/ppermute | solution.py:474
  152.4 14.8 %collective-permute-start.41 = (bf16[384,768]{1,0:T(8,128)(2,1)S(1)}, bf16[384,768]{1,0:T(8,128)(2,1)S(1)}, u32[]{:S(2)}, u32[]{:S(2)}) collective-permute-start(bf16[384,768]{1,0:T(8,128)(2,1)S(1)} %get-tuple-element.258), channel_id=1, source_target_pairs={{0,4},{4,0},{8,12},{12,8},{16,20},{20,16},{24,28},{28,24},{1,5},{5... | collective-permute-start | bytes 1769480 | tf_op jit(solution)/shard_map/ppermute | solution.py:474
  153.4 13.8 %collective-permute-start.33 = (bf16[1,256,768]{2,1,0:T(8,128)(2,1)S(1)}, bf16[1,256,768]{2,1,0:T(8,128)(2,1)S(1)}, u32[]{:S(2)}, u32[]{:S(2)}) collective-permute-start(bf16[1,256,768]{2,1,0:T(8,128)(2,1)S(1)} %get-tuple-element.229.refs_2_), channel_id=1, source_target_pairs={{0,2},{1,3},{2,0},{3,1},{4,6},{5,7},{6,4},{7,5},{8,10},{9,11},{10,... | collective-permute-start | bytes 1179656 | tf_op jit(solution)/shard_map/ppermute | solution.py:471
  168.9 12.8 %collective-permute-start.47 = (bf16[3,256,768]{2,1,0:T(8,128)(2,1)S(1)}, bf16[3,256,768]{2,1,0:T(8,128)(2,1)S(1)}, u32[]{:S(2)}, u32[]{:S(2)}) collective-permute-start(bf16[3,256,768]{2,1,0:T(8,128)(2,1)S(1)} %get-tuple-element.284.rest_3_), channel_id=1, source_target_pairs={{0,1},{1,0},{2,3},{3,2},{4,5},{5,4},{6,7},{7,6},{8,9},{9,8},{10,11... | collective-permute-start | bytes 3538952 | tf_op jit(solution)/shard_map/ppermute | solution.py:471
  169.7 14.6 %collective-permute-start.60 = (bf16[192,768]{1,0:T(8,128)(2,1)S(1)}, bf16[192,768]{1,0:T(8,128)(2,1)S(1)}, u32[]{:S(2)}, u32[]{:S(2)}) collective-permute-start(bf16[192,768]{1,0:T(8,128)(2,1)S(1)} %get-tuple-element.307), channel_id=1, source_target_pairs={{0,8},{4,12},{8,0},{12,4},{16,24},{20,28},{24,16},{28,20},{1,9},{5... | collective-permute-start | bytes 884744 | tf_op jit(solution)/shard_map/ppermute | solution.py:474
  171.7 12.7 %collective-permute-start.61 = (bf16[192,768]{1,0:T(8,128)(2,1)S(1)}, bf16[192,768]{1,0:T(8,128)(2,1)S(1)}, u32[]{:S(2)}, u32[]{:S(2)}) collective-permute-start(bf16[192,768]{1,0:T(8,128)(2,1)S(1)} %get-tuple-element.309), channel_id=1, source_target_pairs={{0,4},{4,0},{8,12},{12,8},{16,20},{20,16},{24,28},{28,24},{1,5},{5... | collective-permute-start | bytes 884744 | tf_op jit(solution)/shard_map/ppermute | solution.py:474
  185.1 16.3 %collective-permute-start.62 = (bf16[192,768]{1,0:T(8,128)(2,1)S(1)}, bf16[192,768]{1,0:T(8,128)(2,1)S(1)}, u32[]{:S(2)}, u32[]{:S(2)}) collective-permute-start(bf16[192,768]{1,0:T(8,128)(2,1)S(1)} %get-tuple-element.311), channel_id=1, source_target_pairs={{0,16},{4,20},{8,24},{12,28},{16,0},{20,4},{24,8},{28,12},{1,17},{... | collective-permute-start | bytes 884744 | tf_op jit(solution)/shard_map/ppermute | solution.py:474
  185.9 17.6 %collective-permute-start.50 = (bf16[400,768]{1,0:T(8,128)(2,1)S(1)}, bf16[400,768]{1,0:T(8,128)(2,1)S(1)}, u32[]{:S(2)}, u32[]{:S(2)}) collective-permute-start(bf16[400,768]{1,0:T(8,128)(2,1)S(1)} %get-tuple-element.294), channel_id=1, source_target_pairs={{0,4},{4,0},{8,12},{12,8},{16,20},{20,16},{24,28},{28,24},{1,5},{5... | collective-permute-start | bytes 1843208 | tf_op jit(solution)/shard_map/ppermute | solution.py:474
  187.1 24.3 %collective-permute-start.45 = (bf16[3,192,512]{2,1,0:T(8,128)(2,1)S(1)}, bf16[3,192,512]{2,1,0:T(8,128)(2,1)S(1)}, u32[]{:S(2)}, u32[]{:S(2)}) collective-permute-start(bf16[3,192,512]{2,1,0:T(8,128)(2,1)S(1)} %get-tuple-element.280), channel_id=1, source_target_pairs={{0,1},{1,0},{2,3},{3,2},{4,5},{5,4},{6,7},{7,6},{8,9},{9,8},{10,11... | collective-permute-start | bytes 1769480 | tf_op jit(solution)/shard_map/ppermute | solution.py:471
  201.4 8.7 %collective-permute-start.63 = (bf16[192,768]{1,0:T(8,128)(2,1)S(1)}, bf16[192,768]{1,0:T(8,128)(2,1)S(1)}, u32[]{:S(2)}, u32[]{:S(2)}) collective-permute-start(bf16[192,768]{1,0:T(8,128)(2,1)S(1)} %add_convert_fusion.2.rest_0_), channel_id=1, source_target_pairs={{0,8},{8,16},{16,24},{24,28},{28,20},{20,12},{12,4},{4,0},{1,9},{9... | collective-permute-start | bytes 884744 | tf_op jit(solution)/shard_map/ppermute | solution.py:486
  201.5 10.0 %collective-permute-start.64 = (bf16[192,768]{1,0:T(8,128)(2,1)S(1)}, bf16[192,768]{1,0:T(8,128)(2,1)S(1)}, u32[]{:S(2)}, u32[]{:S(2)}) collective-permute-start(bf16[192,768]{1,0:T(8,128)(2,1)S(1)} %add_convert_fusion.2.rest_0_), channel_id=1, source_target_pairs={{8,0},{16,8},{24,16},{28,24},{20,28},{12,20},{4,12},{0,4},{9,1},{1... | collective-permute-start | bytes 884744 | tf_op jit(solution)/shard_map/ppermute | solution.py:486
  204.2 12.9 %collective-permute-start.51 = (bf16[208,768]{1,0:T(8,128)(2,1)S(1)}, bf16[208,768]{1,0:T(8,128)(2,1)S(1)}, u32[]{:S(2)}, u32[]{:S(2)}) collective-permute-start(bf16[208,768]{1,0:T(8,128)(2,1)S(1)} %get-tuple-element.296), channel_id=1, source_target_pairs={{0,8},{4,12},{8,0},{12,4},{16,24},{20,28},{24,16},{28,20},{1,9},{5... | collective-permute-start | bytes 958472 | tf_op jit(solution)/shard_map/ppermute | solution.py:474
  204.4 27.4 %collective-permute-start.32 = (bf16[3,192,256]{2,1,0:T(8,128)(2,1)S(1)}, bf16[3,192,256]{2,1,0:T(8,128)(2,1)}, u32[]{:S(2)}, u32[]{:S(2)}) collective-permute-start(bf16[3,192,256]{2,1,0:T(8,128)(2,1)S(1)} %get-tuple-element.224), channel_id=1, source_target_pairs={{0,1},{1,0},{2,3},{3,2},{4,5},{5,4},{6,7},{7,6},{8,9},{9,8},{10,11... | collective-permute-start | bytes 884744 | tf_op jit(solution)/shard_map/ppermute | solution.py:471
  210.2 32.7 %collective-permute-start.44 = (bf16[3,192,512]{2,1,0:T(8,128)(2,1)S(1)}, bf16[3,192,512]{2,1,0:T(8,128)(2,1)}, u32[]{:S(2)}, u32[]{:S(2)}) collective-permute-start(bf16[3,192,512]{2,1,0:T(8,128)(2,1)S(1)} %get-tuple-element.278), channel_id=1, source_target_pairs={{0,1},{1,0},{2,3},{3,2},{4,5},{5,4},{6,7},{7,6},{8,9},{9,8},{10,11... | collective-permute-start | bytes 1769480 | tf_op jit(solution)/shard_map/ppermute | solution.py:471
  211.5 21.1 %collective-permute-start.65 = (bf16[192,768]{1,0:T(8,128)(2,1)S(1)}, bf16[192,768]{1,0:T(8,128)(2,1)S(1)}, u32[]{:S(2)}, u32[]{:S(2)}) collective-permute-start(bf16[192,768]{1,0:T(8,128)(2,1)S(1)} %collective-permute-done.63.rest_1_), channel_id=1, source_target_pairs={{0,8},{8,16},{16,24},{24,28},{28,20},{20,12},{12,4},{4,0},{1,9},{9... | collective-permute-start | bytes 884744 | tf_op jit(solution)/shard_map/ppermute | solution.py:486
  212.4 30.5 %collective-permute-start.46 = (bf16[3,192,512]{2,1,0:T(8,128)(2,1)}, bf16[3,192,512]{2,1,0:T(8,128)(2,1)}, u32[]{:S(2)}, u32[]{:S(2)}) collective-permute-start(bf16[3,192,512]{2,1,0:T(8,128)(2,1)} %add_convert_fusion.1), channel_id=1, source_target_pairs={{0,2},{1,3},{2,0},{3,1},{4,6},{5,7},{6,4},{7,5},{8,10},{9,11},{10,... | collective-permute-start | bytes 1769480 | tf_op jit(solution)/shard_map/ppermute | solution.py:471
  218.3 9.9 %collective-permute-start.52 = (bf16[112,768]{1,0:T(8,128)(2,1)}, bf16[112,768]{1,0:T(8,128)(2,1)S(1)}, u32[]{:S(2)}, u32[]{:S(2)}) collective-permute-start(bf16[112,768]{1,0:T(8,128)(2,1)} %get-tuple-element.298), channel_id=1, source_target_pairs={{0,16},{4,20},{8,24},{12,28},{16,0},{20,4},{24,8},{28,12},{1,17},{... | collective-permute-start | bytes 516104 | tf_op jit(solution)/shard_map/ppermute | solution.py:474
  229.0 9.9 %collective-permute-start.66 = (bf16[192,768]{1,0:T(8,128)(2,1)S(1)}, bf16[192,768]{1,0:T(8,128)(2,1)S(1)}, u32[]{:S(2)}, u32[]{:S(2)}) collective-permute-start(bf16[192,768]{1,0:T(8,128)(2,1)S(1)} %collective-permute-done.64.rest_2_), channel_id=1, source_target_pairs={{8,0},{16,8},{24,16},{28,24},{20,28},{12,20},{4,12},{0,4},{9,1},{1... | collective-permute-start | bytes 884744 | tf_op jit(solution)/shard_map/ppermute | solution.py:486
  232.6 8.3 %collective-permute-start.54 = (bf16[96,768]{1,0:T(8,128)(2,1)S(1)}, bf16[96,768]{1,0:T(8,128)(2,1)S(1)}, u32[]{:S(2)}, u32[]{:S(2)}) collective-permute-start(bf16[96,768]{1,0:T(8,128)(2,1)S(1)} %get-tuple-element.299.rest_0_), channel_id=1, source_target_pairs={{8,0},{16,8},{24,16},{28,24},{20,28},{12,20},{4,12},{0,4},{9,1},{1... | collective-permute-start | bytes 442376 | tf_op jit(solution)/shard_map/ppermute | solution.py:486
  238.8 11.5 %collective-permute-start.67 = (bf16[192,768]{1,0:T(8,128)(2,1)S(1)}, bf16[192,768]{1,0:T(8,128)(2,1)S(1)}, u32[]{:S(2)}, u32[]{:S(2)}) collective-permute-start(bf16[192,768]{1,0:T(8,128)(2,1)S(1)} %collective-permute-done.65.rest_3_), channel_id=1, source_target_pairs={{0,8},{8,16},{16,24},{24,28},{28,20},{20,12},{12,4},{4,0},{1,9},{9... | collective-permute-start | bytes 884744 | tf_op jit(solution)/shard_map/ppermute | solution.py:486
  240.9 8.2 %collective-permute-start.55 = (bf16[96,768]{1,0:T(8,128)(2,1)S(1)}, bf16[96,768]{1,0:T(8,128)(2,1)S(1)}, u32[]{:S(2)}, u32[]{:S(2)}) collective-permute-start(bf16[96,768]{1,0:T(8,128)(2,1)S(1)} %collective-permute-done.53.rest_1_), channel_id=1, source_target_pairs={{0,8},{8,16},{16,24},{24,28},{28,20},{20,12},{12,4},{4,0},{1,9},{9... | collective-permute-start | bytes 442376 | tf_op jit(solution)/shard_map/ppermute | solution.py:486
  240.9 8.2 %collective-permute-start.56 = (bf16[96,768]{1,0:T(8,128)(2,1)S(1)}, bf16[96,768]{1,0:T(8,128)(2,1)}, u32[]{:S(2)}, u32[]{:S(2)}) collective-permute-start(bf16[96,768]{1,0:T(8,128)(2,1)S(1)} %collective-permute-done.54.rest_2_), channel_id=1, source_target_pairs={{8,0},{16,8},{24,16},{28,24},{20,28},{12,20},{4,12},{0,4},{9,1},{1... | collective-permute-start | bytes 442376 | tf_op jit(solution)/shard_map/ppermute | solution.py:486
  245.2 12.5 %collective-permute-start.68 = (bf16[192,768]{1,0:T(8,128)(2,1)S(1)}, bf16[192,768]{1,0:T(8,128)(2,1)S(1)}, u32[]{:S(2)}, u32[]{:S(2)}) collective-permute-start(bf16[192,768]{1,0:T(8,128)(2,1)S(1)} %collective-permute-done.66.rest_4_), channel_id=1, source_target_pairs={{8,0},{16,8},{24,16},{28,24},{20,28},{12,20},{4,12},{0,4},{9,1},{1... | collective-permute-start | bytes 884744 | tf_op jit(solution)/shard_map/ppermute | solution.py:486
  250.4 9.5 %collective-permute-start.69 = (bf16[192,768]{1,0:T(8,128)(2,1)S(1)}, bf16[192,768]{1,0:T(8,128)(2,1)S(1)}, u32[]{:S(2)}, u32[]{:S(2)}) collective-permute-start(bf16[192,768]{1,0:T(8,128)(2,1)S(1)} %collective-permute-done.67.rest_5_), channel_id=1, source_target_pairs={{0,8},{8,16},{16,24},{24,28},{28,20},{20,12},{12,4},{4,0},{1,9},{9... | collective-permute-start | bytes 884744 | tf_op jit(solution)/shard_map/ppermute | solution.py:750
  250.4 7.4 %collective-permute-start.58 = (bf16[96,768]{1,0:T(8,128)(2,1)}, bf16[96,768]{1,0:T(8,128)(2,1)S(1)}, u32[]{:S(2)}, u32[]{:S(2)}) collective-permute-start(bf16[96,768]{1,0:T(8,128)(2,1)} %collective-permute-done.56.rest_4_), channel_id=1, source_target_pairs={{8,0},{16,8},{24,16},{28,24},{20,28},{12,20},{4,12},{0,4},{9,1},{1... | collective-permute-start | bytes 442376 | tf_op jit(solution)/shard_map/ppermute | solution.py:486
  (63 other events, 407.5 us)

commit v4 on v3

--- a/solution.py
+++ b/solution.py
@@ -73,8 +73,9 @@
         xt_ref[0, pl.ds(start, width), :] = piece[0]
     bias = jnp.transpose(jnp.broadcast_to(b_ref[0:1, :], (128, width)))[:, 0:1]
     bias_v = jnp.transpose(jnp.broadcast_to(b_ref[1:2, :], (128, width)))[:, 0:1]
-    packed = dot_tn(w_ref[:, : 3 * width], xt_ref[0])
-    qkv_ref[0, 0] = (packed[:width] + bias).astype(BF)
+    packed = dot_tn(w_ref[...], xt_ref[0])
+    scale = 1.0 / (size**0.5)
+    qkv_ref[0, 0] = ((packed[:width] + bias).astype(BF).astype(F32) * scale).astype(BF)
     qkv_ref[0, 1] = packed[width : 2 * width].astype(BF)
     qkv_ref[0, 2] = (packed[2 * width :] + bias_v).astype(BF)
     mine = pl.ds(pl.multiple_of(core * half, half), half)
@@ -82,13 +83,12 @@
     xh_ref[0] = jnp.transpose(xt_ref[0, :, mine])
     row = seg_ref[pl.ds(pl.program_id(0), 1), :].astype(F32)
     column = jnp.transpose(jnp.broadcast_to(row, (128, slots)))[:, 0:1]
-    scale = 1.0 / (size**0.5)
     for block in range(2):
         rows = slice(block * half, (block + 1) * half)
         allowed = column[rows] == row
         for h in range(heads):
             feats = slice(h * size, (h + 1) * size)
-            scores = dot_tn(qkv_ref[0, 0, feats, rows], qkv_ref[0, 1, feats, :]) * scale
+            scores = dot_tn(qkv_ref[0, 0, feats, rows], qkv_ref[0, 1, feats, :])
             scores = scores + prev_ref[0, h, rows, :].astype(F32)
             raw_ref[0, h, rows, :] = scores.astype(BF)
             masked = jnp.where(allowed, scores, NEG)
@@ -96,7 +96,8 @@
             prob = expanded * (1.0 / jnp.sum(expanded, axis=-1, keepdims=True))
             prob = prob.astype(BF)
             p_ref[0, h, rows, :] = prob
-            o_scr[feats, rows] = dot_nt(qkv_ref[0, 2, feats, :], prob).astype(BF)
+            heads_out = dot_nt(prob, qkv_ref[0, 2, feats, :])
+            o_scr[feats, rows] = jnp.transpose(heads_out).astype(BF)
     own_ref[0] = o_scr[:, mine]
     oth_ref[0] = o_scr[:, other]
 
@@ -223,8 +224,8 @@
             weighted = grad_prob * prob
             inner = jnp.sum(weighted, axis=-1, keepdims=True)
             lg_ref[0, h, rows, :] = (weighted - prob * inner).astype(BF)
-        grad_query = dot_nt(key, lg_ref[0, h]) * scale
-        grad_key = dot(query, lg_ref[0, h]) * scale
+        grad_query = jnp.transpose(dot_nt(lg_ref[0, h], key)) * scale
+        grad_key = dot(query, lg_ref[0, h])
         grad_value = dot(out_grad, p_ref[0, h])
         for number, grad in ((0, grad_query), (1, grad_value)):
             line = jnp.sum(grad, axis=1, keepdims=True)
@@ -237,7 +238,7 @@
     lax.fori_loop(0, heads, one_head, 0)
     for number in range(2):
         vec_ref[0, number : number + 1, :] = jnp.transpose(sum_scr[number])[0:1, :]
-    dx_scr[...] = dot(w_ref[:, : 3 * width], dqkv_ref[0])
+    dx_scr[...] = dot(w_ref[...], dqkv_ref[0])
     near = pl.ds(pl.multiple_of(chip * 2 * width, width), 2 * width)
     dx_scr[near, mine] = dx_scr[near, mine] + near_ref[0]
     for step, out in enumerate((e0, e1, e2, e3)):
@@ -353,30 +354,48 @@
     return jnp.where(there < count // 2, 2 * there, 2 * (count - 1 - there) + 1)
 
 
+def shard_kernel(me_ref, *rest):
+    out_ref = rest[-1]
+    low = 0
+    for block in rest[:-1]:
+        parts = [block[i] for i in range(block.shape[0])] if len(block.shape) == 3 else [block[...]]
+        for part in parts:
+            out_ref[:, low : low + part.shape[1]] = part.astype(BF)
+            low += part.shape[1]
+
+
+def stack_kernel(me_ref, first, second, out_ref):
+    rows = first.shape[0]
+    out_ref[:rows, :] = first[...]
+    out_ref[rows:, :] = second[...]
+
+
+def lanes_kernel(me_ref, whole_ref, mine_ref, other_ref):
+    core = lax.rem(me_ref[0], 2)
+    half = mine_ref.shape[2]
+    for out, place in ((mine_ref, core), (other_ref, 1 - core)):
+        lanes = pl.ds(pl.multiple_of(place * half, half), half)
+        for row in range(out.shape[0]):
+            out[row] = whole_ref[row, :, lanes]
+
+
 def pairs_kernel(me_ref, *rest):
-    count = len(rest) - 3
-    blocks, out_a, out_b, sems = rest[:count], rest[-3], rest[-2], rest[-1]
+    blocks, outs = rest[:-6], rest[-6:]
+    count = len(blocks)
     core = lax.rem(me_ref[0], 2)
     rows = blocks[0].shape[0] // 2
-    copies = []
     for number in range(count):
         steps = number if number <= count // 2 else number - count // 2
         ahead = core if number <= count // 2 else 1 - core
         back = jnp.where(ahead == 1, lax.rem(count - steps, count), steps)
         place = pl.ds(pl.multiple_of(group_at(me_ref, back, count) * rows, rows), rows)
-        first, second = (out_a, out_b) if number <= count // 2 else (out_b, out_a)
-        for part, out in enumerate((first, second)):
-            copies.append(
-                pltpu.make_async_copy(
-                    blocks[number].at[pl.ds(part * rows, rows), :],
-                    out.at[place, :],
-                    sems.at[number, part],
-                )
-            )
-    for copy in copies:
-        copy.start()
-    for copy in copies:
-        copy.wait()
+        first, second = (outs[:3], outs[3:]) if number <= count // 2 else (outs[3:], outs[:3])
+        for part, three in enumerate((first, second)):
+            low = 0
+            for out in three:
+                high = low + out.shape[1]
+                out[place, :] = blocks[number][part * rows : (part + 1) * rows, low:high]
+                low = high
 
 
 def small_kernel(me_ref, vec1, vec2, bup_a, bup_b, own_ref, oth_ref):
@@ -486,11 +505,10 @@
         return lax.ppermute(ahead, "dp", onward), lax.ppermute(behind, "dp", backward)
 
     def place_pairs(blocks):
-        outs = [sds((full, blocks[0].shape[1]), BF)] * 2
+        outs = [sds((full, wide), BF) for wide in (2 * units, width, width)] * 2
         return call(
-            pairs_kernel, (1,),
-            [(me_ref, None)] + [(b, held(b)) for b in blocks], outs, [held(o) for o in outs],
-            [pltpu.SemaphoreType.DMA((groups, 2))], "pairs", 2, None, 8,
+            pairs_kernel, (1,), [(me_ref, None)] + [(b, held(b)) for b in blocks], outs,
+            [held(o) for o in outs], [], "pairs", 2, None, 8,
         )
 
     both_ways = []
@@ -502,28 +520,48 @@
 
     tokens = jnp.swapaxes(tokens, 1, 2)
     cotangent = jnp.swapaxes(cotangent, 1, 2)
-    shard_in = w_qkv.astype(BF).reshape(w_qkv.shape[0], 3 * width)
-    x_y = pp(tokens, 2)
-    x_c = pp(tokens, 1)
-    shard_in = jnp.concatenate([shard_in, w_out.T.astype(BF)], 1)
-    shard_big = jnp.concatenate([w_up.astype(BF), w_down.T.astype(BF)], 1)
+    def joined(kernel, outs, *arrays):
+        ins = [(me_ref, None)] + [(a, whole(a)) for a in arrays]
+        return call(kernel, (1,), ins, outs, [whole(o) for o in outs], [], "joined", 1, None, 8)
+
+    shard_out = w_out.T.astype(BF)
     if near_dp:
-        pair_big = jnp.concatenate([shard_big, pp(shard_big, 1)], 0)
+        own = w_up.shape[0]
+        shard_in = joined(
+            shard_kernel, [sds((own, 3 * width), BF)], jnp.transpose(w_qkv, (1, 0, 2))
+        )[0]
+        out_y = pp(shard_out, 2)
+        x_y = pp(after(tokens, out_y), 2)
+        x_c = pp(tokens, 1)
         ring = [ring_step(shard_in, shard_in)]
         ring.append(ring_step(*together(ring[-1])))
+        shard_big = joined(
+            shard_kernel, [sds((own, 2 * units + 2 * width), BF)], w_up, w_down.T, shard_out, out_y
+        )[0]
         ring.append(ring_step(*together(ring[-1])))
         last = lax.ppermute(together(ring[-1])[0], "dp", onward)
-        pair_big = after(pair_big, last)
-        came = [pair_step(pair_big)]
+        pair_big = joined(
+            stack_kernel, [sds((2 * own, 2 * units + 2 * width), BF)], shard_big, pp(shard_big, 1)
+        )[0]
+        came = [pair_step(after(pair_big, last))]
         pieces_in = [shard_in, *ring[0], *ring[1], *ring[2], last]
+        dy_mine, dy_other = joined(
+            lanes_kernel, [sds((rows, width, half), BF)] * 2, after(cotangent, x_y)
+        )
     else:
+        x_y = pp(tokens, 2)
+        x_c = pp(tokens, 1)
+        shard_in = w_qkv.astype(BF).reshape(w_qkv.shape[0], 3 * width)
+        shard_big = jnp.concatenate(
+            [w_up.astype(BF), w_down.T.astype(BF), shard_out, pp(shard_out, 2)], 1
+        )
         pieces_in = [lax.all_gather(shard_in, "dp", axis=0, tiled=True)]
         big_a = lax.all_gather(shard_big, "dp", axis=0, tiled=True)
+        cot = after(cotangent, x_y)
+        dy_mine = lax.dynamic_slice_in_dim(cot, core * half, half, 2)
+        dy_other = lax.dynamic_slice_in_dim(cot, (1 - core) * half, half, 2)
     x_d = pp(x_y, 1)
     x_pieces = (tokens, x_c, x_y, x_d)
-    cot = after(cotangent, x_y)
-    dy_mine = lax.dynamic_slice_in_dim(cot, core * half, half, 2)
-    dy_other = lax.dynamic_slice_in_dim(cot, (1 - core) * half, half, 2)
     dy1, dy2, dy3 = pp(dy_other, 1), pp(dy_mine, 2), pp(dy_other, 3)
     b_up_a = b_up.reshape(1, units)
     b_up_b = pp(b_up_a, 1)
@@ -561,7 +599,7 @@
 
     ins = [(me_ref, None)] + [(p, by_row(p)) for p in x_pieces]
     ins += [(b_qv, whole(b_qv)), (prev_logits, by_row(prev_logits))]
-    ins += [(segment_ids, whole(segment_ids))] + [(b, whole(b)) for b in pieces_in]
+    ins += [(segment_ids, whole(segment_ids))] + [(b, held(b)) for b in pieces_in]
     outs = [
         sds(prev_logits.shape, BF),
         sds(prev_logits.shape, BF),
@@ -570,7 +608,7 @@
         sds3(width, half, BF),
         sds3(full, slots, BF),
         sds3(half, full, BF),
-        sds((full, full), BF),
+        sds((full, 3 * width), BF),
     ]
     raw, prob, qkv, o_own, o_oth, xt, xh, w_in = call(
         functools.partial(attend_kernel, heads, ring_steps if near_dp else [0]), (rows,), ins,
@@ -578,19 +616,19 @@
         [pltpu.VMEM((width, slots), BF)], "attend", 1, None, 48,
     )
     o1, o2, o3 = pp(o_oth, 1), pp(o_own, 2), pp(o_oth, 3)
-    wo0 = w_in[:, 3 * width :]
-    wo2 = pp(wo0, 2)
-    wo1, wo3 = pp(wo0, 1), pp(wo2, 1)
     if near_dp:
         came.append(pair_step(after(came[0], o_own, dy1, dy2, dy3)))
         came.append(pair_step(after(came[1], o2)))
         came.append(pair_step(after(came[2], o1, o3)))
-        big_a, big_b = place_pairs(
-            [pair_big, *came[:3], after(came[3], wo2), *[pp(b, 1) for b in came[:3]]]
+        big_a, wo0, wo2, big_b, wo1, wo3 = place_pairs(
+            [pair_big, *came, *[pp(b, 1) for b in came[:3]]]
         )
     else:
         big_a = after(big_a, o_own)
         big_b = pp(big_a, 1)
+        wo0, wo1 = (b[:, 2 * units : 2 * units + width] for b in (big_a, big_b))
+        wo2, wo3 = (b[:, 2 * units + width :] for b in (big_a, big_b))
+        big_a, big_b = big_a[:, : 2 * units], big_b[:, : 2 * units]
 
     one = (1, half, full)
     up = Stage(

time: 267 us -> 254 us (0.951)
  local copies, waits for them, and re-layouts: 16.2 us -> 7.63 us
  starting transfers between devices: 51.7 us -> 48.5 us
    ppermute x4, waiting for transfers between devices: 1.14 us -> 13.5 us  [pair_step(): return lax.ppermute(pair, ('dp', 'tensor'), both_ways)]
    ppermute x37 -> x35, waiting for transfers between devices: 43.4 us -> 32.6 us  [pp(): return lax.ppermute(array, 'tensor', [(i, i ^ step) for i in range(4)])]
    unnamed x83 -> x43, local copies, waits for them, and re-layouts: 12.6 us -> 6.25 us
    ppermute x37 -> x35, starting transfers between devices: 22.4 us -> 19.9 us  [pp(): return lax.ppermute(array, 'tensor', [(i, i ^ step) for i in range(4)])]
    pallas_call x26 -> x30, Pallas kernels: 81 us -> 80.9 us  [call(): pl.pallas_call(kernel, out_shape=outs, grid_spec=pltpu.PrefetchScalarGrid...]
  transfers between devices with their start and end apart: 70 -> 68, of which waited for: 29 -> 31; matrix products, arithmetic and copies ran while one was open for 4% -> 3% of each run, Pallas kernels for 26% -> 28%
where the time goes in v4:
time: 254 us; the launch traced here: 253 us
  waiting for transfers between devices  109 us (43%)
  Pallas kernels  80.9 us (32%)
  starting transfers between devices  48.5 us (19%)
  local copies, waits for them, and re-layouts  7.63 us (3%)
  other arithmetic  6.44 us (3%)
    pallas_call x30, Pallas kernels, call(): pl.pallas_call(kernel, out_shape=outs, grid_spec=pltpu.PrefetchScalarGrid...  80.9 us
    ppermute x35, waiting for transfers between devices, pp(): return lax.ppermute(array, 'tensor', [(i, i ^ step) for i in range(4)])  32.6 us
    ppermute x8, waiting for transfers between devices, swap(): return lax.ppermute(array, 'dp', [(i, i ^ 1 << bit) for i in range(groups)])  28 us
    ppermute x35, starting transfers between devices, pp(): return lax.ppermute(array, 'tensor', [(i, i ^ step) for i in range(4)])  19.9 us
    ppermute x9, waiting for transfers between devices, ring_step(): lax.ppermute(ahead, 'dp', onward)  18.4 us
    ppermute x4, waiting for transfers between devices, pair_step(): return lax.ppermute(pair, ('dp', 'tensor'), both_ways)  13.5 us
    ppermute x9, waiting for transfers between devices, ring_step(): lax.ppermute(behind, 'dp', backward)  11.3 us
    ppermute x9, starting transfers between devices, ring_step(): lax.ppermute(behind, 'dp', backward)  9.76 us
  transfers between devices with their start and end apart: 68, of which 31 were waited for; matrix products, arithmetic and copies ran while one was open for 3% of the time, Pallas kernels for 28%

profile of v4, /device:TPU:0, one launch (start us, length us, event | category | flops | bytes accessed | tf_op | source)
XLA Modules:
  0.0 253.3 jit_solution(11196024228911772552)
XLA Ops:
  1.7 3.0 %collective-permute-start.1 = (bf16[96,192]{1,0:T(8,128)(2,1)S(1)}, bf16[96,192]{1,0:T(8,128)(2,1)S(1)}, u32[]{:S(2)}, u32[]{:S(2)}) collective-permute-start(bf16[96,192]{1,0:T(8,128)(2,1)S(1)} %bitcast.27), channel_id=1, source_target_pairs={{0,2},{1,3},{2,0},{3,1},{4,6},{5,7},{6,4},{7,5},{8,10},{9,11},{10,... | collective-permute-start | bytes 110600 | tf_op jit(solution)/shard_map/ppermute | solution.py:490
  6.4 1.6 collective-permute-start.4
  12.9 1.6 collective-permute-start.6
  14.9 2.9 %collective-permute-done.6.rest_3_ = bf16[96,576]{1,0:T(8,128)(2,1)S(1)} collective-permute-done((bf16[96,576]{1,0:T(8,128)(2,1)S(1)}, bf16[96,576]{1,0:T(8,128)(2,1)S(1)}, u32[]{:S(2)}, u32[]{:S(2)}) %collective-permute-start.6) | collective-permute-done | bytes 110624 | tf_op jit(solution)/shard_map/ppermute | solution.py:505
  17.8 1.6 collective-permute-done.7.rest_4_
  21.4 2.8 %collective-permute-done.8.rest_5_ = bf16[96,576]{1,0:T(8,128)(2,1)S(1)} collective-permute-done((bf16[96,576]{1,0:T(8,128)(2,1)S(1)}, bf16[96,576]{1,0:T(8,128)(2,1)S(1)}, u32[]{:S(2)}, u32[]{:S(2)}) %collective-permute-start.8) | collective-permute-done | bytes 110624 | tf_op jit(solution)/shard_map/ppermute | solution.py:505
  27.9 2.8 %collective-permute-done.10.rest_7_ = bf16[96,576]{1,0:T(8,128)(2,1)S(1)} collective-permute-done((bf16[96,576]{1,0:T(8,128)(2,1)S(1)}, bf16[96,576]{1,0:T(8,128)(2,1)S(1)}, u32[]{:S(2)}, u32[]{:S(2)}) %collective-permute-start.10) | collective-permute-done | bytes 110624 | tf_op jit(solution)/shard_map/ppermute | solution.py:542
  34.8 12.6 %attend.1 = (bf16[3,3,512,512]{3,2,1,0:T(8,128)(2,1)}, bf16[3,3,512,512]{3,2,1,0:T(8,128)(2,1)}, bf16[3,3,192,512]{3,2,1,0:T(8,128)(2,1)}, bf16[3,192,256]{2,1,0...) custom-call(s32[5]{0:T(128)S(1)} %stack.32.me_ref.refs_0_, ...), custom_call_target="tpu_custom_call" | custom-call | flops 10 | bytes 1 | tf_op jit(solution)/shard_map/attend/pallas_call | solution.py:450
  50.3 7.4 %collective-permute-done.12.refs_3_ = bf16[3,192,256]{2,1,0:T(8,128)(2,1)S(1)} collective-permute-done((bf16[3,192,256]{2,1,0:T(8,128)(2,1)S(1)}, bf16[3,192,256]{2,1,0:T(8,128)(2,1)S(1)}, u32[]{:S(2)}, u32[]{:S(2)}) %collective-permute-start.12) | collective-permute-done | bytes 294944 | tf_op jit(solution)/shard_map/ppermute | solution.py:490
  57.7 1.6 collective-permute-done.19.rest_2_
  60.2 1.6 collective-permute-start.13
  62.3 6.5 %collective-permute-done.13.refs_4_ = bf16[3,192,256]{2,1,0:T(8,128)(2,1)S(1)} collective-permute-done((bf16[3,192,256]{2,1,0:T(8,128)(2,1)S(1)}, bf16[3,192,256]{2,1,0:T(8,128)(2,1)S(1)}, u32[]{:S(2)}, u32[]{:S(2)}) %collective-permute-start.13) | collective-permute-done | bytes 294944 | tf_op jit(solution)/shard_map/ppermute | solution.py:490
  68.8 1.9 collective-permute-done.20.rest_3_
  72.3 10.0 %collective-permute-done.21.rest_4_ = bf16[192,1920]{1,0:T(8,128)(2,1)S(1)} collective-permute-done((bf16[192,1920]{1,0:T(8,128)(2,1)S(1)}, bf16[192,1920]{1,0:T(8,128)(2,1)S(1)}, u32[]{:S(2)}, u32[]{:S(2)}) %collective-permute-start.21) | collective-permute-done | bytes 737312 | tf_op jit(solution)/shard_map/ppermute | solution.py:519
  83.6 4.0 %up.3 = (f32[3,256,768]{2,1,0:T(8,128)S(1)}, f32[3,256,128]{2,1,0:T(8,128)S(1)}, bf16[3,256,768]{2,1,0:T(8,128)(2,1)S(1)}, bf16[3,256,768]{2,1,0:T(8,128)(2,1)S(...) custom-call(s32[5]{0:T(128)S(1)} %stack.32.me_ref.refs_0_, ...), custom_call_target="tpu_custom_call" | custom-call | flops 10 | bytes 1 | tf_op jit(solution)/shard_map/up/pallas_call | solution.py:450
  88.6 3.8 %up.4 = (f32[3,256,768]{2,1,0:T(8,128)S(1)}, f32[3,256,128]{2,1,0:T(8,128)S(1)}, bf16[3,256,768]{2,1,0:T(8,128)(2,1)S(1)}, bf16[3,256,768]{2,1,0:T(8,128)(2,1)S(...) custom-call(s32[5]{0:T(128)S(1)} %stack.32.me_ref.refs_0_, ...), custom_call_target="tpu_custom_call", output_to_operand_aliasing={{0}: (17, {}), {1}: (18, {}), {2}: (19, {}), {3}: (20, {}),... | custom-call | flops 10 | bytes 1 | tf_op jit(solution)/shard_map/up/pallas_call | solution.py:450
  93.6 3.8 %up.5 = (f32[3,256,768]{2,1,0:T(8,128)S(1)}, f32[3,256,128]{2,1,0:T(8,128)S(1)}, bf16[3,256,768]{2,1,0:T(8,128)(2,1)S(1)}, bf16[3,256,768]{2,1,0:T(8,128)(2,1)S(...) custom-call(s32[5]{0:T(128)S(1)} %stack.32.me_ref.refs_0_, ...), custom_call_target="tpu_custom_call", output_to_operand_aliasing={{0}: (17, {}), {1}: (18, {}), {2}: (19, {}), {3}: (20, {}),... | custom-call | flops 10 | bytes 1 | tf_op jit(solution)/shard_map/up/pallas_call | solution.py:450
  99.7 3.7 %down.3 = (bf16[3,192,256]{2,1,0:T(8,128)(2,1)S(1)}, bf16[3,192,256]{2,1,0:T(8,128)(2,1)S(1)}, f32[3,256,768]{2,1,0:T(8,128)S(1)}, bf16[3,256,768]{2,1,0:T(8,128...) custom-call(s32[5]{0:T(128)S(1)} %stack.32.me_ref.refs_0_, ...), custom_call_target="tpu_custom_call" | custom-call | flops 10 | bytes 1 | tf_op jit(solution)/shard_map/down/pallas_call | solution.py:450
  104.4 3.7 %collective-permute-done.29.refs_3_ = bf16[1,256,768]{2,1,0:T(8,128)(2,1)S(1)} collective-permute-done((bf16[1,256,768]{2,1,0:T(8,128)(2,1)S(1)}, bf16[1,256,768]{2,1,0:T(8,128)(2,1)S(1)}, u32[]{:S(2)}, u32[]{:S(2)}) %collective-permute-start.29) | collective-permute-done | bytes 393248 | tf_op jit(solution)/shard_map/ppermute | solution.py:490
  108.2 3.7 %down.4 = (bf16[3,192,256]{2,1,0:T(8,128)(2,1)S(1)}, bf16[3,192,256]{2,1,0:T(8,128)(2,1)S(1)}, f32[3,256,768]{2,1,0:T(8,128)S(1)}, bf16[3,256,768]{2,1,0:T(8,128...) custom-call(s32[5]{0:T(128)S(1)} %stack.32.me_ref.refs_0_, ...), custom_call_target="tpu_custom_call", output_to_operand_aliasing={{0}: (15, {}), {1}: (16, {}), {2}: (17, {}), {3}: (18, {}),... | custom-call | flops 10 | bytes 1 | tf_op jit(solution)/shard_map/down/pallas_call | solution.py:450
  111.8 4.7 %collective-permute-done.26.refs_3_ = bf16[1,256,768]{2,1,0:T(8,128)(2,1)S(1)} collective-permute-done((bf16[1,256,768]{2,1,0:T(8,128)(2,1)S(1)}, bf16[1,256,768]{2,1,0:T(8,128)(2,1)S(1)}, u32[]{:S(2)}, u32[]{:S(2)}) %collective-permute-start.26) | collective-permute-done | bytes 393248 | tf_op jit(solution)/shard_map/ppermute | solution.py:490
  116.6 5.5 %collective-permute-done.28.refs_3_ = bf16[1,256,768]{2,1,0:T(8,128)(2,1)S(1)} collective-permute-done((bf16[1,256,768]{2,1,0:T(8,128)(2,1)S(1)}, bf16[1,256,768]{2,1,0:T(8,128)(2,1)S(1)}, u32[]{:S(2)}, u32[]{:S(2)}) %collective-permute-start.28) | collective-permute-done | bytes 393248 | tf_op jit(solution)/shard_map/ppermute | solution.py:490
  122.1 3.7 %down.5 = (bf16[3,192,256]{2,1,0:T(8,128)(2,1)S(1)}, bf16[3,192,256]{2,1,0:T(8,128)(2,1)S(1)}, f32[3,256,768]{2,1,0:T(8,128)S(1)}, bf16[3,256,768]{2,1,0:T(8,128...) custom-call(s32[5]{0:T(128)S(1)} %stack.32.me_ref.refs_0_, ...), custom_call_target="tpu_custom_call", output_to_operand_aliasing={{0}: (15, {}), {1}: (16, {}), {2}: (17, {}), {3}: (18, {}),... | custom-call | flops 10 | bytes 1 | tf_op jit(solution)/shard_map/down/pallas_call | solution.py:450
  127.9 1.6 mid.3
  129.5 3.7 %ffn_grad.3 = (bf16[384,768]{1,0:T(8,128)(2,1)S(1)}, bf16[384,768]{1,0:T(8,128)(2,1)S(1)}) custom-call(s32[5]{0:T(128)S(1)} %stack.32.me_ref.refs_0_, bf16[3,256,768]{2,1,0:T(8,128)(2,1)S(1)} %get-tuple-element.246.rest_0_, bf16[3,256,768]{2,1,0:T(8,128)(2,1)S(1)} %collective-permute-done.35.rest_1_, bf16[3,256,768]{2,1,0:T(8,128)(2,1)S(1)} %get-tuple-element.247.rest_2_, ...), custom_call_target="tpu_custom_call" | custom-call | flops 30 | bytes 1 | tf_op jit(solution)/shard_map/ffn_grad/pallas_call | solution.py:450
  133.2 3.4 %ffn_grad.2 = (bf16[384,768]{1,0:T(8,128)(2,1)S(1)}, bf16[384,768]{1,0:T(8,128)(2,1)S(1)}) custom-call(s32[5]{0:T(128)S(1)} %stack.32.me_ref.refs_0_, bf16[3,256,768]{2,1,0:T(8,128)(2,1)S(1)} %get-tuple-element.242.rest_0_, bf16[3,256,768]{2,1,0:T(8,128)(2,1)S(1)} %collective-permute-done.33.rest_1_, bf16[3,256,768]{2,1,0:T(8,128)(2,1)S(1)} %get-tuple-element.244.rest_2_, ...), custom_call_target="tpu_custom_call" | custom-call | flops 30 | bytes 1 | tf_op jit(solution)/shard_map/ffn_grad/pallas_call | solution.py:450
  137.9 1.6 mid.4
  143.3 5.3 %back.3 = (bf16[3,3,512,512]{3,2,1,0:T(8,128)(2,1)}, bf16[3,576,512]{2,1,0:T(8,128)(2,1)S(1)}, bf16[3,192,512]{2,1,0:T(8,128)(2,1)S(1)}, bf16[3,192,512]{2,1,0:T...) custom-call(s32[5]{0:T(128)S(1)} %stack.32.me_ref.refs_0_, ...), custom_call_target="tpu_custom_call" | custom-call | flops 10 | bytes 1 | tf_op jit(solution)/shard_map/back/pallas_call | solution.py:450
  148.6 5.2 %back.4 = (bf16[3,3,512,512]{3,2,1,0:T(8,128)(2,1)}, bf16[3,576,512]{2,1,0:T(8,128)(2,1)S(1)}, bf16[3,192,512]{2,1,0:T(8,128)(2,1)S(1)}, bf16[3,192,512]{2,1,0:T...) custom-call(s32[5]{0:T(128)S(1)} %stack.32.me_ref.refs_0_, ...), custom_call_target="tpu_custom_call", output_to_operand_aliasing={{0}: (7, {}), {1}: (8, {}), {2}: (9, {}), {3}: (10, {}), {4... | custom-call | flops 10 | bytes 1 | tf_op jit(solution)/shard_map/back/pallas_call | solution.py:450
  155.1 1.6 mid.5
  163.4 5.3 %back.5 = (bf16[3,3,512,512]{3,2,1,0:T(8,128)(2,1)}, bf16[3,576,512]{2,1,0:T(8,128)(2,1)S(1)}, bf16[3,192,512]{2,1,0:T(8,128)(2,1)S(1)}, bf16[3,192,512]{2,1,0:T...) custom-call(s32[5]{0:T(128)S(1)} %stack.32.me_ref.refs_0_, ...), custom_call_target="tpu_custom_call", output_to_operand_aliasing={{0}: (7, {}), {1}: (8, {}), {2}: (9, {}), {3}: (10, {}), {4... | custom-call | flops 10 | bytes 1 | tf_op jit(solution)/shard_map/back/pallas_call | solution.py:450
  168.6 2.7 %qkv_grad.1 = (bf16[400,768]{1,0:T(8,128)(2,1)S(1)}, bf16[400,768]{1,0:T(8,128)(2,1)S(1)}) custom-call(s32[5]{0:T(128)S(1)} %stack.32.me_ref.refs_0_, bf16[3,768,512]{2,1,0:T(8,128)(2,1)S(1)} %copy-done.1, bf16[3,576,512]{2,1,0:T(8,128)(2,1)S(1)} %get-tuple-element.295.rest_1_, bf16[3,192,256]{2,1,0:T(8,128)(2,1)S(1)} %get-tuple-element.178.refs_1_.rest_2_, ...), custom_call_target="tpu_custom_call" | custom-call | flops 40 | bytes 1 | tf_op jit(solution)/shard_map/qkv_grad/pallas_call | solution.py:450
  172.9 1.7 collective-permute-start.48
  174.6 13.7 %collective-permute-done.60 = bf16[192,768]{1,0:T(8,128)(2,1)S(1)} collective-permute-done((bf16[192,768]{1,0:T(8,128)(2,1)S(1)}, bf16[192,768]{1,0:T(8,128)(2,1)S(1)}, u32[]{:S(2)}, u32[]{:S(2)}) %collective-permute-start.60) | collective-permute-done | bytes 294944 | tf_op jit(solution)/shard_map/ppermute | solution.py:493
  188.5 2.0 collective-permute-start.62
  191.3 5.8 %collective-permute-done.61.rest_1_ = bf16[192,768]{1,0:T(8,128)(2,1)S(1)} collective-permute-done((bf16[192,768]{1,0:T(8,128)(2,1)S(1)}, bf16[192,768]{1,0:T(8,128)(2,1)S(1)}, u32[]{:S(2)}, u32[]{:S(2)}) %collective-permute-start.61) | collective-permute-done | bytes 294944 | tf_op jit(solution)/shard_map/ppermute | solution.py:505
  200.5 3.6 %collective-permute-done.49.rest_1_ = bf16[208,768]{1,0:T(8,128)(2,1)S(1)} collective-permute-done((bf16[208,768]{1,0:T(8,128)(2,1)S(1)}, bf16[208,768]{1,0:T(8,128)(2,1)S(1)}, u32[]{:S(2)}, u32[]{:S(2)}) %collective-permute-start.49) | collective-permute-done | bytes 319520 | tf_op jit(solution)/shard_map/ppermute | solution.py:493
  205.8 9.5 %collective-permute-done.50.came = bf16[112,768]{1,0:T(8,128)(2,1)S(1)} collective-permute-done((bf16[112,768]{1,0:T(8,128)(2,1)}, bf16[112,768]{1,0:T(8,128)(2,1)S(1)}, u32[]{:S(2)}, u32[]{:S(2)}) %collective-permute-start.50) | collective-permute-done | bytes 172064 | tf_op jit(solution)/shard_map/ppermute | solution.py:493
  222.5 3.4 %collective-permute-done.64.rest_4_ = bf16[192,768]{1,0:T(8,128)(2,1)S(1)} collective-permute-done((bf16[192,768]{1,0:T(8,128)(2,1)S(1)}, bf16[192,768]{1,0:T(8,128)(2,1)S(1)}, u32[]{:S(2)}, u32[]{:S(2)}) %collective-permute-start.64) | collective-permute-done | bytes 294944 | tf_op jit(solution)/shard_map/ppermute | solution.py:505
  225.9 2.1 collective-permute-done.52.rest_2_
  228.0 2.0 collective-permute-start.54
  230.0 2.3 fusion
  232.6 3.5 %collective-permute-done.53.rest_3_ = bf16[96,768]{1,0:T(8,128)(2,1)S(1)} collective-permute-done((bf16[96,768]{1,0:T(8,128)(2,1)S(1)}, bf16[96,768]{1,0:T(8,128)(2,1)S(1)}, u32[]{:S(2)}, u32[]{:S(2)}) %collective-permute-start.53) | collective-permute-done | bytes 147488 | tf_op jit(solution)/shard_map/ppermute | solution.py:505
  237.5 2.1 collective-permute-start.56
  239.5 3.3 %collective-permute-done.55.rest_5_ = bf16[96,768]{1,0:T(8,128)(2,1)S(1)} collective-permute-done((bf16[96,768]{1,0:T(8,128)(2,1)S(1)}, bf16[96,768]{1,0:T(8,128)(2,1)S(1)}, u32[]{:S(2)}, u32[]{:S(2)}) %collective-permute-start.55) | collective-permute-done | bytes 147488 | tf_op jit(solution)/shard_map/ppermute | solution.py:505
  244.8 2.1 collective-permute-done.67.rest_7_
  246.9 3.1 %finish.3 = (f32[768,768]{1,0:T(8,128)}, f32[768,768]{1,0:T(8,128)}) custom-call(s32[5]{0:T(128)S(1)} %stack.32.me_ref.refs_0_, bf16[192,768]{1,0:T(8,128)(2,1)S(1)} %add_convert_fusion.2.rest_0_, bf16[192,768]{1,0:T(8,128)(2,1)S(1)} %collective-permute-done.61.rest_1_, bf16[192,768]{1,0:T(8,128)(2,1)S(1)} %collective-permute-done.62.rest_2_, ...), custom_call_target="tpu_custom_call" | custom-call | flops 20 | bytes 1 | tf_op jit(solution)/shard_map/finish/pallas_call | solution.py:450
  250.1 3.3 %finish.2 = (f32[576,768]{1,0:T(8,128)}, f32[192,768]{1,0:T(8,128)}) custom-call(s32[5]{0:T(128)S(1)} %stack.32.me_ref.refs_0_, bf16[96,768]{1,0:T(8,128)(2,1)S(1)} %copy-done.13, bf16[96,768]{1,0:T(8,128)(2,1)S(1)} %collective-permute-done.51.rest_1_, bf16[96,768]{1,0:T(8,128)(2,1)S(1)} %collective-permute-done.52.rest_2_, bf16[96,768]{1,0:T(8,128)(2,1)S(1)} %copy-done.15, ...), custom_call_target="tpu_custom_call" | custom-call | flops 20 | bytes 1 | tf_op jit(solution)/shard_map/finish/pallas_call | solution.py:450
  (175 shorter events, 63.6 us)
Async XLA Ops:
  8.5 23.7 %collective-permute-start.2 = (bf16[3,192,512]{2,1,0:T(8,128)(2,1)}, bf16[3,192,512]{2,1,0:T(8,128)(2,1)S(1)}, u32[]{:S(2)}, u32[]{:S(2)}) collective-permute-start(bf16[3,192,512]{2,1,0:T(8,128)(2,1)} %bitcast.22), channel_id=1, source_target_pairs={{0,2},{1,3},{2,0},{3,1},{4,6},{5,7},{6,4},{7,5},{8,10},{9,11},{10,... | collective-permute-start | bytes 1769480 | tf_op jit(solution)/shard_map/ppermute | solution.py:490
  11.4 15.9 %collective-permute-start.14 = (bf16[96,1920]{1,0:T(8,128)(2,1)S(1)}, bf16[96,1920]{1,0:T(8,128)(2,1)S(1)}, u32[]{:S(2)}, u32[]{:S(2)}) collective-permute-start(bf16[96,1920]{1,0:T(8,128)(2,1)S(1)} %joined.5.first), channel_id=1, source_target_pairs={{0,1},{1,0},{2,3},{3,2},{4,5},{5,4},{6,7},{7,6},{8,9},{9,8},{10,11... | collective-permute-start | bytes 1105928 | tf_op jit(solution)/shard_map/ppermute | solution.py:490
  21.4 12.9 %collective-permute-start = (bf16[3,192,512]{2,1,0:T(8,128)(2,1)S(1)}, bf16[3,192,512]{2,1,0:T(8,128)(2,1)S(1)}, u32[]{:S(2)}, u32[]{:S(2)}) collective-permute-start(bf16[3,192,512]{2,1,0:T(8,128)(2,1)S(1)} %bitcast.23), channel_id=1, source_target_pairs={{0,1},{1,0},{2,3},{3,2},{4,5},{5,4},{6,7},{7,6},{8,9},{9,8},{10,11... | collective-permute-start | bytes 1769480 | tf_op jit(solution)/shard_map/ppermute | solution.py:490
  30.7 17.1 %collective-permute-start.15 = (bf16[192,1920]{1,0:T(8,128)(2,1)S(1)}, bf16[192,1920]{1,0:T(8,128)(2,1)S(1)}, u32[]{:S(2)}, u32[]{:S(2)}) collective-permute-start(bf16[192,1920]{1,0:T(8,128)(2,1)S(1)} %joined.6.rest_0_), channel_id=1, source_target_pairs={{0,8},{9,1},{2,10},{11,3},{8,16},{17,9},{10,18},{19,11},{16,24},{2... | collective-permute-start | bytes 2211848 | tf_op jit(solution)/shard_map/ppermute | solution.py:519
  32.8 14.6 %collective-permute-start.16 = (bf16[3,192,256]{2,1,0:T(8,128)(2,1)S(1)}, bf16[3,192,256]{2,1,0:T(8,128)(2,1)S(1)}, u32[]{:S(2)}, u32[]{:S(2)}) collective-permute-start(bf16[3,192,256]{2,1,0:T(8,128)(2,1)S(1)} %get-tuple-element.182), channel_id=1, source_target_pairs={{0,1},{1,0},{2,3},{3,2},{4,5},{5,4},{6,7},{7,6},{8,9},{9,8},{10,11... | collective-permute-start | bytes 884744 | tf_op jit(solution)/shard_map/ppermute | solution.py:490
  33.4 14.1 %collective-permute-start.17 = (bf16[3,192,256]{2,1,0:T(8,128)(2,1)S(1)}, bf16[3,192,256]{2,1,0:T(8,128)(2,1)S(1)}, u32[]{:S(2)}, u32[]{:S(2)}) collective-permute-start(bf16[3,192,256]{2,1,0:T(8,128)(2,1)S(1)} %get-tuple-element.183.refs_4_), channel_id=1, source_target_pairs={{0,2},{1,3},{2,0},{3,1},{4,6},{5,7},{6,4},{7,5},{8,10},{9,11},{10,... | collective-permute-start | bytes 884744 | tf_op jit(solution)/shard_map/ppermute | solution.py:490
  34.3 13.5 %collective-permute-start.18 = (bf16[3,192,256]{2,1,0:T(8,128)(2,1)S(1)}, bf16[3,192,256]{2,1,0:T(8,128)(2,1)S(1)}, u32[]{:S(2)}, u32[]{:S(2)}) collective-permute-start(bf16[3,192,256]{2,1,0:T(8,128)(2,1)S(1)} %get-tuple-element.182), channel_id=1, source_target_pairs={{0,3},{1,2},{2,1},{3,0},{4,7},{5,6},{6,5},{7,4},{8,11},{9,10},{10,... | collective-permute-start | bytes 884744 | tf_op jit(solution)/shard_map/ppermute | solution.py:490
  47.8 11.5 %collective-permute-start.19 = (bf16[192,1920]{1,0:T(8,128)(2,1)S(1)}, bf16[192,1920]{1,0:T(8,128)(2,1)S(1)}, u32[]{:S(2)}, u32[]{:S(2)}) collective-permute-start(bf16[192,1920]{1,0:T(8,128)(2,1)S(1)} %collective-permute-done.15.rest_1_), channel_id=1, source_target_pairs={{0,8},{9,1},{2,10},{11,3},{8,16},{17,9},{10,18},{19,11},{16,24},{2... | collective-permute-start | bytes 2211848 | tf_op jit(solution)/shard_map/ppermute | solution.py:519
  48.7 9.0 %collective-permute-start.12 = (bf16[3,192,256]{2,1,0:T(8,128)(2,1)S(1)}, bf16[3,192,256]{2,1,0:T(8,128)(2,1)S(1)}, u32[]{:S(2)}, u32[]{:S(2)}) collective-permute-start(bf16[3,192,256]{2,1,0:T(8,128)(2,1)S(1)} %get-tuple-element.178.refs_1_.rest_2_), channel_id=1, source_target_pairs={{0,2},{1,3},{2,0},{3,1},{4,6},{5,7},{6,4},{7,5},{8,10},{9,11},{10,... | collective-permute-start | bytes 884744 | tf_op jit(solution)/shard_map/ppermute | solution.py:490
  59.3 11.5 %collective-permute-start.20 = (bf16[192,1920]{1,0:T(8,128)(2,1)S(1)}, bf16[192,1920]{1,0:T(8,128)(2,1)S(1)}, u32[]{:S(2)}, u32[]{:S(2)}) collective-permute-start(bf16[192,1920]{1,0:T(8,128)(2,1)S(1)} %collective-permute-done.19.rest_2_), channel_id=1, source_target_pairs={{0,8},{9,1},{2,10},{11,3},{8,16},{17,9},{10,18},{19,11},{16,24},{2... | collective-permute-start | bytes 2211848 | tf_op jit(solution)/shard_map/ppermute | solution.py:519
  60.2 8.7 %collective-permute-start.13 = (bf16[3,192,256]{2,1,0:T(8,128)(2,1)S(1)}, bf16[3,192,256]{2,1,0:T(8,128)(2,1)S(1)}, u32[]{:S(2)}, u32[]{:S(2)}) collective-permute-start(bf16[3,192,256]{2,1,0:T(8,128)(2,1)S(1)} %get-tuple-element.179.rest_4_), channel_id=1, source_target_pairs={{0,3},{1,2},{2,1},{3,0},{4,7},{5,6},{6,5},{7,4},{8,11},{9,10},{10,... | collective-permute-start | bytes 884744 | tf_op jit(solution)/shard_map/ppermute | solution.py:490
  61.8 10.4 %collective-permute-start.22 = (bf16[192,1920]{1,0:T(8,128)(2,1)S(1)}, bf16[192,1920]{1,0:T(8,128)(2,1)S(1)}, u32[]{:S(2)}, u32[]{:S(2)}) collective-permute-start(bf16[192,1920]{1,0:T(8,128)(2,1)S(1)} %collective-permute-done.15.rest_1_), channel_id=1, source_target_pairs={{0,1},{1,0},{2,3},{3,2},{4,5},{5,4},{6,7},{7,6},{8,9},{9,8},{10,11... | collective-permute-start | bytes 2211848 | tf_op jit(solution)/shard_map/ppermute | solution.py:490
  61.8 10.4 %collective-permute-start.23 = (bf16[192,1920]{1,0:T(8,128)(2,1)S(1)}, bf16[192,1920]{1,0:T(8,128)(2,1)S(1)}, u32[]{:S(2)}, u32[]{:S(2)}) collective-permute-start(bf16[192,1920]{1,0:T(8,128)(2,1)S(1)} %collective-permute-done.19.rest_2_), channel_id=1, source_target_pairs={{0,1},{1,0},{2,3},{3,2},{4,5},{5,4},{6,7},{7,6},{8,9},{9,8},{10,11... | collective-permute-start | bytes 2211848 | tf_op jit(solution)/shard_map/ppermute | solution.py:490
  70.8 11.5 %collective-permute-start.21 = (bf16[192,1920]{1,0:T(8,128)(2,1)S(1)}, bf16[192,1920]{1,0:T(8,128)(2,1)S(1)}, u32[]{:S(2)}, u32[]{:S(2)}) collective-permute-start(bf16[192,1920]{1,0:T(8,128)(2,1)S(1)} %collective-permute-done.20.rest_3_), channel_id=1, source_target_pairs={{0,8},{9,1},{2,10},{11,3},{8,16},{17,9},{10,18},{19,11},{16,24},{2... | collective-permute-start | bytes 2211848 | tf_op jit(solution)/shard_map/ppermute | solution.py:519
  71.6 10.6 %collective-permute-start.24 = (bf16[192,1920]{1,0:T(8,128)(2,1)S(1)}, bf16[192,1920]{1,0:T(8,128)(2,1)S(1)}, u32[]{:S(2)}, u32[]{:S(2)}) collective-permute-start(bf16[192,1920]{1,0:T(8,128)(2,1)S(1)} %collective-permute-done.20.rest_3_), channel_id=1, source_target_pairs={{0,1},{1,0},{2,3},{3,2},{4,5},{5,4},{6,7},{7,6},{8,9},{9,8},{10,11... | collective-permute-start | bytes 2211848 | tf_op jit(solution)/shard_map/ppermute | solution.py:490
  71.7 11.8 %collective-permute-start.25 = (f32[1,768]{1,0:T(1,128)S(1)}, f32[1,768]{1,0:T(1,128)S(1)}, u32[]{:S(2)}, u32[]{:S(2)}) collective-permute-start(f32[1,768]{1,0:T(1,128)S(1)} %reshape.32.refs_15_), channel_id=1, source_target_pairs={{0,1},{1,0},{2,3},{3,2},{4,5},{5,4},{6,7},{7,6},{8,9},{9,8},{10,11... | collective-permute-start | bytes 9224 | tf_op jit(solution)/shard_map/ppermute | solution.py:490
  87.6 12.1 %collective-permute-start.27 = (bf16[1,256,768]{2,1,0:T(8,128)(2,1)S(1)}, bf16[1,256,768]{2,1,0:T(8,128)(2,1)S(1)}, u32[]{:S(2)}, u32[]{:S(2)}) collective-permute-start(bf16[1,256,768]{2,1,0:T(8,128)(2,1)S(1)} %get-tuple-element.210.refs_2_), channel_id=1, source_target_pairs={{0,2},{1,3},{2,0},{3,1},{4,6},{5,7},{6,4},{7,5},{8,10},{9,11},{10,... | collective-permute-start | bytes 1179656 | tf_op jit(solution)/shard_map/ppermute | solution.py:490
  92.4 15.7 %collective-permute-start.29 = (bf16[1,256,768]{2,1,0:T(8,128)(2,1)S(1)}, bf16[1,256,768]{2,1,0:T(8,128)(2,1)S(1)}, u32[]{:S(2)}, u32[]{:S(2)}) collective-permute-start(bf16[1,256,768]{2,1,0:T(8,128)(2,1)S(1)} %get-tuple-element.215.refs_2_), channel_id=1, source_target_pairs={{0,2},{1,3},{2,0},{3,1},{4,6},{5,7},{6,4},{7,5},{8,10},{9,11},{10,... | collective-permute-start | bytes 1179656 | tf_op jit(solution)/shard_map/ppermute | solution.py:490
  97.5 19.1 %collective-permute-start.26 = (bf16[1,256,768]{2,1,0:T(8,128)(2,1)S(1)}, bf16[1,256,768]{2,1,0:T(8,128)(2,1)S(1)}, u32[]{:S(2)}, u32[]{:S(2)}) collective-permute-start(bf16[1,256,768]{2,1,0:T(8,128)(2,1)S(1)} %get-tuple-element.209.refs_2_), channel_id=1, source_target_pairs={{0,2},{1,3},{2,0},{3,1},{4,6},{5,7},{6,4},{7,5},{8,10},{9,11},{10,... | collective-permute-start | bytes 1179656 | tf_op jit(solution)/shard_map/ppermute | solution.py:490
  103.4 18.7 %collective-permute-start.28 = (bf16[1,256,768]{2,1,0:T(8,128)(2,1)S(1)}, bf16[1,256,768]{2,1,0:T(8,128)(2,1)S(1)}, u32[]{:S(2)}, u32[]{:S(2)}) collective-permute-start(bf16[1,256,768]{2,1,0:T(8,128)(2,1)S(1)} %get-tuple-element.213.refs_2_), channel_id=1, source_target_pairs={{0,2},{1,3},{2,0},{3,1},{4,6},{5,7},{6,4},{7,5},{8,10},{9,11},{10,... | collective-permute-start | bytes 1179656 | tf_op jit(solution)/shard_map/ppermute | solution.py:490
  104.4 25.0 %collective-permute-start.35 = (bf16[3,256,768]{2,1,0:T(8,128)(2,1)S(1)}, bf16[3,256,768]{2,1,0:T(8,128)(2,1)S(1)}, u32[]{:S(2)}, u32[]{:S(2)}) collective-permute-start(bf16[3,256,768]{2,1,0:T(8,128)(2,1)S(1)} %get-tuple-element.246.rest_0_), channel_id=1, source_target_pairs={{0,1},{1,0},{2,3},{3,2},{4,5},{5,4},{6,7},{7,6},{8,9},{9,8},{10,11... | collective-permute-start | bytes 3538952 | tf_op jit(solution)/shard_map/ppermute | solution.py:490
  126.5 11.5 %collective-permute-start.32 = (bf16[1,256,768]{2,1,0:T(8,128)(2,1)S(1)}, bf16[1,256,768]{2,1,0:T(8,128)(2,1)S(1)}, u32[]{:S(2)}, u32[]{:S(2)}) collective-permute-start(bf16[1,256,768]{2,1,0:T(8,128)(2,1)S(1)} %get-tuple-element.241.refs_2_), channel_id=1, source_target_pairs={{0,2},{1,3},{2,0},{3,1},{4,6},{5,7},{6,4},{7,5},{8,10},{9,11},{10,... | collective-permute-start | bytes 1179656 | tf_op jit(solution)/shard_map/ppermute | solution.py:490
  139.5 15.0 %collective-permute-start.40 = (bf16[384,768]{1,0:T(8,128)(2,1)S(1)}, bf16[384,768]{1,0:T(8,128)(2,1)S(1)}, u32[]{:S(2)}, u32[]{:S(2)}) collective-permute-start(bf16[384,768]{1,0:T(8,128)(2,1)S(1)} %get-tuple-element.272), channel_id=1, source_target_pairs={{0,8},{4,12},{8,0},{12,4},{16,24},{20,28},{24,16},{28,20},{1,9},{5... | collective-permute-start | bytes 1769480 | tf_op jit(solution)/shard_map/ppermute | solution.py:493
  140.5 14.6 %collective-permute-start.39 = (bf16[384,768]{1,0:T(8,128)(2,1)S(1)}, bf16[384,768]{1,0:T(8,128)(2,1)S(1)}, u32[]{:S(2)}, u32[]{:S(2)}) collective-permute-start(bf16[384,768]{1,0:T(8,128)(2,1)S(1)} %get-tuple-element.270), channel_id=1, source_target_pairs={{0,4},{4,0},{8,12},{12,8},{16,20},{20,16},{24,28},{28,24},{1,5},{5... | collective-permute-start | bytes 1769480 | tf_op jit(solution)/shard_map/ppermute | solution.py:493
  141.1 12.7 %collective-permute-start.31 = (bf16[1,256,768]{2,1,0:T(8,128)(2,1)S(1)}, bf16[1,256,768]{2,1,0:T(8,128)(2,1)S(1)}, u32[]{:S(2)}, u32[]{:S(2)}) collective-permute-start(bf16[1,256,768]{2,1,0:T(8,128)(2,1)S(1)} %get-tuple-element.240.refs_2_), channel_id=1, source_target_pairs={{0,2},{1,3},{2,0},{3,1},{4,6},{5,7},{6,4},{7,5},{8,10},{9,11},{10,... | collective-permute-start | bytes 1179656 | tf_op jit(solution)/shard_map/ppermute | solution.py:490
  156.7 11.9 %collective-permute-start.45 = (bf16[3,256,768]{2,1,0:T(8,128)(2,1)S(1)}, bf16[3,256,768]{2,1,0:T(8,128)(2,1)S(1)}, u32[]{:S(2)}, u32[]{:S(2)}) collective-permute-start(bf16[3,256,768]{2,1,0:T(8,128)(2,1)S(1)} %get-tuple-element.296.rest_3_), channel_id=1, source_target_pairs={{0,1},{1,0},{2,3},{3,2},{4,5},{5,4},{6,7},{7,6},{8,9},{9,8},{10,11... | collective-permute-start | bytes 3538952 | tf_op jit(solution)/shard_map/ppermute | solution.py:490
  157.5 13.9 %collective-permute-start.58 = (bf16[192,768]{1,0:T(8,128)(2,1)S(1)}, bf16[192,768]{1,0:T(8,128)(2,1)S(1)}, u32[]{:S(2)}, u32[]{:S(2)}) collective-permute-start(bf16[192,768]{1,0:T(8,128)(2,1)S(1)} %get-tuple-element.319), channel_id=1, source_target_pairs={{0,8},{4,12},{8,0},{12,4},{16,24},{20,28},{24,16},{28,20},{1,9},{5... | collective-permute-start | bytes 884744 | tf_op jit(solution)/shard_map/ppermute | solution.py:493
  159.4 12.0 %collective-permute-start.59 = (bf16[192,768]{1,0:T(8,128)(2,1)S(1)}, bf16[192,768]{1,0:T(8,128)(2,1)S(1)}, u32[]{:S(2)}, u32[]{:S(2)}) collective-permute-start(bf16[192,768]{1,0:T(8,128)(2,1)S(1)} %get-tuple-element.321), channel_id=1, source_target_pairs={{0,4},{4,0},{8,12},{12,8},{16,20},{20,16},{24,28},{28,24},{1,5},{5... | collective-permute-start | bytes 884744 | tf_op jit(solution)/shard_map/ppermute | solution.py:493
  172.0 16.3 %collective-permute-start.60 = (bf16[192,768]{1,0:T(8,128)(2,1)S(1)}, bf16[192,768]{1,0:T(8,128)(2,1)S(1)}, u32[]{:S(2)}, u32[]{:S(2)}) collective-permute-start(bf16[192,768]{1,0:T(8,128)(2,1)S(1)} %get-tuple-element.323), channel_id=1, source_target_pairs={{0,16},{4,20},{8,24},{12,28},{16,0},{20,4},{24,8},{28,12},{1,17},{... | collective-permute-start | bytes 884744 | tf_op jit(solution)/shard_map/ppermute | solution.py:493
  172.9 17.6 %collective-permute-start.48 = (bf16[400,768]{1,0:T(8,128)(2,1)S(1)}, bf16[400,768]{1,0:T(8,128)(2,1)S(1)}, u32[]{:S(2)}, u32[]{:S(2)}) collective-permute-start(bf16[400,768]{1,0:T(8,128)(2,1)S(1)} %get-tuple-element.306), channel_id=1, source_target_pairs={{0,4},{4,0},{8,12},{12,8},{16,20},{20,16},{24,28},{28,24},{1,5},{5... | collective-permute-start | bytes 1843208 | tf_op jit(solution)/shard_map/ppermute | solution.py:493
  174.6 23.8 %collective-permute-start.43 = (bf16[3,192,512]{2,1,0:T(8,128)(2,1)S(1)}, bf16[3,192,512]{2,1,0:T(8,128)(2,1)S(1)}, u32[]{:S(2)}, u32[]{:S(2)}) collective-permute-start(bf16[3,192,512]{2,1,0:T(8,128)(2,1)S(1)} %get-tuple-element.292), channel_id=1, source_target_pairs={{0,1},{1,0},{2,3},{3,2},{4,5},{5,4},{6,7},{7,6},{8,9},{9,8},{10,11... | collective-permute-start | bytes 1769480 | tf_op jit(solution)/shard_map/ppermute | solution.py:490
  188.4 8.8 %collective-permute-start.61 = (bf16[192,768]{1,0:T(8,128)(2,1)S(1)}, bf16[192,768]{1,0:T(8,128)(2,1)S(1)}, u32[]{:S(2)}, u32[]{:S(2)}) collective-permute-start(bf16[192,768]{1,0:T(8,128)(2,1)S(1)} %add_convert_fusion.2.rest_0_), channel_id=1, source_target_pairs={{0,8},{8,16},{16,24},{24,28},{28,20},{20,12},{12,4},{4,0},{1,9},{9... | collective-permute-start | bytes 884744 | tf_op jit(solution)/shard_map/ppermute | solution.py:505
  188.5 10.0 %collective-permute-start.62 = (bf16[192,768]{1,0:T(8,128)(2,1)S(1)}, bf16[192,768]{1,0:T(8,128)(2,1)S(1)}, u32[]{:S(2)}, u32[]{:S(2)}) collective-permute-start(bf16[192,768]{1,0:T(8,128)(2,1)S(1)} %add_convert_fusion.2.rest_0_), channel_id=1, source_target_pairs={{8,0},{16,8},{24,16},{28,24},{20,28},{12,20},{4,12},{0,4},{9,1},{1... | collective-permute-start | bytes 884744 | tf_op jit(solution)/shard_map/ppermute | solution.py:505
  191.2 12.9 %collective-permute-start.49 = (bf16[208,768]{1,0:T(8,128)(2,1)S(1)}, bf16[208,768]{1,0:T(8,128)(2,1)S(1)}, u32[]{:S(2)}, u32[]{:S(2)}) collective-permute-start(bf16[208,768]{1,0:T(8,128)(2,1)S(1)} %get-tuple-element.308), channel_id=1, source_target_pairs={{0,8},{4,12},{8,0},{12,4},{16,24},{20,28},{24,16},{28,20},{1,9},{5... | collective-permute-start | bytes 958472 | tf_op jit(solution)/shard_map/ppermute | solution.py:493
  191.3 27.2 %collective-permute-start.30 = (bf16[3,192,256]{2,1,0:T(8,128)(2,1)S(1)}, bf16[3,192,256]{2,1,0:T(8,128)(2,1)}, u32[]{:S(2)}, u32[]{:S(2)}) collective-permute-start(bf16[3,192,256]{2,1,0:T(8,128)(2,1)S(1)} %get-tuple-element.235), channel_id=1, source_target_pairs={{0,1},{1,0},{2,3},{3,2},{4,5},{5,4},{6,7},{7,6},{8,9},{9,8},{10,11... | collective-permute-start | bytes 884744 | tf_op jit(solution)/shard_map/ppermute | solution.py:490
  197.2 32.8 %collective-permute-start.42 = (bf16[3,192,512]{2,1,0:T(8,128)(2,1)S(1)}, bf16[3,192,512]{2,1,0:T(8,128)(2,1)}, u32[]{:S(2)}, u32[]{:S(2)}) collective-permute-start(bf16[3,192,512]{2,1,0:T(8,128)(2,1)S(1)} %get-tuple-element.290), channel_id=1, source_target_pairs={{0,1},{1,0},{2,3},{3,2},{4,5},{5,4},{6,7},{7,6},{8,9},{9,8},{10,11... | collective-permute-start | bytes 1769480 | tf_op jit(solution)/shard_map/ppermute | solution.py:490
  198.4 21.2 %collective-permute-start.63 = (bf16[192,768]{1,0:T(8,128)(2,1)S(1)}, bf16[192,768]{1,0:T(8,128)(2,1)S(1)}, u32[]{:S(2)}, u32[]{:S(2)}) collective-permute-start(bf16[192,768]{1,0:T(8,128)(2,1)S(1)} %collective-permute-done.61.rest_1_), channel_id=1, source_target_pairs={{0,8},{8,16},{16,24},{24,28},{28,20},{20,12},{12,4},{4,0},{1,9},{9... | collective-permute-start | bytes 884744 | tf_op jit(solution)/shard_map/ppermute | solution.py:505
  199.4 30.6 %collective-permute-start.44 = (bf16[3,192,512]{2,1,0:T(8,128)(2,1)}, bf16[3,192,512]{2,1,0:T(8,128)(2,1)}, u32[]{:S(2)}, u32[]{:S(2)}) collective-permute-start(bf16[3,192,512]{2,1,0:T(8,128)(2,1)} %add_convert_fusion.1), channel_id=1, source_target_pairs={{0,2},{1,3},{2,0},{3,1},{4,6},{5,7},{6,4},{7,5},{8,10},{9,11},{10,... | collective-permute-start | bytes 1769480 | tf_op jit(solution)/shard_map/ppermute | solution.py:490
  205.3 10.0 %collective-permute-start.50 = (bf16[112,768]{1,0:T(8,128)(2,1)}, bf16[112,768]{1,0:T(8,128)(2,1)S(1)}, u32[]{:S(2)}, u32[]{:S(2)}) collective-permute-start(bf16[112,768]{1,0:T(8,128)(2,1)} %get-tuple-element.310), channel_id=1, source_target_pairs={{0,16},{4,20},{8,24},{12,28},{16,0},{20,4},{24,8},{28,12},{1,17},{... | collective-permute-start | bytes 516104 | tf_op jit(solution)/shard_map/ppermute | solution.py:493
  216.0 9.9 %collective-permute-start.64 = (bf16[192,768]{1,0:T(8,128)(2,1)S(1)}, bf16[192,768]{1,0:T(8,128)(2,1)S(1)}, u32[]{:S(2)}, u32[]{:S(2)}) collective-permute-start(bf16[192,768]{1,0:T(8,128)(2,1)S(1)} %collective-permute-done.62.rest_2_), channel_id=1, source_target_pairs={{8,0},{16,8},{24,16},{28,24},{20,28},{12,20},{4,12},{0,4},{9,1},{1... | collective-permute-start | bytes 884744 | tf_op jit(solution)/shard_map/ppermute | solution.py:505
  218.5 7.4 %collective-permute-start.51 = (bf16[96,768]{1,0:T(8,128)(2,1)S(1)}, bf16[96,768]{1,0:T(8,128)(2,1)S(1)}, u32[]{:S(2)}, u32[]{:S(2)}) collective-permute-start(bf16[96,768]{1,0:T(8,128)(2,1)S(1)} %get-tuple-element.311.rest_0_), channel_id=1, source_target_pairs={{0,8},{8,16},{16,24},{24,28},{28,20},{20,12},{12,4},{4,0},{1,9},{9... | collective-permute-start | bytes 442376 | tf_op jit(solution)/shard_map/ppermute | solution.py:505
  219.6 8.4 %collective-permute-start.52 = (bf16[96,768]{1,0:T(8,128)(2,1)S(1)}, bf16[96,768]{1,0:T(8,128)(2,1)S(1)}, u32[]{:S(2)}, u32[]{:S(2)}) collective-permute-start(bf16[96,768]{1,0:T(8,128)(2,1)S(1)} %get-tuple-element.311.rest_0_), channel_id=1, source_target_pairs={{8,0},{16,8},{24,16},{28,24},{20,28},{12,20},{4,12},{0,4},{9,1},{1... | collective-permute-start | bytes 442376 | tf_op jit(solution)/shard_map/ppermute | solution.py:505
  225.9 11.6 %collective-permute-start.65 = (bf16[192,768]{1,0:T(8,128)(2,1)S(1)}, bf16[192,768]{1,0:T(8,128)(2,1)S(1)}, u32[]{:S(2)}, u32[]{:S(2)}) collective-permute-start(bf16[192,768]{1,0:T(8,128)(2,1)S(1)} %collective-permute-done.63.rest_3_), channel_id=1, source_target_pairs={{0,8},{8,16},{16,24},{24,28},{28,20},{20,12},{12,4},{4,0},{1,9},{9... | collective-permute-start | bytes 884744 | tf_op jit(solution)/shard_map/ppermute | solution.py:505
  228.0 8.2 %collective-permute-start.53 = (bf16[96,768]{1,0:T(8,128)(2,1)S(1)}, bf16[96,768]{1,0:T(8,128)(2,1)S(1)}, u32[]{:S(2)}, u32[]{:S(2)}) collective-permute-start(bf16[96,768]{1,0:T(8,128)(2,1)S(1)} %collective-permute-done.51.rest_1_), channel_id=1, source_target_pairs={{0,8},{8,16},{16,24},{24,28},{28,20},{20,12},{12,4},{4,0},{1,9},{9... | collective-permute-start | bytes 442376 | tf_op jit(solution)/shard_map/ppermute | solution.py:505
  228.0 8.2 %collective-permute-start.54 = (bf16[96,768]{1,0:T(8,128)(2,1)S(1)}, bf16[96,768]{1,0:T(8,128)(2,1)}, u32[]{:S(2)}, u32[]{:S(2)}) collective-permute-start(bf16[96,768]{1,0:T(8,128)(2,1)S(1)} %collective-permute-done.52.rest_2_), channel_id=1, source_target_pairs={{8,0},{16,8},{24,16},{28,24},{20,28},{12,20},{4,12},{0,4},{9,1},{1... | collective-permute-start | bytes 442376 | tf_op jit(solution)/shard_map/ppermute | solution.py:505
  232.3 12.6 %collective-permute-start.66 = (bf16[192,768]{1,0:T(8,128)(2,1)S(1)}, bf16[192,768]{1,0:T(8,128)(2,1)S(1)}, u32[]{:S(2)}, u32[]{:S(2)}) collective-permute-start(bf16[192,768]{1,0:T(8,128)(2,1)S(1)} %collective-permute-done.64.rest_4_), channel_id=1, source_target_pairs={{8,0},{16,8},{24,16},{28,24},{20,28},{12,20},{4,12},{0,4},{9,1},{1... | collective-permute-start | bytes 884744 | tf_op jit(solution)/shard_map/ppermute | solution.py:505
  237.5 9.5 %collective-permute-start.67 = (bf16[192,768]{1,0:T(8,128)(2,1)S(1)}, bf16[192,768]{1,0:T(8,128)(2,1)S(1)}, u32[]{:S(2)}, u32[]{:S(2)}) collective-permute-start(bf16[192,768]{1,0:T(8,128)(2,1)S(1)} %collective-permute-done.65.rest_5_), channel_id=1, source_target_pairs={{0,8},{8,16},{16,24},{24,28},{28,20},{20,12},{12,4},{4,0},{1,9},{9... | collective-permute-start | bytes 884744 | tf_op jit(solution)/shard_map/ppermute | solution.py:788
  237.5 7.4 %collective-permute-start.56 = (bf16[96,768]{1,0:T(8,128)(2,1)}, bf16[96,768]{1,0:T(8,128)(2,1)S(1)}, u32[]{:S(2)}, u32[]{:S(2)}) collective-permute-start(bf16[96,768]{1,0:T(8,128)(2,1)} %collective-permute-done.54.rest_4_), channel_id=1, source_target_pairs={{8,0},{16,8},{24,16},{28,24},{20,28},{12,20},{4,12},{0,4},{9,1},{1... | collective-permute-start | bytes 442376 | tf_op jit(solution)/shard_map/ppermute | solution.py:505
  (41 other events, 304.8 us)

commit v5 on v4

--- a/solution.py
+++ b/solution.py
@@ -312,15 +312,19 @@
         send_ref[rows:, :] = both
 
 
+def halve_two_kernel(bits, me_ref, *rest):
+    for number, bit in enumerate(bits):
+        halve_kernel(bit, 0, me_ref, *rest[2 * number : 2 * number + 2], *rest[4 + 2 * number : 6 + 2 * number])
+
+
 def last_kernel(me_ref, kept, came, out_ref, small_ref):
     rows = out_ref.shape[0]
     out_ref[...] = (kept[:rows, :].astype(F32) + came[:rows, :].astype(F32)).astype(BF)
     small_ref[...] = from_halves(kept[rows:, :]) + from_halves(came[rows:, :])
 
 
-def finish_kernel(steps, pair, me_ref, *rest):
-    count = len(steps)
-    blocks, outs = rest[:count], rest[count:]
+def finish_kernel(steps, count, pair, me_ref, *rest):
+    blocks, outs = rest[: len(steps)], rest[len(steps) :]
     rows = blocks[0].shape[0]
     for number, back in enumerate(steps):
         group = group_at(me_ref, back, count)
@@ -343,6 +347,41 @@
                 out[pl.ds(pl.multiple_of((index - before) * rows, rows), rows), :] = block
 
             before += held
+
+
+def late_kernel(pair, me_ref, block_ref, *rest):
+    half = (len(rest) - 2) // 2
+    outs, scr, sems = rest[half : 2 * half], rest[-2], rest[-1]
+    group = group_at(me_ref, 4, 8)
+    bits = lax.rem(group, 2), lax.rem(group // 2, 2), group // 4
+    index = bits[0] * 4 + bits[1] * 2 + bits[2]
+    rows = block_ref.shape[0]
+    scr[...] = block_ref[...].astype(F32)
+    if pair:
+        part = rows // 2
+        other = bits[1] * 4 + bits[0] * 2 + bits[2]
+        copies = []
+        for number, place in enumerate((index, other)):
+            place = pl.ds(pl.multiple_of(place * part, part), part)
+            source = scr.at[pl.ds(number * part, part), :]
+            copies.append(pltpu.make_async_copy(source, outs[number].at[place, :], sems.at[number]))
+        for copy in copies:
+            copy.start()
+        for copy in copies:
+            copy.wait()
+        return
+    before = 0
+    for number, out in enumerate(outs):
+        held = out.shape[0] // rows
+
+        @pl.when((index >= before) & (index < before + held))
+        def _():
+            place = pl.ds(pl.multiple_of((index - before) * rows, rows), rows)
+            copy = pltpu.make_async_copy(scr, out.at[place, :], sems.at[number])
+            copy.start()
+            copy.wait()
+
+        before += held
 
 
 def ring_place(group, groups):
@@ -695,11 +734,23 @@
     def added(keep, got):
         return (keep.astype(F32) + got.astype(F32)).astype(BF)
 
-    def finish(blocks, outs, pair=False):
+    def finish(blocks, outs, pair=False, split=False):
+        early = blocks[:-1] if split else blocks
+        placed = call(
+            functools.partial(finish_kernel, ring_steps[: len(early)], groups, pair), (1,),
+            [(me_ref, None)] + [(b, whole(b)) for b in early],
+            outs, [whole(o) for o in outs], [], "finish", 2,
+        )
+        return (blocks[-1], outs, pair, placed) if split else placed
+
+    def finish_late(late, outs, pair, placed):
+        anywhere = pl.BlockSpec(memory_space=pl.ANY)
         return call(
-            functools.partial(finish_kernel, ring_steps, pair), (1,),
-            [(me_ref, None)] + [(b, whole(b)) for b in blocks],
-            outs, [whole(o) for o in outs], [], "finish", 2,
+            functools.partial(late_kernel, pair), (1,),
+            [(me_ref, None), (late, whole(late))] + [(p, anywhere) for p in placed],
+            outs, [anywhere] * len(outs),
+            [pltpu.VMEM(late.shape, F32), pltpu.SemaphoreType.DMA((len(outs),))], "late", 1,
+            {2 + i: i for i in range(len(outs))}, 8,
         )
 
     def whole_of(keep, send, bit):
@@ -740,8 +791,13 @@
     if near_dp:
         got_d, got_u = (swap(after(g, mids[1][0]), b) for g, b in ((send_d, 0), (send_u, 1)))
         mids.append(mid_step(2, sums[1], got_d, got_u))
-        keep_d, send_d = halve(1, (keep_d, after(got_d, mids[2][0])))
-        keep_u, send_u = halve(0, (keep_u, got_u))
+        ins = (keep_d, after(got_d, mids[2][0]), keep_u, got_u)
+        outs = [sds((full // 4, full), BF)] * 4
+        keep_d, send_d, keep_u, send_u = call(
+            functools.partial(halve_two_kernel, (1, 0)), (1,),
+            [(me_ref, None)] + [(a, whole(a)) for a in ins], outs, [whole(o) for o in outs], [],
+            "halve", 1,
+        )
         got_d, got_u = swap(send_d, 1), swap(send_u, 0)
         sums.append(back_step(2, mids[2], keep_d, keep_u))
     else:
@@ -766,13 +822,20 @@
         [pltpu.VMEM((full, full), F32)], "qkv_grad", 4,
     )
 
+    act_c = pp(act_oth, 1)
+    block_out = jnp.concatenate(
+        [jnp.where(core == 0, act_own, act_c), jnp.where(core == 0, act_c, act_own)], 2
+    )
+    near_sum = e2.astype(F32) + pp(e3, 1).astype(F32)
+    far = pp(near_sum.astype(BF), 2).astype(F32)
+    grad_x = (e0.astype(F32) + pp(e1, 1).astype(F32) + far).astype(BF)
     if near_dp:
         got = swap(send, 0)
         keep_du, send_du = halve(2, (keep_d, after(got_d, send)), (keep_u, got_u))
         got_du = swap(send_du, 2)
         keep, send = halve(1, (keep, got), tail=16)
         got = swap(send, 1)
-        pair = added(keep_du, got_du)
+        pair = after(added(keep_du, got_du), block_out, near_sum)
         ring_u = [ring_step(pair, pair)]
         keep, send = halve(2, (keep, got), tail=16)
         got = swap(send, 2)
@@ -786,12 +849,13 @@
         ring_u.append(ring_step(*together(ring_u[-1])))
         ring.append(ring_step(*together(ring[-1])))
         last_u = lax.ppermute(ring_u[-1][0], "dp", onward)
+        most = finish(
+            [after(pair, *ring[1]), *ring_u[0], *ring_u[1], *ring_u[2], last_u],
+            [sds((units, full), F32), sds((full, units), F32)], True, True,
+        )
         ring.append(ring_step(*together(ring[-1])))
-        last = lax.ppermute(ring[-1][0], "dp", onward)
-        grad_down, grad_up = finish(
-            [after(pair, *ring[2]), *ring_u[0], *ring_u[1], *ring_u[2], last_u],
-            [sds((units, full), F32), sds((full, units), F32)], True,
-        )
+        last = lax.ppermute(after(ring[-1], *most[3])[0], "dp", onward)
+        grad_down, grad_up = finish_late(*most)
         grad_in, grad_out = finish(
             [total, *ring[0], *ring[1], *ring[2], last],
             [sds((3 * width, full), F32), sds((width, full), F32)],
@@ -806,13 +870,6 @@
 
     grad_in = jnp.transpose(grad_in.reshape(3, width, full), (2, 0, 1))
 
-    act_c = pp(act_oth, 1)
-    block_out = jnp.concatenate(
-        [jnp.where(core == 0, act_own, act_c), jnp.where(core == 0, act_c, act_own)], 2
-    )
-    near_sum = e2.astype(F32) + pp(e3, 1).astype(F32)
-    far = pp(near_sum.astype(BF), 2).astype(F32)
-    grad_x = (e0.astype(F32) + pp(e1, 1).astype(F32) + far).astype(BF)
     return (
         jnp.swapaxes(block_out, 1, 2),
         raw,

time: 254 us -> 250 us (0.984)
    ppermute x9, waiting for transfers between devices: 18.4 us -> 15.1 us  [ring_step(): lax.ppermute(ahead, 'dp', onward)]
    ppermute x9, waiting for transfers between devices: 11.3 us -> 14.1 us  [ring_step(): lax.ppermute(behind, 'dp', backward)]
    unnamed x43 -> x39, local copies, waits for them, and re-layouts: 6.25 us -> 4 us
  transfers between devices with their start and end apart: 68 -> 68, of which waited for: 31 -> 32; matrix products, arithmetic and copies ran while one was open for 3% -> 3% of each run, Pallas kernels for 28% -> 28%
where the time goes in v5:
time: 250 us
  waiting for transfers between devices  107 us (43%)
  Pallas kernels  80.3 us (32%)
  starting transfers between devices  49.2 us (20%)
  other arithmetic  6.42 us (3%)
  local copies, waits for them, and re-layouts  5.38 us (2%)
    pallas_call x30, Pallas kernels, call(): pl.pallas_call(kernel, out_shape=outs, grid_spec=pltpu.PrefetchScalarGrid...  80.3 us
    ppermute x35, waiting for transfers between devices, pp(): return lax.ppermute(array, 'tensor', [(i, i ^ step) for i in range(4)])  32.6 us
    ppermute x8, waiting for transfers between devices, swap(): return lax.ppermute(array, 'dp', [(i, i ^ 1 << bit) for i in range(groups)])  27.8 us
    ppermute x35, starting transfers between devices, pp(): return lax.ppermute(array, 'tensor', [(i, i ^ step) for i in range(4)])  19.9 us
    ppermute x9, waiting for transfers between devices, ring_step(): lax.ppermute(ahead, 'dp', onward)  15.1 us
    ppermute x9, waiting for transfers between devices, ring_step(): lax.ppermute(behind, 'dp', backward)  14.1 us
    ppermute x4, waiting for transfers between devices, pair_step(): return lax.ppermute(pair, ('dp', 'tensor'), both_ways)  13.5 us
    ppermute x9, starting transfers between devices, ring_step(): lax.ppermute(behind, 'dp', backward)  10.6 us
  transfers between devices with their start and end apart: 68, of which 32 were waited for; matrix products, arithmetic and copies ran while one was open for 3% of the time, Pallas kernels for 28%

profile of v5, /device:TPU:0, one launch (start us, length us, event | category | flops | bytes accessed | tf_op | source)
XLA Modules:
  0.0 249.9 jit_solution(1559166334065989484)
XLA Ops:
  1.7 3.0 %collective-permute-start.1 = (bf16[96,192]{1,0:T(8,128)(2,1)S(1)}, bf16[96,192]{1,0:T(8,128)(2,1)S(1)}, u32[]{:S(2)}, u32[]{:S(2)}) collective-permute-start(bf16[96,192]{1,0:T(8,128)(2,1)S(1)} %bitcast.27), channel_id=1, source_target_pairs={{0,2},{1,3},{2,0},{3,1},{4,6},{5,7},{6,4},{7,5},{8,10},{9,11},{10,... | collective-permute-start | bytes 110600 | tf_op jit(solution)/shard_map/ppermute | solution.py:529
  6.4 1.6 collective-permute-start.4
  12.9 1.6 collective-permute-start.6
  14.9 2.9 %collective-permute-done.6.rest_3_ = bf16[96,576]{1,0:T(8,128)(2,1)S(1)} collective-permute-done((bf16[96,576]{1,0:T(8,128)(2,1)S(1)}, bf16[96,576]{1,0:T(8,128)(2,1)S(1)}, u32[]{:S(2)}, u32[]{:S(2)}) %collective-permute-start.6) | collective-permute-done | bytes 110624 | tf_op jit(solution)/shard_map/ppermute | solution.py:544
  17.8 1.6 collective-permute-done.7.rest_4_
  21.4 2.8 %collective-permute-done.8.rest_5_ = bf16[96,576]{1,0:T(8,128)(2,1)S(1)} collective-permute-done((bf16[96,576]{1,0:T(8,128)(2,1)S(1)}, bf16[96,576]{1,0:T(8,128)(2,1)S(1)}, u32[]{:S(2)}, u32[]{:S(2)}) %collective-permute-start.8) | collective-permute-done | bytes 110624 | tf_op jit(solution)/shard_map/ppermute | solution.py:544
  24.3 1.6 collective-permute-done.9.rest_6_
  27.9 2.8 %collective-permute-done.10.rest_7_ = bf16[96,576]{1,0:T(8,128)(2,1)S(1)} collective-permute-done((bf16[96,576]{1,0:T(8,128)(2,1)S(1)}, bf16[96,576]{1,0:T(8,128)(2,1)S(1)}, u32[]{:S(2)}, u32[]{:S(2)}) %collective-permute-start.10) | collective-permute-done | bytes 110624 | tf_op jit(solution)/shard_map/ppermute | solution.py:581
  34.8 12.6 %attend.1 = (bf16[3,3,512,512]{3,2,1,0:T(8,128)(2,1)}, bf16[3,3,512,512]{3,2,1,0:T(8,128)(2,1)}, bf16[3,3,192,512]{3,2,1,0:T(8,128)(2,1)}, bf16[3,192,256]{2,1,0...) custom-call(s32[5]{0:T(128)S(1)} %stack.32.me_ref.refs_0_, ...), custom_call_target="tpu_custom_call" | custom-call | flops 10 | bytes 1 | tf_op jit(solution)/shard_map/attend/pallas_call | solution.py:489
  50.3 7.4 %collective-permute-done.12.refs_3_ = bf16[3,192,256]{2,1,0:T(8,128)(2,1)S(1)} collective-permute-done((bf16[3,192,256]{2,1,0:T(8,128)(2,1)S(1)}, bf16[3,192,256]{2,1,0:T(8,128)(2,1)S(1)}, u32[]{:S(2)}, u32[]{:S(2)}) %collective-permute-start.12) | collective-permute-done | bytes 294944 | tf_op jit(solution)/shard_map/ppermute | solution.py:529
  57.7 1.6 collective-permute-done.19.rest_2_
  60.2 1.6 collective-permute-start.13
  62.3 6.5 %collective-permute-done.13.refs_4_ = bf16[3,192,256]{2,1,0:T(8,128)(2,1)S(1)} collective-permute-done((bf16[3,192,256]{2,1,0:T(8,128)(2,1)S(1)}, bf16[3,192,256]{2,1,0:T(8,128)(2,1)S(1)}, u32[]{:S(2)}, u32[]{:S(2)}) %collective-permute-start.13) | collective-permute-done | bytes 294944 | tf_op jit(solution)/shard_map/ppermute | solution.py:529
  68.8 1.9 collective-permute-done.20.rest_3_
  72.3 10.0 %collective-permute-done.21.rest_4_ = bf16[192,1920]{1,0:T(8,128)(2,1)S(1)} collective-permute-done((bf16[192,1920]{1,0:T(8,128)(2,1)S(1)}, bf16[192,1920]{1,0:T(8,128)(2,1)S(1)}, u32[]{:S(2)}, u32[]{:S(2)}) %collective-permute-start.21) | collective-permute-done | bytes 737312 | tf_op jit(solution)/shard_map/ppermute | solution.py:558
  83.6 4.0 %up.3 = (f32[3,256,768]{2,1,0:T(8,128)S(1)}, f32[3,256,128]{2,1,0:T(8,128)S(1)}, bf16[3,256,768]{2,1,0:T(8,128)(2,1)S(1)}, bf16[3,256,768]{2,1,0:T(8,128)(2,1)S(...) custom-call(s32[5]{0:T(128)S(1)} %stack.32.me_ref.refs_0_, ...), custom_call_target="tpu_custom_call" | custom-call | flops 10 | bytes 1 | tf_op jit(solution)/shard_map/up/pallas_call | solution.py:489
  88.6 3.8 %up.4 = (f32[3,256,768]{2,1,0:T(8,128)S(1)}, f32[3,256,128]{2,1,0:T(8,128)S(1)}, bf16[3,256,768]{2,1,0:T(8,128)(2,1)S(1)}, bf16[3,256,768]{2,1,0:T(8,128)(2,1)S(...) custom-call(s32[5]{0:T(128)S(1)} %stack.32.me_ref.refs_0_, ...), custom_call_target="tpu_custom_call", output_to_operand_aliasing={{0}: (17, {}), {1}: (18, {}), {2}: (19, {}), {3}: (20, {}),... | custom-call | flops 10 | bytes 1 | tf_op jit(solution)/shard_map/up/pallas_call | solution.py:489
  93.6 3.8 %up.5 = (f32[3,256,768]{2,1,0:T(8,128)S(1)}, f32[3,256,128]{2,1,0:T(8,128)S(1)}, bf16[3,256,768]{2,1,0:T(8,128)(2,1)S(1)}, bf16[3,256,768]{2,1,0:T(8,128)(2,1)S(...) custom-call(s32[5]{0:T(128)S(1)} %stack.32.me_ref.refs_0_, ...), custom_call_target="tpu_custom_call", output_to_operand_aliasing={{0}: (17, {}), {1}: (18, {}), {2}: (19, {}), {3}: (20, {}),... | custom-call | flops 10 | bytes 1 | tf_op jit(solution)/shard_map/up/pallas_call | solution.py:489
  99.7 3.7 %down.3 = (bf16[3,192,256]{2,1,0:T(8,128)(2,1)S(1)}, bf16[3,192,256]{2,1,0:T(8,128)(2,1)S(1)}, f32[3,256,768]{2,1,0:T(8,128)S(1)}, bf16[3,256,768]{2,1,0:T(8,128...) custom-call(s32[5]{0:T(128)S(1)} %stack.32.me_ref.refs_0_, ...), custom_call_target="tpu_custom_call" | custom-call | flops 10 | bytes 1 | tf_op jit(solution)/shard_map/down/pallas_call | solution.py:489
  104.4 3.8 %collective-permute-done.29.refs_3_ = bf16[1,256,768]{2,1,0:T(8,128)(2,1)S(1)} collective-permute-done((bf16[1,256,768]{2,1,0:T(8,128)(2,1)S(1)}, bf16[1,256,768]{2,1,0:T(8,128)(2,1)S(1)}, u32[]{:S(2)}, u32[]{:S(2)}) %collective-permute-start.29) | collective-permute-done | bytes 393248 | tf_op jit(solution)/shard_map/ppermute | solution.py:529
  108.2 3.7 %down.4 = (bf16[3,192,256]{2,1,0:T(8,128)(2,1)S(1)}, bf16[3,192,256]{2,1,0:T(8,128)(2,1)S(1)}, f32[3,256,768]{2,1,0:T(8,128)S(1)}, bf16[3,256,768]{2,1,0:T(8,128...) custom-call(s32[5]{0:T(128)S(1)} %stack.32.me_ref.refs_0_, ...), custom_call_target="tpu_custom_call", output_to_operand_aliasing={{0}: (15, {}), {1}: (16, {}), {2}: (17, {}), {3}: (18, {}),... | custom-call | flops 10 | bytes 1 | tf_op jit(solution)/shard_map/down/pallas_call | solution.py:489
  111.8 4.7 %collective-permute-done.26.refs_3_ = bf16[1,256,768]{2,1,0:T(8,128)(2,1)S(1)} collective-permute-done((bf16[1,256,768]{2,1,0:T(8,128)(2,1)S(1)}, bf16[1,256,768]{2,1,0:T(8,128)(2,1)S(1)}, u32[]{:S(2)}, u32[]{:S(2)}) %collective-permute-start.26) | collective-permute-done | bytes 393248 | tf_op jit(solution)/shard_map/ppermute | solution.py:529
  116.6 5.5 %collective-permute-done.28.refs_3_ = bf16[1,256,768]{2,1,0:T(8,128)(2,1)S(1)} collective-permute-done((bf16[1,256,768]{2,1,0:T(8,128)(2,1)S(1)}, bf16[1,256,768]{2,1,0:T(8,128)(2,1)S(1)}, u32[]{:S(2)}, u32[]{:S(2)}) %collective-permute-start.28) | collective-permute-done | bytes 393248 | tf_op jit(solution)/shard_map/ppermute | solution.py:529
  122.1 3.7 %down.5 = (bf16[3,192,256]{2,1,0:T(8,128)(2,1)S(1)}, bf16[3,192,256]{2,1,0:T(8,128)(2,1)S(1)}, f32[3,256,768]{2,1,0:T(8,128)S(1)}, bf16[3,256,768]{2,1,0:T(8,128...) custom-call(s32[5]{0:T(128)S(1)} %stack.32.me_ref.refs_0_, ...), custom_call_target="tpu_custom_call", output_to_operand_aliasing={{0}: (15, {}), {1}: (16, {}), {2}: (17, {}), {3}: (18, {}),... | custom-call | flops 10 | bytes 1 | tf_op jit(solution)/shard_map/down/pallas_call | solution.py:489
  127.8 1.6 mid.3
  129.5 3.7 %ffn_grad.3 = (bf16[384,768]{1,0:T(8,128)(2,1)S(1)}, bf16[384,768]{1,0:T(8,128)(2,1)S(1)}) custom-call(s32[5]{0:T(128)S(1)} %stack.32.me_ref.refs_0_, bf16[3,256,768]{2,1,0:T(8,128)(2,1)S(1)} %get-tuple-element.250.rest_0_, bf16[3,256,768]{2,1,0:T(8,128)(2,1)S(1)} %collective-permute-done.35.rest_1_, bf16[3,256,768]{2,1,0:T(8,128)(2,1)S(1)} %get-tuple-element.251.rest_2_, ...), custom_call_target="tpu_custom_call" | custom-call | flops 30 | bytes 1 | tf_op jit(solution)/shard_map/ffn_grad/pallas_call | solution.py:489
  133.2 3.5 %ffn_grad.2 = (bf16[384,768]{1,0:T(8,128)(2,1)S(1)}, bf16[384,768]{1,0:T(8,128)(2,1)S(1)}) custom-call(s32[5]{0:T(128)S(1)} %stack.32.me_ref.refs_0_, bf16[3,256,768]{2,1,0:T(8,128)(2,1)S(1)} %get-tuple-element.246.rest_0_, bf16[3,256,768]{2,1,0:T(8,128)(2,1)S(1)} %collective-permute-done.33.rest_1_, bf16[3,256,768]{2,1,0:T(8,128)(2,1)S(1)} %get-tuple-element.248.rest_2_, ...), custom_call_target="tpu_custom_call" | custom-call | flops 30 | bytes 1 | tf_op jit(solution)/shard_map/ffn_grad/pallas_call | solution.py:489
  137.9 1.6 mid.4
  143.3 5.3 %back.3 = (bf16[3,3,512,512]{3,2,1,0:T(8,128)(2,1)}, bf16[3,576,512]{2,1,0:T(8,128)(2,1)S(1)}, bf16[3,192,512]{2,1,0:T(8,128)(2,1)S(1)}, bf16[3,192,512]{2,1,0:T...) custom-call(s32[5]{0:T(128)S(1)} %stack.32.me_ref.refs_0_, ...), custom_call_target="tpu_custom_call" | custom-call | flops 10 | bytes 1 | tf_op jit(solution)/shard_map/back/pallas_call | solution.py:489
  148.6 5.3 %back.4 = (bf16[3,3,512,512]{3,2,1,0:T(8,128)(2,1)}, bf16[3,576,512]{2,1,0:T(8,128)(2,1)S(1)}, bf16[3,192,512]{2,1,0:T(8,128)(2,1)S(1)}, bf16[3,192,512]{2,1,0:T...) custom-call(s32[5]{0:T(128)S(1)} %stack.32.me_ref.refs_0_, ...), custom_call_target="tpu_custom_call", output_to_operand_aliasing={{0}: (7, {}), {1}: (8, {}), {2}: (9, {}), {3}: (10, {}), {4... | custom-call | flops 10 | bytes 1 | tf_op jit(solution)/shard_map/back/pallas_call | solution.py:489
  155.1 1.6 mid.5
  162.7 5.2 %back.5 = (bf16[3,3,512,512]{3,2,1,0:T(8,128)(2,1)}, bf16[3,576,512]{2,1,0:T(8,128)(2,1)S(1)}, bf16[3,192,512]{2,1,0:T(8,128)(2,1)S(1)}, bf16[3,192,512]{2,1,0:T...) custom-call(s32[5]{0:T(128)S(1)} %stack.32.me_ref.refs_0_, ...), custom_call_target="tpu_custom_call", output_to_operand_aliasing={{0}: (7, {}), {1}: (8, {}), {2}: (9, {}), {3}: (10, {}), {4... | custom-call | flops 10 | bytes 1 | tf_op jit(solution)/shard_map/back/pallas_call | solution.py:489
  168.0 2.7 %qkv_grad.1 = (bf16[400,768]{1,0:T(8,128)(2,1)S(1)}, bf16[400,768]{1,0:T(8,128)(2,1)S(1)}) custom-call(s32[5]{0:T(128)S(1)} %stack.32.me_ref.refs_0_, bf16[3,768,512]{2,1,0:T(8,128)(2,1)S(1)} %copy-done.1, bf16[3,576,512]{2,1,0:T(8,128)(2,1)S(1)} %get-tuple-element.299.rest_1_, bf16[3,192,256]{2,1,0:T(8,128)(2,1)S(1)} %get-tuple-element.182.refs_1_.rest_2_, ...), custom_call_target="tpu_custom_call" | custom-call | flops 40 | bytes 1 | tf_op jit(solution)/shard_map/qkv_grad/pallas_call | solution.py:489
  172.2 1.7 collective-permute-start.48
  174.0 13.7 %collective-permute-done.59 = bf16[192,768]{1,0:T(8,128)(2,1)S(1)} collective-permute-done((bf16[192,768]{1,0:T(8,128)(2,1)S(1)}, bf16[192,768]{1,0:T(8,128)(2,1)S(1)}, u32[]{:S(2)}, u32[]{:S(2)}) %collective-permute-start.59) | collective-permute-done | bytes 294944 | tf_op jit(solution)/shard_map/ppermute | solution.py:532
  187.8 2.0 collective-permute-start.61
  190.7 5.8 %collective-permute-done.60.rest_1_ = bf16[192,768]{1,0:T(8,128)(2,1)S(1)} collective-permute-done((bf16[192,768]{1,0:T(8,128)(2,1)S(1)}, bf16[192,768]{1,0:T(8,128)(2,1)S(1)}, u32[]{:S(2)}, u32[]{:S(2)}) %collective-permute-start.60) | collective-permute-done | bytes 294944 | tf_op jit(solution)/shard_map/ppermute | solution.py:544
  199.9 3.6 %collective-permute-done.49.rest_1_ = bf16[208,768]{1,0:T(8,128)(2,1)S(1)} collective-permute-done((bf16[208,768]{1,0:T(8,128)(2,1)S(1)}, bf16[208,768]{1,0:T(8,128)(2,1)S(1)}, u32[]{:S(2)}, u32[]{:S(2)}) %collective-permute-start.49) | collective-permute-done | bytes 319520 | tf_op jit(solution)/shard_map/ppermute | solution.py:532
  204.6 9.3 %collective-permute-done.50.came = bf16[112,768]{1,0:T(8,128)(2,1)S(1)} collective-permute-done((bf16[112,768]{1,0:T(8,128)(2,1)S(1)}, bf16[112,768]{1,0:T(8,128)(2,1)S(1)}, u32[]{:S(2)}, u32[]{:S(2)}) %collective-permute-start.50) | collective-permute-done | bytes 172064 | tf_op jit(solution)/shard_map/ppermute | solution.py:532
  220.0 3.9 %collective-permute-done.63.rest_4_ = bf16[192,768]{1,0:T(8,128)(2,1)S(1)} collective-permute-done((bf16[192,768]{1,0:T(8,128)(2,1)S(1)}, bf16[192,768]{1,0:T(8,128)(2,1)S(1)}, u32[]{:S(2)}, u32[]{:S(2)}) %collective-permute-start.63) | collective-permute-done | bytes 294944 | tf_op jit(solution)/shard_map/ppermute | solution.py:544
  223.8 2.1 collective-permute-done.52.rest_2_
  225.9 2.0 collective-permute-start.54
  227.9 2.3 fusion
  230.5 3.6 %collective-permute-done.53.rest_3_ = bf16[96,768]{1,0:T(8,128)(2,1)S(1)} collective-permute-done((bf16[96,768]{1,0:T(8,128)(2,1)S(1)}, bf16[96,768]{1,0:T(8,128)(2,1)S(1)}, u32[]{:S(2)}, u32[]{:S(2)}) %collective-permute-start.53) | collective-permute-done | bytes 147488 | tf_op jit(solution)/shard_map/ppermute | solution.py:544
  234.2 2.0 collective-permute-start.56
  236.9 2.3 collective-permute-done.65.rest_6_
  239.2 3.1 %finish.2 = (f32[768,768]{1,0:T(8,128)}, f32[768,768]{1,0:T(8,128)}) custom-call(s32[5]{0:T(128)S(1)} %stack.32.me_ref.refs_0_, bf16[192,768]{1,0:T(8,128)(2,1)S(1)} %add_convert_fusion.1.rest_0_, bf16[192,768]{1,0:T(8,128)(2,1)S(1)} %collective-permute-done.60.rest_1_, bf16[192,768]{1,0:T(8,128)(2,1)S(1)} %collective-permute-done.61.rest_2_, ...), custom_call_target="tpu_custom_call" | custom-call | flops 20 | bytes 1 | tf_op jit(solution)/shard_map/finish/pallas_call | solution.py:489
  247.5 2.4 finish.3
  (171 shorter events, 62.3 us)
Async XLA Ops:
  8.5 23.7 %collective-permute-start.2 = (bf16[3,192,512]{2,1,0:T(8,128)(2,1)}, bf16[3,192,512]{2,1,0:T(8,128)(2,1)S(1)}, u32[]{:S(2)}, u32[]{:S(2)}) collective-permute-start(bf16[3,192,512]{2,1,0:T(8,128)(2,1)} %bitcast.22), channel_id=1, source_target_pairs={{0,2},{1,3},{2,0},{3,1},{4,6},{5,7},{6,4},{7,5},{8,10},{9,11},{10,... | collective-permute-start | bytes 1769480 | tf_op jit(solution)/shard_map/ppermute | solution.py:529
  11.4 15.9 %collective-permute-start.14 = (bf16[96,1920]{1,0:T(8,128)(2,1)S(1)}, bf16[96,1920]{1,0:T(8,128)(2,1)S(1)}, u32[]{:S(2)}, u32[]{:S(2)}) collective-permute-start(bf16[96,1920]{1,0:T(8,128)(2,1)S(1)} %joined.5.first), channel_id=1, source_target_pairs={{0,1},{1,0},{2,3},{3,2},{4,5},{5,4},{6,7},{7,6},{8,9},{9,8},{10,11... | collective-permute-start | bytes 1105928 | tf_op jit(solution)/shard_map/ppermute | solution.py:529
  21.4 12.9 %collective-permute-start = (bf16[3,192,512]{2,1,0:T(8,128)(2,1)S(1)}, bf16[3,192,512]{2,1,0:T(8,128)(2,1)S(1)}, u32[]{:S(2)}, u32[]{:S(2)}) collective-permute-start(bf16[3,192,512]{2,1,0:T(8,128)(2,1)S(1)} %bitcast.23), channel_id=1, source_target_pairs={{0,1},{1,0},{2,3},{3,2},{4,5},{5,4},{6,7},{7,6},{8,9},{9,8},{10,11... | collective-permute-start | bytes 1769480 | tf_op jit(solution)/shard_map/ppermute | solution.py:529
  30.7 17.1 %collective-permute-start.15 = (bf16[192,1920]{1,0:T(8,128)(2,1)S(1)}, bf16[192,1920]{1,0:T(8,128)(2,1)S(1)}, u32[]{:S(2)}, u32[]{:S(2)}) collective-permute-start(bf16[192,1920]{1,0:T(8,128)(2,1)S(1)} %joined.6.rest_0_), channel_id=1, source_target_pairs={{0,8},{9,1},{2,10},{11,3},{8,16},{17,9},{10,18},{19,11},{16,24},{2... | collective-permute-start | bytes 2211848 | tf_op jit(solution)/shard_map/ppermute | solution.py:558
  32.8 14.6 %collective-permute-start.16 = (bf16[3,192,256]{2,1,0:T(8,128)(2,1)S(1)}, bf16[3,192,256]{2,1,0:T(8,128)(2,1)S(1)}, u32[]{:S(2)}, u32[]{:S(2)}) collective-permute-start(bf16[3,192,256]{2,1,0:T(8,128)(2,1)S(1)} %get-tuple-element.186), channel_id=1, source_target_pairs={{0,1},{1,0},{2,3},{3,2},{4,5},{5,4},{6,7},{7,6},{8,9},{9,8},{10,11... | collective-permute-start | bytes 884744 | tf_op jit(solution)/shard_map/ppermute | solution.py:529
  33.4 14.1 %collective-permute-start.17 = (bf16[3,192,256]{2,1,0:T(8,128)(2,1)S(1)}, bf16[3,192,256]{2,1,0:T(8,128)(2,1)S(1)}, u32[]{:S(2)}, u32[]{:S(2)}) collective-permute-start(bf16[3,192,256]{2,1,0:T(8,128)(2,1)S(1)} %get-tuple-element.187.refs_4_), channel_id=1, source_target_pairs={{0,2},{1,3},{2,0},{3,1},{4,6},{5,7},{6,4},{7,5},{8,10},{9,11},{10,... | collective-permute-start | bytes 884744 | tf_op jit(solution)/shard_map/ppermute | solution.py:529
  34.3 13.5 %collective-permute-start.18 = (bf16[3,192,256]{2,1,0:T(8,128)(2,1)S(1)}, bf16[3,192,256]{2,1,0:T(8,128)(2,1)S(1)}, u32[]{:S(2)}, u32[]{:S(2)}) collective-permute-start(bf16[3,192,256]{2,1,0:T(8,128)(2,1)S(1)} %get-tuple-element.186), channel_id=1, source_target_pairs={{0,3},{1,2},{2,1},{3,0},{4,7},{5,6},{6,5},{7,4},{8,11},{9,10},{10,... | collective-permute-start | bytes 884744 | tf_op jit(solution)/shard_map/ppermute | solution.py:529
  47.8 11.5 %collective-permute-start.19 = (bf16[192,1920]{1,0:T(8,128)(2,1)S(1)}, bf16[192,1920]{1,0:T(8,128)(2,1)S(1)}, u32[]{:S(2)}, u32[]{:S(2)}) collective-permute-start(bf16[192,1920]{1,0:T(8,128)(2,1)S(1)} %collective-permute-done.15.rest_1_), channel_id=1, source_target_pairs={{0,8},{9,1},{2,10},{11,3},{8,16},{17,9},{10,18},{19,11},{16,24},{2... | collective-permute-start | bytes 2211848 | tf_op jit(solution)/shard_map/ppermute | solution.py:558
  48.7 9.0 %collective-permute-start.12 = (bf16[3,192,256]{2,1,0:T(8,128)(2,1)S(1)}, bf16[3,192,256]{2,1,0:T(8,128)(2,1)S(1)}, u32[]{:S(2)}, u32[]{:S(2)}) collective-permute-start(bf16[3,192,256]{2,1,0:T(8,128)(2,1)S(1)} %get-tuple-element.182.refs_1_.rest_2_), channel_id=1, source_target_pairs={{0,2},{1,3},{2,0},{3,1},{4,6},{5,7},{6,4},{7,5},{8,10},{9,11},{10,... | collective-permute-start | bytes 884744 | tf_op jit(solution)/shard_map/ppermute | solution.py:529
  59.3 11.5 %collective-permute-start.20 = (bf16[192,1920]{1,0:T(8,128)(2,1)S(1)}, bf16[192,1920]{1,0:T(8,128)(2,1)S(1)}, u32[]{:S(2)}, u32[]{:S(2)}) collective-permute-start(bf16[192,1920]{1,0:T(8,128)(2,1)S(1)} %collective-permute-done.19.rest_2_), channel_id=1, source_target_pairs={{0,8},{9,1},{2,10},{11,3},{8,16},{17,9},{10,18},{19,11},{16,24},{2... | collective-permute-start | bytes 2211848 | tf_op jit(solution)/shard_map/ppermute | solution.py:558
  60.2 8.7 %collective-permute-start.13 = (bf16[3,192,256]{2,1,0:T(8,128)(2,1)S(1)}, bf16[3,192,256]{2,1,0:T(8,128)(2,1)S(1)}, u32[]{:S(2)}, u32[]{:S(2)}) collective-permute-start(bf16[3,192,256]{2,1,0:T(8,128)(2,1)S(1)} %get-tuple-element.183.rest_4_), channel_id=1, source_target_pairs={{0,3},{1,2},{2,1},{3,0},{4,7},{5,6},{6,5},{7,4},{8,11},{9,10},{10,... | collective-permute-start | bytes 884744 | tf_op jit(solution)/shard_map/ppermute | solution.py:529
  61.8 10.4 %collective-permute-start.22 = (bf16[192,1920]{1,0:T(8,128)(2,1)S(1)}, bf16[192,1920]{1,0:T(8,128)(2,1)S(1)}, u32[]{:S(2)}, u32[]{:S(2)}) collective-permute-start(bf16[192,1920]{1,0:T(8,128)(2,1)S(1)} %collective-permute-done.15.rest_1_), channel_id=1, source_target_pairs={{0,1},{1,0},{2,3},{3,2},{4,5},{5,4},{6,7},{7,6},{8,9},{9,8},{10,11... | collective-permute-start | bytes 2211848 | tf_op jit(solution)/shard_map/ppermute | solution.py:529
  61.8 10.4 %collective-permute-start.23 = (bf16[192,1920]{1,0:T(8,128)(2,1)S(1)}, bf16[192,1920]{1,0:T(8,128)(2,1)S(1)}, u32[]{:S(2)}, u32[]{:S(2)}) collective-permute-start(bf16[192,1920]{1,0:T(8,128)(2,1)S(1)} %collective-permute-done.19.rest_2_), channel_id=1, source_target_pairs={{0,1},{1,0},{2,3},{3,2},{4,5},{5,4},{6,7},{7,6},{8,9},{9,8},{10,11... | collective-permute-start | bytes 2211848 | tf_op jit(solution)/shard_map/ppermute | solution.py:529
  70.8 11.5 %collective-permute-start.21 = (bf16[192,1920]{1,0:T(8,128)(2,1)S(1)}, bf16[192,1920]{1,0:T(8,128)(2,1)S(1)}, u32[]{:S(2)}, u32[]{:S(2)}) collective-permute-start(bf16[192,1920]{1,0:T(8,128)(2,1)S(1)} %collective-permute-done.20.rest_3_), channel_id=1, source_target_pairs={{0,8},{9,1},{2,10},{11,3},{8,16},{17,9},{10,18},{19,11},{16,24},{2... | collective-permute-start | bytes 2211848 | tf_op jit(solution)/shard_map/ppermute | solution.py:558
  71.6 10.6 %collective-permute-start.24 = (bf16[192,1920]{1,0:T(8,128)(2,1)S(1)}, bf16[192,1920]{1,0:T(8,128)(2,1)S(1)}, u32[]{:S(2)}, u32[]{:S(2)}) collective-permute-start(bf16[192,1920]{1,0:T(8,128)(2,1)S(1)} %collective-permute-done.20.rest_3_), channel_id=1, source_target_pairs={{0,1},{1,0},{2,3},{3,2},{4,5},{5,4},{6,7},{7,6},{8,9},{9,8},{10,11... | collective-permute-start | bytes 2211848 | tf_op jit(solution)/shard_map/ppermute | solution.py:529
  71.7 11.8 %collective-permute-start.25 = (f32[1,768]{1,0:T(1,128)S(1)}, f32[1,768]{1,0:T(1,128)S(1)}, u32[]{:S(2)}, u32[]{:S(2)}) collective-permute-start(f32[1,768]{1,0:T(1,128)S(1)} %reshape.32.refs_15_), channel_id=1, source_target_pairs={{0,1},{1,0},{2,3},{3,2},{4,5},{5,4},{6,7},{7,6},{8,9},{9,8},{10,11... | collective-permute-start | bytes 9224 | tf_op jit(solution)/shard_map/ppermute | solution.py:529
  87.6 12.1 %collective-permute-start.27 = (bf16[1,256,768]{2,1,0:T(8,128)(2,1)S(1)}, bf16[1,256,768]{2,1,0:T(8,128)(2,1)S(1)}, u32[]{:S(2)}, u32[]{:S(2)}) collective-permute-start(bf16[1,256,768]{2,1,0:T(8,128)(2,1)S(1)} %get-tuple-element.214.refs_2_), channel_id=1, source_target_pairs={{0,2},{1,3},{2,0},{3,1},{4,6},{5,7},{6,4},{7,5},{8,10},{9,11},{10,... | collective-permute-start | bytes 1179656 | tf_op jit(solution)/shard_map/ppermute | solution.py:529
  92.4 15.7 %collective-permute-start.29 = (bf16[1,256,768]{2,1,0:T(8,128)(2,1)S(1)}, bf16[1,256,768]{2,1,0:T(8,128)(2,1)S(1)}, u32[]{:S(2)}, u32[]{:S(2)}) collective-permute-start(bf16[1,256,768]{2,1,0:T(8,128)(2,1)S(1)} %get-tuple-element.219.refs_2_), channel_id=1, source_target_pairs={{0,2},{1,3},{2,0},{3,1},{4,6},{5,7},{6,4},{7,5},{8,10},{9,11},{10,... | collective-permute-start | bytes 1179656 | tf_op jit(solution)/shard_map/ppermute | solution.py:529
  97.5 19.1 %collective-permute-start.26 = (bf16[1,256,768]{2,1,0:T(8,128)(2,1)S(1)}, bf16[1,256,768]{2,1,0:T(8,128)(2,1)S(1)}, u32[]{:S(2)}, u32[]{:S(2)}) collective-permute-start(bf16[1,256,768]{2,1,0:T(8,128)(2,1)S(1)} %get-tuple-element.213.refs_2_), channel_id=1, source_target_pairs={{0,2},{1,3},{2,0},{3,1},{4,6},{5,7},{6,4},{7,5},{8,10},{9,11},{10,... | collective-permute-start | bytes 1179656 | tf_op jit(solution)/shard_map/ppermute | solution.py:529
  103.4 18.7 %collective-permute-start.28 = (bf16[1,256,768]{2,1,0:T(8,128)(2,1)S(1)}, bf16[1,256,768]{2,1,0:T(8,128)(2,1)S(1)}, u32[]{:S(2)}, u32[]{:S(2)}) collective-permute-start(bf16[1,256,768]{2,1,0:T(8,128)(2,1)S(1)} %get-tuple-element.217.refs_2_), channel_id=1, source_target_pairs={{0,2},{1,3},{2,0},{3,1},{4,6},{5,7},{6,4},{7,5},{8,10},{9,11},{10,... | collective-permute-start | bytes 1179656 | tf_op jit(solution)/shard_map/ppermute | solution.py:529
  104.4 25.1 %collective-permute-start.35 = (bf16[3,256,768]{2,1,0:T(8,128)(2,1)S(1)}, bf16[3,256,768]{2,1,0:T(8,128)(2,1)S(1)}, u32[]{:S(2)}, u32[]{:S(2)}) collective-permute-start(bf16[3,256,768]{2,1,0:T(8,128)(2,1)S(1)} %get-tuple-element.250.rest_0_), channel_id=1, source_target_pairs={{0,1},{1,0},{2,3},{3,2},{4,5},{5,4},{6,7},{7,6},{8,9},{9,8},{10,11... | collective-permute-start | bytes 3538952 | tf_op jit(solution)/shard_map/ppermute | solution.py:529
  126.4 11.5 %collective-permute-start.32 = (bf16[1,256,768]{2,1,0:T(8,128)(2,1)S(1)}, bf16[1,256,768]{2,1,0:T(8,128)(2,1)S(1)}, u32[]{:S(2)}, u32[]{:S(2)}) collective-permute-start(bf16[1,256,768]{2,1,0:T(8,128)(2,1)S(1)} %get-tuple-element.245.refs_2_), channel_id=1, source_target_pairs={{0,2},{1,3},{2,0},{3,1},{4,6},{5,7},{6,4},{7,5},{8,10},{9,11},{10,... | collective-permute-start | bytes 1179656 | tf_op jit(solution)/shard_map/ppermute | solution.py:529
  139.5 15.0 %collective-permute-start.40 = (bf16[384,768]{1,0:T(8,128)(2,1)S(1)}, bf16[384,768]{1,0:T(8,128)(2,1)S(1)}, u32[]{:S(2)}, u32[]{:S(2)}) collective-permute-start(bf16[384,768]{1,0:T(8,128)(2,1)S(1)} %get-tuple-element.276), channel_id=1, source_target_pairs={{0,8},{4,12},{8,0},{12,4},{16,24},{20,28},{24,16},{28,20},{1,9},{5... | collective-permute-start | bytes 1769480 | tf_op jit(solution)/shard_map/ppermute | solution.py:532
  140.5 14.6 %collective-permute-start.39 = (bf16[384,768]{1,0:T(8,128)(2,1)S(1)}, bf16[384,768]{1,0:T(8,128)(2,1)S(1)}, u32[]{:S(2)}, u32[]{:S(2)}) collective-permute-start(bf16[384,768]{1,0:T(8,128)(2,1)S(1)} %get-tuple-element.274), channel_id=1, source_target_pairs={{0,4},{4,0},{8,12},{12,8},{16,20},{20,16},{24,28},{28,24},{1,5},{5... | collective-permute-start | bytes 1769480 | tf_op jit(solution)/shard_map/ppermute | solution.py:532
  141.1 12.7 %collective-permute-start.31 = (bf16[1,256,768]{2,1,0:T(8,128)(2,1)S(1)}, bf16[1,256,768]{2,1,0:T(8,128)(2,1)S(1)}, u32[]{:S(2)}, u32[]{:S(2)}) collective-permute-start(bf16[1,256,768]{2,1,0:T(8,128)(2,1)S(1)} %get-tuple-element.244.refs_2_), channel_id=1, source_target_pairs={{0,2},{1,3},{2,0},{3,1},{4,6},{5,7},{6,4},{7,5},{8,10},{9,11},{10,... | collective-permute-start | bytes 1179656 | tf_op jit(solution)/shard_map/ppermute | solution.py:529
  156.7 11.3 %collective-permute-start.45 = (bf16[3,256,768]{2,1,0:T(8,128)(2,1)S(1)}, bf16[3,256,768]{2,1,0:T(8,128)(2,1)S(1)}, u32[]{:S(2)}, u32[]{:S(2)}) collective-permute-start(bf16[3,256,768]{2,1,0:T(8,128)(2,1)S(1)} %get-tuple-element.300.rest_3_), channel_id=1, source_target_pairs={{0,1},{1,0},{2,3},{3,2},{4,5},{5,4},{6,7},{7,6},{8,9},{9,8},{10,11... | collective-permute-start | bytes 3538952 | tf_op jit(solution)/shard_map/ppermute | solution.py:529
  157.6 13.1 %collective-permute-start.57 = (bf16[192,768]{1,0:T(8,128)(2,1)S(1)}, bf16[192,768]{1,0:T(8,128)(2,1)S(1)}, u32[]{:S(2)}, u32[]{:S(2)}) collective-permute-start(bf16[192,768]{1,0:T(8,128)(2,1)S(1)} %get-tuple-element.320), channel_id=1, source_target_pairs={{0,8},{4,12},{8,0},{12,4},{16,24},{20,28},{24,16},{28,20},{1,9},{5... | collective-permute-start | bytes 884744 | tf_op jit(solution)/shard_map/ppermute | solution.py:532
  158.8 11.9 %collective-permute-start.58 = (bf16[192,768]{1,0:T(8,128)(2,1)S(1)}, bf16[192,768]{1,0:T(8,128)(2,1)S(1)}, u32[]{:S(2)}, u32[]{:S(2)}) collective-permute-start(bf16[192,768]{1,0:T(8,128)(2,1)S(1)} %get-tuple-element.322), channel_id=1, source_target_pairs={{0,4},{4,0},{8,12},{12,8},{16,20},{20,16},{24,28},{28,24},{1,5},{5... | collective-permute-start | bytes 884744 | tf_op jit(solution)/shard_map/ppermute | solution.py:532
  171.4 16.3 %collective-permute-start.59 = (bf16[192,768]{1,0:T(8,128)(2,1)S(1)}, bf16[192,768]{1,0:T(8,128)(2,1)S(1)}, u32[]{:S(2)}, u32[]{:S(2)}) collective-permute-start(bf16[192,768]{1,0:T(8,128)(2,1)S(1)} %get-tuple-element.324), channel_id=1, source_target_pairs={{0,16},{4,20},{8,24},{12,28},{16,0},{20,4},{24,8},{28,12},{1,17},{... | collective-permute-start | bytes 884744 | tf_op jit(solution)/shard_map/ppermute | solution.py:532
  172.2 17.6 %collective-permute-start.48 = (bf16[400,768]{1,0:T(8,128)(2,1)S(1)}, bf16[400,768]{1,0:T(8,128)(2,1)S(1)}, u32[]{:S(2)}, u32[]{:S(2)}) collective-permute-start(bf16[400,768]{1,0:T(8,128)(2,1)S(1)} %get-tuple-element.310), channel_id=1, source_target_pairs={{0,4},{4,0},{8,12},{12,8},{16,20},{20,16},{24,28},{28,24},{1,5},{5... | collective-permute-start | bytes 1843208 | tf_op jit(solution)/shard_map/ppermute | solution.py:532
  174.0 23.8 %collective-permute-start.43 = (bf16[3,192,512]{2,1,0:T(8,128)(2,1)S(1)}, bf16[3,192,512]{2,1,0:T(8,128)(2,1)S(1)}, u32[]{:S(2)}, u32[]{:S(2)}) collective-permute-start(bf16[3,192,512]{2,1,0:T(8,128)(2,1)S(1)} %get-tuple-element.296), channel_id=1, source_target_pairs={{0,1},{1,0},{2,3},{3,2},{4,5},{5,4},{6,7},{7,6},{8,9},{9,8},{10,11... | collective-permute-start | bytes 1769480 | tf_op jit(solution)/shard_map/ppermute | solution.py:529
  187.8 8.8 %collective-permute-start.60 = (bf16[192,768]{1,0:T(8,128)(2,1)S(1)}, bf16[192,768]{1,0:T(8,128)(2,1)S(1)}, u32[]{:S(2)}, u32[]{:S(2)}) collective-permute-start(bf16[192,768]{1,0:T(8,128)(2,1)S(1)} %add_convert_fusion.1.rest_0_), channel_id=1, source_target_pairs={{0,8},{8,16},{16,24},{24,28},{28,20},{20,12},{12,4},{4,0},{1,9},{9... | collective-permute-start | bytes 884744 | tf_op jit(solution)/shard_map/ppermute | solution.py:544
  187.8 9.9 %collective-permute-start.61 = (bf16[192,768]{1,0:T(8,128)(2,1)S(1)}, bf16[192,768]{1,0:T(8,128)(2,1)S(1)}, u32[]{:S(2)}, u32[]{:S(2)}) collective-permute-start(bf16[192,768]{1,0:T(8,128)(2,1)S(1)} %add_convert_fusion.1.rest_0_), channel_id=1, source_target_pairs={{8,0},{16,8},{24,16},{28,24},{20,28},{12,20},{4,12},{0,4},{9,1},{1... | collective-permute-start | bytes 884744 | tf_op jit(solution)/shard_map/ppermute | solution.py:544
  190.5 12.9 %collective-permute-start.49 = (bf16[208,768]{1,0:T(8,128)(2,1)S(1)}, bf16[208,768]{1,0:T(8,128)(2,1)S(1)}, u32[]{:S(2)}, u32[]{:S(2)}) collective-permute-start(bf16[208,768]{1,0:T(8,128)(2,1)S(1)} %get-tuple-element.312), channel_id=1, source_target_pairs={{0,8},{4,12},{8,0},{12,4},{16,24},{20,28},{24,16},{28,20},{1,9},{5... | collective-permute-start | bytes 958472 | tf_op jit(solution)/shard_map/ppermute | solution.py:532
  190.7 25.3 %collective-permute-start.30 = (bf16[3,192,256]{2,1,0:T(8,128)(2,1)S(1)}, bf16[3,192,256]{2,1,0:T(8,128)(2,1)}, u32[]{:S(2)}, u32[]{:S(2)}) collective-permute-start(bf16[3,192,256]{2,1,0:T(8,128)(2,1)S(1)} %get-tuple-element.239), channel_id=1, source_target_pairs={{0,1},{1,0},{2,3},{3,2},{4,5},{5,4},{6,7},{7,6},{8,9},{9,8},{10,11... | collective-permute-start | bytes 884744 | tf_op jit(solution)/shard_map/ppermute | solution.py:529
  196.5 31.4 %collective-permute-start.42 = (bf16[3,192,512]{2,1,0:T(8,128)(2,1)S(1)}, bf16[3,192,512]{2,1,0:T(8,128)(2,1)}, u32[]{:S(2)}, u32[]{:S(2)}) collective-permute-start(bf16[3,192,512]{2,1,0:T(8,128)(2,1)S(1)} %get-tuple-element.294), channel_id=1, source_target_pairs={{0,1},{1,0},{2,3},{3,2},{4,5},{5,4},{6,7},{7,6},{8,9},{9,8},{10,11... | collective-permute-start | bytes 1769480 | tf_op jit(solution)/shard_map/ppermute | solution.py:529
  197.8 18.8 %collective-permute-start.62 = (bf16[192,768]{1,0:T(8,128)(2,1)S(1)}, bf16[192,768]{1,0:T(8,128)(2,1)S(1)}, u32[]{:S(2)}, u32[]{:S(2)}) collective-permute-start(bf16[192,768]{1,0:T(8,128)(2,1)S(1)} %collective-permute-done.60.rest_1_), channel_id=1, source_target_pairs={{0,8},{8,16},{16,24},{24,28},{28,20},{20,12},{12,4},{4,0},{1,9},{9... | collective-permute-start | bytes 884744 | tf_op jit(solution)/shard_map/ppermute | solution.py:544
  198.7 29.2 %collective-permute-start.44 = (bf16[3,192,512]{2,1,0:T(8,128)(2,1)}, bf16[3,192,512]{2,1,0:T(8,128)(2,1)}, u32[]{:S(2)}, u32[]{:S(2)}) collective-permute-start(bf16[3,192,512]{2,1,0:T(8,128)(2,1)} %fusion.1), channel_id=1, source_target_pairs={{0,2},{1,3},{2,0},{3,1},{4,6},{5,7},{6,4},{7,5},{8,10},{9,11},{10,... | collective-permute-start | bytes 1769480 | tf_op jit(solution)/shard_map/ppermute | solution.py:529
  204.1 9.9 %collective-permute-start.50 = (bf16[112,768]{1,0:T(8,128)(2,1)S(1)}, bf16[112,768]{1,0:T(8,128)(2,1)S(1)}, u32[]{:S(2)}, u32[]{:S(2)}) collective-permute-start(bf16[112,768]{1,0:T(8,128)(2,1)S(1)} %get-tuple-element.314), channel_id=1, source_target_pairs={{0,16},{4,20},{8,24},{12,28},{16,0},{20,4},{24,8},{28,12},{1,17},{... | collective-permute-start | bytes 516104 | tf_op jit(solution)/shard_map/ppermute | solution.py:532
  213.9 9.9 %collective-permute-start.63 = (bf16[192,768]{1,0:T(8,128)(2,1)S(1)}, bf16[192,768]{1,0:T(8,128)(2,1)S(1)}, u32[]{:S(2)}, u32[]{:S(2)}) collective-permute-start(bf16[192,768]{1,0:T(8,128)(2,1)S(1)} %collective-permute-done.61.rest_2_), channel_id=1, source_target_pairs={{8,0},{16,8},{24,16},{28,24},{20,28},{12,20},{4,12},{0,4},{9,1},{1... | collective-permute-start | bytes 884744 | tf_op jit(solution)/shard_map/ppermute | solution.py:544
  216.6 9.3 %collective-permute-start.52 = (bf16[96,768]{1,0:T(8,128)(2,1)S(1)}, bf16[96,768]{1,0:T(8,128)(2,1)S(1)}, u32[]{:S(2)}, u32[]{:S(2)}) collective-permute-start(bf16[96,768]{1,0:T(8,128)(2,1)S(1)} %get-tuple-element.315.rest_0_), channel_id=1, source_target_pairs={{8,0},{16,8},{24,16},{28,24},{20,28},{12,20},{4,12},{0,4},{9,1},{1... | collective-permute-start | bytes 442376 | tf_op jit(solution)/shard_map/ppermute | solution.py:544
  223.8 13.0 %collective-permute-start.64 = (bf16[192,768]{1,0:T(8,128)(2,1)S(1)}, bf16[192,768]{1,0:T(8,128)(2,1)S(1)}, u32[]{:S(2)}, u32[]{:S(2)}) collective-permute-start(bf16[192,768]{1,0:T(8,128)(2,1)S(1)} %collective-permute-done.62.rest_3_), channel_id=1, source_target_pairs={{0,8},{8,16},{16,24},{24,28},{28,20},{20,12},{12,4},{4,0},{1,9},{9... | collective-permute-start | bytes 884744 | tf_op jit(solution)/shard_map/ppermute | solution.py:544
  225.9 8.2 %collective-permute-start.53 = (bf16[96,768]{1,0:T(8,128)(2,1)S(1)}, bf16[96,768]{1,0:T(8,128)(2,1)S(1)}, u32[]{:S(2)}, u32[]{:S(2)}) collective-permute-start(bf16[96,768]{1,0:T(8,128)(2,1)S(1)} %collective-permute-done.51.rest_1_), channel_id=1, source_target_pairs={{0,8},{8,16},{16,24},{24,28},{28,20},{20,12},{12,4},{4,0},{1,9},{9... | collective-permute-start | bytes 442376 | tf_op jit(solution)/shard_map/ppermute | solution.py:544
  225.9 8.2 %collective-permute-start.54 = (bf16[96,768]{1,0:T(8,128)(2,1)S(1)}, bf16[96,768]{1,0:T(8,128)(2,1)S(1)}, u32[]{:S(2)}, u32[]{:S(2)}) collective-permute-start(bf16[96,768]{1,0:T(8,128)(2,1)S(1)} %collective-permute-done.52.rest_2_), channel_id=1, source_target_pairs={{8,0},{16,8},{24,16},{28,24},{20,28},{12,20},{4,12},{0,4},{9,1},{1... | collective-permute-start | bytes 442376 | tf_op jit(solution)/shard_map/ppermute | solution.py:544
  230.2 9.0 %collective-permute-start.65 = (bf16[192,768]{1,0:T(8,128)(2,1)S(1)}, bf16[192,768]{1,0:T(8,128)(2,1)S(1)}, u32[]{:S(2)}, u32[]{:S(2)}) collective-permute-start(bf16[192,768]{1,0:T(8,128)(2,1)S(1)} %collective-permute-done.63.rest_4_), channel_id=1, source_target_pairs={{8,0},{16,8},{24,16},{28,24},{20,28},{12,20},{4,12},{0,4},{9,1},{1... | collective-permute-start | bytes 884744 | tf_op jit(solution)/shard_map/ppermute | solution.py:544
  234.1 8.2 %collective-permute-start.55 = (bf16[96,768]{1,0:T(8,128)(2,1)S(1)}, bf16[96,768]{1,0:T(8,128)(2,1)S(1)}, u32[]{:S(2)}, u32[]{:S(2)}) collective-permute-start(bf16[96,768]{1,0:T(8,128)(2,1)S(1)} %collective-permute-done.53.rest_3_), channel_id=1, source_target_pairs={{0,8},{8,16},{16,24},{24,28},{28,20},{20,12},{12,4},{4,0},{1,9},{9... | collective-permute-start | bytes 442376 | tf_op jit(solution)/shard_map/ppermute | solution.py:544
  234.2 8.1 %collective-permute-start.56 = (bf16[96,768]{1,0:T(8,128)(2,1)S(1)}, bf16[96,768]{1,0:T(8,128)(2,1)S(1)}, u32[]{:S(2)}, u32[]{:S(2)}) collective-permute-start(bf16[96,768]{1,0:T(8,128)(2,1)S(1)} %collective-permute-done.54.rest_4_), channel_id=1, source_target_pairs={{8,0},{16,8},{24,16},{28,24},{20,28},{12,20},{4,12},{0,4},{9,1},{1... | collective-permute-start | bytes 442376 | tf_op jit(solution)/shard_map/ppermute | solution.py:544
  236.8 8.2 %collective-permute-start.67 = (bf16[192,768]{1,0:T(8,128)(2,1)S(1)}, bf16[192,768]{1,0:T(8,128)(2,1)S(1)}, u32[]{:S(2)}, u32[]{:S(2)}) collective-permute-start(bf16[192,768]{1,0:T(8,128)(2,1)S(1)} %collective-permute-done.64.rest_5_), channel_id=1, source_target_pairs={{0,8},{8,16},{16,24},{24,28},{28,20},{20,12},{12,4},{4,0},{1,9},{9... | collective-permute-start | bytes 884744 | tf_op jit(solution)/shard_map/ppermute | solution.py:851
  (39 other events, 309.4 us)

commit v6 on v5

--- a/solution.py
+++ b/solution.py
@@ -200,7 +200,7 @@
 
 
 def back_kernel(
-    heads, me_ref, p_ref, qkv_ref, do_own_ref, do_oth_ref, w_ref, near_ref,
+    heads, unroll, me_ref, p_ref, qkv_ref, do_own_ref, do_oth_ref, w_ref, near_ref,
     lg_ref, dqkv_ref, e0, e1, e2, e3, vec_ref, do_scr, dx_scr, sum_scr,
 ):
     me = me_ref[0]
@@ -235,7 +235,7 @@
         dqkv_ref[0, pl.ds(pl.multiple_of(2 * width + h * size, size), size), :] = grad_value.astype(BF)
         return carry
 
-    lax.fori_loop(0, heads, one_head, 0)
+    lax.fori_loop(0, heads, one_head, 0, unroll=unroll)
     for number in range(2):
         vec_ref[0, number : number + 1, :] = jnp.transpose(sum_scr[number])[0:1, :]
     dx_scr[...] = dot(w_ref[...], dqkv_ref[0])
@@ -764,7 +764,7 @@
         [pltpu.VMEM((half, full), F32)], "mid", 16,
     )
     back = Stage(
-        functools.partial(back_kernel, heads),
+        functools.partial(back_kernel, heads, False),
         [sds(prev_logits.shape, BF), sds3(3 * width, slots, BF)] + [sds3(width, slots, BF)] * 4,
         [sds((1, 2, width), F32)],
         [pltpu.VMEM((width, slots), BF), pltpu.VMEM((full, slots), F32), pltpu.VMEM((2, width, 128), F32)],
@@ -799,6 +799,7 @@
             "halve", 1,
         )
         got_d, got_u = swap(send_d, 1), swap(send_u, 0)
+        back.kernel = functools.partial(back_kernel, heads, True)
         sums.append(back_step(2, mids[2], keep_d, keep_u))
     else:
         mids.append(mid_step(2, sums[1]))
@@ -847,13 +848,13 @@
         )
         ring = [ring_step(total, total)]
         ring_u.append(ring_step(*together(ring_u[-1])))
-        ring.append(ring_step(*together(ring[-1])))
+        ring.append(ring_step(*ring[-1]))
         last_u = lax.ppermute(ring_u[-1][0], "dp", onward)
         most = finish(
             [after(pair, *ring[1]), *ring_u[0], *ring_u[1], *ring_u[2], last_u],
             [sds((units, full), F32), sds((full, units), F32)], True, True,
         )
-        ring.append(ring_step(*together(ring[-1])))
+        ring.append(ring_step(*ring[-1]))
         last = lax.ppermute(after(ring[-1], *most[3])[0], "dp", onward)
         grad_down, grad_up = finish_late(*most)
         grad_in, grad_out = finish(

time: 250 us -> 249 us (level)
  no operation moved by 1% of the time
where the time goes in v6:
time: 249 us
  waiting for transfers between devices  106 us (43%)
  Pallas kernels  79.6 us (32%)
  starting transfers between devices  50.1 us (20%)
  other arithmetic  6.42 us (3%)
  local copies, waits for them, and re-layouts  5.38 us (2%)
    pallas_call x30, Pallas kernels, call(): pl.pallas_call(kernel, out_shape=outs, grid_spec=pltpu.PrefetchScalarGrid...  79.6 us
    ppermute x35, waiting for transfers between devices, pp(): return lax.ppermute(array, 'tensor', [(i, i ^ step) for i in range(4)])  32.6 us
    ppermute x8, waiting for transfers between devices, swap(): return lax.ppermute(array, 'dp', [(i, i ^ 1 << bit) for i in range(groups)])  27.8 us
    ppermute x35, starting transfers between devices, pp(): return lax.ppermute(array, 'tensor', [(i, i ^ step) for i in range(4)])  19.9 us
    ppermute x9, waiting for transfers between devices, ring_step(): lax.ppermute(ahead, 'dp', onward)  15.3 us
    ppermute x4, waiting for transfers between devices, pair_step(): return lax.ppermute(pair, ('dp', 'tensor'), both_ways)  13.5 us
    ppermute x9, waiting for transfers between devices, ring_step(): lax.ppermute(behind, 'dp', backward)  12.3 us
    ppermute x9, starting transfers between devices, ring_step(): lax.ppermute(behind, 'dp', backward)  10.7 us
  transfers between devices with their start and end apart: 68, of which 32 were waited for; matrix products, arithmetic and copies ran while one was open for 3% of the time, Pallas kernels for 28%

profile of v6, /device:TPU:0, one launch (start us, length us, event | category | flops | bytes accessed | tf_op | source)
XLA Modules:
  0.0 248.7 jit_solution(15706010821175718357)
XLA Ops:
  1.7 3.0 %collective-permute-start.1 = (bf16[96,192]{1,0:T(8,128)(2,1)S(1)}, bf16[96,192]{1,0:T(8,128)(2,1)S(1)}, u32[]{:S(2)}, u32[]{:S(2)}) collective-permute-start(bf16[96,192]{1,0:T(8,128)(2,1)S(1)} %bitcast.27), channel_id=1, source_target_pairs={{0,2},{1,3},{2,0},{3,1},{4,6},{5,7},{6,4},{7,5},{8,10},{9,11},{10,... | collective-permute-start | bytes 110600 | tf_op jit(solution)/shard_map/ppermute | solution.py:529
  6.4 1.6 collective-permute-start.4
  12.9 1.6 collective-permute-start.6
  14.9 2.9 %collective-permute-done.6.rest_3_ = bf16[96,576]{1,0:T(8,128)(2,1)S(1)} collective-permute-done((bf16[96,576]{1,0:T(8,128)(2,1)S(1)}, bf16[96,576]{1,0:T(8,128)(2,1)S(1)}, u32[]{:S(2)}, u32[]{:S(2)}) %collective-permute-start.6) | collective-permute-done | bytes 110624 | tf_op jit(solution)/shard_map/ppermute | solution.py:544
  17.8 1.6 collective-permute-done.7.rest_4_
  19.4 1.6 collective-permute-start.8
  21.4 2.8 %collective-permute-done.8.rest_5_ = bf16[96,576]{1,0:T(8,128)(2,1)S(1)} collective-permute-done((bf16[96,576]{1,0:T(8,128)(2,1)S(1)}, bf16[96,576]{1,0:T(8,128)(2,1)S(1)}, u32[]{:S(2)}, u32[]{:S(2)}) %collective-permute-start.8) | collective-permute-done | bytes 110624 | tf_op jit(solution)/shard_map/ppermute | solution.py:544
  24.3 1.6 collective-permute-done.9.rest_6_
  27.9 2.8 %collective-permute-done.10.rest_7_ = bf16[96,576]{1,0:T(8,128)(2,1)S(1)} collective-permute-done((bf16[96,576]{1,0:T(8,128)(2,1)S(1)}, bf16[96,576]{1,0:T(8,128)(2,1)S(1)}, u32[]{:S(2)}, u32[]{:S(2)}) %collective-permute-start.10) | collective-permute-done | bytes 110624 | tf_op jit(solution)/shard_map/ppermute | solution.py:581
  34.8 12.6 %attend.1 = (bf16[3,3,512,512]{3,2,1,0:T(8,128)(2,1)}, bf16[3,3,512,512]{3,2,1,0:T(8,128)(2,1)}, bf16[3,3,192,512]{3,2,1,0:T(8,128)(2,1)}, bf16[3,192,256]{2,1,0...) custom-call(s32[5]{0:T(128)S(1)} %stack.32.me_ref.refs_0_, ...), custom_call_target="tpu_custom_call" | custom-call | flops 10 | bytes 1 | tf_op jit(solution)/shard_map/attend/pallas_call | solution.py:489
  50.3 7.4 %collective-permute-done.12.refs_3_ = bf16[3,192,256]{2,1,0:T(8,128)(2,1)S(1)} collective-permute-done((bf16[3,192,256]{2,1,0:T(8,128)(2,1)S(1)}, bf16[3,192,256]{2,1,0:T(8,128)(2,1)S(1)}, u32[]{:S(2)}, u32[]{:S(2)}) %collective-permute-start.12) | collective-permute-done | bytes 294944 | tf_op jit(solution)/shard_map/ppermute | solution.py:529
  57.7 1.6 collective-permute-done.19.rest_2_
  60.2 1.6 collective-permute-start.13
  62.3 6.5 %collective-permute-done.13.refs_4_ = bf16[3,192,256]{2,1,0:T(8,128)(2,1)S(1)} collective-permute-done((bf16[3,192,256]{2,1,0:T(8,128)(2,1)S(1)}, bf16[3,192,256]{2,1,0:T(8,128)(2,1)S(1)}, u32[]{:S(2)}, u32[]{:S(2)}) %collective-permute-start.13) | collective-permute-done | bytes 294944 | tf_op jit(solution)/shard_map/ppermute | solution.py:529
  68.8 1.9 collective-permute-done.20.rest_3_
  72.3 10.0 %collective-permute-done.21.rest_4_ = bf16[192,1920]{1,0:T(8,128)(2,1)S(1)} collective-permute-done((bf16[192,1920]{1,0:T(8,128)(2,1)S(1)}, bf16[192,1920]{1,0:T(8,128)(2,1)S(1)}, u32[]{:S(2)}, u32[]{:S(2)}) %collective-permute-start.21) | collective-permute-done | bytes 737312 | tf_op jit(solution)/shard_map/ppermute | solution.py:558
  83.6 4.0 %up.3 = (f32[3,256,768]{2,1,0:T(8,128)S(1)}, f32[3,256,128]{2,1,0:T(8,128)S(1)}, bf16[3,256,768]{2,1,0:T(8,128)(2,1)S(1)}, bf16[3,256,768]{2,1,0:T(8,128)(2,1)S(...) custom-call(s32[5]{0:T(128)S(1)} %stack.32.me_ref.refs_0_, ...), custom_call_target="tpu_custom_call" | custom-call | flops 10 | bytes 1 | tf_op jit(solution)/shard_map/up/pallas_call | solution.py:489
  88.6 3.8 %up.4 = (f32[3,256,768]{2,1,0:T(8,128)S(1)}, f32[3,256,128]{2,1,0:T(8,128)S(1)}, bf16[3,256,768]{2,1,0:T(8,128)(2,1)S(1)}, bf16[3,256,768]{2,1,0:T(8,128)(2,1)S(...) custom-call(s32[5]{0:T(128)S(1)} %stack.32.me_ref.refs_0_, ...), custom_call_target="tpu_custom_call", output_to_operand_aliasing={{0}: (17, {}), {1}: (18, {}), {2}: (19, {}), {3}: (20, {}),... | custom-call | flops 10 | bytes 1 | tf_op jit(solution)/shard_map/up/pallas_call | solution.py:489
  93.6 3.8 %up.5 = (f32[3,256,768]{2,1,0:T(8,128)S(1)}, f32[3,256,128]{2,1,0:T(8,128)S(1)}, bf16[3,256,768]{2,1,0:T(8,128)(2,1)S(1)}, bf16[3,256,768]{2,1,0:T(8,128)(2,1)S(...) custom-call(s32[5]{0:T(128)S(1)} %stack.32.me_ref.refs_0_, ...), custom_call_target="tpu_custom_call", output_to_operand_aliasing={{0}: (17, {}), {1}: (18, {}), {2}: (19, {}), {3}: (20, {}),... | custom-call | flops 10 | bytes 1 | tf_op jit(solution)/shard_map/up/pallas_call | solution.py:489
  99.7 3.7 %down.3 = (bf16[3,192,256]{2,1,0:T(8,128)(2,1)S(1)}, bf16[3,192,256]{2,1,0:T(8,128)(2,1)S(1)}, f32[3,256,768]{2,1,0:T(8,128)S(1)}, bf16[3,256,768]{2,1,0:T(8,128...) custom-call(s32[5]{0:T(128)S(1)} %stack.32.me_ref.refs_0_, ...), custom_call_target="tpu_custom_call" | custom-call | flops 10 | bytes 1 | tf_op jit(solution)/shard_map/down/pallas_call | solution.py:489
  104.4 3.8 %collective-permute-done.29.refs_3_ = bf16[1,256,768]{2,1,0:T(8,128)(2,1)S(1)} collective-permute-done((bf16[1,256,768]{2,1,0:T(8,128)(2,1)S(1)}, bf16[1,256,768]{2,1,0:T(8,128)(2,1)S(1)}, u32[]{:S(2)}, u32[]{:S(2)}) %collective-permute-start.29) | collective-permute-done | bytes 393248 | tf_op jit(solution)/shard_map/ppermute | solution.py:529
  108.2 3.7 %down.4 = (bf16[3,192,256]{2,1,0:T(8,128)(2,1)S(1)}, bf16[3,192,256]{2,1,0:T(8,128)(2,1)S(1)}, f32[3,256,768]{2,1,0:T(8,128)S(1)}, bf16[3,256,768]{2,1,0:T(8,128...) custom-call(s32[5]{0:T(128)S(1)} %stack.32.me_ref.refs_0_, ...), custom_call_target="tpu_custom_call", output_to_operand_aliasing={{0}: (15, {}), {1}: (16, {}), {2}: (17, {}), {3}: (18, {}),... | custom-call | flops 10 | bytes 1 | tf_op jit(solution)/shard_map/down/pallas_call | solution.py:489
  111.8 4.7 %collective-permute-done.26.refs_3_ = bf16[1,256,768]{2,1,0:T(8,128)(2,1)S(1)} collective-permute-done((bf16[1,256,768]{2,1,0:T(8,128)(2,1)S(1)}, bf16[1,256,768]{2,1,0:T(8,128)(2,1)S(1)}, u32[]{:S(2)}, u32[]{:S(2)}) %collective-permute-start.26) | collective-permute-done | bytes 393248 | tf_op jit(solution)/shard_map/ppermute | solution.py:529
  116.6 5.5 %collective-permute-done.28.refs_3_ = bf16[1,256,768]{2,1,0:T(8,128)(2,1)S(1)} collective-permute-done((bf16[1,256,768]{2,1,0:T(8,128)(2,1)S(1)}, bf16[1,256,768]{2,1,0:T(8,128)(2,1)S(1)}, u32[]{:S(2)}, u32[]{:S(2)}) %collective-permute-start.28) | collective-permute-done | bytes 393248 | tf_op jit(solution)/shard_map/ppermute | solution.py:529
  122.1 3.7 %down.5 = (bf16[3,192,256]{2,1,0:T(8,128)(2,1)S(1)}, bf16[3,192,256]{2,1,0:T(8,128)(2,1)S(1)}, f32[3,256,768]{2,1,0:T(8,128)S(1)}, bf16[3,256,768]{2,1,0:T(8,128...) custom-call(s32[5]{0:T(128)S(1)} %stack.32.me_ref.refs_0_, ...), custom_call_target="tpu_custom_call", output_to_operand_aliasing={{0}: (15, {}), {1}: (16, {}), {2}: (17, {}), {3}: (18, {}),... | custom-call | flops 10 | bytes 1 | tf_op jit(solution)/shard_map/down/pallas_call | solution.py:489
  127.8 1.6 mid.3
  129.5 3.7 %ffn_grad.3 = (bf16[384,768]{1,0:T(8,128)(2,1)S(1)}, bf16[384,768]{1,0:T(8,128)(2,1)S(1)}) custom-call(s32[5]{0:T(128)S(1)} %stack.32.me_ref.refs_0_, bf16[3,256,768]{2,1,0:T(8,128)(2,1)S(1)} %get-tuple-element.246.rest_0_, bf16[3,256,768]{2,1,0:T(8,128)(2,1)S(1)} %collective-permute-done.35.rest_1_, bf16[3,256,768]{2,1,0:T(8,128)(2,1)S(1)} %get-tuple-element.247.rest_2_, ...), custom_call_target="tpu_custom_call" | custom-call | flops 30 | bytes 1 | tf_op jit(solution)/shard_map/ffn_grad/pallas_call | solution.py:489
  133.2 3.5 %ffn_grad.2 = (bf16[384,768]{1,0:T(8,128)(2,1)S(1)}, bf16[384,768]{1,0:T(8,128)(2,1)S(1)}) custom-call(s32[5]{0:T(128)S(1)} %stack.32.me_ref.refs_0_, bf16[3,256,768]{2,1,0:T(8,128)(2,1)S(1)} %get-tuple-element.242.rest_0_, bf16[3,256,768]{2,1,0:T(8,128)(2,1)S(1)} %collective-permute-done.33.rest_1_, bf16[3,256,768]{2,1,0:T(8,128)(2,1)S(1)} %get-tuple-element.244.rest_2_, ...), custom_call_target="tpu_custom_call" | custom-call | flops 30 | bytes 1 | tf_op jit(solution)/shard_map/ffn_grad/pallas_call | solution.py:489
  137.9 1.6 mid.4
  143.3 5.3 %back.3 = (bf16[3,3,512,512]{3,2,1,0:T(8,128)(2,1)}, bf16[3,576,512]{2,1,0:T(8,128)(2,1)S(1)}, bf16[3,192,512]{2,1,0:T(8,128)(2,1)S(1)}, bf16[3,192,512]{2,1,0:T...) custom-call(s32[5]{0:T(128)S(1)} %stack.32.me_ref.refs_0_, ...), custom_call_target="tpu_custom_call" | custom-call | flops 10 | bytes 1 | tf_op jit(solution)/shard_map/back/pallas_call | solution.py:489
  148.6 5.3 %back.4 = (bf16[3,3,512,512]{3,2,1,0:T(8,128)(2,1)}, bf16[3,576,512]{2,1,0:T(8,128)(2,1)S(1)}, bf16[3,192,512]{2,1,0:T(8,128)(2,1)S(1)}, bf16[3,192,512]{2,1,0:T...) custom-call(s32[5]{0:T(128)S(1)} %stack.32.me_ref.refs_0_, ...), custom_call_target="tpu_custom_call", output_to_operand_aliasing={{0}: (7, {}), {1}: (8, {}), {2}: (9, {}), {3}: (10, {}), {4... | custom-call | flops 10 | bytes 1 | tf_op jit(solution)/shard_map/back/pallas_call | solution.py:489
  155.1 1.6 mid.5
  162.7 4.6 %back.5 = (bf16[3,3,512,512]{3,2,1,0:T(8,128)(2,1)}, bf16[3,576,512]{2,1,0:T(8,128)(2,1)S(1)}, bf16[3,192,512]{2,1,0:T(8,128)(2,1)S(1)}, bf16[3,192,512]{2,1,0:T...) custom-call(s32[5]{0:T(128)S(1)} %stack.32.me_ref.refs_0_, ...), custom_call_target="tpu_custom_call", output_to_operand_aliasing={{0}: (7, {}), {1}: (8, {}), {2}: (9, {}), {3}: (10, {}), {4... | custom-call | flops 10 | bytes 1 | tf_op jit(solution)/shard_map/back/pallas_call | solution.py:489
  167.4 2.7 %qkv_grad.1 = (bf16[400,768]{1,0:T(8,128)(2,1)S(1)}, bf16[400,768]{1,0:T(8,128)(2,1)S(1)}) custom-call(s32[5]{0:T(128)S(1)} %stack.32.me_ref.refs_0_, bf16[3,768,512]{2,1,0:T(8,128)(2,1)S(1)} %copy-done.1, bf16[3,576,512]{2,1,0:T(8,128)(2,1)S(1)} %get-tuple-element.295.rest_1_, bf16[3,192,256]{2,1,0:T(8,128)(2,1)S(1)} %get-tuple-element.178.refs_1_.rest_2_, ...), custom_call_target="tpu_custom_call" | custom-call | flops 40 | bytes 1 | tf_op jit(solution)/shard_map/qkv_grad/pallas_call | solution.py:489
  171.6 1.8 collective-permute-start.48
  173.4 13.7 %collective-permute-done.59 = bf16[192,768]{1,0:T(8,128)(2,1)S(1)} collective-permute-done((bf16[192,768]{1,0:T(8,128)(2,1)S(1)}, bf16[192,768]{1,0:T(8,128)(2,1)S(1)}, u32[]{:S(2)}, u32[]{:S(2)}) %collective-permute-start.59) | collective-permute-done | bytes 294944 | tf_op jit(solution)/shard_map/ppermute | solution.py:532
  187.2 2.0 collective-permute-start.61
  190.3 5.6 %collective-permute-done.60.rest_1_ = bf16[192,768]{1,0:T(8,128)(2,1)S(1)} collective-permute-done((bf16[192,768]{1,0:T(8,128)(2,1)S(1)}, bf16[192,768]{1,0:T(8,128)(2,1)S(1)}, u32[]{:S(2)}, u32[]{:S(2)}) %collective-permute-start.60) | collective-permute-done | bytes 294944 | tf_op jit(solution)/shard_map/ppermute | solution.py:544
  199.5 3.6 %collective-permute-done.49.rest_1_ = bf16[208,768]{1,0:T(8,128)(2,1)S(1)} collective-permute-done((bf16[208,768]{1,0:T(8,128)(2,1)S(1)}, bf16[208,768]{1,0:T(8,128)(2,1)S(1)}, u32[]{:S(2)}, u32[]{:S(2)}) %collective-permute-start.49) | collective-permute-done | bytes 319520 | tf_op jit(solution)/shard_map/ppermute | solution.py:532
  204.0 9.3 %collective-permute-done.50.came = bf16[112,768]{1,0:T(8,128)(2,1)S(1)} collective-permute-done((bf16[112,768]{1,0:T(8,128)(2,1)S(1)}, bf16[112,768]{1,0:T(8,128)(2,1)S(1)}, u32[]{:S(2)}, u32[]{:S(2)}) %collective-permute-start.50) | collective-permute-done | bytes 172064 | tf_op jit(solution)/shard_map/ppermute | solution.py:532
  219.3 3.9 %collective-permute-done.63.rest_4_ = bf16[192,768]{1,0:T(8,128)(2,1)S(1)} collective-permute-done((bf16[192,768]{1,0:T(8,128)(2,1)S(1)}, bf16[192,768]{1,0:T(8,128)(2,1)S(1)}, u32[]{:S(2)}, u32[]{:S(2)}) %collective-permute-start.63) | collective-permute-done | bytes 294944 | tf_op jit(solution)/shard_map/ppermute | solution.py:544
  225.3 2.3 fusion
  227.6 2.0 collective-permute-start.65
  229.6 4.0 %collective-permute-done.53.rest_3_ = bf16[96,768]{1,0:T(8,128)(2,1)S(1)} collective-permute-done((bf16[96,768]{1,0:T(8,128)(2,1)S(1)}, bf16[96,768]{1,0:T(8,128)(2,1)S(1)}, u32[]{:S(2)}, u32[]{:S(2)}) %collective-permute-start.53) | collective-permute-done | bytes 147488 | tf_op jit(solution)/shard_map/ppermute | solution.py:544
  233.6 2.0 collective-permute-start.56
  236.3 1.7 collective-permute-done.65.rest_6_
  238.0 3.1 %finish.2 = (f32[768,768]{1,0:T(8,128)}, f32[768,768]{1,0:T(8,128)}) custom-call(s32[5]{0:T(128)S(1)} %stack.32.me_ref.refs_0_, bf16[192,768]{1,0:T(8,128)(2,1)S(1)} %add_convert_fusion.1.rest_0_, bf16[192,768]{1,0:T(8,128)(2,1)S(1)} %collective-permute-done.60.rest_1_, bf16[192,768]{1,0:T(8,128)(2,1)S(1)} %collective-permute-done.61.rest_2_, ...), custom_call_target="tpu_custom_call" | custom-call | flops 20 | bytes 1 | tf_op jit(solution)/shard_map/finish/pallas_call | solution.py:489
  246.3 2.4 finish.3
  (171 shorter events, 62.7 us)
Async XLA Ops:
  8.5 23.7 %collective-permute-start.2 = (bf16[3,192,512]{2,1,0:T(8,128)(2,1)}, bf16[3,192,512]{2,1,0:T(8,128)(2,1)S(1)}, u32[]{:S(2)}, u32[]{:S(2)}) collective-permute-start(bf16[3,192,512]{2,1,0:T(8,128)(2,1)} %bitcast.22), channel_id=1, source_target_pairs={{0,2},{1,3},{2,0},{3,1},{4,6},{5,7},{6,4},{7,5},{8,10},{9,11},{10,... | collective-permute-start | bytes 1769480 | tf_op jit(solution)/shard_map/ppermute | solution.py:529
  11.4 15.9 %collective-permute-start.14 = (bf16[96,1920]{1,0:T(8,128)(2,1)S(1)}, bf16[96,1920]{1,0:T(8,128)(2,1)S(1)}, u32[]{:S(2)}, u32[]{:S(2)}) collective-permute-start(bf16[96,1920]{1,0:T(8,128)(2,1)S(1)} %joined.5.first), channel_id=1, source_target_pairs={{0,1},{1,0},{2,3},{3,2},{4,5},{5,4},{6,7},{7,6},{8,9},{9,8},{10,11... | collective-permute-start | bytes 1105928 | tf_op jit(solution)/shard_map/ppermute | solution.py:529
  21.4 12.9 %collective-permute-start = (bf16[3,192,512]{2,1,0:T(8,128)(2,1)S(1)}, bf16[3,192,512]{2,1,0:T(8,128)(2,1)S(1)}, u32[]{:S(2)}, u32[]{:S(2)}) collective-permute-start(bf16[3,192,512]{2,1,0:T(8,128)(2,1)S(1)} %bitcast.23), channel_id=1, source_target_pairs={{0,1},{1,0},{2,3},{3,2},{4,5},{5,4},{6,7},{7,6},{8,9},{9,8},{10,11... | collective-permute-start | bytes 1769480 | tf_op jit(solution)/shard_map/ppermute | solution.py:529
  30.7 17.1 %collective-permute-start.15 = (bf16[192,1920]{1,0:T(8,128)(2,1)S(1)}, bf16[192,1920]{1,0:T(8,128)(2,1)S(1)}, u32[]{:S(2)}, u32[]{:S(2)}) collective-permute-start(bf16[192,1920]{1,0:T(8,128)(2,1)S(1)} %joined.6.rest_0_), channel_id=1, source_target_pairs={{0,8},{9,1},{2,10},{11,3},{8,16},{17,9},{10,18},{19,11},{16,24},{2... | collective-permute-start | bytes 2211848 | tf_op jit(solution)/shard_map/ppermute | solution.py:558
  32.8 14.6 %collective-permute-start.16 = (bf16[3,192,256]{2,1,0:T(8,128)(2,1)S(1)}, bf16[3,192,256]{2,1,0:T(8,128)(2,1)S(1)}, u32[]{:S(2)}, u32[]{:S(2)}) collective-permute-start(bf16[3,192,256]{2,1,0:T(8,128)(2,1)S(1)} %get-tuple-element.182), channel_id=1, source_target_pairs={{0,1},{1,0},{2,3},{3,2},{4,5},{5,4},{6,7},{7,6},{8,9},{9,8},{10,11... | collective-permute-start | bytes 884744 | tf_op jit(solution)/shard_map/ppermute | solution.py:529
  33.4 14.1 %collective-permute-start.17 = (bf16[3,192,256]{2,1,0:T(8,128)(2,1)S(1)}, bf16[3,192,256]{2,1,0:T(8,128)(2,1)S(1)}, u32[]{:S(2)}, u32[]{:S(2)}) collective-permute-start(bf16[3,192,256]{2,1,0:T(8,128)(2,1)S(1)} %get-tuple-element.183.refs_4_), channel_id=1, source_target_pairs={{0,2},{1,3},{2,0},{3,1},{4,6},{5,7},{6,4},{7,5},{8,10},{9,11},{10,... | collective-permute-start | bytes 884744 | tf_op jit(solution)/shard_map/ppermute | solution.py:529
  34.3 13.5 %collective-permute-start.18 = (bf16[3,192,256]{2,1,0:T(8,128)(2,1)S(1)}, bf16[3,192,256]{2,1,0:T(8,128)(2,1)S(1)}, u32[]{:S(2)}, u32[]{:S(2)}) collective-permute-start(bf16[3,192,256]{2,1,0:T(8,128)(2,1)S(1)} %get-tuple-element.182), channel_id=1, source_target_pairs={{0,3},{1,2},{2,1},{3,0},{4,7},{5,6},{6,5},{7,4},{8,11},{9,10},{10,... | collective-permute-start | bytes 884744 | tf_op jit(solution)/shard_map/ppermute | solution.py:529
  47.8 11.5 %collective-permute-start.19 = (bf16[192,1920]{1,0:T(8,128)(2,1)S(1)}, bf16[192,1920]{1,0:T(8,128)(2,1)S(1)}, u32[]{:S(2)}, u32[]{:S(2)}) collective-permute-start(bf16[192,1920]{1,0:T(8,128)(2,1)S(1)} %collective-permute-done.15.rest_1_), channel_id=1, source_target_pairs={{0,8},{9,1},{2,10},{11,3},{8,16},{17,9},{10,18},{19,11},{16,24},{2... | collective-permute-start | bytes 2211848 | tf_op jit(solution)/shard_map/ppermute | solution.py:558
  48.7 9.0 %collective-permute-start.12 = (bf16[3,192,256]{2,1,0:T(8,128)(2,1)S(1)}, bf16[3,192,256]{2,1,0:T(8,128)(2,1)S(1)}, u32[]{:S(2)}, u32[]{:S(2)}) collective-permute-start(bf16[3,192,256]{2,1,0:T(8,128)(2,1)S(1)} %get-tuple-element.178.refs_1_.rest_2_), channel_id=1, source_target_pairs={{0,2},{1,3},{2,0},{3,1},{4,6},{5,7},{6,4},{7,5},{8,10},{9,11},{10,... | collective-permute-start | bytes 884744 | tf_op jit(solution)/shard_map/ppermute | solution.py:529
  59.3 11.5 %collective-permute-start.20 = (bf16[192,1920]{1,0:T(8,128)(2,1)S(1)}, bf16[192,1920]{1,0:T(8,128)(2,1)S(1)}, u32[]{:S(2)}, u32[]{:S(2)}) collective-permute-start(bf16[192,1920]{1,0:T(8,128)(2,1)S(1)} %collective-permute-done.19.rest_2_), channel_id=1, source_target_pairs={{0,8},{9,1},{2,10},{11,3},{8,16},{17,9},{10,18},{19,11},{16,24},{2... | collective-permute-start | bytes 2211848 | tf_op jit(solution)/shard_map/ppermute | solution.py:558
  60.2 8.7 %collective-permute-start.13 = (bf16[3,192,256]{2,1,0:T(8,128)(2,1)S(1)}, bf16[3,192,256]{2,1,0:T(8,128)(2,1)S(1)}, u32[]{:S(2)}, u32[]{:S(2)}) collective-permute-start(bf16[3,192,256]{2,1,0:T(8,128)(2,1)S(1)} %get-tuple-element.179.rest_4_), channel_id=1, source_target_pairs={{0,3},{1,2},{2,1},{3,0},{4,7},{5,6},{6,5},{7,4},{8,11},{9,10},{10,... | collective-permute-start | bytes 884744 | tf_op jit(solution)/shard_map/ppermute | solution.py:529
  61.8 10.4 %collective-permute-start.22 = (bf16[192,1920]{1,0:T(8,128)(2,1)S(1)}, bf16[192,1920]{1,0:T(8,128)(2,1)S(1)}, u32[]{:S(2)}, u32[]{:S(2)}) collective-permute-start(bf16[192,1920]{1,0:T(8,128)(2,1)S(1)} %collective-permute-done.15.rest_1_), channel_id=1, source_target_pairs={{0,1},{1,0},{2,3},{3,2},{4,5},{5,4},{6,7},{7,6},{8,9},{9,8},{10,11... | collective-permute-start | bytes 2211848 | tf_op jit(solution)/shard_map/ppermute | solution.py:529
  61.8 10.4 %collective-permute-start.23 = (bf16[192,1920]{1,0:T(8,128)(2,1)S(1)}, bf16[192,1920]{1,0:T(8,128)(2,1)S(1)}, u32[]{:S(2)}, u32[]{:S(2)}) collective-permute-start(bf16[192,1920]{1,0:T(8,128)(2,1)S(1)} %collective-permute-done.19.rest_2_), channel_id=1, source_target_pairs={{0,1},{1,0},{2,3},{3,2},{4,5},{5,4},{6,7},{7,6},{8,9},{9,8},{10,11... | collective-permute-start | bytes 2211848 | tf_op jit(solution)/shard_map/ppermute | solution.py:529
  70.8 11.5 %collective-permute-start.21 = (bf16[192,1920]{1,0:T(8,128)(2,1)S(1)}, bf16[192,1920]{1,0:T(8,128)(2,1)S(1)}, u32[]{:S(2)}, u32[]{:S(2)}) collective-permute-start(bf16[192,1920]{1,0:T(8,128)(2,1)S(1)} %collective-permute-done.20.rest_3_), channel_id=1, source_target_pairs={{0,8},{9,1},{2,10},{11,3},{8,16},{17,9},{10,18},{19,11},{16,24},{2... | collective-permute-start | bytes 2211848 | tf_op jit(solution)/shard_map/ppermute | solution.py:558
  71.6 10.6 %collective-permute-start.24 = (bf16[192,1920]{1,0:T(8,128)(2,1)S(1)}, bf16[192,1920]{1,0:T(8,128)(2,1)S(1)}, u32[]{:S(2)}, u32[]{:S(2)}) collective-permute-start(bf16[192,1920]{1,0:T(8,128)(2,1)S(1)} %collective-permute-done.20.rest_3_), channel_id=1, source_target_pairs={{0,1},{1,0},{2,3},{3,2},{4,5},{5,4},{6,7},{7,6},{8,9},{9,8},{10,11... | collective-permute-start | bytes 2211848 | tf_op jit(solution)/shard_map/ppermute | solution.py:529
  71.7 11.8 %collective-permute-start.25 = (f32[1,768]{1,0:T(1,128)S(1)}, f32[1,768]{1,0:T(1,128)S(1)}, u32[]{:S(2)}, u32[]{:S(2)}) collective-permute-start(f32[1,768]{1,0:T(1,128)S(1)} %reshape.32.refs_15_), channel_id=1, source_target_pairs={{0,1},{1,0},{2,3},{3,2},{4,5},{5,4},{6,7},{7,6},{8,9},{9,8},{10,11... | collective-permute-start | bytes 9224 | tf_op jit(solution)/shard_map/ppermute | solution.py:529
  87.6 12.1 %collective-permute-start.27 = (bf16[1,256,768]{2,1,0:T(8,128)(2,1)S(1)}, bf16[1,256,768]{2,1,0:T(8,128)(2,1)S(1)}, u32[]{:S(2)}, u32[]{:S(2)}) collective-permute-start(bf16[1,256,768]{2,1,0:T(8,128)(2,1)S(1)} %get-tuple-element.210.refs_2_), channel_id=1, source_target_pairs={{0,2},{1,3},{2,0},{3,1},{4,6},{5,7},{6,4},{7,5},{8,10},{9,11},{10,... | collective-permute-start | bytes 1179656 | tf_op jit(solution)/shard_map/ppermute | solution.py:529
  92.4 15.7 %collective-permute-start.29 = (bf16[1,256,768]{2,1,0:T(8,128)(2,1)S(1)}, bf16[1,256,768]{2,1,0:T(8,128)(2,1)S(1)}, u32[]{:S(2)}, u32[]{:S(2)}) collective-permute-start(bf16[1,256,768]{2,1,0:T(8,128)(2,1)S(1)} %get-tuple-element.215.refs_2_), channel_id=1, source_target_pairs={{0,2},{1,3},{2,0},{3,1},{4,6},{5,7},{6,4},{7,5},{8,10},{9,11},{10,... | collective-permute-start | bytes 1179656 | tf_op jit(solution)/shard_map/ppermute | solution.py:529
  97.5 19.1 %collective-permute-start.26 = (bf16[1,256,768]{2,1,0:T(8,128)(2,1)S(1)}, bf16[1,256,768]{2,1,0:T(8,128)(2,1)S(1)}, u32[]{:S(2)}, u32[]{:S(2)}) collective-permute-start(bf16[1,256,768]{2,1,0:T(8,128)(2,1)S(1)} %get-tuple-element.209.refs_2_), channel_id=1, source_target_pairs={{0,2},{1,3},{2,0},{3,1},{4,6},{5,7},{6,4},{7,5},{8,10},{9,11},{10,... | collective-permute-start | bytes 1179656 | tf_op jit(solution)/shard_map/ppermute | solution.py:529
  103.4 18.7 %collective-permute-start.28 = (bf16[1,256,768]{2,1,0:T(8,128)(2,1)S(1)}, bf16[1,256,768]{2,1,0:T(8,128)(2,1)S(1)}, u32[]{:S(2)}, u32[]{:S(2)}) collective-permute-start(bf16[1,256,768]{2,1,0:T(8,128)(2,1)S(1)} %get-tuple-element.213.refs_2_), channel_id=1, source_target_pairs={{0,2},{1,3},{2,0},{3,1},{4,6},{5,7},{6,4},{7,5},{8,10},{9,11},{10,... | collective-permute-start | bytes 1179656 | tf_op jit(solution)/shard_map/ppermute | solution.py:529
  104.4 25.1 %collective-permute-start.35 = (bf16[3,256,768]{2,1,0:T(8,128)(2,1)S(1)}, bf16[3,256,768]{2,1,0:T(8,128)(2,1)S(1)}, u32[]{:S(2)}, u32[]{:S(2)}) collective-permute-start(bf16[3,256,768]{2,1,0:T(8,128)(2,1)S(1)} %get-tuple-element.246.rest_0_), channel_id=1, source_target_pairs={{0,1},{1,0},{2,3},{3,2},{4,5},{5,4},{6,7},{7,6},{8,9},{9,8},{10,11... | collective-permute-start | bytes 3538952 | tf_op jit(solution)/shard_map/ppermute | solution.py:529
  126.4 11.5 %collective-permute-start.32 = (bf16[1,256,768]{2,1,0:T(8,128)(2,1)S(1)}, bf16[1,256,768]{2,1,0:T(8,128)(2,1)S(1)}, u32[]{:S(2)}, u32[]{:S(2)}) collective-permute-start(bf16[1,256,768]{2,1,0:T(8,128)(2,1)S(1)} %get-tuple-element.241.refs_2_), channel_id=1, source_target_pairs={{0,2},{1,3},{2,0},{3,1},{4,6},{5,7},{6,4},{7,5},{8,10},{9,11},{10,... | collective-permute-start | bytes 1179656 | tf_op jit(solution)/shard_map/ppermute | solution.py:529
  139.5 15.0 %collective-permute-start.40 = (bf16[384,768]{1,0:T(8,128)(2,1)S(1)}, bf16[384,768]{1,0:T(8,128)(2,1)S(1)}, u32[]{:S(2)}, u32[]{:S(2)}) collective-permute-start(bf16[384,768]{1,0:T(8,128)(2,1)S(1)} %get-tuple-element.272), channel_id=1, source_target_pairs={{0,8},{4,12},{8,0},{12,4},{16,24},{20,28},{24,16},{28,20},{1,9},{5... | collective-permute-start | bytes 1769480 | tf_op jit(solution)/shard_map/ppermute | solution.py:532
  140.5 14.6 %collective-permute-start.39 = (bf16[384,768]{1,0:T(8,128)(2,1)S(1)}, bf16[384,768]{1,0:T(8,128)(2,1)S(1)}, u32[]{:S(2)}, u32[]{:S(2)}) collective-permute-start(bf16[384,768]{1,0:T(8,128)(2,1)S(1)} %get-tuple-element.270), channel_id=1, source_target_pairs={{0,4},{4,0},{8,12},{12,8},{16,20},{20,16},{24,28},{28,24},{1,5},{5... | collective-permute-start | bytes 1769480 | tf_op jit(solution)/shard_map/ppermute | solution.py:532
  141.1 12.7 %collective-permute-start.31 = (bf16[1,256,768]{2,1,0:T(8,128)(2,1)S(1)}, bf16[1,256,768]{2,1,0:T(8,128)(2,1)S(1)}, u32[]{:S(2)}, u32[]{:S(2)}) collective-permute-start(bf16[1,256,768]{2,1,0:T(8,128)(2,1)S(1)} %get-tuple-element.240.refs_2_), channel_id=1, source_target_pairs={{0,2},{1,3},{2,0},{3,1},{4,6},{5,7},{6,4},{7,5},{8,10},{9,11},{10,... | collective-permute-start | bytes 1179656 | tf_op jit(solution)/shard_map/ppermute | solution.py:529
  156.7 10.7 %collective-permute-start.45 = (bf16[3,256,768]{2,1,0:T(8,128)(2,1)S(1)}, bf16[3,256,768]{2,1,0:T(8,128)(2,1)S(1)}, u32[]{:S(2)}, u32[]{:S(2)}) collective-permute-start(bf16[3,256,768]{2,1,0:T(8,128)(2,1)S(1)} %get-tuple-element.296.rest_3_), channel_id=1, source_target_pairs={{0,1},{1,0},{2,3},{3,2},{4,5},{5,4},{6,7},{7,6},{8,9},{9,8},{10,11... | collective-permute-start | bytes 3538952 | tf_op jit(solution)/shard_map/ppermute | solution.py:529
  157.6 12.5 %collective-permute-start.57 = (bf16[192,768]{1,0:T(8,128)(2,1)S(1)}, bf16[192,768]{1,0:T(8,128)(2,1)S(1)}, u32[]{:S(2)}, u32[]{:S(2)}) collective-permute-start(bf16[192,768]{1,0:T(8,128)(2,1)S(1)} %get-tuple-element.312), channel_id=1, source_target_pairs={{0,8},{4,12},{8,0},{12,4},{16,24},{20,28},{24,16},{28,20},{1,9},{5... | collective-permute-start | bytes 884744 | tf_op jit(solution)/shard_map/ppermute | solution.py:532
  158.8 11.3 %collective-permute-start.58 = (bf16[192,768]{1,0:T(8,128)(2,1)S(1)}, bf16[192,768]{1,0:T(8,128)(2,1)S(1)}, u32[]{:S(2)}, u32[]{:S(2)}) collective-permute-start(bf16[192,768]{1,0:T(8,128)(2,1)S(1)} %get-tuple-element.314), channel_id=1, source_target_pairs={{0,4},{4,0},{8,12},{12,8},{16,20},{20,16},{24,28},{28,24},{1,5},{5... | collective-permute-start | bytes 884744 | tf_op jit(solution)/shard_map/ppermute | solution.py:532
  170.8 16.3 %collective-permute-start.59 = (bf16[192,768]{1,0:T(8,128)(2,1)S(1)}, bf16[192,768]{1,0:T(8,128)(2,1)S(1)}, u32[]{:S(2)}, u32[]{:S(2)}) collective-permute-start(bf16[192,768]{1,0:T(8,128)(2,1)S(1)} %get-tuple-element.316), channel_id=1, source_target_pairs={{0,16},{4,20},{8,24},{12,28},{16,0},{20,4},{24,8},{28,12},{1,17},{... | collective-permute-start | bytes 884744 | tf_op jit(solution)/shard_map/ppermute | solution.py:532
  171.6 17.6 %collective-permute-start.48 = (bf16[400,768]{1,0:T(8,128)(2,1)S(1)}, bf16[400,768]{1,0:T(8,128)(2,1)S(1)}, u32[]{:S(2)}, u32[]{:S(2)}) collective-permute-start(bf16[400,768]{1,0:T(8,128)(2,1)S(1)} %get-tuple-element.306), channel_id=1, source_target_pairs={{0,4},{4,0},{8,12},{12,8},{16,20},{20,16},{24,28},{28,24},{1,5},{5... | collective-permute-start | bytes 1843208 | tf_op jit(solution)/shard_map/ppermute | solution.py:532
  173.4 24.0 %collective-permute-start.43 = (bf16[3,192,512]{2,1,0:T(8,128)(2,1)S(1)}, bf16[3,192,512]{2,1,0:T(8,128)(2,1)S(1)}, u32[]{:S(2)}, u32[]{:S(2)}) collective-permute-start(bf16[3,192,512]{2,1,0:T(8,128)(2,1)S(1)} %get-tuple-element.292), channel_id=1, source_target_pairs={{0,1},{1,0},{2,3},{3,2},{4,5},{5,4},{6,7},{7,6},{8,9},{9,8},{10,11... | collective-permute-start | bytes 1769480 | tf_op jit(solution)/shard_map/ppermute | solution.py:529
  187.1 8.8 %collective-permute-start.60 = (bf16[192,768]{1,0:T(8,128)(2,1)S(1)}, bf16[192,768]{1,0:T(8,128)(2,1)S(1)}, u32[]{:S(2)}, u32[]{:S(2)}) collective-permute-start(bf16[192,768]{1,0:T(8,128)(2,1)S(1)} %add_convert_fusion.1.rest_0_), channel_id=1, source_target_pairs={{0,8},{8,16},{16,24},{24,28},{28,20},{20,12},{12,4},{4,0},{1,9},{9... | collective-permute-start | bytes 884744 | tf_op jit(solution)/shard_map/ppermute | solution.py:544
  187.2 10.2 %collective-permute-start.61 = (bf16[192,768]{1,0:T(8,128)(2,1)S(1)}, bf16[192,768]{1,0:T(8,128)(2,1)S(1)}, u32[]{:S(2)}, u32[]{:S(2)}) collective-permute-start(bf16[192,768]{1,0:T(8,128)(2,1)S(1)} %add_convert_fusion.1.rest_0_), channel_id=1, source_target_pairs={{8,0},{16,8},{24,16},{28,24},{20,28},{12,20},{4,12},{0,4},{9,1},{1... | collective-permute-start | bytes 884744 | tf_op jit(solution)/shard_map/ppermute | solution.py:544
  189.9 13.2 %collective-permute-start.49 = (bf16[208,768]{1,0:T(8,128)(2,1)S(1)}, bf16[208,768]{1,0:T(8,128)(2,1)S(1)}, u32[]{:S(2)}, u32[]{:S(2)}) collective-permute-start(bf16[208,768]{1,0:T(8,128)(2,1)S(1)} %get-tuple-element.308), channel_id=1, source_target_pairs={{0,8},{4,12},{8,0},{12,4},{16,24},{20,28},{24,16},{28,20},{1,9},{5... | collective-permute-start | bytes 958472 | tf_op jit(solution)/shard_map/ppermute | solution.py:532
  190.3 25.1 %collective-permute-start.30 = (bf16[3,192,256]{2,1,0:T(8,128)(2,1)S(1)}, bf16[3,192,256]{2,1,0:T(8,128)(2,1)}, u32[]{:S(2)}, u32[]{:S(2)}) collective-permute-start(bf16[3,192,256]{2,1,0:T(8,128)(2,1)S(1)} %get-tuple-element.235), channel_id=1, source_target_pairs={{0,1},{1,0},{2,3},{3,2},{4,5},{5,4},{6,7},{7,6},{8,9},{9,8},{10,11... | collective-permute-start | bytes 884744 | tf_op jit(solution)/shard_map/ppermute | solution.py:529
  195.9 29.4 %collective-permute-start.42 = (bf16[3,192,512]{2,1,0:T(8,128)(2,1)S(1)}, bf16[3,192,512]{2,1,0:T(8,128)(2,1)}, u32[]{:S(2)}, u32[]{:S(2)}) collective-permute-start(bf16[3,192,512]{2,1,0:T(8,128)(2,1)S(1)} %get-tuple-element.290), channel_id=1, source_target_pairs={{0,1},{1,0},{2,3},{3,2},{4,5},{5,4},{6,7},{7,6},{8,9},{9,8},{10,11... | collective-permute-start | bytes 1769480 | tf_op jit(solution)/shard_map/ppermute | solution.py:529
  197.4 18.6 %collective-permute-start.62 = (bf16[192,768]{1,0:T(8,128)(2,1)S(1)}, bf16[192,768]{1,0:T(8,128)(2,1)S(1)}, u32[]{:S(2)}, u32[]{:S(2)}) collective-permute-start(bf16[192,768]{1,0:T(8,128)(2,1)S(1)} %collective-permute-done.60.rest_1_), channel_id=1, source_target_pairs={{0,8},{8,16},{16,24},{24,28},{28,20},{20,12},{12,4},{4,0},{1,9},{9... | collective-permute-start | bytes 884744 | tf_op jit(solution)/shard_map/ppermute | solution.py:544
  198.4 26.9 %collective-permute-start.44 = (bf16[3,192,512]{2,1,0:T(8,128)(2,1)}, bf16[3,192,512]{2,1,0:T(8,128)(2,1)}, u32[]{:S(2)}, u32[]{:S(2)}) collective-permute-start(bf16[3,192,512]{2,1,0:T(8,128)(2,1)} %fusion.1), channel_id=1, source_target_pairs={{0,2},{1,3},{2,0},{3,1},{4,6},{5,7},{6,4},{7,5},{8,10},{9,11},{10,... | collective-permute-start | bytes 1769480 | tf_op jit(solution)/shard_map/ppermute | solution.py:529
  203.7 9.6 %collective-permute-start.50 = (bf16[112,768]{1,0:T(8,128)(2,1)S(1)}, bf16[112,768]{1,0:T(8,128)(2,1)S(1)}, u32[]{:S(2)}, u32[]{:S(2)}) collective-permute-start(bf16[112,768]{1,0:T(8,128)(2,1)S(1)} %get-tuple-element.310), channel_id=1, source_target_pairs={{0,16},{4,20},{8,24},{12,28},{16,0},{20,4},{24,8},{28,12},{1,17},{... | collective-permute-start | bytes 516104 | tf_op jit(solution)/shard_map/ppermute | solution.py:532
  213.3 9.9 %collective-permute-start.63 = (bf16[192,768]{1,0:T(8,128)(2,1)S(1)}, bf16[192,768]{1,0:T(8,128)(2,1)S(1)}, u32[]{:S(2)}, u32[]{:S(2)}) collective-permute-start(bf16[192,768]{1,0:T(8,128)(2,1)S(1)} %collective-permute-done.61.rest_2_), channel_id=1, source_target_pairs={{8,0},{16,8},{24,16},{28,24},{20,28},{12,20},{4,12},{0,4},{9,1},{1... | collective-permute-start | bytes 884744 | tf_op jit(solution)/shard_map/ppermute | solution.py:544
  215.4 7.8 %collective-permute-start.51 = (bf16[96,768]{1,0:T(8,128)(2,1)S(1)}, bf16[96,768]{1,0:T(8,128)(2,1)S(1)}, u32[]{:S(2)}, u32[]{:S(2)}) collective-permute-start(bf16[96,768]{1,0:T(8,128)(2,1)S(1)} %get-tuple-element.311.rest_0_), channel_id=1, source_target_pairs={{0,8},{8,16},{16,24},{24,28},{28,20},{20,12},{12,4},{4,0},{1,9},{9... | collective-permute-start | bytes 442376 | tf_op jit(solution)/shard_map/ppermute | solution.py:544
  216.0 9.0 %collective-permute-start.52 = (bf16[96,768]{1,0:T(8,128)(2,1)S(1)}, bf16[96,768]{1,0:T(8,128)(2,1)S(1)}, u32[]{:S(2)}, u32[]{:S(2)}) collective-permute-start(bf16[96,768]{1,0:T(8,128)(2,1)S(1)} %get-tuple-element.311.rest_0_), channel_id=1, source_target_pairs={{8,0},{16,8},{24,16},{28,24},{20,28},{12,20},{4,12},{0,4},{9,1},{1... | collective-permute-start | bytes 442376 | tf_op jit(solution)/shard_map/ppermute | solution.py:544
  223.2 13.0 %collective-permute-start.64 = (bf16[192,768]{1,0:T(8,128)(2,1)S(1)}, bf16[192,768]{1,0:T(8,128)(2,1)S(1)}, u32[]{:S(2)}, u32[]{:S(2)}) collective-permute-start(bf16[192,768]{1,0:T(8,128)(2,1)S(1)} %collective-permute-done.62.rest_3_), channel_id=1, source_target_pairs={{0,8},{8,16},{16,24},{24,28},{28,20},{20,12},{12,4},{4,0},{1,9},{9... | collective-permute-start | bytes 884744 | tf_op jit(solution)/shard_map/ppermute | solution.py:544
  223.2 10.3 %collective-permute-start.53 = (bf16[96,768]{1,0:T(8,128)(2,1)S(1)}, bf16[96,768]{1,0:T(8,128)(2,1)S(1)}, u32[]{:S(2)}, u32[]{:S(2)}) collective-permute-start(bf16[96,768]{1,0:T(8,128)(2,1)S(1)} %collective-permute-done.51.rest_1_), channel_id=1, source_target_pairs={{0,8},{8,16},{16,24},{24,28},{28,20},{20,12},{12,4},{4,0},{1,9},{9... | collective-permute-start | bytes 442376 | tf_op jit(solution)/shard_map/ppermute | solution.py:544
  225.0 8.6 %collective-permute-start.54 = (bf16[96,768]{1,0:T(8,128)(2,1)S(1)}, bf16[96,768]{1,0:T(8,128)(2,1)S(1)}, u32[]{:S(2)}, u32[]{:S(2)}) collective-permute-start(bf16[96,768]{1,0:T(8,128)(2,1)S(1)} %collective-permute-done.52.rest_2_), channel_id=1, source_target_pairs={{8,0},{16,8},{24,16},{28,24},{20,28},{12,20},{4,12},{0,4},{9,1},{1... | collective-permute-start | bytes 442376 | tf_op jit(solution)/shard_map/ppermute | solution.py:544
  227.6 10.4 %collective-permute-start.65 = (bf16[192,768]{1,0:T(8,128)(2,1)S(1)}, bf16[192,768]{1,0:T(8,128)(2,1)S(1)}, u32[]{:S(2)}, u32[]{:S(2)}) collective-permute-start(bf16[192,768]{1,0:T(8,128)(2,1)S(1)} %collective-permute-done.63.rest_4_), channel_id=1, source_target_pairs={{8,0},{16,8},{24,16},{28,24},{20,28},{12,20},{4,12},{0,4},{9,1},{1... | collective-permute-start | bytes 884744 | tf_op jit(solution)/shard_map/ppermute | solution.py:544
  233.6 7.5 %collective-permute-start.55 = (bf16[96,768]{1,0:T(8,128)(2,1)S(1)}, bf16[96,768]{1,0:T(8,128)(2,1)S(1)}, u32[]{:S(2)}, u32[]{:S(2)}) collective-permute-start(bf16[96,768]{1,0:T(8,128)(2,1)S(1)} %collective-permute-done.53.rest_3_), channel_id=1, source_target_pairs={{0,8},{8,16},{16,24},{24,28},{28,20},{20,12},{12,4},{4,0},{1,9},{9... | collective-permute-start | bytes 442376 | tf_op jit(solution)/shard_map/ppermute | solution.py:544
  236.2 8.3 %collective-permute-start.67 = (bf16[192,768]{1,0:T(8,128)(2,1)S(1)}, bf16[192,768]{1,0:T(8,128)(2,1)S(1)}, u32[]{:S(2)}, u32[]{:S(2)}) collective-permute-start(bf16[192,768]{1,0:T(8,128)(2,1)S(1)} %collective-permute-done.64.rest_5_), channel_id=1, source_target_pairs={{0,8},{8,16},{16,24},{24,28},{28,20},{20,12},{12,4},{4,0},{1,9},{9... | collective-permute-start | bytes 884744 | tf_op jit(solution)/shard_map/ppermute | solution.py:852
  (39 other events, 306.7 us)

commit v7 on v6

--- a/solution.py
+++ b/solution.py
@@ -135,7 +135,7 @@
 
 
 def down_kernel(
-    me_ref, n1_ref, pa_ref, pb_ref, dy0, dy1, dy2, dy3, bias_ref, gain_ref, shift_ref,
+    unroll, me_ref, n1_ref, pa_ref, pb_ref, dy0, dy1, dy2, dy3, bias_ref, gain_ref, shift_ref,
     big_a, big_b, gpa_ref, gpb_ref,
     act_own_ref, act_oth_ref, ds_ref, dsb_ref, da_ref, db_ref, vec_ref, bup_a_ref, bup_b_ref, part_ref,
     scr,
@@ -174,7 +174,7 @@
             dh_ref[0, :, lanes] = grad_hidden.astype(BF)
         return carry
 
-    lax.fori_loop(0, units // block, one_block, 0)
+    lax.fori_loop(0, units // block, one_block, 0, unroll=unroll)
     part_ref[0] = (dot_nt(da_ref[0], w1a[...]) + dot_nt(db_ref[0], w1b[...])).astype(BF)
 
 
@@ -689,7 +689,7 @@
     gc, x1_c = pp(gb, 1), pp(x1, 1)
 
     down = Stage(
-        down_kernel,
+        functools.partial(down_kernel, False),
         [
             sds3(width, half, BF), sds3(width, half, BF), sds3(half, full, F32),
             sds3(half, full, BF), sds3(half, units, BF), sds3(half, units, BF),
@@ -700,6 +700,8 @@
     part2, part2_y = [], []
     for row in range(rows):
         got = after(part_y[row], part2_y[0]) if row == 2 else part_y[row]
+        if row == rows - 1:
+            down.kernel = functools.partial(down_kernel, True)
         given = [(n1, "row"), (part[row], "all"), (got, "all")]
         given += [(d, "row") for d in (dy_mine, dy1, dy2, dy3)]
         given += [(w, "all") for w in (biases, gains, shifts, big_a, big_b)]

time: 249 us -> 249 us (level)
  no operation moved by 1% of the time
where the time goes in v7:
time: 249 us; the launch traced here: 248 us
  waiting for transfers between devices  105 us (42%)
  Pallas kernels  79.5 us (32%)
  starting transfers between devices  50.5 us (20%)
  other arithmetic  6.42 us (3%)
  local copies, waits for them, and re-layouts  5.38 us (2%)
    pallas_call x30, Pallas kernels, call(): pl.pallas_call(kernel, out_shape=outs, grid_spec=pltpu.PrefetchScalarGrid...  79.5 us
    ppermute x35, waiting for transfers between devices, pp(): return lax.ppermute(array, 'tensor', [(i, i ^ step) for i in range(4)])  32.6 us
    ppermute x8, waiting for transfers between devices, swap(): return lax.ppermute(array, 'dp', [(i, i ^ 1 << bit) for i in range(groups)])  27.5 us
    ppermute x35, starting transfers between devices, pp(): return lax.ppermute(array, 'tensor', [(i, i ^ step) for i in range(4)])  19.9 us
    ppermute x9, waiting for transfers between devices, ring_step(): lax.ppermute(ahead, 'dp', onward)  15.5 us
    ppermute x4, waiting for transfers between devices, pair_step(): return lax.ppermute(pair, ('dp', 'tensor'), both_ways)  13.5 us
    ppermute x9, waiting for transfers between devices, ring_step(): lax.ppermute(behind, 'dp', backward)  12.4 us
    ppermute x9, starting transfers between devices, ring_step(): lax.ppermute(behind, 'dp', backward)  10.4 us
  transfers between devices with their start and end apart: 68, of which 32 were waited for; matrix products, arithmetic and copies ran while one was open for 3% of the time, Pallas kernels for 28%

profile of v7, /device:TPU:0, one launch (start us, length us, event | category | flops | bytes accessed | tf_op | source)
XLA Modules:
  0.0 248.3 jit_solution(10055156441668880144)
XLA Ops:
  1.7 3.0 %collective-permute-start.1 = (bf16[96,192]{1,0:T(8,128)(2,1)S(1)}, bf16[96,192]{1,0:T(8,128)(2,1)S(1)}, u32[]{:S(2)}, u32[]{:S(2)}) collective-permute-start(bf16[96,192]{1,0:T(8,128)(2,1)S(1)} %bitcast.27), channel_id=1, source_target_pairs={{0,2},{1,3},{2,0},{3,1},{4,6},{5,7},{6,4},{7,5},{8,10},{9,11},{10,... | collective-permute-start | bytes 110600 | tf_op jit(solution)/shard_map/ppermute | solution.py:529
  6.4 1.6 collective-permute-start.4
  12.9 1.6 collective-permute-start.6
  14.9 2.9 %collective-permute-done.6.rest_3_ = bf16[96,576]{1,0:T(8,128)(2,1)S(1)} collective-permute-done((bf16[96,576]{1,0:T(8,128)(2,1)S(1)}, bf16[96,576]{1,0:T(8,128)(2,1)S(1)}, u32[]{:S(2)}, u32[]{:S(2)}) %collective-permute-start.6) | collective-permute-done | bytes 110624 | tf_op jit(solution)/shard_map/ppermute | solution.py:544
  17.8 1.6 collective-permute-done.7.rest_4_
  19.4 1.6 collective-permute-start.8
  21.4 2.8 %collective-permute-done.8.rest_5_ = bf16[96,576]{1,0:T(8,128)(2,1)S(1)} collective-permute-done((bf16[96,576]{1,0:T(8,128)(2,1)S(1)}, bf16[96,576]{1,0:T(8,128)(2,1)S(1)}, u32[]{:S(2)}, u32[]{:S(2)}) %collective-permute-start.8) | collective-permute-done | bytes 110624 | tf_op jit(solution)/shard_map/ppermute | solution.py:544
  24.3 1.6 collective-permute-done.9.rest_6_
  27.9 2.8 %collective-permute-done.10.rest_7_ = bf16[96,576]{1,0:T(8,128)(2,1)S(1)} collective-permute-done((bf16[96,576]{1,0:T(8,128)(2,1)S(1)}, bf16[96,576]{1,0:T(8,128)(2,1)S(1)}, u32[]{:S(2)}, u32[]{:S(2)}) %collective-permute-start.10) | collective-permute-done | bytes 110624 | tf_op jit(solution)/shard_map/ppermute | solution.py:581
  34.8 12.6 %attend.1 = (bf16[3,3,512,512]{3,2,1,0:T(8,128)(2,1)}, bf16[3,3,512,512]{3,2,1,0:T(8,128)(2,1)}, bf16[3,3,192,512]{3,2,1,0:T(8,128)(2,1)}, bf16[3,192,256]{2,1,0...) custom-call(s32[5]{0:T(128)S(1)} %stack.32.me_ref.refs_0_, ...), custom_call_target="tpu_custom_call" | custom-call | flops 10 | bytes 1 | tf_op jit(solution)/shard_map/attend/pallas_call | solution.py:489
  50.3 7.4 %collective-permute-done.12.refs_3_ = bf16[3,192,256]{2,1,0:T(8,128)(2,1)S(1)} collective-permute-done((bf16[3,192,256]{2,1,0:T(8,128)(2,1)S(1)}, bf16[3,192,256]{2,1,0:T(8,128)(2,1)S(1)}, u32[]{:S(2)}, u32[]{:S(2)}) %collective-permute-start.12) | collective-permute-done | bytes 294944 | tf_op jit(solution)/shard_map/ppermute | solution.py:529
  57.7 1.6 collective-permute-done.19.rest_2_
  60.2 1.6 collective-permute-start.13
  62.3 6.5 %collective-permute-done.13.refs_4_ = bf16[3,192,256]{2,1,0:T(8,128)(2,1)S(1)} collective-permute-done((bf16[3,192,256]{2,1,0:T(8,128)(2,1)S(1)}, bf16[3,192,256]{2,1,0:T(8,128)(2,1)S(1)}, u32[]{:S(2)}, u32[]{:S(2)}) %collective-permute-start.13) | collective-permute-done | bytes 294944 | tf_op jit(solution)/shard_map/ppermute | solution.py:529
  68.8 1.9 collective-permute-done.20.rest_3_
  72.3 10.0 %collective-permute-done.21.rest_4_ = bf16[192,1920]{1,0:T(8,128)(2,1)S(1)} collective-permute-done((bf16[192,1920]{1,0:T(8,128)(2,1)S(1)}, bf16[192,1920]{1,0:T(8,128)(2,1)S(1)}, u32[]{:S(2)}, u32[]{:S(2)}) %collective-permute-start.21) | collective-permute-done | bytes 737312 | tf_op jit(solution)/shard_map/ppermute | solution.py:558
  83.6 3.9 %up.3 = (f32[3,256,768]{2,1,0:T(8,128)S(1)}, f32[3,256,128]{2,1,0:T(8,128)S(1)}, bf16[3,256,768]{2,1,0:T(8,128)(2,1)S(1)}, bf16[3,256,768]{2,1,0:T(8,128)(2,1)S(...) custom-call(s32[5]{0:T(128)S(1)} %stack.32.me_ref.refs_0_, ...), custom_call_target="tpu_custom_call" | custom-call | flops 10 | bytes 1 | tf_op jit(solution)/shard_map/up/pallas_call | solution.py:489
  88.4 3.8 %up.4 = (f32[3,256,768]{2,1,0:T(8,128)S(1)}, f32[3,256,128]{2,1,0:T(8,128)S(1)}, bf16[3,256,768]{2,1,0:T(8,128)(2,1)S(1)}, bf16[3,256,768]{2,1,0:T(8,128)(2,1)S(...) custom-call(s32[5]{0:T(128)S(1)} %stack.32.me_ref.refs_0_, ...), custom_call_target="tpu_custom_call", output_to_operand_aliasing={{0}: (17, {}), {1}: (18, {}), {2}: (19, {}), {3}: (20, {}),... | custom-call | flops 10 | bytes 1 | tf_op jit(solution)/shard_map/up/pallas_call | solution.py:489
  93.4 3.8 %up.5 = (f32[3,256,768]{2,1,0:T(8,128)S(1)}, f32[3,256,128]{2,1,0:T(8,128)S(1)}, bf16[3,256,768]{2,1,0:T(8,128)(2,1)S(1)}, bf16[3,256,768]{2,1,0:T(8,128)(2,1)S(...) custom-call(s32[5]{0:T(128)S(1)} %stack.32.me_ref.refs_0_, ...), custom_call_target="tpu_custom_call", output_to_operand_aliasing={{0}: (17, {}), {1}: (18, {}), {2}: (19, {}), {3}: (20, {}),... | custom-call | flops 10 | bytes 1 | tf_op jit(solution)/shard_map/up/pallas_call | solution.py:489
  99.6 3.7 %down.3 = (bf16[3,192,256]{2,1,0:T(8,128)(2,1)S(1)}, bf16[3,192,256]{2,1,0:T(8,128)(2,1)S(1)}, f32[3,256,768]{2,1,0:T(8,128)S(1)}, bf16[3,256,768]{2,1,0:T(8,128...) custom-call(s32[5]{0:T(128)S(1)} %stack.32.me_ref.refs_0_, ...), custom_call_target="tpu_custom_call" | custom-call | flops 10 | bytes 1 | tf_op jit(solution)/shard_map/down/pallas_call | solution.py:489
  104.2 3.8 %collective-permute-done.29.refs_3_ = bf16[1,256,768]{2,1,0:T(8,128)(2,1)S(1)} collective-permute-done((bf16[1,256,768]{2,1,0:T(8,128)(2,1)S(1)}, bf16[1,256,768]{2,1,0:T(8,128)(2,1)S(1)}, u32[]{:S(2)}, u32[]{:S(2)}) %collective-permute-start.29) | collective-permute-done | bytes 393248 | tf_op jit(solution)/shard_map/ppermute | solution.py:529
  108.0 3.9 %down.4 = (bf16[3,192,256]{2,1,0:T(8,128)(2,1)S(1)}, bf16[3,192,256]{2,1,0:T(8,128)(2,1)S(1)}, f32[3,256,768]{2,1,0:T(8,128)S(1)}, bf16[3,256,768]{2,1,0:T(8,128...) custom-call(s32[5]{0:T(128)S(1)} %stack.32.me_ref.refs_0_, ...), custom_call_target="tpu_custom_call", output_to_operand_aliasing={{0}: (15, {}), {1}: (16, {}), {2}: (17, {}), {3}: (18, {}),... | custom-call | flops 10 | bytes 1 | tf_op jit(solution)/shard_map/down/pallas_call | solution.py:489
  111.9 4.5 %collective-permute-done.26.refs_3_ = bf16[1,256,768]{2,1,0:T(8,128)(2,1)S(1)} collective-permute-done((bf16[1,256,768]{2,1,0:T(8,128)(2,1)S(1)}, bf16[1,256,768]{2,1,0:T(8,128)(2,1)S(1)}, u32[]{:S(2)}, u32[]{:S(2)}) %collective-permute-start.26) | collective-permute-done | bytes 393248 | tf_op jit(solution)/shard_map/ppermute | solution.py:529
  116.4 5.5 %collective-permute-done.28.refs_3_ = bf16[1,256,768]{2,1,0:T(8,128)(2,1)S(1)} collective-permute-done((bf16[1,256,768]{2,1,0:T(8,128)(2,1)S(1)}, bf16[1,256,768]{2,1,0:T(8,128)(2,1)S(1)}, u32[]{:S(2)}, u32[]{:S(2)}) %collective-permute-start.28) | collective-permute-done | bytes 393248 | tf_op jit(solution)/shard_map/ppermute | solution.py:529
  121.9 3.4 %down.5 = (bf16[3,192,256]{2,1,0:T(8,128)(2,1)S(1)}, bf16[3,192,256]{2,1,0:T(8,128)(2,1)S(1)}, f32[3,256,768]{2,1,0:T(8,128)S(1)}, bf16[3,256,768]{2,1,0:T(8,128...) custom-call(s32[5]{0:T(128)S(1)} %stack.32.me_ref.refs_0_, ...), custom_call_target="tpu_custom_call", output_to_operand_aliasing={{0}: (15, {}), {1}: (16, {}), {2}: (17, {}), {3}: (18, {}),... | custom-call | flops 10 | bytes 1 | tf_op jit(solution)/shard_map/down/pallas_call | solution.py:489
  127.4 1.6 mid.3
  129.0 3.5 %ffn_grad.3 = (bf16[384,768]{1,0:T(8,128)(2,1)S(1)}, bf16[384,768]{1,0:T(8,128)(2,1)S(1)}) custom-call(s32[5]{0:T(128)S(1)} %stack.32.me_ref.refs_0_, bf16[3,256,768]{2,1,0:T(8,128)(2,1)S(1)} %get-tuple-element.246.rest_0_, bf16[3,256,768]{2,1,0:T(8,128)(2,1)S(1)} %collective-permute-done.35.rest_1_, bf16[3,256,768]{2,1,0:T(8,128)(2,1)S(1)} %get-tuple-element.247.rest_2_, ...), custom_call_target="tpu_custom_call" | custom-call | flops 30 | bytes 1 | tf_op jit(solution)/shard_map/ffn_grad/pallas_call | solution.py:489
  132.6 3.5 %ffn_grad.2 = (bf16[384,768]{1,0:T(8,128)(2,1)S(1)}, bf16[384,768]{1,0:T(8,128)(2,1)S(1)}) custom-call(s32[5]{0:T(128)S(1)} %stack.32.me_ref.refs_0_, bf16[3,256,768]{2,1,0:T(8,128)(2,1)S(1)} %get-tuple-element.242.rest_0_, bf16[3,256,768]{2,1,0:T(8,128)(2,1)S(1)} %collective-permute-done.33.rest_1_, bf16[3,256,768]{2,1,0:T(8,128)(2,1)S(1)} %get-tuple-element.244.rest_2_, ...), custom_call_target="tpu_custom_call" | custom-call | flops 30 | bytes 1 | tf_op jit(solution)/shard_map/ffn_grad/pallas_call | solution.py:489
  137.5 1.6 mid.4
  142.9 5.3 %back.3 = (bf16[3,3,512,512]{3,2,1,0:T(8,128)(2,1)}, bf16[3,576,512]{2,1,0:T(8,128)(2,1)S(1)}, bf16[3,192,512]{2,1,0:T(8,128)(2,1)S(1)}, bf16[3,192,512]{2,1,0:T...) custom-call(s32[5]{0:T(128)S(1)} %stack.32.me_ref.refs_0_, ...), custom_call_target="tpu_custom_call" | custom-call | flops 10 | bytes 1 | tf_op jit(solution)/shard_map/back/pallas_call | solution.py:489
  148.2 5.5 %back.4 = (bf16[3,3,512,512]{3,2,1,0:T(8,128)(2,1)}, bf16[3,576,512]{2,1,0:T(8,128)(2,1)S(1)}, bf16[3,192,512]{2,1,0:T(8,128)(2,1)S(1)}, bf16[3,192,512]{2,1,0:T...) custom-call(s32[5]{0:T(128)S(1)} %stack.32.me_ref.refs_0_, ...), custom_call_target="tpu_custom_call", output_to_operand_aliasing={{0}: (7, {}), {1}: (8, {}), {2}: (9, {}), {3}: (10, {}), {4... | custom-call | flops 10 | bytes 1 | tf_op jit(solution)/shard_map/back/pallas_call | solution.py:489
  154.7 1.6 mid.5
  162.3 4.6 %back.5 = (bf16[3,3,512,512]{3,2,1,0:T(8,128)(2,1)}, bf16[3,576,512]{2,1,0:T(8,128)(2,1)S(1)}, bf16[3,192,512]{2,1,0:T(8,128)(2,1)S(1)}, bf16[3,192,512]{2,1,0:T...) custom-call(s32[5]{0:T(128)S(1)} %stack.32.me_ref.refs_0_, ...), custom_call_target="tpu_custom_call", output_to_operand_aliasing={{0}: (7, {}), {1}: (8, {}), {2}: (9, {}), {3}: (10, {}), {4... | custom-call | flops 10 | bytes 1 | tf_op jit(solution)/shard_map/back/pallas_call | solution.py:489
  167.0 2.7 %qkv_grad.1 = (bf16[400,768]{1,0:T(8,128)(2,1)S(1)}, bf16[400,768]{1,0:T(8,128)(2,1)S(1)}) custom-call(s32[5]{0:T(128)S(1)} %stack.32.me_ref.refs_0_, bf16[3,768,512]{2,1,0:T(8,128)(2,1)S(1)} %copy-done.1, bf16[3,576,512]{2,1,0:T(8,128)(2,1)S(1)} %get-tuple-element.295.rest_1_, bf16[3,192,256]{2,1,0:T(8,128)(2,1)S(1)} %get-tuple-element.178.refs_1_.rest_2_, ...), custom_call_target="tpu_custom_call" | custom-call | flops 40 | bytes 1 | tf_op jit(solution)/shard_map/qkv_grad/pallas_call | solution.py:489
  171.2 1.7 collective-permute-start.48
  173.0 13.7 %collective-permute-done.59 = bf16[192,768]{1,0:T(8,128)(2,1)S(1)} collective-permute-done((bf16[192,768]{1,0:T(8,128)(2,1)S(1)}, bf16[192,768]{1,0:T(8,128)(2,1)S(1)}, u32[]{:S(2)}, u32[]{:S(2)}) %collective-permute-start.59) | collective-permute-done | bytes 294944 | tf_op jit(solution)/shard_map/ppermute | solution.py:532
  186.8 2.0 collective-permute-start.61
  189.7 5.8 %collective-permute-done.60.rest_1_ = bf16[192,768]{1,0:T(8,128)(2,1)S(1)} collective-permute-done((bf16[192,768]{1,0:T(8,128)(2,1)S(1)}, bf16[192,768]{1,0:T(8,128)(2,1)S(1)}, u32[]{:S(2)}, u32[]{:S(2)}) %collective-permute-start.60) | collective-permute-done | bytes 294944 | tf_op jit(solution)/shard_map/ppermute | solution.py:544
  198.9 3.5 %collective-permute-done.49.rest_1_ = bf16[208,768]{1,0:T(8,128)(2,1)S(1)} collective-permute-done((bf16[208,768]{1,0:T(8,128)(2,1)S(1)}, bf16[208,768]{1,0:T(8,128)(2,1)S(1)}, u32[]{:S(2)}, u32[]{:S(2)}) %collective-permute-start.49) | collective-permute-done | bytes 319520 | tf_op jit(solution)/shard_map/ppermute | solution.py:532
  203.6 9.3 %collective-permute-done.50.came = bf16[112,768]{1,0:T(8,128)(2,1)S(1)} collective-permute-done((bf16[112,768]{1,0:T(8,128)(2,1)S(1)}, bf16[112,768]{1,0:T(8,128)(2,1)S(1)}, u32[]{:S(2)}, u32[]{:S(2)}) %collective-permute-start.50) | collective-permute-done | bytes 172064 | tf_op jit(solution)/shard_map/ppermute | solution.py:532
  218.9 3.8 %collective-permute-done.63.rest_4_ = bf16[192,768]{1,0:T(8,128)(2,1)S(1)} collective-permute-done((bf16[192,768]{1,0:T(8,128)(2,1)S(1)}, bf16[192,768]{1,0:T(8,128)(2,1)S(1)}, u32[]{:S(2)}, u32[]{:S(2)}) %collective-permute-start.63) | collective-permute-done | bytes 294944 | tf_op jit(solution)/shard_map/ppermute | solution.py:544
  225.1 2.3 fusion
  227.4 1.7 collective-permute-start.65
  229.1 4.0 %collective-permute-done.53.rest_3_ = bf16[96,768]{1,0:T(8,128)(2,1)S(1)} collective-permute-done((bf16[96,768]{1,0:T(8,128)(2,1)S(1)}, bf16[96,768]{1,0:T(8,128)(2,1)S(1)}, u32[]{:S(2)}, u32[]{:S(2)}) %collective-permute-start.53) | collective-permute-done | bytes 147488 | tf_op jit(solution)/shard_map/ppermute | solution.py:544
  233.1 2.0 collective-permute-start.56
  235.8 1.8 collective-permute-done.65.rest_6_
  237.6 3.1 %finish.2 = (f32[768,768]{1,0:T(8,128)}, f32[768,768]{1,0:T(8,128)}) custom-call(s32[5]{0:T(128)S(1)} %stack.32.me_ref.refs_0_, bf16[192,768]{1,0:T(8,128)(2,1)S(1)} %add_convert_fusion.1.rest_0_, bf16[192,768]{1,0:T(8,128)(2,1)S(1)} %collective-permute-done.60.rest_1_, bf16[192,768]{1,0:T(8,128)(2,1)S(1)} %collective-permute-done.61.rest_2_, ...), custom_call_target="tpu_custom_call" | custom-call | flops 20 | bytes 1 | tf_op jit(solution)/shard_map/finish/pallas_call | solution.py:489
  245.9 2.4 finish.3
  (171 shorter events, 62.8 us)
Async XLA Ops:
  8.5 23.7 %collective-permute-start.2 = (bf16[3,192,512]{2,1,0:T(8,128)(2,1)}, bf16[3,192,512]{2,1,0:T(8,128)(2,1)S(1)}, u32[]{:S(2)}, u32[]{:S(2)}) collective-permute-start(bf16[3,192,512]{2,1,0:T(8,128)(2,1)} %bitcast.22), channel_id=1, source_target_pairs={{0,2},{1,3},{2,0},{3,1},{4,6},{5,7},{6,4},{7,5},{8,10},{9,11},{10,... | collective-permute-start | bytes 1769480 | tf_op jit(solution)/shard_map/ppermute | solution.py:529
  11.4 15.9 %collective-permute-start.14 = (bf16[96,1920]{1,0:T(8,128)(2,1)S(1)}, bf16[96,1920]{1,0:T(8,128)(2,1)S(1)}, u32[]{:S(2)}, u32[]{:S(2)}) collective-permute-start(bf16[96,1920]{1,0:T(8,128)(2,1)S(1)} %joined.5.first), channel_id=1, source_target_pairs={{0,1},{1,0},{2,3},{3,2},{4,5},{5,4},{6,7},{7,6},{8,9},{9,8},{10,11... | collective-permute-start | bytes 1105928 | tf_op jit(solution)/shard_map/ppermute | solution.py:529
  21.4 12.9 %collective-permute-start = (bf16[3,192,512]{2,1,0:T(8,128)(2,1)S(1)}, bf16[3,192,512]{2,1,0:T(8,128)(2,1)S(1)}, u32[]{:S(2)}, u32[]{:S(2)}) collective-permute-start(bf16[3,192,512]{2,1,0:T(8,128)(2,1)S(1)} %bitcast.23), channel_id=1, source_target_pairs={{0,1},{1,0},{2,3},{3,2},{4,5},{5,4},{6,7},{7,6},{8,9},{9,8},{10,11... | collective-permute-start | bytes 1769480 | tf_op jit(solution)/shard_map/ppermute | solution.py:529
  30.7 17.1 %collective-permute-start.15 = (bf16[192,1920]{1,0:T(8,128)(2,1)S(1)}, bf16[192,1920]{1,0:T(8,128)(2,1)S(1)}, u32[]{:S(2)}, u32[]{:S(2)}) collective-permute-start(bf16[192,1920]{1,0:T(8,128)(2,1)S(1)} %joined.6.rest_0_), channel_id=1, source_target_pairs={{0,8},{9,1},{2,10},{11,3},{8,16},{17,9},{10,18},{19,11},{16,24},{2... | collective-permute-start | bytes 2211848 | tf_op jit(solution)/shard_map/ppermute | solution.py:558
  32.8 14.6 %collective-permute-start.16 = (bf16[3,192,256]{2,1,0:T(8,128)(2,1)S(1)}, bf16[3,192,256]{2,1,0:T(8,128)(2,1)S(1)}, u32[]{:S(2)}, u32[]{:S(2)}) collective-permute-start(bf16[3,192,256]{2,1,0:T(8,128)(2,1)S(1)} %get-tuple-element.182), channel_id=1, source_target_pairs={{0,1},{1,0},{2,3},{3,2},{4,5},{5,4},{6,7},{7,6},{8,9},{9,8},{10,11... | collective-permute-start | bytes 884744 | tf_op jit(solution)/shard_map/ppermute | solution.py:529
  33.4 14.1 %collective-permute-start.17 = (bf16[3,192,256]{2,1,0:T(8,128)(2,1)S(1)}, bf16[3,192,256]{2,1,0:T(8,128)(2,1)S(1)}, u32[]{:S(2)}, u32[]{:S(2)}) collective-permute-start(bf16[3,192,256]{2,1,0:T(8,128)(2,1)S(1)} %get-tuple-element.183.refs_4_), channel_id=1, source_target_pairs={{0,2},{1,3},{2,0},{3,1},{4,6},{5,7},{6,4},{7,5},{8,10},{9,11},{10,... | collective-permute-start | bytes 884744 | tf_op jit(solution)/shard_map/ppermute | solution.py:529
  34.3 13.5 %collective-permute-start.18 = (bf16[3,192,256]{2,1,0:T(8,128)(2,1)S(1)}, bf16[3,192,256]{2,1,0:T(8,128)(2,1)S(1)}, u32[]{:S(2)}, u32[]{:S(2)}) collective-permute-start(bf16[3,192,256]{2,1,0:T(8,128)(2,1)S(1)} %get-tuple-element.182), channel_id=1, source_target_pairs={{0,3},{1,2},{2,1},{3,0},{4,7},{5,6},{6,5},{7,4},{8,11},{9,10},{10,... | collective-permute-start | bytes 884744 | tf_op jit(solution)/shard_map/ppermute | solution.py:529
  47.8 11.5 %collective-permute-start.19 = (bf16[192,1920]{1,0:T(8,128)(2,1)S(1)}, bf16[192,1920]{1,0:T(8,128)(2,1)S(1)}, u32[]{:S(2)}, u32[]{:S(2)}) collective-permute-start(bf16[192,1920]{1,0:T(8,128)(2,1)S(1)} %collective-permute-done.15.rest_1_), channel_id=1, source_target_pairs={{0,8},{9,1},{2,10},{11,3},{8,16},{17,9},{10,18},{19,11},{16,24},{2... | collective-permute-start | bytes 2211848 | tf_op jit(solution)/shard_map/ppermute | solution.py:558
  48.7 9.0 %collective-permute-start.12 = (bf16[3,192,256]{2,1,0:T(8,128)(2,1)S(1)}, bf16[3,192,256]{2,1,0:T(8,128)(2,1)S(1)}, u32[]{:S(2)}, u32[]{:S(2)}) collective-permute-start(bf16[3,192,256]{2,1,0:T(8,128)(2,1)S(1)} %get-tuple-element.178.refs_1_.rest_2_), channel_id=1, source_target_pairs={{0,2},{1,3},{2,0},{3,1},{4,6},{5,7},{6,4},{7,5},{8,10},{9,11},{10,... | collective-permute-start | bytes 884744 | tf_op jit(solution)/shard_map/ppermute | solution.py:529
  59.3 11.5 %collective-permute-start.20 = (bf16[192,1920]{1,0:T(8,128)(2,1)S(1)}, bf16[192,1920]{1,0:T(8,128)(2,1)S(1)}, u32[]{:S(2)}, u32[]{:S(2)}) collective-permute-start(bf16[192,1920]{1,0:T(8,128)(2,1)S(1)} %collective-permute-done.19.rest_2_), channel_id=1, source_target_pairs={{0,8},{9,1},{2,10},{11,3},{8,16},{17,9},{10,18},{19,11},{16,24},{2... | collective-permute-start | bytes 2211848 | tf_op jit(solution)/shard_map/ppermute | solution.py:558
  60.2 8.7 %collective-permute-start.13 = (bf16[3,192,256]{2,1,0:T(8,128)(2,1)S(1)}, bf16[3,192,256]{2,1,0:T(8,128)(2,1)S(1)}, u32[]{:S(2)}, u32[]{:S(2)}) collective-permute-start(bf16[3,192,256]{2,1,0:T(8,128)(2,1)S(1)} %get-tuple-element.179.rest_4_), channel_id=1, source_target_pairs={{0,3},{1,2},{2,1},{3,0},{4,7},{5,6},{6,5},{7,4},{8,11},{9,10},{10,... | collective-permute-start | bytes 884744 | tf_op jit(solution)/shard_map/ppermute | solution.py:529
  61.8 10.4 %collective-permute-start.22 = (bf16[192,1920]{1,0:T(8,128)(2,1)S(1)}, bf16[192,1920]{1,0:T(8,128)(2,1)S(1)}, u32[]{:S(2)}, u32[]{:S(2)}) collective-permute-start(bf16[192,1920]{1,0:T(8,128)(2,1)S(1)} %collective-permute-done.15.rest_1_), channel_id=1, source_target_pairs={{0,1},{1,0},{2,3},{3,2},{4,5},{5,4},{6,7},{7,6},{8,9},{9,8},{10,11... | collective-permute-start | bytes 2211848 | tf_op jit(solution)/shard_map/ppermute | solution.py:529
  61.8 10.4 %collective-permute-start.23 = (bf16[192,1920]{1,0:T(8,128)(2,1)S(1)}, bf16[192,1920]{1,0:T(8,128)(2,1)S(1)}, u32[]{:S(2)}, u32[]{:S(2)}) collective-permute-start(bf16[192,1920]{1,0:T(8,128)(2,1)S(1)} %collective-permute-done.19.rest_2_), channel_id=1, source_target_pairs={{0,1},{1,0},{2,3},{3,2},{4,5},{5,4},{6,7},{7,6},{8,9},{9,8},{10,11... | collective-permute-start | bytes 2211848 | tf_op jit(solution)/shard_map/ppermute | solution.py:529
  70.8 11.5 %collective-permute-start.21 = (bf16[192,1920]{1,0:T(8,128)(2,1)S(1)}, bf16[192,1920]{1,0:T(8,128)(2,1)S(1)}, u32[]{:S(2)}, u32[]{:S(2)}) collective-permute-start(bf16[192,1920]{1,0:T(8,128)(2,1)S(1)} %collective-permute-done.20.rest_3_), channel_id=1, source_target_pairs={{0,8},{9,1},{2,10},{11,3},{8,16},{17,9},{10,18},{19,11},{16,24},{2... | collective-permute-start | bytes 2211848 | tf_op jit(solution)/shard_map/ppermute | solution.py:558
  71.6 10.6 %collective-permute-start.24 = (bf16[192,1920]{1,0:T(8,128)(2,1)S(1)}, bf16[192,1920]{1,0:T(8,128)(2,1)S(1)}, u32[]{:S(2)}, u32[]{:S(2)}) collective-permute-start(bf16[192,1920]{1,0:T(8,128)(2,1)S(1)} %collective-permute-done.20.rest_3_), channel_id=1, source_target_pairs={{0,1},{1,0},{2,3},{3,2},{4,5},{5,4},{6,7},{7,6},{8,9},{9,8},{10,11... | collective-permute-start | bytes 2211848 | tf_op jit(solution)/shard_map/ppermute | solution.py:529
  71.7 11.8 %collective-permute-start.25 = (f32[1,768]{1,0:T(1,128)S(1)}, f32[1,768]{1,0:T(1,128)S(1)}, u32[]{:S(2)}, u32[]{:S(2)}) collective-permute-start(f32[1,768]{1,0:T(1,128)S(1)} %reshape.32.refs_15_), channel_id=1, source_target_pairs={{0,1},{1,0},{2,3},{3,2},{4,5},{5,4},{6,7},{7,6},{8,9},{9,8},{10,11... | collective-permute-start | bytes 9224 | tf_op jit(solution)/shard_map/ppermute | solution.py:529
  87.4 12.1 %collective-permute-start.27 = (bf16[1,256,768]{2,1,0:T(8,128)(2,1)S(1)}, bf16[1,256,768]{2,1,0:T(8,128)(2,1)S(1)}, u32[]{:S(2)}, u32[]{:S(2)}) collective-permute-start(bf16[1,256,768]{2,1,0:T(8,128)(2,1)S(1)} %get-tuple-element.210.refs_2_), channel_id=1, source_target_pairs={{0,2},{1,3},{2,0},{3,1},{4,6},{5,7},{6,4},{7,5},{8,10},{9,11},{10,... | collective-permute-start | bytes 1179656 | tf_op jit(solution)/shard_map/ppermute | solution.py:529
  92.3 15.7 %collective-permute-start.29 = (bf16[1,256,768]{2,1,0:T(8,128)(2,1)S(1)}, bf16[1,256,768]{2,1,0:T(8,128)(2,1)S(1)}, u32[]{:S(2)}, u32[]{:S(2)}) collective-permute-start(bf16[1,256,768]{2,1,0:T(8,128)(2,1)S(1)} %get-tuple-element.215.refs_2_), channel_id=1, source_target_pairs={{0,2},{1,3},{2,0},{3,1},{4,6},{5,7},{6,4},{7,5},{8,10},{9,11},{10,... | collective-permute-start | bytes 1179656 | tf_op jit(solution)/shard_map/ppermute | solution.py:529
  97.3 19.1 %collective-permute-start.26 = (bf16[1,256,768]{2,1,0:T(8,128)(2,1)S(1)}, bf16[1,256,768]{2,1,0:T(8,128)(2,1)S(1)}, u32[]{:S(2)}, u32[]{:S(2)}) collective-permute-start(bf16[1,256,768]{2,1,0:T(8,128)(2,1)S(1)} %get-tuple-element.209.refs_2_), channel_id=1, source_target_pairs={{0,2},{1,3},{2,0},{3,1},{4,6},{5,7},{6,4},{7,5},{8,10},{9,11},{10,... | collective-permute-start | bytes 1179656 | tf_op jit(solution)/shard_map/ppermute | solution.py:529
  103.3 18.7 %collective-permute-start.28 = (bf16[1,256,768]{2,1,0:T(8,128)(2,1)S(1)}, bf16[1,256,768]{2,1,0:T(8,128)(2,1)S(1)}, u32[]{:S(2)}, u32[]{:S(2)}) collective-permute-start(bf16[1,256,768]{2,1,0:T(8,128)(2,1)S(1)} %get-tuple-element.213.refs_2_), channel_id=1, source_target_pairs={{0,2},{1,3},{2,0},{3,1},{4,6},{5,7},{6,4},{7,5},{8,10},{9,11},{10,... | collective-permute-start | bytes 1179656 | tf_op jit(solution)/shard_map/ppermute | solution.py:529
  104.2 24.8 %collective-permute-start.35 = (bf16[3,256,768]{2,1,0:T(8,128)(2,1)S(1)}, bf16[3,256,768]{2,1,0:T(8,128)(2,1)S(1)}, u32[]{:S(2)}, u32[]{:S(2)}) collective-permute-start(bf16[3,256,768]{2,1,0:T(8,128)(2,1)S(1)} %get-tuple-element.246.rest_0_), channel_id=1, source_target_pairs={{0,1},{1,0},{2,3},{3,2},{4,5},{5,4},{6,7},{7,6},{8,9},{9,8},{10,11... | collective-permute-start | bytes 3538952 | tf_op jit(solution)/shard_map/ppermute | solution.py:529
  126.0 11.5 %collective-permute-start.32 = (bf16[1,256,768]{2,1,0:T(8,128)(2,1)S(1)}, bf16[1,256,768]{2,1,0:T(8,128)(2,1)S(1)}, u32[]{:S(2)}, u32[]{:S(2)}) collective-permute-start(bf16[1,256,768]{2,1,0:T(8,128)(2,1)S(1)} %get-tuple-element.241.refs_2_), channel_id=1, source_target_pairs={{0,2},{1,3},{2,0},{3,1},{4,6},{5,7},{6,4},{7,5},{8,10},{9,11},{10,... | collective-permute-start | bytes 1179656 | tf_op jit(solution)/shard_map/ppermute | solution.py:529
  139.1 15.0 %collective-permute-start.40 = (bf16[384,768]{1,0:T(8,128)(2,1)S(1)}, bf16[384,768]{1,0:T(8,128)(2,1)S(1)}, u32[]{:S(2)}, u32[]{:S(2)}) collective-permute-start(bf16[384,768]{1,0:T(8,128)(2,1)S(1)} %get-tuple-element.272), channel_id=1, source_target_pairs={{0,8},{4,12},{8,0},{12,4},{16,24},{20,28},{24,16},{28,20},{1,9},{5... | collective-permute-start | bytes 1769480 | tf_op jit(solution)/shard_map/ppermute | solution.py:532
  140.0 14.6 %collective-permute-start.39 = (bf16[384,768]{1,0:T(8,128)(2,1)S(1)}, bf16[384,768]{1,0:T(8,128)(2,1)S(1)}, u32[]{:S(2)}, u32[]{:S(2)}) collective-permute-start(bf16[384,768]{1,0:T(8,128)(2,1)S(1)} %get-tuple-element.270), channel_id=1, source_target_pairs={{0,4},{4,0},{8,12},{12,8},{16,20},{20,16},{24,28},{28,24},{1,5},{5... | collective-permute-start | bytes 1769480 | tf_op jit(solution)/shard_map/ppermute | solution.py:532
  140.7 13.0 %collective-permute-start.31 = (bf16[1,256,768]{2,1,0:T(8,128)(2,1)S(1)}, bf16[1,256,768]{2,1,0:T(8,128)(2,1)S(1)}, u32[]{:S(2)}, u32[]{:S(2)}) collective-permute-start(bf16[1,256,768]{2,1,0:T(8,128)(2,1)S(1)} %get-tuple-element.240.refs_2_), channel_id=1, source_target_pairs={{0,2},{1,3},{2,0},{3,1},{4,6},{5,7},{6,4},{7,5},{8,10},{9,11},{10,... | collective-permute-start | bytes 1179656 | tf_op jit(solution)/shard_map/ppermute | solution.py:529
  156.3 10.7 %collective-permute-start.45 = (bf16[3,256,768]{2,1,0:T(8,128)(2,1)S(1)}, bf16[3,256,768]{2,1,0:T(8,128)(2,1)S(1)}, u32[]{:S(2)}, u32[]{:S(2)}) collective-permute-start(bf16[3,256,768]{2,1,0:T(8,128)(2,1)S(1)} %get-tuple-element.296.rest_3_), channel_id=1, source_target_pairs={{0,1},{1,0},{2,3},{3,2},{4,5},{5,4},{6,7},{7,6},{8,9},{9,8},{10,11... | collective-permute-start | bytes 3538952 | tf_op jit(solution)/shard_map/ppermute | solution.py:529
  157.2 12.5 %collective-permute-start.57 = (bf16[192,768]{1,0:T(8,128)(2,1)S(1)}, bf16[192,768]{1,0:T(8,128)(2,1)S(1)}, u32[]{:S(2)}, u32[]{:S(2)}) collective-permute-start(bf16[192,768]{1,0:T(8,128)(2,1)S(1)} %get-tuple-element.312), channel_id=1, source_target_pairs={{0,8},{4,12},{8,0},{12,4},{16,24},{20,28},{24,16},{28,20},{1,9},{5... | collective-permute-start | bytes 884744 | tf_op jit(solution)/shard_map/ppermute | solution.py:532
  158.4 11.3 %collective-permute-start.58 = (bf16[192,768]{1,0:T(8,128)(2,1)S(1)}, bf16[192,768]{1,0:T(8,128)(2,1)S(1)}, u32[]{:S(2)}, u32[]{:S(2)}) collective-permute-start(bf16[192,768]{1,0:T(8,128)(2,1)S(1)} %get-tuple-element.314), channel_id=1, source_target_pairs={{0,4},{4,0},{8,12},{12,8},{16,20},{20,16},{24,28},{28,24},{1,5},{5... | collective-permute-start | bytes 884744 | tf_op jit(solution)/shard_map/ppermute | solution.py:532
  170.4 16.3 %collective-permute-start.59 = (bf16[192,768]{1,0:T(8,128)(2,1)S(1)}, bf16[192,768]{1,0:T(8,128)(2,1)S(1)}, u32[]{:S(2)}, u32[]{:S(2)}) collective-permute-start(bf16[192,768]{1,0:T(8,128)(2,1)S(1)} %get-tuple-element.316), channel_id=1, source_target_pairs={{0,16},{4,20},{8,24},{12,28},{16,0},{20,4},{24,8},{28,12},{1,17},{... | collective-permute-start | bytes 884744 | tf_op jit(solution)/shard_map/ppermute | solution.py:532
  171.2 17.6 %collective-permute-start.48 = (bf16[400,768]{1,0:T(8,128)(2,1)S(1)}, bf16[400,768]{1,0:T(8,128)(2,1)S(1)}, u32[]{:S(2)}, u32[]{:S(2)}) collective-permute-start(bf16[400,768]{1,0:T(8,128)(2,1)S(1)} %get-tuple-element.306), channel_id=1, source_target_pairs={{0,4},{4,0},{8,12},{12,8},{16,20},{20,16},{24,28},{28,24},{1,5},{5... | collective-permute-start | bytes 1843208 | tf_op jit(solution)/shard_map/ppermute | solution.py:532
  173.0 23.8 %collective-permute-start.43 = (bf16[3,192,512]{2,1,0:T(8,128)(2,1)S(1)}, bf16[3,192,512]{2,1,0:T(8,128)(2,1)S(1)}, u32[]{:S(2)}, u32[]{:S(2)}) collective-permute-start(bf16[3,192,512]{2,1,0:T(8,128)(2,1)S(1)} %get-tuple-element.292), channel_id=1, source_target_pairs={{0,1},{1,0},{2,3},{3,2},{4,5},{5,4},{6,7},{7,6},{8,9},{9,8},{10,11... | collective-permute-start | bytes 1769480 | tf_op jit(solution)/shard_map/ppermute | solution.py:529
  186.7 8.8 %collective-permute-start.60 = (bf16[192,768]{1,0:T(8,128)(2,1)S(1)}, bf16[192,768]{1,0:T(8,128)(2,1)S(1)}, u32[]{:S(2)}, u32[]{:S(2)}) collective-permute-start(bf16[192,768]{1,0:T(8,128)(2,1)S(1)} %add_convert_fusion.1.rest_0_), channel_id=1, source_target_pairs={{0,8},{8,16},{16,24},{24,28},{28,20},{20,12},{12,4},{4,0},{1,9},{9... | collective-permute-start | bytes 884744 | tf_op jit(solution)/shard_map/ppermute | solution.py:544
  186.8 10.0 %collective-permute-start.61 = (bf16[192,768]{1,0:T(8,128)(2,1)S(1)}, bf16[192,768]{1,0:T(8,128)(2,1)S(1)}, u32[]{:S(2)}, u32[]{:S(2)}) collective-permute-start(bf16[192,768]{1,0:T(8,128)(2,1)S(1)} %add_convert_fusion.1.rest_0_), channel_id=1, source_target_pairs={{8,0},{16,8},{24,16},{28,24},{20,28},{12,20},{4,12},{0,4},{9,1},{1... | collective-permute-start | bytes 884744 | tf_op jit(solution)/shard_map/ppermute | solution.py:544
  189.5 12.9 %collective-permute-start.49 = (bf16[208,768]{1,0:T(8,128)(2,1)S(1)}, bf16[208,768]{1,0:T(8,128)(2,1)S(1)}, u32[]{:S(2)}, u32[]{:S(2)}) collective-permute-start(bf16[208,768]{1,0:T(8,128)(2,1)S(1)} %get-tuple-element.308), channel_id=1, source_target_pairs={{0,8},{4,12},{8,0},{12,4},{16,24},{20,28},{24,16},{28,20},{1,9},{5... | collective-permute-start | bytes 958472 | tf_op jit(solution)/shard_map/ppermute | solution.py:532
  189.6 25.3 %collective-permute-start.30 = (bf16[3,192,256]{2,1,0:T(8,128)(2,1)S(1)}, bf16[3,192,256]{2,1,0:T(8,128)(2,1)}, u32[]{:S(2)}, u32[]{:S(2)}) collective-permute-start(bf16[3,192,256]{2,1,0:T(8,128)(2,1)S(1)} %get-tuple-element.235), channel_id=1, source_target_pairs={{0,1},{1,0},{2,3},{3,2},{4,5},{5,4},{6,7},{7,6},{8,9},{9,8},{10,11... | collective-permute-start | bytes 884744 | tf_op jit(solution)/shard_map/ppermute | solution.py:529
  195.5 29.6 %collective-permute-start.42 = (bf16[3,192,512]{2,1,0:T(8,128)(2,1)S(1)}, bf16[3,192,512]{2,1,0:T(8,128)(2,1)}, u32[]{:S(2)}, u32[]{:S(2)}) collective-permute-start(bf16[3,192,512]{2,1,0:T(8,128)(2,1)S(1)} %get-tuple-element.290), channel_id=1, source_target_pairs={{0,1},{1,0},{2,3},{3,2},{4,5},{5,4},{6,7},{7,6},{8,9},{9,8},{10,11... | collective-permute-start | bytes 1769480 | tf_op jit(solution)/shard_map/ppermute | solution.py:529
  196.7 18.8 %collective-permute-start.62 = (bf16[192,768]{1,0:T(8,128)(2,1)S(1)}, bf16[192,768]{1,0:T(8,128)(2,1)S(1)}, u32[]{:S(2)}, u32[]{:S(2)}) collective-permute-start(bf16[192,768]{1,0:T(8,128)(2,1)S(1)} %collective-permute-done.60.rest_1_), channel_id=1, source_target_pairs={{0,8},{8,16},{16,24},{24,28},{28,20},{20,12},{12,4},{4,0},{1,9},{9... | collective-permute-start | bytes 884744 | tf_op jit(solution)/shard_map/ppermute | solution.py:544
  197.7 27.4 %collective-permute-start.44 = (bf16[3,192,512]{2,1,0:T(8,128)(2,1)}, bf16[3,192,512]{2,1,0:T(8,128)(2,1)}, u32[]{:S(2)}, u32[]{:S(2)}) collective-permute-start(bf16[3,192,512]{2,1,0:T(8,128)(2,1)} %fusion.1), channel_id=1, source_target_pairs={{0,2},{1,3},{2,0},{3,1},{4,6},{5,7},{6,4},{7,5},{8,10},{9,11},{10,... | collective-permute-start | bytes 1769480 | tf_op jit(solution)/shard_map/ppermute | solution.py:529
  203.0 9.8 %collective-permute-start.50 = (bf16[112,768]{1,0:T(8,128)(2,1)S(1)}, bf16[112,768]{1,0:T(8,128)(2,1)S(1)}, u32[]{:S(2)}, u32[]{:S(2)}) collective-permute-start(bf16[112,768]{1,0:T(8,128)(2,1)S(1)} %get-tuple-element.310), channel_id=1, source_target_pairs={{0,16},{4,20},{8,24},{12,28},{16,0},{20,4},{24,8},{28,12},{1,17},{... | collective-permute-start | bytes 516104 | tf_op jit(solution)/shard_map/ppermute | solution.py:532
  212.9 9.9 %collective-permute-start.63 = (bf16[192,768]{1,0:T(8,128)(2,1)S(1)}, bf16[192,768]{1,0:T(8,128)(2,1)S(1)}, u32[]{:S(2)}, u32[]{:S(2)}) collective-permute-start(bf16[192,768]{1,0:T(8,128)(2,1)S(1)} %collective-permute-done.61.rest_2_), channel_id=1, source_target_pairs={{8,0},{16,8},{24,16},{28,24},{20,28},{12,20},{4,12},{0,4},{9,1},{1... | collective-permute-start | bytes 884744 | tf_op jit(solution)/shard_map/ppermute | solution.py:544
  215.0 7.8 %collective-permute-start.51 = (bf16[96,768]{1,0:T(8,128)(2,1)S(1)}, bf16[96,768]{1,0:T(8,128)(2,1)S(1)}, u32[]{:S(2)}, u32[]{:S(2)}) collective-permute-start(bf16[96,768]{1,0:T(8,128)(2,1)S(1)} %get-tuple-element.311.rest_0_), channel_id=1, source_target_pairs={{0,8},{8,16},{16,24},{24,28},{28,20},{20,12},{12,4},{4,0},{1,9},{9... | collective-permute-start | bytes 442376 | tf_op jit(solution)/shard_map/ppermute | solution.py:544
  215.5 9.3 %collective-permute-start.52 = (bf16[96,768]{1,0:T(8,128)(2,1)S(1)}, bf16[96,768]{1,0:T(8,128)(2,1)S(1)}, u32[]{:S(2)}, u32[]{:S(2)}) collective-permute-start(bf16[96,768]{1,0:T(8,128)(2,1)S(1)} %get-tuple-element.311.rest_0_), channel_id=1, source_target_pairs={{8,0},{16,8},{24,16},{28,24},{20,28},{12,20},{4,12},{0,4},{9,1},{1... | collective-permute-start | bytes 442376 | tf_op jit(solution)/shard_map/ppermute | solution.py:544
  222.8 13.0 %collective-permute-start.64 = (bf16[192,768]{1,0:T(8,128)(2,1)S(1)}, bf16[192,768]{1,0:T(8,128)(2,1)S(1)}, u32[]{:S(2)}, u32[]{:S(2)}) collective-permute-start(bf16[192,768]{1,0:T(8,128)(2,1)S(1)} %collective-permute-done.62.rest_3_), channel_id=1, source_target_pairs={{0,8},{8,16},{16,24},{24,28},{28,20},{20,12},{12,4},{4,0},{1,9},{9... | collective-permute-start | bytes 884744 | tf_op jit(solution)/shard_map/ppermute | solution.py:544
  222.8 10.3 %collective-permute-start.53 = (bf16[96,768]{1,0:T(8,128)(2,1)S(1)}, bf16[96,768]{1,0:T(8,128)(2,1)S(1)}, u32[]{:S(2)}, u32[]{:S(2)}) collective-permute-start(bf16[96,768]{1,0:T(8,128)(2,1)S(1)} %collective-permute-done.51.rest_1_), channel_id=1, source_target_pairs={{0,8},{8,16},{16,24},{24,28},{28,20},{20,12},{12,4},{4,0},{1,9},{9... | collective-permute-start | bytes 442376 | tf_op jit(solution)/shard_map/ppermute | solution.py:544
  224.8 8.3 %collective-permute-start.54 = (bf16[96,768]{1,0:T(8,128)(2,1)S(1)}, bf16[96,768]{1,0:T(8,128)(2,1)S(1)}, u32[]{:S(2)}, u32[]{:S(2)}) collective-permute-start(bf16[96,768]{1,0:T(8,128)(2,1)S(1)} %collective-permute-done.52.rest_2_), channel_id=1, source_target_pairs={{8,0},{16,8},{24,16},{28,24},{20,28},{12,20},{4,12},{0,4},{9,1},{1... | collective-permute-start | bytes 442376 | tf_op jit(solution)/shard_map/ppermute | solution.py:544
  227.4 10.2 %collective-permute-start.65 = (bf16[192,768]{1,0:T(8,128)(2,1)S(1)}, bf16[192,768]{1,0:T(8,128)(2,1)S(1)}, u32[]{:S(2)}, u32[]{:S(2)}) collective-permute-start(bf16[192,768]{1,0:T(8,128)(2,1)S(1)} %collective-permute-done.63.rest_4_), channel_id=1, source_target_pairs={{8,0},{16,8},{24,16},{28,24},{20,28},{12,20},{4,12},{0,4},{9,1},{1... | collective-permute-start | bytes 884744 | tf_op jit(solution)/shard_map/ppermute | solution.py:544
  233.1 7.6 %collective-permute-start.55 = (bf16[96,768]{1,0:T(8,128)(2,1)S(1)}, bf16[96,768]{1,0:T(8,128)(2,1)S(1)}, u32[]{:S(2)}, u32[]{:S(2)}) collective-permute-start(bf16[96,768]{1,0:T(8,128)(2,1)S(1)} %collective-permute-done.53.rest_3_), channel_id=1, source_target_pairs={{0,8},{8,16},{16,24},{24,28},{28,20},{20,12},{12,4},{4,0},{1,9},{9... | collective-permute-start | bytes 442376 | tf_op jit(solution)/shard_map/ppermute | solution.py:544
  235.7 8.3 %collective-permute-start.67 = (bf16[192,768]{1,0:T(8,128)(2,1)S(1)}, bf16[192,768]{1,0:T(8,128)(2,1)S(1)}, u32[]{:S(2)}, u32[]{:S(2)}) collective-permute-start(bf16[192,768]{1,0:T(8,128)(2,1)S(1)} %collective-permute-done.64.rest_5_), channel_id=1, source_target_pairs={{0,8},{8,16},{16,24},{24,28},{28,20},{20,12},{12,4},{4,0},{1,9},{9... | collective-permute-start | bytes 884744 | tf_op jit(solution)/shard_map/ppermute | solution.py:854
  (39 other events, 305.5 us)
